TPU v7x, 32 devices: a whole 2x2x4 slice. The times are simulated.
32 devices in a mesh: fsdp: 4 (over y, x), ctx: 8 (over z, core).
Axes of the slice: x: 2, y: 2, z: 4, core: 2. Of those that a mesh axis runs over, the one named last changes fastest.
Arguments:
- tokens: bfloat16 [4, 1024, 2048], P('fsdp', 'ctx'), may hold values from -6 to 6
- cotangent: bfloat16 [4, 1024, 2048], P('fsdp', 'ctx'), may hold values from -6 to 6
- lengths: int32 [4], P('fsdp'), may hold values from 256 to 1024, as said below
- attn_gain: bfloat16 [2048], P('fsdp'), may hold values from 0.5 to 1.5
- w_query: bfloat16 [2048, 2048], P('fsdp'), may hold values from -0.125 to 0.125
- w_key: bfloat16 [2048, 256], P('fsdp'), may hold values from -0.125 to 0.125
- w_value: bfloat16 [2048, 256], P('fsdp'), may hold values from -0.125 to 0.125
- w_out: bfloat16 [2048, 2048], P('fsdp'), may hold values from -1 to 1
- mlp_gain: bfloat16 [2048], P('fsdp'), may hold values from 0.5 to 1.5
- w_gate: bfloat16 [2048, 5632], P('fsdp'), may hold values from -0.125 to 0.125
- w_up: bfloat16 [2048, 5632], P('fsdp'), may hold values from -0.125 to 0.125
- w_down: bfloat16 [5632, 2048], P('fsdp'), may hold values from -0.078125 to 0.078125
Outputs:
- outputs: float32 [4, 1024, 2048], P('fsdp', 'ctx')
- input_grad: float32 [4, 1024, 2048], P('fsdp', 'ctx')
- attn_gain_grad: float32 [2048], P('fsdp')
- query_grad: float32 [2048, 2048], P('fsdp')
- key_grad: float32 [2048, 256], P('fsdp')
- value_grad: float32 [2048, 256], P('fsdp')
- out_grad: float32 [2048, 2048], P('fsdp')
- mlp_gain_grad: float32 [2048], P('fsdp')
- gate_grad: float32 [2048, 5632], P('fsdp')
- up_grad: float32 [2048, 5632], P('fsdp')
- down_grad: float32 [5632, 2048], P('fsdp')
Inputs may be any that keep to these rules, and one draw needn't show every extreme that they name: Each slot holds 256 to 1024 valid positions, which lie at the slot's end (rows 1024 - lengths to 1023); the rows before them are padding. One slot is full and one holds exactly 256.
All inputs are finite; a program needn't handle non-finite values.
Results may differ from a plain program's by a relative error of at most 0.024.
Values may be sent and summed in bfloat16 or wider, within the bound.
A program may use at most 512 MiB of HBM per device.

v0:
```python
import jax
import jax.numpy as jnp
from jax import lax
from jax.sharding import PartitionSpec as P

HEADS = 32
KV_HEADS = 4
HEAD_DIM = 64


EPSILON = 1e-05
ROPE_BASE = 10000.0
MASKED = -1e30


def passed_along(value, axis, steps):
    count = lax.axis_size(axis)
    initial, last = (max(0, -steps), min(count, count - steps))
    return lax.ppermute(value, axis, [(source, source + steps) for source in range(initial, last)])


def rope_tables(positions, head_dim):
    half_dim = head_dim // 2
    frequency = jnp.power(ROPE_BASE, jnp.arange(half_dim, dtype=jnp.float32) * (-2.0 / head_dim))
    angles = positions.astype(jnp.float32)[:, None] * frequency[None, :]
    return (jnp.cos(angles), jnp.sin(angles))


def rotate(tensor, cosine, sine_table):
    half_dim = tensor.shape[-1] // 2
    leading = tensor[..., :half_dim]
    trailing = tensor[..., half_dim:]
    cosine = cosine[:, None, :]
    sine_table = sine_table[:, None, :]
    return jnp.concatenate(
        [leading * cosine - trailing * sine_table, trailing * cosine + leading * sine_table],
        axis=-1,
    )


def unrotate(tensor, cosine, sine_table):
    half_dim = tensor.shape[-1] // 2
    leading = tensor[..., :half_dim]
    trailing = tensor[..., half_dim:]
    cosine = cosine[:, None, :]
    sine_table = sine_table[:, None, :]
    return jnp.concatenate(
        [leading * cosine + trailing * sine_table, trailing * cosine - leading * sine_table],
        axis=-1,
    )


def rms_forward(row_block, gain_vec):
    inverse = lax.rsqrt(jnp.mean(row_block * row_block, axis=1, keepdims=True) + EPSILON)
    return (inverse, (row_block * inverse * gain_vec).astype(jnp.bfloat16))


def rms_backward(row_block, inverse, gain_vec, gradient):
    normed = row_block * inverse
    gain_grad = jnp.sum(gradient * normed, axis=0)
    scaled = gradient * gain_vec
    back = inverse * (scaled - normed * jnp.mean(scaled * normed, axis=1, keepdims=True))
    return (back, gain_grad)


def score_block(queries, key_blk, query_pos, key_pos, lengths, score_scale):
    scores = (
        jnp.einsum("sqkgd,stkd->skgqt", queries, key_blk, preferred_element_type=jnp.float32)
        * score_scale
    )
    allowed = (
        (key_pos[None, None, :] <= query_pos[None, :, None])
        & (key_pos[None, None, :] < lengths[:, None, None])
        & (key_pos[None, None, :] >= 0)
    )
    return (scores, allowed[:, None, None])


def forward_block(running, queries, key_blk, value_blk, query_pos, key_pos, lengths, score_scale):
    running_max, running_sum, weighted = running
    scores, allowed = score_block(queries, key_blk, query_pos, key_pos, lengths, score_scale)
    scores = jnp.where(allowed, scores, MASKED)
    new_max = jnp.maximum(running_max, jnp.max(scores, axis=4))
    weights = jnp.where(allowed, jnp.exp(scores - new_max[..., None]), 0.0)
    factor = jnp.exp(running_max - new_max)
    running_sum = running_sum * factor + jnp.sum(weights, axis=4)
    weighted = weighted * factor[..., None] + jnp.einsum(
        "skgqt,stkd->skgqd",
        weights.astype(jnp.bfloat16),
        value_blk,
        preferred_element_type=jnp.float32,
    )
    return (new_max, running_sum, weighted)


def backward_block(
    queries,
    key_blk,
    value_blk,
    query_pos,
    key_pos,
    lengths,
    score_scale,
    log_total,
    row_dot,
    grad_heads,
):
    scores, allowed = score_block(queries, key_blk, query_pos, key_pos, lengths, score_scale)
    probability = jnp.where(allowed, jnp.exp(scores - log_total[..., None]), 0.0)
    prob_grad = jnp.einsum(
        "skgqd,stkd->skgqt", grad_heads, value_blk, preferred_element_type=jnp.float32
    )
    score_grad = (probability * (prob_grad - row_dot[..., None])).astype(jnp.bfloat16)
    query_part = (
        jnp.einsum("skgqt,stkd->sqkgd", score_grad, key_blk, preferred_element_type=jnp.float32)
        * score_scale
    )
    key_part = (
        jnp.einsum("skgqt,sqkgd->stkd", score_grad, queries, preferred_element_type=jnp.float32)
        * score_scale
    )
    value_part = jnp.einsum(
        "skgqt,skgqd->stkd",
        probability.astype(jnp.bfloat16),
        grad_heads,
        preferred_element_type=jnp.float32,
    )
    return (query_part, key_part, value_part)


def weight_tile(left, right):
    return jnp.einsum("rd,re->de", left, right, preferred_element_type=jnp.float32)


def body(
    tokens,
    cotangent,
    lengths,
    attn_gain,
    w_query,
    w_key,
    w_value,
    w_out,
    mlp_gain,
    w_gate,
    w_up,
    w_down,
):
    seq_count, ctx_tok, model_width = tokens.shape
    cycle_size = lax.axis_size("ctx")
    ctx_place = lax.axis_index("ctx")
    slot_len = ctx_tok * cycle_size
    group_size = HEADS // KV_HEADS
    kv_width = KV_HEADS * HEAD_DIM
    score_scale = HEAD_DIM ** (-0.5)
    row_count = seq_count * ctx_tok
    gain_one, query_w, key_w, value_w, out_w = (
        lax.all_gather(attn_gain, "fsdp", axis=0, tiled=True),
        lax.all_gather(w_query, "fsdp", axis=0, tiled=True),
        lax.all_gather(w_key, "fsdp", axis=0, tiled=True),
        lax.all_gather(w_value, "fsdp", axis=0, tiled=True),
        lax.all_gather(w_out, "fsdp", axis=0, tiled=True),
    )
    gain_two, gate_w, up_w, down_w = (
        lax.all_gather(mlp_gain, "fsdp", axis=0, tiled=True),
        lax.all_gather(w_gate, "fsdp", axis=0, tiled=True),
        lax.all_gather(w_up, "fsdp", axis=0, tiled=True),
        lax.all_gather(w_down, "fsdp", axis=0, tiled=True),
    )
    gain_one = gain_one.astype(jnp.float32)
    gain_two = gain_two.astype(jnp.float32)
    query_pos = slot_len - 1 - (ctx_place * ctx_tok + jnp.arange(ctx_tok, dtype=jnp.int32))
    cosine, sine_table = rope_tables(query_pos, HEAD_DIM)
    inputs = tokens.reshape(row_count, model_width).astype(jnp.float32)
    inv_one, normed_one = rms_forward(inputs, gain_one)
    queries = jnp.dot(normed_one, query_w, preferred_element_type=jnp.float32).reshape(
        seq_count, ctx_tok, HEADS, HEAD_DIM
    )
    queries = (
        rotate(queries, cosine, sine_table)
        .astype(jnp.bfloat16)
        .reshape(seq_count, ctx_tok, KV_HEADS, group_size, HEAD_DIM)
    )
    key_rows = jnp.dot(normed_one, key_w, preferred_element_type=jnp.float32).reshape(
        seq_count, ctx_tok, KV_HEADS, HEAD_DIM
    )
    key_rows = (
        rotate(key_rows, cosine, sine_table)
        .astype(jnp.bfloat16)
        .reshape(seq_count, ctx_tok, kv_width)
    )
    value_rows = (
        jnp.dot(normed_one, value_w, preferred_element_type=jnp.float32)
        .astype(jnp.bfloat16)
        .reshape(seq_count, ctx_tok, kv_width)
    )
    kv_pair = jnp.stack([key_rows, value_rows])
    stat_shape = (seq_count, KV_HEADS, group_size, ctx_tok)
    initial = (
        jnp.full(stat_shape, MASKED, jnp.float32),
        jnp.zeros(stat_shape, jnp.float32),
        jnp.zeros(stat_shape + (HEAD_DIM,), jnp.float32),
    )

    def split_pair(pair_blk):
        return (
            pair_blk[0].reshape(seq_count, -1, KV_HEADS, HEAD_DIM),
            pair_blk[1].reshape(seq_count, -1, KV_HEADS, HEAD_DIM),
        )

    def source_pos(source):
        return slot_len - 1 - (source * ctx_tok + jnp.arange(ctx_tok, dtype=jnp.int32))

    key_own, value_own = split_pair(kv_pair)
    running = forward_block(
        initial, queries, key_own, value_own, query_pos, query_pos, lengths, score_scale
    )
    kept_zero = jnp.zeros((2, seq_count, slot_len, kv_width), jnp.bfloat16)
    kept_pairs = lax.dynamic_update_slice_in_dim(kept_zero, kv_pair, ctx_place * ctx_tok, 2)

    def cycle_forward(offset, carry):
        running, pair_blk, kept = carry
        pair_blk = passed_along(pair_blk, "ctx", -1)
        source = ctx_place + offset
        key_pos = source_pos(source)
        key_blk, value_blk = split_pair(pair_blk)
        running = forward_block(
            running, queries, key_blk, value_blk, query_pos, key_pos, lengths, score_scale
        )
        place = jnp.minimum(source, cycle_size - 1)
        current = lax.dynamic_slice_in_dim(kept, place * ctx_tok, ctx_tok, 2)
        fresh = jnp.where(source < cycle_size, pair_blk, current)
        kept = lax.dynamic_update_slice_in_dim(kept, fresh, place * ctx_tok, 2)
        return (running, pair_blk, kept)

    running, kv_last, kept_pairs = lax.fori_loop(
        1, cycle_size, cycle_forward, (running, kv_pair, kept_pairs)
    )
    running_max, running_sum, weighted = running
    log_total = running_max + jnp.log(running_sum)
    attended = weighted / running_sum[..., None]
    attended_low = (
        jnp.transpose(attended, (0, 3, 1, 2, 4))
        .reshape(row_count, model_width)
        .astype(jnp.bfloat16)
    )
    mixed = inputs + jnp.dot(attended_low, out_w, preferred_element_type=jnp.float32)
    inv_two, normed_two = rms_forward(mixed, gain_two)
    gate = jnp.dot(normed_two, gate_w, preferred_element_type=jnp.float32)
    up_proj = jnp.dot(normed_two, up_w, preferred_element_type=jnp.float32)
    sigmoid = jax.nn.sigmoid(gate)
    hidden = (gate * sigmoid * up_proj).astype(jnp.bfloat16)
    outputs = mixed + jnp.dot(hidden, down_w, preferred_element_type=jnp.float32)
    valid = (query_pos[None, :] < lengths[:, None]).astype(jnp.float32).reshape(row_count, 1)
    out_back = cotangent.reshape(row_count, model_width).astype(jnp.float32) * valid
    branch_grad = out_back.astype(jnp.bfloat16)
    hidden_grad = jnp.einsum("rd,fd->rf", branch_grad, down_w, preferred_element_type=jnp.float32)
    gate_back = (hidden_grad * up_proj * sigmoid * (1.0 + gate * (1.0 - sigmoid))).astype(
        jnp.bfloat16
    )
    up_back = (hidden_grad * gate * sigmoid).astype(jnp.bfloat16)
    normed_grad = jnp.einsum("rf,df->rd", gate_back, gate_w, preferred_element_type=jnp.float32)
    normed_grad = normed_grad + jnp.einsum(
        "rf,df->rd", up_back, up_w, preferred_element_type=jnp.float32
    )
    mixed_back, gain_two_grad = rms_backward(mixed, inv_two, gain_two, normed_grad)
    mixed_grad = out_back + mixed_back
    down_term = jnp.einsum("rf,rd->fd", hidden, branch_grad, preferred_element_type=jnp.float32)
    gate_term = weight_tile(normed_two, gate_back)
    up_term = weight_tile(normed_two, up_back)
    mlp_parts = (
        lax.psum_scatter(
            gain_two_grad.astype(jnp.bfloat16), "fsdp", scatter_dimension=0, tiled=True
        ).astype(jnp.float32),
        lax.psum_scatter(
            gate_term.astype(jnp.bfloat16), "fsdp", scatter_dimension=0, tiled=True
        ).astype(jnp.float32),
        lax.psum_scatter(
            up_term.astype(jnp.bfloat16), "fsdp", scatter_dimension=0, tiled=True
        ).astype(jnp.float32),
        lax.psum_scatter(
            down_term.astype(jnp.bfloat16), "fsdp", scatter_dimension=0, tiled=True
        ).astype(jnp.float32),
    )
    attn_back = mixed_grad.astype(jnp.bfloat16)
    attended_grad = jnp.einsum(
        "rd,cd->rc", attn_back, out_w, preferred_element_type=jnp.float32
    ).astype(jnp.bfloat16)
    grad_heads = jnp.transpose(
        attended_grad.reshape(seq_count, ctx_tok, KV_HEADS, group_size, HEAD_DIM), (0, 2, 3, 1, 4)
    )
    row_dot = jnp.sum(grad_heads.astype(jnp.float32) * attended, axis=4)

    def grad_step(step):
        target = ctx_place + cycle_size - 1 - step
        place = jnp.clip(target, 0, cycle_size - 1)
        piece = lax.dynamic_slice_in_dim(kept_pairs, place * ctx_tok, ctx_tok, 2)
        key_pos = source_pos(target)
        key_blk, value_blk = split_pair(piece)
        query_part, key_part, value_part = backward_block(
            queries,
            key_blk,
            value_blk,
            query_pos,
            key_pos,
            lengths,
            score_scale,
            log_total,
            row_dot,
            grad_heads,
        )
        stacked = jnp.stack(
            [
                key_part.reshape(seq_count, ctx_tok, kv_width),
                value_part.reshape(seq_count, ctx_tok, kv_width),
            ]
        )
        return (query_part, stacked)

    query_first, grads_first = grad_step(0)

    def cycle_backward(step, carry):
        query_acc, grads_pair = carry
        grads_pair = passed_along(grads_pair.astype(jnp.bfloat16), "ctx", 1).astype(
            grads_pair.dtype
        )
        query_part, stacked = grad_step(step)
        return (query_acc + query_part, grads_pair + stacked)

    query_acc, grads_pair = lax.fori_loop(1, cycle_size, cycle_backward, (query_first, grads_first))
    query_pre = (
        unrotate(query_acc.reshape(seq_count, ctx_tok, HEADS, HEAD_DIM), cosine, sine_table)
        .astype(jnp.bfloat16)
        .reshape(row_count, model_width)
    )
    key_pre = (
        unrotate(grads_pair[0].reshape(seq_count, ctx_tok, KV_HEADS, HEAD_DIM), cosine, sine_table)
        .astype(jnp.bfloat16)
        .reshape(row_count, kv_width)
    )
    value_pre = grads_pair[1].astype(jnp.bfloat16).reshape(row_count, kv_width)
    normed_back = jnp.einsum("re,de->rd", query_pre, query_w, preferred_element_type=jnp.float32)
    normed_back = normed_back + jnp.einsum(
        "re,de->rd", key_pre, key_w, preferred_element_type=jnp.float32
    )
    normed_back = normed_back + jnp.einsum(
        "re,de->rd", value_pre, value_w, preferred_element_type=jnp.float32
    )
    input_back, gain_one_grad = rms_backward(inputs, inv_one, gain_one, normed_back)
    input_grad = mixed_grad + input_back
    query_term = weight_tile(normed_one, query_pre)
    key_term = weight_tile(normed_one, key_pre)
    value_term = weight_tile(normed_one, value_pre)
    out_term = weight_tile(attended_low, attn_back)
    attn_parts = (
        lax.psum_scatter(
            gain_one_grad.astype(jnp.bfloat16), "fsdp", scatter_dimension=0, tiled=True
        ).astype(jnp.float32),
        lax.psum_scatter(
            query_term.astype(jnp.bfloat16), "fsdp", scatter_dimension=0, tiled=True
        ).astype(jnp.float32),
        lax.psum_scatter(
            key_term.astype(jnp.bfloat16), "fsdp", scatter_dimension=0, tiled=True
        ).astype(jnp.float32),
        lax.psum_scatter(
            value_term.astype(jnp.bfloat16), "fsdp", scatter_dimension=0, tiled=True
        ).astype(jnp.float32),
        lax.psum_scatter(
            out_term.astype(jnp.bfloat16), "fsdp", scatter_dimension=0, tiled=True
        ).astype(jnp.float32),
    )
    summed = (
        lax.psum(attn_parts[0].astype(jnp.bfloat16), "ctx").astype(jnp.float32),
        lax.psum(attn_parts[1].astype(jnp.bfloat16), "ctx").astype(jnp.float32),
        lax.psum(attn_parts[2].astype(jnp.bfloat16), "ctx").astype(jnp.float32),
        lax.psum(attn_parts[3].astype(jnp.bfloat16), "ctx").astype(jnp.float32),
        lax.psum(attn_parts[4].astype(jnp.bfloat16), "ctx").astype(jnp.float32),
        lax.psum(mlp_parts[0].astype(jnp.bfloat16), "ctx").astype(jnp.float32),
        lax.psum(mlp_parts[1].astype(jnp.bfloat16), "ctx").astype(jnp.float32),
        lax.psum(mlp_parts[2].astype(jnp.bfloat16), "ctx").astype(jnp.float32),
        lax.psum(mlp_parts[3].astype(jnp.bfloat16), "ctx").astype(jnp.float32),
    )
    return (
        outputs.reshape(seq_count, ctx_tok, model_width),
        input_grad.reshape(seq_count, ctx_tok, model_width),
        summed[0],
        summed[1],
        summed[2],
        summed[3],
        summed[4],
        summed[5],
        summed[6],
        summed[7],
        summed[8],
    )


def solution(mesh):
    placed = (
        P("fsdp", "ctx", None),
        P("fsdp", "ctx", None),
        P("fsdp"),
        P("fsdp"),
        P("fsdp", None),
        P("fsdp", None),
        P("fsdp", None),
        P("fsdp", None),
        P("fsdp"),
        P("fsdp", None),
        P("fsdp", None),
        P("fsdp", None),
    )
    return jax.shard_map(
        body,
        mesh=mesh,
        in_specs=placed,
        out_specs=(
            P("fsdp", "ctx", None),
            P("fsdp", "ctx", None),
            P("fsdp"),
            P("fsdp", None),
            P("fsdp", None),
            P("fsdp", None),
            P("fsdp", None),
            P("fsdp"),
            P("fsdp", None),
            P("fsdp", None),
            P("fsdp", None),
        ),
        check_vma=False,
    )
```

profile of v0, /device:TPU:0, one launch (start us, length us, event | category | flops | bytes accessed | tf_op | source)
XLA Modules:
  0.0 2323.7 jit_solution(15793644969821790894)
XLA Ops:
  12.6 9.5 all-gather
  22.2 8.0 all-gather.1
  30.9 8.4 all-gather.10.cloned.1.call-done
  39.2 1.5 copy.59
  40.7 27.0 %all-gather.14.cloned.1.call-done = bf16[2048,256]{1,0:T(8,128)(2,1)} async-done(((bf16[512,256]{1,0:T(8,128)(2,1)}), bf16[2048,256]{1,0:T(8,128)(2,1)}) %all-gather.14.cloned.1.call-update) | async-done | bytes 1048592 | tf_op jit(solution)/shard_map/all_gather | solution.py:161
  67.7 1.6 convolution_convert_fusion.8
  70.4 86.8 %all-gather.12.cloned.1.call-done = bf16[2048,2048]{1,0:T(8,128)(2,1)} async-done(((bf16[512,2048]{1,0:T(8,128)(2,1)}), bf16[2048,2048]{1,0:T(8,128)(2,1)}) %all-gather.12.cloned.1.call-update) | async-done | bytes 8388624 | tf_op jit(solution)/shard_map/all_gather | solution.py:159
  157.2 12.3 copy.60
  169.5 6.2 convolution_bitcast_fusion.2
  177.8 57.3 %while.40 = (s32[]{:T(128)}, f32[1,4,8,128]{3,2,1,0:T(8,128)S(1)}, f32[1,4,8,128]{3,2,1,0:T(8,128)S(1)}, f32[1,4,8,128,64]{3,4,2,1,0:T(8,128)S(1)}, bf16[2,1,128...) while((s32[]{:T(128)}, f32[1,4,8,128]{3,2,1,0:T(8,128)S(1)}, ...), condition=%wide.region_6.7_spmd.clone, body=%wide.region_3.6_spmd.clone.sunk | while | flops 141685760 | bytes 10816301 | solution.py:236
  185.2 4.1 collective-permute-done
  193.4 4.6 collective-permute-done
  202.2 4.2 collective-permute-done
  210.5 4.6 collective-permute-done
  219.2 4.6 collective-permute-done
  227.9 4.6 collective-permute-done
  236.2 10.4 all-gather.16.cloned.1.call-done
  246.6 5.0 multiply_reduce_fusion.3
  251.6 1.9 fusion.37
  254.5 204.3 %all-gather.18.cloned.1.call-done = bf16[2048,5632]{1,0:T(8,128)(2,1)} async-done(((bf16[512,5632]{1,0:T(8,128)(2,1)}), bf16[2048,5632]{1,0:T(8,128)(2,1)}) %all-gather.18.cloned.1.call-update) | async-done | bytes 23068688 | tf_op jit(solution)/shard_map/all_gather | solution.py:166
  458.8 12.7 fusion.109
  471.5 199.5 %all-gather.20.cloned.1.call-done = bf16[2048,5632]{1,0:T(8,128)(2,1)} async-done(((bf16[512,5632]{1,0:T(8,128)(2,1)}), bf16[2048,5632]{1,0:T(8,128)(2,1)}) %all-gather.20.cloned.1.call-update) | async-done | bytes 23068688 | tf_op jit(solution)/shard_map/all_gather | solution.py:167
  671.0 12.7 fusion.110
  683.7 199.6 %all-gather.22.cloned.1.call-done = bf16[5632,2048]{1,0:T(8,128)(2,1)} async-done(((bf16[1408,2048]{1,0:T(8,128)(2,1)}), bf16[5632,2048]{1,0:T(8,128)(2,1)}) %all-gather.22.cloned.1.call-update) | async-done | bytes 23068688 | tf_op jit(solution)/shard_map/all_gather | solution.py:168
  883.3 15.4 multiply_convert_fusion
  898.8 13.2 fusion.111
  912.0 13.4 multiply_reduce_fusion
  925.4 1.7 fusion.64
  928.1 6.3 convolution_convert_fusion.7
  934.9 2.2 fusion.66
  938.6 47.9 %while.41 = (s32[]{:T(128)}, f32[1,128,4,8,64]{1,4,3,2,0:T(8,128)S(1)}, f32[2,1,128,256]{2,3,1,0:T(8,128)S(1)}, s32[]{:T(128)}, bf16[2,1,1024,256]{2,3,1,0:T(8,1...) while((s32[]{:T(128)}, ...), condition=%wide.region_11.12_spmd.clone, body=%wide.region_10.11_spmd.clone.sunk | while | flops 340083712 | bytes 15993671 | solution.py:330
  938.7 1.7 collective-permute-start.1
  944.6 3.7 collective-permute-start.1
  952.5 2.2 collective-permute-start.1
  958.9 3.3 collective-permute-start.1
  966.4 2.1 collective-permute-start.1
  972.7 3.3 collective-permute-start.1
  980.2 2.1 collective-permute-start.1
  986.6 1.5 convolution_convert_fusion.6
  988.2 1.5 convolution_convert_fusion.5
  990.2 5.8 convolution_convert_fusion.4
  997.5 5.7 convolution_convert_fusion.3
  1004.3 12.2 convolution_convert_fusion.2
  1016.6 12.4 convolution_convert_fusion.1
  1030.0 12.5 convolution_convert_fusion
  1042.6 2.2 reduce-scatter.12.cloned.1.call-done
  1044.8 89.9 %reduce-scatter.8.cloned.1.call-done = bf16[512,2048]{1,0:T(8,128)(2,1)} async-done(((bf16[2048,2048]{1,0:T(8,128)(2,1)}), bf16[512,2048]{1,0:T(8,128)(2,1)}) %reduce-scatter.8.cloned.1.call-update) | async-done | bytes 2097168 | tf_op jit(solution)/shard_map/reduce_scatter | solution.py:359
  1134.7 90.4 %reduce-scatter.14.cloned.1.call-done = bf16[512,2048]{1,0:T(8,128)(2,1)} async-done(((bf16[2048,2048]{1,0:T(8,128)(2,1)}), bf16[512,2048]{1,0:T(8,128)(2,1)}) %reduce-scatter.14.cloned.1.call-update) | async-done | bytes 2097168 | tf_op jit(solution)/shard_map/reduce_scatter | solution.py:368
  1225.1 207.8 %reduce-scatter.16.cloned.1.call-done = bf16[512,5632]{1,0:T(8,128)(2,1)} async-done(((bf16[2048,5632]{1,0:T(8,128)(2,1)}), bf16[512,5632]{1,0:T(8,128)(2,1)}) %reduce-scatter.16.cloned.1.call-update) | async-done | bytes 5767184 | tf_op jit(solution)/shard_map/reduce_scatter | solution.py:275
  1432.9 208.3 %reduce-scatter.18.cloned.1.call-done = bf16[512,5632]{1,0:T(8,128)(2,1)} async-done(((bf16[2048,5632]{1,0:T(8,128)(2,1)}), bf16[512,5632]{1,0:T(8,128)(2,1)}) %reduce-scatter.18.cloned.1.call-update) | async-done | bytes 5767184 | tf_op jit(solution)/shard_map/reduce_scatter | solution.py:278
  1641.2 207.8 %reduce-scatter.20.cloned.1.call-done = bf16[1408,2048]{1,0:T(8,128)(2,1)} async-done(((bf16[5632,2048]{1,0:T(8,128)(2,1)}), bf16[1408,2048]{1,0:T(8,128)(2,1)}) %reduce-scatter.20.cloned.1.call-update) | async-done | bytes 5767184 | tf_op jit(solution)/shard_map/reduce_scatter | solution.py:281
  1850.9 6.4 fusion.112
  1858.8 1.5 fusion.58
  1860.3 8.9 all-reduce.4
  1869.4 15.7 all-reduce.2
  1886.2 2.6 fusion.57
  1888.8 12.0 fusion.35
  1900.8 387.9 %all-reduce.7.cloned.1.call-done = (bf16[512,2048]{1,0:T(8,128)(2,1)}, bf16[512,256]{1,0:T(8,128)(2,1)}, bf16[512,256]{1,0:T(8,128)(2,1)}, bf16[512,2048]{1,0:T(...) async-done(((bf16[512,2048]{1,0:T(8,128)(2,1)}, bf16[512,256]{1,0:T(8,128)(2,1)}, bf16[512,256]{1,0:T(8,128)(2,1)}, ...) | async-done | bytes 22020112 | tf_op jit(solution)/shard_map/psum | solution.py:374
  2288.7 4.3 convert_element_type.328
  2294.6 2.7 convert_element_type.334
  2297.3 1.5 copy-done.11
  2298.8 5.9 convert_element_type.338
  2304.7 5.9 convert_element_type.340
  2310.7 6.0 convert_element_type.342
  (333 shorter events, 81.2 us)
Async XLA Ops:
  7.2 32.1 %all-gather.10.cloned.1.call-start = ((), (), s32[]{:S(2)}) async-start(), calls=%async_computation.7 | async-start | bytes 1310720 | tf_op jit(solution)/shard_map/all_gather | solution.py:160
  7.9 59.8 %all-gather.14.cloned.1.call-start = ((), (), s32[]{:S(2)}) async-start(), calls=%async_computation.9 | async-start | bytes 1310720 | tf_op jit(solution)/shard_map/all_gather | solution.py:161
  8.7 148.6 %all-gather.12.cloned.1.call-start = ((), (), s32[]{:S(2)}) async-start(), calls=%async_computation.8 | async-start | bytes 10485760 | tf_op jit(solution)/shard_map/all_gather | solution.py:159
  9.4 237.2 %all-gather.16.cloned.1.call-start = ((), (), s32[]{:S(2)}) async-start(), calls=%async_computation.10 | async-start | bytes 10485760 | tf_op jit(solution)/shard_map/all_gather | solution.py:162
  10.0 448.8 %all-gather.18.cloned.1.call-start = ((), (), s32[]{:S(2)}) async-start(), calls=%async_computation.11 | async-start | bytes 28835840 | tf_op jit(solution)/shard_map/all_gather | solution.py:166
  10.6 660.4 %all-gather.20.cloned.1.call-start = ((), (), s32[]{:S(2)}) async-start(), calls=%async_computation.12 | async-start | bytes 28835840 | tf_op jit(solution)/shard_map/all_gather | solution.py:167
  11.1 1.5 copy-start.24
  11.1 11.0 copy-start.25
  11.2 19.2 copy-start
  11.2 872.2 %all-gather.22.cloned.1.call-start = ((), (), s32[]{:S(2)}) async-start(), calls=%async_computation.13 | async-start | bytes 28835840 | tf_op jit(solution)/shard_map/all_gather | solution.py:168
  11.9 1030.7 %reduce-scatter.10.cloned.1.call-start = ((), (), s32[]{:S(2)}) async-start(), calls=%async_computation.15 | async-start | bytes 1310720 | tf_op jit(solution)/shard_map/reduce_scatter | solution.py:362
  175.9 1.2 copy-start.16
  175.9 1.2 copy-start.19
  177.8 3.2 collective-permute-start
  183.0 6.3 collective-permute-start
  191.3 6.7 collective-permute-start
  200.1 6.3 collective-permute-start
  208.4 6.7 collective-permute-start
  217.1 6.7 collective-permute-start
  225.8 6.7 collective-permute-start
  235.1 11.5 copy-start.10
  246.6 5.0 copy-start.17
  246.6 5.0 copy-start.20
  251.5 673.9 %copy-start.1 = (f32[128,2048]{1,0:T(8,128)}, f32[128,2048]{1,0:T(8,128)S(1)}, u32[]{:S(2)}) copy-start(f32[128,2048]{1,0:T(8,128)S(1)} %get-tuple-element.620) | copy-start | bytes 3145732
  898.8 13.2 copy-start.6
  927.1 1.0 copy-start.3
  934.7 2.4 copy-start.9
  937.1 1.0 copy-start.18
  937.1 1.0 copy-start.21
  938.7 5.9 collective-permute-start.1
  944.6 7.8 collective-permute-start.1
  952.5 6.3 collective-permute-start.1
  958.9 7.4 collective-permute-start.1
  966.4 6.3 collective-permute-start.1
  972.7 7.4 collective-permute-start.1
  980.2 6.3 collective-permute-start.1
  988.2 56.6 %reduce-scatter.12.cloned.1.call-start = ((), (), s32[]{:S(2)}) async-start(), calls=%async_computation.16 | async-start | bytes 1310720 | tf_op jit(solution)/shard_map/reduce_scatter | solution.py:365
  989.7 144.9 %reduce-scatter.8.cloned.1.call-start = ((), (), s32[]{:S(2)}) async-start(), calls=%async_computation.14 | async-start | bytes 10485760 | tf_op jit(solution)/shard_map/reduce_scatter | solution.py:359
  996.1 1.3 copy-start.4
  996.1 1.4 copy-start.7
  996.1 229.0 %reduce-scatter.14.cloned.1.call-start = ((), (), s32[]{:S(2)}) async-start(), calls=%async_computation.17 | async-start | bytes 10485760 | tf_op jit(solution)/shard_map/reduce_scatter | solution.py:368
  1003.2 1.0 copy-start.5
  1003.3 429.6 %reduce-scatter.16.cloned.1.call-start = ((), (), s32[]{:S(2)}) async-start(), calls=%async_computation.18 | async-start | bytes 28835840 | tf_op jit(solution)/shard_map/reduce_scatter | solution.py:275
  1016.5 624.6 %reduce-scatter.18.cloned.1.call-start = ((), (), s32[]{:S(2)}) async-start(), calls=%async_computation.19 | async-start | bytes 28835840 | tf_op jit(solution)/shard_map/reduce_scatter | solution.py:278
  1028.9 1.1 copy-start.13
  1029.0 820.0 %reduce-scatter.20.cloned.1.call-start = ((), (), s32[]{:S(2)}) async-start(), calls=%async_computation.20 | async-start | bytes 28835840 | tf_op jit(solution)/shard_map/reduce_scatter | solution.py:281
  1042.5 1246.1 %all-reduce.7.cloned.1.call-start = ((), (), s32[]{:S(2)}) async-start(), calls=%async_computation.21 | async-start | bytes 44040192 | tf_op jit(solution)/shard_map/psum | solution.py:374
  1849.0 0.7 copy-start.26
  1850.8 6.4 copy-start.12
  1857.3 1.5 copy-start.15
  1860.3 28.5 %copy-start.2 = (f32[128,2048]{1,0:T(8,128)S(1)}, f32[128,2048]{1,0:T(8,128)}, u32[]{:S(2)}) copy-start(f32[128,2048]{1,0:T(8,128)} %copy-done.1) | copy-start | bytes 3145732
  1885.0 3.7 copy-start.8
  2288.7 4.3 copy-start.23
  2288.7 5.1 copy-start.22
  2288.7 5.9 copy-start.14
  2294.6 4.1 copy-start.11
  2294.6 10.1 slice-start.2
  2298.8 5.9 slice-start.3
  2298.8 11.9 slice-start
  2304.7 5.9 slice-start.1
Sparse Core Ops, SparseCore 0:
  9.9 29.3 all-gather.9
  41.1 26.6 all-gather.13
  69.6 87.5 all-gather.11
  158.9 87.6 all-gather.15
  248.3 210.4 all-gather.17
  460.5 210.4 all-gather.19
  672.8 210.4 all-gather.21
  988.3 24.9 reduce-scatter.9
  1017.0 27.7 reduce-scatter.11
  1048.2 86.3 reduce-scatter.7
  1138.6 86.4 reduce-scatter.13
  1228.0 204.8 reduce-scatter.15
  1436.3 204.8 reduce-scatter.17
  1644.1 204.7 reduce-scatter.19
  1852.6 435.9 all-reduce.6
where the time goes:
time: 2330 us; the launch traced here: 2320 us
  waiting for transfers between devices  1960 us (84%)
  matrix products  191 us (8%)
  other arithmetic  51.6 us (2%)
  blocking collectives  42.1 us (2%)
  local copies, waits for them, and re-layouts  29.2 us (1%)
  starting transfers between devices  28.5 us (1%)
    psum x1, waiting for transfers between devices, body(): lax.psum(attn_parts[1].astype(jnp.bfloat16), 'ctx').astype(jnp.float32)  388 us
    reduce_scatter x1, waiting for transfers between devices, body(): lax.psum_scatter(up_term.astype(jnp.bfloat16), 'fsdp', scatter_dimension=...  208 us
    reduce_scatter x1, waiting for transfers between devices, body(): lax.psum_scatter(gate_term.astype(jnp.bfloat16), 'fsdp', scatter_dimensio...  208 us
    reduce_scatter x1, waiting for transfers between devices, body(): lax.psum_scatter(down_term.astype(jnp.bfloat16), 'fsdp', scatter_dimensio...  208 us
    all_gather x1, waiting for transfers between devices, body(): lax.all_gather(w_gate, 'fsdp', axis=0, tiled=True)  204 us
    all_gather x1, waiting for transfers between devices, body(): lax.all_gather(w_down, 'fsdp', axis=0, tiled=True)  200 us
    all_gather x1, waiting for transfers between devices, body(): lax.all_gather(w_up, 'fsdp', axis=0, tiled=True)  200 us
    reduce_scatter x1, waiting for transfers between devices, body(): lax.psum_scatter(out_term.astype(jnp.bfloat16), 'fsdp', scatter_dimension...  90.4 us
  transfers between devices with their start and end apart: 29, of which 21 were waited for; matrix products, arithmetic and copies ran while one was open for 8% of the time, Pallas kernels for 0%

commit v1 on v0

v1 whole, which is shorter than its diff:
```python
import jax
import jax.numpy as jnp
from jax import lax
from jax.experimental import pallas as pl
from jax.experimental.pallas import tpu as pltpu
from jax.sharding import Mesh
from jax.sharding import PartitionSpec as P

HEADS = 32
KV_HEADS = 4
HEAD_DIM = 64
EPSILON = 1e-05
ROPE_BASE = 10000.0
MASKED = -1e30
FAR = 1 << 30
BF = jnp.bfloat16
F32 = jnp.float32
VMEM_BYTES = 56 * 1024 * 1024


def params(**kw):
    return pltpu.CompilerParams(vmem_limit_bytes=VMEM_BYTES, **kw)


def along_plane(value, step):
    count = lax.axis_size("fsdp")
    return lax.ppermute(value, "fsdp", [(i, i ^ step) for i in range(count)])


def to_sibling(value):
    return lax.ppermute(value, "core", [(0, 1), (1, 0)])


def along_line(value, shift):
    count = lax.axis_size("z")
    return lax.ppermute(
        value, "z", [(i, i + shift) for i in range(count) if 0 <= i + shift < count]
    )


def plane_bits():
    count = lax.axis_size("fsdp")
    return [1 << b for b in range(count.bit_length() - 1)]


def plane_gather(block):
    half = block.shape[0] // 2
    parts = []
    for which, bits in ((0, plane_bits()), (1, plane_bits()[::-1])):
        held = {0: block[which * half : (which + 1) * half]}
        for bit in bits:
            order = sorted(held)
            got = along_plane(jnp.stack([held[j] for j in order]), bit)
            for n, j in enumerate(order):
                held[j ^ bit] = got[n]
        parts.append(held)
    return [jnp.concatenate([parts[0][j], parts[1][j]]) for j in range(lax.axis_size("fsdp"))]


def plane_reduce(partial):
    half = partial.shape[1] // 2
    done = []
    for which, bits in ((0, plane_bits()[::-1]), (1, plane_bits())):
        held = {j: partial[j, which * half : (which + 1) * half] for j in range(partial.shape[0])}
        for bit in bits:
            going = [j for j in sorted(held) if j & bit]
            got = along_plane(jnp.stack([held[j].astype(BF) for j in going]), bit)
            for n, j in enumerate(going):
                held[j ^ bit] = held[j ^ bit].astype(F32) + got[n].astype(F32)
                del held[j]
        done.append(held[0])
    return jnp.concatenate(done)


def line_sum(value):
    count = lax.axis_size("z")
    place = lax.axis_index("z")
    half = count // 2
    for i in range(half - 1):
        got = lax.ppermute(value, "z", [(i, i + 1), (count - 1 - i, count - 2 - i)])
        value = value + got
    value = value + lax.ppermute(value, "z", [(half - 1, half), (half, half - 1)])
    for i in range(half - 2, -1, -1):
        got = lax.ppermute(value, "z", [(i + 1, i), (count - 2 - i, count - 1 - i)])
        outer = (place == i) | (place == count - 1 - i)
        value = jnp.where(outer, got, value)
    return value


def move_kernel(idx_ref, x_ref, o_ref):
    o_ref[...] = x_ref[...]


def pick_columns(x, index, count):
    rows, width = x.shape
    size = width // count
    spec = pltpu.PrefetchScalarGridSpec(
        num_scalar_prefetch=1,
        grid=(count,),
        in_specs=[pl.BlockSpec((rows, size), lambda b, idx: (0, idx[b]))],
        out_specs=pl.BlockSpec((rows, size), lambda b, idx: (0, b)),
    )
    return pl.pallas_call(
        move_kernel,
        grid_spec=spec,
        out_shape=jax.ShapeDtypeStruct(x.shape, x.dtype),
        compiler_params=params(),
        name="pick_columns",
    )(index, x)


def put_columns(x, index, count):
    rows, width = x.shape
    size = width // count
    spec = pltpu.PrefetchScalarGridSpec(
        num_scalar_prefetch=1,
        grid=(count,),
        in_specs=[pl.BlockSpec((rows, size), lambda b, idx: (0, b))],
        out_specs=pl.BlockSpec((rows, size), lambda b, idx: (0, idx[b])),
    )
    return pl.pallas_call(
        move_kernel,
        grid_spec=spec,
        out_shape=jax.ShapeDtypeStruct(x.shape, x.dtype),
        compiler_params=params(),
        name="put_columns",
    )(index, x)


def cut_blocks(weight, f, k, count, dtype=BF):
    rows, full = weight.shape
    width, half = full // count, rows // 2
    if width % 128:
        own = lax.dynamic_slice_in_dim(weight, k * half, half, 0).reshape(half, count, width)
        return jnp.stack(
            [lax.dynamic_index_in_dim(own, f ^ j, 1, keepdims=False) for j in range(count)]
        )
    spec = pltpu.PrefetchScalarGridSpec(
        num_scalar_prefetch=1,
        grid=(count,),
        in_specs=[pl.BlockSpec((half, width), lambda j, at: (at[1], at[0] ^ j))],
        out_specs=pl.BlockSpec((None, half, width), lambda j, at: (j, 0, 0)),
    )
    return pl.pallas_call(
        move_kernel,
        grid_spec=spec,
        out_shape=jax.ShapeDtypeStruct((count, half, width), weight.dtype),
        compiler_params=params(),
        name="cut_blocks",
    )(jnp.stack([f, k]), weight)


def join_kernel(at_ref, own_ref, sib_ref, o_ref):
    @pl.when(pl.program_id(0) == 0)
    def _():
        o_ref[...] = own_ref[...].astype(o_ref.dtype)

    @pl.when(pl.program_id(0) == 1)
    def _():
        o_ref[...] = sib_ref[...].astype(o_ref.dtype)


def join_rows(own, sib, f, k):
    count, half, width = own.shape
    if width % 128:
        halves = jnp.stack([own, sib])
        return jnp.concatenate(
            [
                jnp.concatenate(
                    [
                        lax.dynamic_index_in_dim(
                            lax.dynamic_index_in_dim(halves, k ^ h, 0, keepdims=False),
                            f ^ i,
                            0,
                            keepdims=False,
                        )
                        for i in range(count)
                    ],
                    axis=1,
                )
                for h in range(2)
            ],
            axis=0,
        ).astype(F32)
    spec = pltpu.PrefetchScalarGridSpec(
        num_scalar_prefetch=1,
        grid=(2, count),
        in_specs=[
            pl.BlockSpec(
                (None, half, width),
                lambda s, i, at: (at[0] ^ jnp.where(s == 0, i, count - 1), 0, 0),
            ),
            pl.BlockSpec(
                (None, half, width), lambda s, i, at: (at[0] ^ jnp.where(s == 1, i, 0), 0, 0)
            ),
        ],
        out_specs=pl.BlockSpec((half, width), lambda s, i, at: (at[1] ^ s, i)),
    )
    return pl.pallas_call(
        join_kernel,
        grid_spec=spec,
        out_shape=jax.ShapeDtypeStruct((2 * half, count * width), F32),
        compiler_params=params(),
        name="join_rows",
    )(jnp.stack([f, k]), own, sib)


def join_columns(own, sib, k):
    rows, half = own.shape
    count = 4
    size = rows // count
    spec = pltpu.PrefetchScalarGridSpec(
        num_scalar_prefetch=1,
        grid=(2, count),
        in_specs=[
            pl.BlockSpec((size, half), lambda s, i, at: (jnp.where(s == 0, i, count - 1), 0)),
            pl.BlockSpec((size, half), lambda s, i, at: (jnp.where(s == 1, i, 0), 0)),
        ],
        out_specs=pl.BlockSpec((size, half), lambda s, i, at: (i, at[0] ^ s)),
    )
    return pl.pallas_call(
        join_kernel,
        grid_spec=spec,
        out_shape=jax.ShapeDtypeStruct((rows, 2 * half), F32),
        compiler_params=params(),
        name="join_columns",
    )(k.reshape(1), own, sib)


def swap_halves(block):
    lane = lax.broadcasted_iota(jnp.int32, block.shape, 1)
    return jnp.where(lane % 64 < 32, pltpu.roll(block, 96, 1), pltpu.roll(block, 32, 1))


def qkv_kernel(idx_ref, x_ref, gain_ref, w_ref, cos_ref, sin_ref, h_ref, q_ref, kv_ref):
    blocks = idx_ref.shape[0]
    size = x_ref.shape[1] // blocks
    x = x_ref[...].astype(F32)
    inverse = lax.rsqrt(jnp.mean(x * x, axis=1, keepdims=True) + EPSILON)
    for b in range(blocks):
        at = pl.ds(pl.multiple_of(idx_ref[b] * size, 128), size)
        part = x_ref[:, at].astype(F32) * inverse * gain_ref[:, at]
        h_ref[:, b * size : (b + 1) * size] = part.astype(BF)
    out = jnp.dot(h_ref[...], w_ref[...], preferred_element_type=F32)
    cosine, sine = cos_ref[...], sin_ref[...]
    pairs = q_ref.shape[1] // 128
    for c in range(pairs):
        block = out[:, c * 128 : (c + 1) * 128]
        q_ref[:, c * 128 : (c + 1) * 128] = (block * cosine + swap_halves(block) * sine).astype(BF)
    block = out[:, pairs * 128 :]
    lane = lax.broadcasted_iota(jnp.int32, block.shape, 1)
    turned = block * cosine + swap_halves(block) * sine
    kv_ref[...] = jnp.where(lane < 64, turned, block).astype(BF)


def qkv_project(idx, x, gain, weight, cosine, sine, rows):
    total, depth = x.shape
    width = weight.shape[1]
    spec = pltpu.PrefetchScalarGridSpec(
        num_scalar_prefetch=1,
        grid=(total // rows,),
        in_specs=[
            pl.BlockSpec((rows, depth), lambda i, idx: (i, 0)),
            pl.BlockSpec((1, depth), lambda i, idx: (0, 0)),
            pl.BlockSpec((depth, width), lambda i, idx: (0, 0)),
            pl.BlockSpec((rows, 128), lambda i, idx: (0, 0)),
            pl.BlockSpec((rows, 128), lambda i, idx: (0, 0)),
        ],
        out_specs=[
            pl.BlockSpec((rows, depth), lambda i, idx: (i, 0)),
            pl.BlockSpec((rows, width - 128), lambda i, idx: (i, 0)),
            pl.BlockSpec((rows, 128), lambda i, idx: (i, 0)),
        ],
    )
    return pl.pallas_call(
        qkv_kernel,
        grid_spec=spec,
        out_shape=[
            jax.ShapeDtypeStruct((total, depth), BF),
            jax.ShapeDtypeStruct((total, width - 128), BF),
            jax.ShapeDtypeStruct((total, 128), BF),
        ],
        compiler_params=params(),
        cost_estimate=pl.CostEstimate(
            flops=2 * total * depth * width,
            bytes_accessed=4 * total * depth + 2 * depth * width + 2 * total * width,
            transcendentals=0,
        ),
        name="qkv_project",
    )(idx, x, gain, weight, cosine, sine)


def nt(a, b):
    return lax.dot_general(a, b, (((1,), (1,)), ((), ())), preferred_element_type=F32)


def tn(a, b):
    return lax.dot_general(a, b, (((0,), (0,)), ((), ())), preferred_element_type=F32)


def nn(a, b):
    return jnp.dot(a, b, preferred_element_type=F32)


def limits(at_ref, rows):
    j = pl.program_id(0)
    place = at_ref[0] - lax.broadcasted_iota(jnp.int32, (rows, 1), 0)
    return jnp.minimum(place, at_ref[1 + j] - 1)


def attend_kernel(at_ref, q_ref, kv_ref, kp_ref, o_ref, lse_ref, vk_ref):
    rows = q_ref.shape[0]
    keys = vk_ref.shape[0]
    kv = kv_ref[...].reshape(keys, 128)

    @pl.when(pl.program_id(1) == 0)
    def _():
        vk_ref[...] = pltpu.roll(kv.astype(F32), 64, 1).astype(BF)

    vk = vk_ref[...]
    allowed = kp_ref[...] <= limits(at_ref, rows)
    lane = lax.broadcasted_iota(jnp.int32, (rows, 128), 1)
    q = q_ref[...]
    zero = jnp.zeros_like(q)
    outs, logs = [], []
    for first in (True, False):
        mine = lane < 64 if first else lane >= 64
        scores = nt(jnp.where(mine, q, zero), kv if first else vk) * (HEAD_DIM**-0.5)
        scores = jnp.where(allowed, scores, MASKED)
        top = jnp.max(scores, axis=1, keepdims=True)
        weights = jnp.exp(scores - top)
        total = jnp.sum(weights, axis=1, keepdims=True)
        outs.append(nn(weights.astype(BF), vk if first else kv) / total)
        logs.append(jnp.broadcast_to(top + jnp.log(total), (rows, 128)))
    o_ref[...] = jnp.where(lane < 64, outs[0], outs[1]).astype(BF)
    lse_ref[...] = jnp.where(lane < 64, logs[0], logs[1])


def attend(at, q, kv, kp):
    chunks, seqs, rows, _ = kv.shape
    pairs = q.shape[2] // 128
    keys = chunks * rows
    spec = pltpu.PrefetchScalarGridSpec(
        num_scalar_prefetch=1,
        grid=(seqs, pairs),
        in_specs=[
            pl.BlockSpec((None, rows, 128), lambda j, p, at: (j, 0, p)),
            pl.BlockSpec((chunks, None, rows, 128), lambda j, p, at: (0, j, 0, 0)),
            pl.BlockSpec((1, keys), lambda j, p, at: (0, 0)),
        ],
        out_specs=[
            pl.BlockSpec((None, rows, 128), lambda j, p, at: (j, 0, p)),
            pl.BlockSpec((None, rows, 128), lambda j, p, at: (j, 0, p)),
        ],
        scratch_shapes=[pltpu.VMEM((keys, 128), BF)],
    )
    size = seqs * pairs * 2 * rows * keys
    return pl.pallas_call(
        attend_kernel,
        grid_spec=spec,
        out_shape=[
            jax.ShapeDtypeStruct(q.shape, BF),
            jax.ShapeDtypeStruct(q.shape, F32),
        ],
        compiler_params=params(),
        cost_estimate=pl.CostEstimate(
            flops=size * 4 * 128, bytes_accessed=4 << 20, transcendentals=size
        ),
        name="attend",
    )(at, q, kv, kp)


def attend_back_kernel(
    at_ref, q_ref, do_ref, lse_ref, kv_ref, kp_ref, cos_ref, sin_ref, dq_ref, dkv_ref, vk_ref, dk_ref, dv_ref
):
    rows = q_ref.shape[0]
    keys = vk_ref.shape[0]
    pair = pl.program_id(1)
    kv = kv_ref[...].reshape(keys, 128)

    @pl.when(pair == 0)
    def _():
        vk_ref[...] = pltpu.roll(kv.astype(F32), 64, 1).astype(BF)
        dk_ref[...] = jnp.zeros_like(dk_ref)
        dv_ref[...] = jnp.zeros_like(dv_ref)

    vk = vk_ref[...]
    allowed = kp_ref[...] <= limits(at_ref, rows)
    lane = lax.broadcasted_iota(jnp.int32, (rows, 128), 1)
    q, do = q_ref[...], do_ref[...]
    zero = jnp.zeros_like(q)
    parts = []
    for first in (True, False):
        mine = lane < 64 if first else lane >= 64
        keyed, valued = (kv, vk) if first else (vk, kv)
        q_own, do_own = jnp.where(mine, q, zero), jnp.where(mine, do, zero)
        scores = nt(q_own, keyed) * (HEAD_DIM**-0.5)
        log_total = lse_ref[:, 0:1] if first else lse_ref[:, 64:65]
        weights = jnp.where(allowed, jnp.exp(scores - log_total), 0.0)
        joint = weights * nt(do_own, valued)
        back = (joint - weights * jnp.sum(joint, axis=1, keepdims=True)).astype(BF)
        parts.append(nn(back, keyed))
        dk_ref[...] += tn(back, q_own)
        dv_ref[...] += tn(weights.astype(BF), do_own)
    turned = jnp.where(lane < 64, parts[0], parts[1]) * (HEAD_DIM**-0.5)
    dq_ref[...] = (turned * cos_ref[...] - swap_halves(turned) * sin_ref[...]).astype(BF)

    @pl.when(pair == pl.num_programs(1) - 1)
    def _():
        dk = dk_ref[...]
        dv = dv_ref[...]
        dk = (dk + pltpu.roll(dk, 64, 1)) * (HEAD_DIM**-0.5)
        dv = dv + pltpu.roll(dv, 64, 1)
        wide = lax.broadcasted_iota(jnp.int32, dk.shape, 1)
        dkv_ref[...] = jnp.where(wide < 64, dk, dv).astype(BF).reshape(dkv_ref.shape)


def attend_back(at, q, do, lse, kv, kp, cosine, sine):
    chunks, seqs, rows, _ = kv.shape
    pairs = q.shape[2] // 128
    keys = chunks * rows
    tall = pl.BlockSpec((None, rows, 128), lambda j, p, at: (j, 0, p))
    whole = pl.BlockSpec((chunks, None, rows, 128), lambda j, p, at: (0, j, 0, 0))
    flat = pl.BlockSpec((rows, 128), lambda j, p, at: (0, 0))
    spec = pltpu.PrefetchScalarGridSpec(
        num_scalar_prefetch=1,
        grid=(seqs, pairs),
        in_specs=[tall, tall, tall, whole, pl.BlockSpec((1, keys), lambda j, p, at: (0, 0)), flat, flat],
        out_specs=[tall, whole],
        scratch_shapes=[
            pltpu.VMEM((keys, 128), BF),
            pltpu.VMEM((keys, 128), F32),
            pltpu.VMEM((keys, 128), F32),
        ],
    )
    size = seqs * pairs * 2 * rows * keys
    return pl.pallas_call(
        attend_back_kernel,
        grid_spec=spec,
        out_shape=[
            jax.ShapeDtypeStruct(q.shape, BF),
            jax.ShapeDtypeStruct(kv.shape, BF),
        ],
        compiler_params=params(),
        cost_estimate=pl.CostEstimate(
            flops=size * 10 * 128, bytes_accessed=8 << 20, transcendentals=size
        ),
        name="attend_back",
    )(at, q, do, lse, kv, kp, cosine, sine)


def rms_backward(row_block, inverse, gain_vec, gradient):
    normed = row_block * inverse
    gain_grad = jnp.sum(gradient * normed, axis=0)
    scaled = gradient * gain_vec
    back = inverse * (scaled - normed * jnp.mean(scaled * normed, axis=1, keepdims=True))
    return (back, gain_grad)


def body(
    tokens, cotangent, lengths, attn_gain, w_query, w_key, w_value, w_out, mlp_gain, w_gate, w_up, w_down
):
    seqs, rows, depth = tokens.shape
    count, line = lax.axis_size("fsdp"), lax.axis_size("z")
    f, z, k = lax.axis_index("fsdp"), lax.axis_index("z"), lax.axis_index("core")
    slot = rows * line * 2
    total = count * rows
    slab = depth // count
    half = slab // 2
    q_width = HEADS * HEAD_DIM // count
    shared = max(1, count // KV_HEADS)

    x_own = tokens.reshape(rows, depth)
    chunk = 2 * z + k
    first_pos = slot - 1 - chunk * rows

    length = lengths[0]
    words = jnp.zeros((slab,), F32).at[0].set((length // 64).astype(F32)).at[1].set((length % 64).astype(F32))
    note = jnp.stack([attn_gain, mlp_gain, words.astype(BF), jnp.zeros((slab,), BF)])
    notes = [note] + [along_plane(note, j) for j in range(1, count)]
    notes_abs = [lax.dynamic_index_in_dim(jnp.stack(notes), f ^ i, 0, keepdims=False) for i in range(count)]
    gain_one = jnp.concatenate([n[0] for n in notes_abs]).astype(F32).reshape(1, depth)
    gain_two = jnp.concatenate([n[1] for n in notes_abs]).astype(F32).reshape(1, depth)
    all_lengths = jnp.stack(
        [n[2, 0].astype(jnp.int32) * 64 + n[2, 1].astype(jnp.int32) for n in notes]
    )

    x_all = jnp.concatenate(plane_gather(x_own))

    wq = cut_blocks(w_query, f, k, count)
    key_cols = lax.dynamic_slice_in_dim(w_key, k * half, half, 0).reshape(half, KV_HEADS, HEAD_DIM)
    value_cols = lax.dynamic_slice_in_dim(w_value, k * half, half, 0).reshape(half, KV_HEADS, HEAD_DIM)

    def head_of(j):
        return (f ^ j) // shared

    wkv = jnp.stack(
        [
            jnp.concatenate(
                [
                    lax.dynamic_index_in_dim(key_cols, head_of(j), 1, keepdims=False),
                    lax.dynamic_index_in_dim(value_cols, head_of(j), 1, keepdims=False),
                ],
                axis=1,
            )
            for j in range(count)
        ]
    )
    wqkv = jnp.concatenate([wq, wkv], axis=2)
    wqkv_own = jnp.stack([wqkv[0]] + [along_plane(wqkv[j], j) for j in range(1, count)])
    wqkv_sib = to_sibling(wqkv_own)
    wqkv_all = jnp.concatenate([wqkv_own, wqkv_sib]).reshape(depth, q_width + 128)

    def fetch(weight):
        cut = cut_blocks(weight, f, k, count)
        width = cut.shape[2]
        own = jnp.stack([cut[0]] + [along_plane(cut[j], j) for j in range(1, count)])
        sib = to_sibling(own)
        return own.reshape(depth // 2, width), sib.reshape(depth // 2, width)

    gate_own, gate_sib = fetch(w_gate)
    up_own, up_sib = fetch(w_up)

    order = jnp.stack([(f ^ j) * 2 + (k ^ h) for h in range(2) for j in range(count)]).astype(jnp.int32)

    half_dim = HEAD_DIM // 2
    frequency = jnp.power(ROPE_BASE, jnp.arange(half_dim, dtype=F32) * (-2.0 / HEAD_DIM))
    positions = first_pos - jnp.arange(rows, dtype=jnp.int32)
    angles = positions.astype(F32)[:, None] * frequency[None, :]
    cos32, sin32 = jnp.cos(angles), jnp.sin(angles)
    cosine = jnp.concatenate([cos32] * 4, axis=1)
    sine = jnp.concatenate([-sin32, sin32, -sin32, sin32], axis=1)

    normed_one, queries, kv = qkv_project(order, x_all, gain_one, wqkv_all, cosine, sine, rows)
    queries = queries.reshape(count, rows, q_width)
    kv = kv.reshape(count, rows, 128)

    mine = [kv] + [along_line(kv, -s) for s in range(1, line)]
    mine = jnp.stack(mine)
    kv_all = jnp.concatenate([mine, to_sibling(mine)])
    places = []
    for h in range(2):
        for s in range(line):
            start = slot - 1 - (2 * (z + s) + (k ^ h)) * rows
            places.append(start - jnp.arange(rows, dtype=jnp.int32))
    kp = jnp.concatenate(places)
    kp = jnp.where(kp < 0, FAR, kp).reshape(1, -1)
    at = jnp.concatenate([first_pos.reshape(1), all_lengths]).astype(jnp.int32)

    attended, log_total = attend(at, queries, kv_all, kp)
    attended = attended.reshape(total, q_width)

    mixed_part = nn(attended, w_out).astype(BF).reshape(count, rows, depth)
    inputs = x_own.astype(F32)
    mixed = inputs + plane_reduce(mixed_part)
    inv_two = lax.rsqrt(jnp.mean(mixed * mixed, axis=1, keepdims=True) + EPSILON)
    normed_two_own = (mixed * inv_two * gain_two).astype(BF)
    normed_two = jnp.concatenate(plane_gather(normed_two_own))
    normed_two = pick_columns(normed_two, order, 2 * count)
    n2_own, n2_sib = normed_two[:, : depth // 2], normed_two[:, depth // 2 :]

    valid = (positions < length).astype(F32)[:, None]
    out_back = cotangent.reshape(rows, depth).astype(F32) * valid
    branch_own = out_back.astype(BF)
    branch = jnp.concatenate(plane_gather(branch_own))

    gate = nn(n2_own, gate_own) + nn(n2_sib, gate_sib)
    up = nn(n2_own, up_own) + nn(n2_sib, up_sib)
    sigmoid = jax.nn.sigmoid(gate)
    hidden = (gate * sigmoid * up).astype(BF)

    half_depth = depth // 2
    branch_mine = lax.dynamic_slice_in_dim(branch, k * half_depth, half_depth, 1)
    branch_other = lax.dynamic_slice_in_dim(branch, (1 - k) * half_depth, half_depth, 1)

    def pair_sum(own, other):
        return (own + to_sibling(other.astype(BF)).astype(F32)).astype(BF)

    def swap_slabs(own):
        return jnp.stack([own[0]] + [along_plane(own[j], j) for j in range(1, count)])

    down_half = line_sum(pair_sum(tn(hidden, branch_mine), tn(hidden, branch_other)))
    down_grad = join_columns(down_half, to_sibling(down_half), k)

    hidden_grad = nt(branch, w_down)
    gate_back = (hidden_grad * up * sigmoid * (1.0 + gate * (1.0 - sigmoid))).astype(BF)
    up_back = (hidden_grad * gate * sigmoid).astype(BF)

    def slab_grad(left_own, left_other, right):
        width = right.shape[1]
        own = pair_sum(tn(left_own, right), tn(left_other, right)).reshape(count, half, width)
        return line_sum(swap_slabs(own))

    gate_half = slab_grad(n2_own, n2_sib, gate_back)
    gate_grad = join_rows(gate_half, to_sibling(gate_half), f, k)
    up_half = slab_grad(n2_own, n2_sib, up_back)
    up_grad = join_rows(up_half, to_sibling(up_half), f, k)

    back_own = (nt(gate_back, gate_own) + nt(up_back, up_own)).astype(BF)
    back_sib = (nt(gate_back, gate_sib) + nt(up_back, up_sib)).astype(BF)
    normed_back = put_columns(jnp.concatenate([back_own, back_sib], axis=1), order, 2 * count)
    normed_back = plane_reduce(normed_back.reshape(count, rows, depth))

    out_part = nn(hidden, w_down).astype(BF).reshape(count, rows, depth)
    outputs = mixed + plane_reduce(out_part)

    mixed_back, gain_two_grad = rms_backward(mixed, inv_two, gain_two, normed_back)
    mixed_grad = out_back + mixed_back
    attn_back = jnp.concatenate(plane_gather(mixed_grad.astype(BF)))
    attended_grad = nt(attn_back, w_out).astype(BF).reshape(count, rows, q_width)

    back_mine = lax.dynamic_slice_in_dim(attn_back, k * half_depth, half_depth, 1)
    back_other = lax.dynamic_slice_in_dim(attn_back, (1 - k) * half_depth, half_depth, 1)
    out_half = line_sum(pair_sum(tn(attended, back_mine), tn(attended, back_other)))
    out_grad = join_columns(out_half, to_sibling(out_half), k)

    query_back, kv_part = attend_back(at, queries, attended_grad, log_total, kv_all, kp, cosine, sine)
    kv_mine = kv_part[:line].astype(F32) + to_sibling(kv_part[line:]).astype(F32)
    kv_back = kv_mine[0]
    for s in range(1, line):
        kv_back = kv_back + along_line(kv_mine[s].astype(BF), s).astype(F32)
    lead, trail, flat = kv_back[..., :32], kv_back[..., 32:64], kv_back[..., 64:]
    kv_back = jnp.concatenate(
        [lead * cos32 + trail * sin32, trail * cos32 - lead * sin32, flat], axis=-1
    ).astype(BF)
    qkv_back = jnp.concatenate(
        [query_back.reshape(total, q_width), kv_back.reshape(total, 128)], axis=1
    )

    normed_one_back = nt(qkv_back, wqkv_all).astype(BF)
    normed_one_back = put_columns(normed_one_back, order, 2 * count)
    normed_one_back = plane_reduce(normed_one_back.reshape(count, rows, depth))
    inv_one = lax.rsqrt(jnp.mean(inputs * inputs, axis=1, keepdims=True) + EPSILON)
    input_back, gain_one_grad = rms_backward(inputs, inv_one, gain_one, normed_one_back)
    input_grad = mixed_grad + input_back

    n1_own, n1_sib = normed_one[:, :half_depth], normed_one[:, half_depth:]
    qkv_own = pair_sum(tn(n1_own, qkv_back), tn(n1_sib, qkv_back)).reshape(count, half, q_width + 128)
    gains = jnp.stack([gain_one_grad, gain_two_grad]).reshape(2, count, slab)
    gains = jnp.stack(
        [lax.dynamic_index_in_dim(gains, f ^ j, 1, keepdims=False) for j in range(count)]
    ).astype(BF)
    gains = line_sum(swap_slabs(gains))
    qkv_half = line_sum(swap_slabs(qkv_own))
    gains = jnp.sum(gains.astype(F32), axis=0) + jnp.sum(to_sibling(gains).astype(F32), axis=0)
    qkv_other = to_sibling(qkv_half)
    query_grad = join_rows(qkv_half[:, :, :q_width], qkv_other[:, :, :q_width], f, k)
    halves = jnp.stack([qkv_half[:, :, q_width:], qkv_other[:, :, q_width:]])

    def by_head(lo, hi):
        both = [lax.dynamic_index_in_dim(halves, k ^ h, 0, keepdims=False) for h in range(2)]
        both = jnp.concatenate(both, axis=1).astype(F32)[:, :, lo:hi]
        cols = jnp.stack([lax.dynamic_index_in_dim(both, f ^ i, 0, keepdims=False) for i in range(count)])
        cols = cols.reshape(KV_HEADS, shared, slab, HEAD_DIM).sum(1)
        return jnp.transpose(cols, (1, 0, 2)).reshape(slab, KV_HEADS * HEAD_DIM)

    key_grad = by_head(0, 64)
    value_grad = by_head(64, 128)

    return (
        outputs.reshape(seqs, rows, depth),
        input_grad.reshape(seqs, rows, depth),
        gains[0],
        query_grad,
        key_grad,
        value_grad,
        out_grad,
        gains[1],
        gate_grad,
        up_grad,
        down_grad,
    )


def solution(mesh):
    count, ctx = mesh.shape["fsdp"], mesh.shape["ctx"]
    split = Mesh(mesh.devices.reshape(count, ctx // 2, 2), ("fsdp", "z", "core"))
    act = P("fsdp", ("z", "core"), None)
    row, mat = P("fsdp"), P("fsdp", None)
    return jax.shard_map(
        body,
        mesh=split,
        in_specs=(act, act, row, row, mat, mat, mat, mat, row, mat, mat, mat),
        out_specs=(act, act, row, mat, mat, mat, mat, row, mat, mat, mat),
        check_vma=False,
    )
```

time: 2330 us -> 1090 us (0.47)
  waiting for transfers between devices: 1960 us -> 614 us
  Pallas kernels: 0 us -> 126 us
  starting transfers between devices: 28.5 us -> 129 us
  matrix products: 191 us -> 90.8 us
  blocking collectives: 42.1 us -> 0 us
  local copies, waits for them, and re-layouts: 29.2 us -> 57.5 us
    reduce_scatter x7 -> x0, waiting for transfers between devices: 806 us -> none  [the longest x1 208 us: body(): lax.psum_scatter(up_term.astype(jnp.bfloat16), 'fsdp', scatter_dimension=...]
    all_gather x7 -> x0, waiting for transfers between devices: 736 us -> none  [the longest x1 204 us: body(): lax.all_gather(w_gate, 'fsdp', axis=0, tiled=True)]
    ppermute x14 -> x96, waiting for transfers between devices: 27.8 us -> 614 us  [the longest x6 308 us: line_sum(): got = lax.ppermute(value, 'z', [(i + 1, i), (count - 2 - i, count - 1 - i)])]
    psum x1 -> x0, waiting for transfers between devices: 388 us -> none  [body(): lax.psum(attn_parts[1].astype(jnp.bfloat16), 'ctx').astype(jnp.float32)]
    pallas_call x0 -> x14, Pallas kernels: none -> 126 us  [the longest x1 26.6 us: attend_back(): pl.pallas_call(attend_back_kernel, grid_spec=spec, out_shape=[jax.ShapeDt...]
    ppermute x14 -> x96, starting transfers between devices: 27.5 us -> 129 us  [the longest x56 64 us: along_plane(): return lax.ppermute(value, 'fsdp', [(i, i ^ step) for i in range(count)])]
    dot_general x77 -> x23, matrix products: 191 us -> 90.8 us  [the longest x6 37.9 us: nn(): return jnp.dot(a, b, preferred_element_type=F32)]
    convert_element_type x23 -> x11, other arithmetic: 29.9 us -> 3 us  [the longest x4 1.3 us: plane_reduce(): got = along_plane(jnp.stack([held[j].astype(BF) for j in going]), bit)]
  transfers between devices with their start and end apart: 29 -> 96, of which waited for: 21 -> 48; matrix products, arithmetic and copies ran while one was open for 8% -> 14% of each run, Pallas kernels for 0% -> 10%
where the time goes in v1:
time: 1090 us
  waiting for transfers between devices  614 us (56%)
  starting transfers between devices  129 us (12%)
  Pallas kernels  126 us (12%)
  matrix products  90.8 us (8%)
  other arithmetic  59.6 us (5%)
  local copies, waits for them, and re-layouts  57.5 us (5%)
    ppermute x6, waiting for transfers between devices, line_sum(): got = lax.ppermute(value, 'z', [(i + 1, i), (count - 2 - i, count - 1 - i)])  308 us
    ppermute x56, waiting for transfers between devices, along_plane(): return lax.ppermute(value, 'fsdp', [(i, i ^ step) for i in range(count)])  182 us
    ppermute x6, waiting for transfers between devices, line_sum(): got = lax.ppermute(value, 'z', [(i, i + 1), (count - 1 - i, count - 2 - i)])  107 us
    ppermute x56, starting transfers between devices, along_plane(): return lax.ppermute(value, 'fsdp', [(i, i ^ step) for i in range(count)])  64 us
    dot_general x6, matrix products, nn(): return jnp.dot(a, b, preferred_element_type=F32)  37.9 us
    ppermute x6, starting transfers between devices, line_sum(): got = lax.ppermute(value, 'z', [(i, i + 1), (count - 1 - i, count - 2 - i)])  31.9 us
    dot_general x10, matrix products, tn(): lax.dot_general(a, b, (((0,), (0,)), ((), ())), preferred_element_type=F32)  26.9 us
    pallas_call x1, Pallas kernels, attend_back(): pl.pallas_call(attend_back_kernel, grid_spec=spec, out_shape=[jax.ShapeDt...  26.6 us
  transfers between devices with their start and end apart: 96, of which 48 were waited for; matrix products, arithmetic and copies ran while one was open for 14% of the time, Pallas kernels for 10%

profile of v1, /device:TPU:0, one launch (start us, length us, event | category | flops | bytes accessed | tf_op | source)
XLA Modules:
  0.0 1085.1 jit_solution(6651803093729433044)
XLA Ops:
  3.7 3.9 collective-permute-start.2
  23.2 4.0 cut_blocks.3
  31.6 4.8 cut_blocks.4
  39.8 4.8 cut_blocks.5
  66.6 5.2 collective-permute-done.35
  77.0 18.7 %collective-permute-done.36 = bf16[1,64,2048]{2,1,0:T(8,128)(2,1)S(1)} collective-permute-done((bf16[1,64,2048]{2,1,0:T(8,128)(2,1)}, bf16[1,64,2048]{2,1,0:T(8,128)(2,1)S(1)}, u32[]{:S(2)}, u32[]{:S(2)}) %collective-permute-start.36) | collective-permute-done | bytes 262176 | tf_op jit(solution)/shard_map/ppermute | solution.py:27
  108.6 20.2 %collective-permute-done.24 = bf16[256,1408]{1,0:T(8,128)(2,1)S(1)} collective-permute-done((bf16[256,1408]{1,0:T(8,128)(2,1)S(1)}, bf16[256,1408]{1,0:T(8,128)(2,1)S(1)}, u32[]{:S(2)}, u32[]{:S(2)}) %collective-permute-start.24) | collective-permute-done | bytes 720928 | tf_op jit(solution)/shard_map/ppermute | solution.py:27
  134.1 11.8 %collective-permute-done.28 = bf16[256,1408]{1,0:T(8,128)(2,1)S(1)} collective-permute-done((bf16[256,1408]{1,0:T(8,128)(2,1)S(1)}, bf16[256,1408]{1,0:T(8,128)(2,1)S(1)}, u32[]{:S(2)}, u32[]{:S(2)}) %collective-permute-start.28) | collective-permute-done | bytes 720928 | tf_op jit(solution)/shard_map/ppermute | solution.py:27
  149.8 4.7 collective-permute-done.5
  165.1 6.9 qkv_project.1
  177.8 4.6 collective-permute-done.13
  182.4 4.1 collective-permute-done.12
  190.5 17.9 %attend.1 = (bf16[4,128,512]{2,1,0:T(8,128)(2,1)}, f32[4,128,512]{2,1,0:T(8,128)}) custom-call(s32[5]{0:T(128)} %concatenate.182.at_ref, bf16[4,128,512]{2,1,0:T(8,128)(2,1)} %bitcast.468, bf16[8,4,128,128]{3,2,1,0:T(8,128)(2,1)} %copy-done.66, s32[1,1024]{1,0:T(1,128)} %compare_select_fusion.kp_ref), custom_call_target="tpu_custom_call" | custom-call | flops 2147483648 | bytes 4194304 | tf_op jit(solution)/shard_map/attend/pallas_call | solution.py:358
  212.5 12.5 %collective-permute-done.15 = bf16[2,64,2048]{2,1,0:T(8,128)(2,1)S(1)} collective-permute-done((bf16[2,64,2048]{2,1,0:T(8,128)(2,1)S(1)}, bf16[2,64,2048]{2,1,0:T(8,128)(2,1)S(1)}, u32[]{:S(2)}, u32[]{:S(2)}) %collective-permute-start.15) | collective-permute-done | bytes 524320 | tf_op jit(solution)/shard_map/ppermute | solution.py:27
  226.0 6.6 collective-permute-done.16
  234.0 5.4 collective-permute-done.18
  241.7 5.0 fusion.117
  250.0 8.9 collective-permute-done.21
  260.4 6.4 pick_columns.1
  266.9 4.1 fusion.30
  271.0 3.6 fusion.32
  274.6 3.8 convolution_add_fusion
  278.4 17.4 %multiply_convert_fusion.1 = (bf16[512,1408]{1,0:T(8,128)(2,1)S(1)}, bf16[512,1408]{1,0:T(8,128)(2,1)}, bf16[512,1408]{1,0:T(8,128)(2,1)S(1)}) fusion(f32[512,1408]{1,0:T(8,128)S(1)} %copy-done.90, f32[512,1408]{1,0:T(8,128)S(1)} %convolution_add_fusion, f32[512,1408]{1,0:T(8,128)S(1)} %fusion.32, bf16[1024,1408]{1,0:T(8,128)(2,1)} %bitcast.88, ...), kind=kOutput, calls=%fused_computation.16 | convolution fusion | flops 1488650240 | bytes 16908288 | tf_op jit(solution)/shard_map/dot_general | solution.py:302
  295.9 4.7 fusion.119
  300.5 3.6 fusion.118
  304.2 3.7 add_convert_fusion.5
  307.9 3.7 add_convert_fusion.6
  313.0 6.3 put_columns.2
  322.9 6.6 convolution_convert_fusion.5
  360.0 11.1 %collective-permute-done.45 = bf16[2,64,2048]{2,1,0:T(8,128)(2,1)S(1)} collective-permute-done((bf16[2,64,2048]{2,1,0:T(8,128)(2,1)S(1)}, bf16[2,64,2048]{2,1,0:T(8,128)(2,1)S(1)}, u32[]{:S(2)}, u32[]{:S(2)}) %collective-permute-start.45) | collective-permute-done | bytes 524320 | tf_op jit(solution)/shard_map/ppermute | solution.py:27
  373.5 26.6 %attend_back.1 = (bf16[4,128,512]{2,1,0:T(8,128)(2,1)}, bf16[8,4,128,128]{3,2,1,0:T(8,128)(2,1)}) custom-call(s32[5]{0:T(128)} %concatenate.182.at_ref, bf16[4,128,512]{2,1,0:T(8,128)(2,1)} %bitcast.469, bf16[4,128,512]{2,1,0:T(8,128)(2,1)} %bitcast.473, f32[4,128,512]{2,1,0:T(8,128)} %get-tuple-element.45.lse_ref, bf16[8,4,128,128]{3,2,1,0:T(8,128)(2,1)} %copy-done.66, ...), custom_call_target="tpu_custom_call" | custom-call | flops 5368709120 | bytes 8388608 | tf_op jit(solution)/shard_map/attend_back/pallas_call | solution.py:437
  403.5 5.3 collective-permute-start.48
  421.1 6.3 put_columns.3
  432.7 3.7 add_convert_fusion.1
  440.1 3.7 add_convert_fusion.2
  446.1 3.5 add_convert_fusion
  449.6 7.1 collective-permute-done.86
  456.6 5.1 collective-permute-start.92
  461.8 26.2 %collective-permute-done.85 = bf16[256,1408]{1,0:T(8,128)(2,1)S(1)} collective-permute-done((bf16[256,1408]{1,0:T(8,128)(2,1)S(1)}, bf16[256,1408]{1,0:T(8,128)(2,1)S(1)}, u32[]{:S(2)}, u32[]{:S(2)}) %collective-permute-start.85) | collective-permute-done | bytes 720928 | tf_op jit(solution)/shard_map/ppermute | solution.py:27
  491.8 5.5 collective-permute-start.87
  497.4 7.1 collective-permute-done.77
  504.4 3.9 collective-permute-done.76
  510.4 9.0 collective-permute-done.53
  519.4 5.7 collective-permute-start.79
  527.9 3.9 collective-permute-done.54
  545.5 40.8 %collective-permute-done.87 = bf16[4,256,1408]{2,1,0:T(8,128)(2,1)S(1)} collective-permute-done((bf16[4,256,1408]{2,1,0:T(8,128)(2,1)S(1)}, bf16[4,256,1408]{2,1,0:T(8,128)(2,1)S(1)}, u32[]{:S(2)}, u32[]{:S(2)}) %collective-permute-start.87) | collective-permute-done | bytes 2883616 | tf_op jit(solution)/shard_map/ppermute | solution.py:80
  596.5 5.7 collective-permute-start.71
  603.2 44.9 %collective-permute-done.79 = bf16[4,256,1408]{2,1,0:T(8,128)(2,1)S(1)} collective-permute-done((bf16[4,256,1408]{2,1,0:T(8,128)(2,1)S(1)}, bf16[4,256,1408]{2,1,0:T(8,128)(2,1)S(1)}, u32[]{:S(2)}, u32[]{:S(2)}) %collective-permute-start.79) | collective-permute-done | bytes 2883616 | tf_op jit(solution)/shard_map/ppermute | solution.py:80
  655.2 4.4 collective-permute-start.58
  660.9 5.7 collective-permute-done.58
  666.5 5.4 collective-permute-start.66
  680.0 15.4 %collective-permute-done.66 = bf16[4,256,640]{2,1,0:T(8,128)(2,1)} collective-permute-done((bf16[4,256,640]{2,1,0:T(8,128)(2,1)}, bf16[4,256,640]{2,1,0:T(8,128)(2,1)}, u32[]{:S(2)}, u32[]{:S(2)}) %collective-permute-start.66) | collective-permute-done | bytes 1310752 | tf_op jit(solution)/shard_map/ppermute | solution.py:80
  699.9 4.1 add.492
  712.3 91.7 %collective-permute-done.60 = bf16[4,2,512]{2,0,1:T(4,128)(2,1)S(1)} collective-permute-done((bf16[4,2,512]{2,0,1:T(4,128)(2,1)S(1)}, bf16[4,2,512]{2,0,1:T(4,128)(2,1)S(1)}, u32[]{:S(2)}, u32[]{:S(2)}) %collective-permute-start.60) | collective-permute-done | bytes 8224 | tf_op jit(solution)/shard_map/ppermute | solution.py:84
  806.5 22.9 %collective-permute-done.73 = bf16[512,1024]{1,0:T(8,128)(2,1)S(1)} collective-permute-done((bf16[512,1024]{1,0:T(8,128)(2,1)S(1)}, bf16[512,1024]{1,0:T(8,128)(2,1)S(1)}, u32[]{:S(2)}, u32[]{:S(2)}) %collective-permute-start.73) | collective-permute-done | bytes 1048608 | tf_op jit(solution)/shard_map/ppermute | solution.py:84
  831.8 59.5 %collective-permute-done.94 = bf16[1408,1024]{1,0:T(8,128)(2,1)S(1)} collective-permute-done((bf16[1408,1024]{1,0:T(8,128)(2,1)S(1)}, bf16[1408,1024]{1,0:T(8,128)(2,1)S(1)}, u32[]{:S(2)}, u32[]{:S(2)}) %collective-permute-start.94) | collective-permute-done | bytes 2883616 | tf_op jit(solution)/shard_map/ppermute | solution.py:84
  894.4 58.6 %collective-permute-done.89 = bf16[4,256,1408]{2,1,0:T(8,128)(2,1)S(1)} collective-permute-done((bf16[4,256,1408]{2,1,0:T(8,128)(2,1)S(1)}, bf16[4,256,1408]{2,1,0:T(8,128)(2,1)S(1)}, u32[]{:S(2)}, u32[]{:S(2)}) %collective-permute-start.89) | collective-permute-done | bytes 2883616 | tf_op jit(solution)/shard_map/ppermute | solution.py:84
  954.9 59.9 %collective-permute-done.81 = bf16[4,256,1408]{2,1,0:T(8,128)(2,1)S(1)} collective-permute-done((bf16[4,256,1408]{2,1,0:T(8,128)(2,1)S(1)}, bf16[4,256,1408]{2,1,0:T(8,128)(2,1)S(1)}, u32[]{:S(2)}, u32[]{:S(2)}) %collective-permute-start.81) | collective-permute-done | bytes 2883616 | tf_op jit(solution)/shard_map/ppermute | solution.py:84
  1016.8 15.5 %collective-permute-done.68 = bf16[4,256,640]{2,1,0:T(8,128)(2,1)S(1)} collective-permute-done((bf16[4,256,640]{2,1,0:T(8,128)(2,1)S(1)}, bf16[4,256,640]{2,1,0:T(8,128)(2,1)S(1)}, u32[]{:S(2)}, u32[]{:S(2)}) %collective-permute-start.68) | collective-permute-done | bytes 1310752 | tf_op jit(solution)/shard_map/ppermute | solution.py:84
  1035.9 6.2 join_columns.2
  1049.5 6.8 join_rows.3
  1056.3 9.0 join_columns.3
  1065.3 9.7 join_rows.4
  1075.0 9.8 join_rows.5
  (550 shorter events, 252.8 us)
Async XLA Ops:
  3.7 47.3 %collective-permute-start.2 = (bf16[4,512]{1,0:T(4,128)(2,1)}, bf16[4,512]{1,0:T(4,128)(2,1)S(1)}, u32[]{:S(2)}, u32[]{:S(2)}) collective-permute-start(bf16[4,512]{1,0:T(4,128)(2,1)} %maximum_maximum_fusion.1), channel_id=1, source_target_pairs={{0,24},{8,16},{16,8},{24,0},{1,25},{9,17},{17,9},{25,1},{2,26},{10... | collective-permute-start | bytes 12296 | tf_op jit(solution)/shard_map/ppermute | solution.py:27
  7.6 43.4 %collective-permute-start.1 = (bf16[4,512]{1,0:T(4,128)(2,1)}, bf16[4,512]{1,0:T(4,128)(2,1)S(1)}, u32[]{:S(2)}, u32[]{:S(2)}) collective-permute-start(bf16[4,512]{1,0:T(4,128)(2,1)} %maximum_maximum_fusion.1), channel_id=1, source_target_pairs={{0,16},{8,24},{16,0},{24,8},{1,17},{9,25},{17,1},{25,9},{2,18},{10... | collective-permute-start | bytes 12296 | tf_op jit(solution)/shard_map/ppermute | solution.py:27
  8.1 44.9 %collective-permute-start = (bf16[4,512]{1,0:T(4,128)(2,1)}, bf16[4,512]{1,0:T(4,128)(2,1)}, u32[]{:S(2)}, u32[]{:S(2)}) collective-permute-start(bf16[4,512]{1,0:T(4,128)(2,1)} %maximum_maximum_fusion.1), channel_id=1, source_target_pairs={{0,8},{8,0},{16,24},{24,16},{1,9},{9,1},{17,25},{25,17},{2,10},{10... | collective-permute-start | bytes 12296 | tf_op jit(solution)/shard_map/ppermute | solution.py:27
  10.0 65.3 %collective-permute-start.4 = (bf16[1,64,2048]{2,1,0:T(8,128)(2,1)}, bf16[1,64,2048]{2,1,0:T(8,128)(2,1)}, u32[]{:S(2)}, u32[]{:S(2)}) collective-permute-start(bf16[1,64,2048]{2,1,0:T(8,128)(2,1)} %get-tuple-element.216), channel_id=1, source_target_pairs={{0,16},{8,24},{16,0},{24,8},{1,17},{9,25},{17,1},{25,9},{2,18},{10... | collective-permute-start | bytes 786440 | tf_op jit(solution)/shard_map/ppermute | solution.py:27
  12.0 52.3 %collective-permute-start.3 = (bf16[1,64,2048]{2,1,0:T(8,128)(2,1)}, bf16[1,64,2048]{2,1,0:T(8,128)(2,1)}, u32[]{:S(2)}, u32[]{:S(2)}) collective-permute-start(bf16[1,64,2048]{2,1,0:T(8,128)(2,1)} %get-tuple-element.217), channel_id=1, source_target_pairs={{0,8},{8,0},{16,24},{24,16},{1,9},{9,1},{17,25},{25,17},{2,10},{10... | collective-permute-start | bytes 786440 | tf_op jit(solution)/shard_map/ppermute | solution.py:27
  50.9 52.2 %collective-permute-start.9 = (bf16[256,640]{1,0:T(8,128)(2,1)}, bf16[256,640]{1,0:T(8,128)(2,1)}, u32[]{:S(2)}, u32[]{:S(2)}) collective-permute-start(bf16[256,640]{1,0:T(8,128)(2,1)} %get-tuple-element.192), channel_id=1, source_target_pairs={{0,24},{8,16},{16,8},{24,0},{1,25},{9,17},{17,9},{25,1},{2,26},{10... | collective-permute-start | bytes 983048 | tf_op jit(solution)/shard_map/ppermute | solution.py:27
  50.9 49.3 %collective-permute-start.8 = (bf16[256,640]{1,0:T(8,128)(2,1)}, bf16[256,640]{1,0:T(8,128)(2,1)}, u32[]{:S(2)}, u32[]{:S(2)}) collective-permute-start(bf16[256,640]{1,0:T(8,128)(2,1)} %get-tuple-element.193), channel_id=1, source_target_pairs={{0,16},{8,24},{16,0},{24,8},{1,17},{9,25},{17,1},{25,9},{2,18},{10... | collective-permute-start | bytes 983048 | tf_op jit(solution)/shard_map/ppermute | solution.py:27
  52.9 45.1 %collective-permute-start.7 = (bf16[256,640]{1,0:T(8,128)(2,1)}, bf16[256,640]{1,0:T(8,128)(2,1)}, u32[]{:S(2)}, u32[]{:S(2)}) collective-permute-start(bf16[256,640]{1,0:T(8,128)(2,1)} %get-tuple-element.194), channel_id=1, source_target_pairs={{0,8},{8,0},{16,24},{24,16},{1,9},{9,1},{17,25},{25,17},{2,10},{10... | collective-permute-start | bytes 983048 | tf_op jit(solution)/shard_map/ppermute | solution.py:27
  71.8 23.9 %collective-permute-start.36 = (bf16[1,64,2048]{2,1,0:T(8,128)(2,1)}, bf16[1,64,2048]{2,1,0:T(8,128)(2,1)S(1)}, u32[]{:S(2)}, u32[]{:S(2)}) collective-permute-start(bf16[1,64,2048]{2,1,0:T(8,128)(2,1)} %get-tuple-element.212), channel_id=1, source_target_pairs={{0,16},{8,24},{16,0},{24,8},{1,17},{9,25},{17,1},{25,9},{2,18},{10... | collective-permute-start | bytes 786440 | tf_op jit(solution)/shard_map/ppermute | solution.py:27
  75.3 29.8 %collective-permute-start.25 = (bf16[256,1408]{1,0:T(8,128)(2,1)S(1)}, bf16[256,1408]{1,0:T(8,128)(2,1)S(1)}, u32[]{:S(2)}, u32[]{:S(2)}) collective-permute-start(bf16[256,1408]{1,0:T(8,128)(2,1)S(1)} %copy-done.54), channel_id=1, source_target_pairs={{0,24},{8,16},{16,8},{24,0},{1,25},{9,17},{17,9},{25,1},{2,26},{10... | collective-permute-start | bytes 2162696 | tf_op jit(solution)/shard_map/ppermute | solution.py:27
  95.7 33.1 %collective-permute-start.24 = (bf16[256,1408]{1,0:T(8,128)(2,1)S(1)}, bf16[256,1408]{1,0:T(8,128)(2,1)S(1)}, u32[]{:S(2)}, u32[]{:S(2)}) collective-permute-start(bf16[256,1408]{1,0:T(8,128)(2,1)S(1)} %copy-done.53), channel_id=1, source_target_pairs={{0,16},{8,24},{16,0},{24,8},{1,17},{9,25},{17,1},{25,9},{2,18},{10... | collective-permute-start | bytes 2162696 | tf_op jit(solution)/shard_map/ppermute | solution.py:27
  98.0 30.9 %collective-permute-start.23 = (bf16[256,1408]{1,0:T(8,128)(2,1)S(1)}, bf16[256,1408]{1,0:T(8,128)(2,1)S(1)}, u32[]{:S(2)}, u32[]{:S(2)}) collective-permute-start(bf16[256,1408]{1,0:T(8,128)(2,1)S(1)} %copy-done.52), channel_id=1, source_target_pairs={{0,8},{8,0},{16,24},{24,16},{1,9},{9,1},{17,25},{25,17},{2,10},{10... | collective-permute-start | bytes 2162696 | tf_op jit(solution)/shard_map/ppermute | solution.py:27
  100.2 31.8 %collective-permute-start.29 = (bf16[256,1408]{1,0:T(8,128)(2,1)S(1)}, bf16[256,1408]{1,0:T(8,128)(2,1)S(1)}, u32[]{:S(2)}, u32[]{:S(2)}) collective-permute-start(bf16[256,1408]{1,0:T(8,128)(2,1)S(1)} %copy-done.51), channel_id=1, source_target_pairs={{0,24},{8,16},{16,8},{24,0},{1,25},{9,17},{17,9},{25,1},{2,26},{10... | collective-permute-start | bytes 2162696 | tf_op jit(solution)/shard_map/ppermute | solution.py:27
  103.1 42.8 %collective-permute-start.28 = (bf16[256,1408]{1,0:T(8,128)(2,1)S(1)}, bf16[256,1408]{1,0:T(8,128)(2,1)S(1)}, u32[]{:S(2)}, u32[]{:S(2)}) collective-permute-start(bf16[256,1408]{1,0:T(8,128)(2,1)S(1)} %copy-done.50), channel_id=1, source_target_pairs={{0,16},{8,24},{16,0},{24,8},{1,17},{9,25},{17,1},{25,9},{2,18},{10... | collective-permute-start | bytes 2162696 | tf_op jit(solution)/shard_map/ppermute | solution.py:27
  105.1 42.9 %collective-permute-start.27 = (bf16[256,1408]{1,0:T(8,128)(2,1)S(1)}, bf16[256,1408]{1,0:T(8,128)(2,1)S(1)}, u32[]{:S(2)}, u32[]{:S(2)}) collective-permute-start(bf16[256,1408]{1,0:T(8,128)(2,1)S(1)} %copy-done.49), channel_id=1, source_target_pairs={{0,8},{8,0},{16,24},{24,16},{1,9},{9,1},{17,25},{25,17},{2,10},{10... | collective-permute-start | bytes 2162696 | tf_op jit(solution)/shard_map/ppermute | solution.py:27
  128.8 28.2 %collective-permute-start.6 = (bf16[2,64,2048]{2,1,0:T(8,128)(2,1)S(1)}, bf16[2,64,2048]{2,1,0:T(8,128)(2,1)S(1)}, u32[]{:S(2)}, u32[]{:S(2)}) collective-permute-start(bf16[2,64,2048]{2,1,0:T(8,128)(2,1)S(1)} %pad_maximum_fusion.11), channel_id=1, source_target_pairs={{0,16},{8,24},{16,0},{24,8},{1,17},{9,25},{17,1},{25,9},{2,18},{10... | collective-permute-start | bytes 1572872 | tf_op jit(solution)/shard_map/ppermute | solution.py:27
  128.9 25.6 %collective-permute-start.5 = (bf16[2,64,2048]{2,1,0:T(8,128)(2,1)S(1)}, bf16[2,64,2048]{2,1,0:T(8,128)(2,1)S(1)}, u32[]{:S(2)}, u32[]{:S(2)}) collective-permute-start(bf16[2,64,2048]{2,1,0:T(8,128)(2,1)S(1)} %pad_maximum_fusion.10), channel_id=1, source_target_pairs={{0,8},{8,0},{16,24},{24,16},{1,9},{9,1},{17,25},{25,17},{2,10},{10... | collective-permute-start | bytes 1572872 | tf_op jit(solution)/shard_map/ppermute | solution.py:27
  132.1 30.6 %collective-permute-start.38 = (bf16[2,64,2048]{2,1,0:T(8,128)(2,1)S(1)}, bf16[2,64,2048]{2,1,0:T(8,128)(2,1)S(1)}, u32[]{:S(2)}, u32[]{:S(2)}) collective-permute-start(bf16[2,64,2048]{2,1,0:T(8,128)(2,1)S(1)} %pad_maximum_fusion.18), channel_id=1, source_target_pairs={{0,16},{8,24},{16,0},{24,8},{1,17},{9,25},{17,1},{25,9},{2,18},{10... | collective-permute-start | bytes 1572872 | tf_op jit(solution)/shard_map/ppermute | solution.py:27
  145.9 15.0 %collective-permute-start.37 = (bf16[2,64,2048]{2,1,0:T(8,128)(2,1)S(1)}, bf16[2,64,2048]{2,1,0:T(8,128)(2,1)S(1)}, u32[]{:S(2)}, u32[]{:S(2)}) collective-permute-start(bf16[2,64,2048]{2,1,0:T(8,128)(2,1)S(1)} %pad_maximum_fusion.17), channel_id=1, source_target_pairs={{0,8},{8,0},{16,24},{24,16},{1,9},{9,1},{17,25},{25,17},{2,10},{10... | collective-permute-start | bytes 1572872 | tf_op jit(solution)/shard_map/ppermute | solution.py:27
  148.1 15.3 %collective-permute-start.10 = (bf16[4,256,640]{2,1,0:T(8,128)(2,1)S(1)}, bf16[4,256,640]{2,1,0:T(8,128)(2,1)S(1)}, u32[]{:S(2)}, u32[]{:S(2)}) collective-permute-start(bf16[4,256,640]{2,1,0:T(8,128)(2,1)S(1)} %pad_maximum_fusion.5), channel_id=1, source_target_pairs={{0,1},{1,0},{2,3},{3,2},{4,5},{5,4},{6,7},{7,6},{8,9},{9,8},{10,11... | collective-permute-start | bytes 3932168 | tf_op jit(solution)/shard_map/ppermute | solution.py:31
  154.5 112.4 %collective-permute-start.30 = (bf16[4,256,1408]{2,1,0:T(8,128)(2,1)}, bf16[4,256,1408]{2,1,0:T(8,128)(2,1)}, u32[]{:S(2)}, u32[]{:S(2)}) collective-permute-start(bf16[4,256,1408]{2,1,0:T(8,128)(2,1)} %pad_maximum_fusion.1), channel_id=1, source_target_pairs={{0,1},{1,0},{2,3},{3,2},{4,5},{5,4},{6,7},{7,6},{8,9},{9,8},{10,11... | collective-permute-start | bytes 8650760 | tf_op jit(solution)/shard_map/ppermute | solution.py:31
  157.0 113.9 %collective-permute-start.26 = (bf16[4,256,1408]{2,1,0:T(8,128)(2,1)}, bf16[4,256,1408]{2,1,0:T(8,128)(2,1)}, u32[]{:S(2)}, u32[]{:S(2)}) collective-permute-start(bf16[4,256,1408]{2,1,0:T(8,128)(2,1)} %pad_maximum_fusion), channel_id=1, source_target_pairs={{0,1},{1,0},{2,3},{3,2},{4,5},{5,4},{6,7},{7,6},{8,9},{9,8},{10,11... | collective-permute-start | bytes 8650760 | tf_op jit(solution)/shard_map/ppermute | solution.py:31
  211.0 14.0 %collective-permute-start.15 = (bf16[2,64,2048]{2,1,0:T(8,128)(2,1)S(1)}, bf16[2,64,2048]{2,1,0:T(8,128)(2,1)S(1)}, u32[]{:S(2)}, u32[]{:S(2)}) collective-permute-start(bf16[2,64,2048]{2,1,0:T(8,128)(2,1)S(1)} %stack.437), channel_id=1, source_target_pairs={{0,16},{8,24},{16,0},{24,8},{1,17},{9,25},{17,1},{25,9},{2,18},{10... | collective-permute-start | bytes 1572872 | tf_op jit(solution)/shard_map/ppermute | solution.py:27
  321.7 19.3 %collective-permute-start.41 = (bf16[2,64,2048]{2,1,0:T(8,128)(2,1)S(1)}, bf16[2,64,2048]{2,1,0:T(8,128)(2,1)S(1)}, u32[]{:S(2)}, u32[]{:S(2)}) collective-permute-start(bf16[2,64,2048]{2,1,0:T(8,128)(2,1)S(1)} %pad_maximum_fusion.19), channel_id=1, source_target_pairs={{0,8},{8,0},{16,24},{24,16},{1,9},{9,1},{17,25},{25,17},{2,10},{10... | collective-permute-start | bytes 1572872 | tf_op jit(solution)/shard_map/ppermute | solution.py:27
  330.5 71.0 %collective-permute-start.31 = (bf16[2,64,2048]{2,1,0:T(8,128)(2,1)}, bf16[2,64,2048]{2,1,0:T(8,128)(2,1)}, u32[]{:S(2)}, u32[]{:S(2)}) collective-permute-start(bf16[2,64,2048]{2,1,0:T(8,128)(2,1)} %stack.438), channel_id=1, source_target_pairs={{0,16},{8,24},{16,0},{24,8},{1,17},{9,25},{17,1},{25,9},{2,18},{10... | collective-permute-start | bytes 1572872 | tf_op jit(solution)/shard_map/ppermute | solution.py:27
  356.7 75.6 %collective-permute-start.83 = (bf16[1024,1408]{1,0:T(8,128)(2,1)}, bf16[1024,1408]{1,0:T(8,128)(2,1)}, u32[]{:S(2)}, u32[]{:S(2)}) collective-permute-start(bf16[1024,1408]{1,0:T(8,128)(2,1)} %convolution_convert_fusion.1), channel_id=1, source_target_pairs={{0,1},{1,0},{2,3},{3,2},{4,5},{5,4},{6,7},{7,6},{8,9},{9,8},{10,11... | collective-permute-start | bytes 8650760 | tf_op jit(solution)/shard_map/ppermute | solution.py:31
  356.7 83.1 %collective-permute-start.75 = (bf16[1024,1408]{1,0:T(8,128)(2,1)}, bf16[1024,1408]{1,0:T(8,128)(2,1)}, u32[]{:S(2)}, u32[]{:S(2)}) collective-permute-start(bf16[1024,1408]{1,0:T(8,128)(2,1)} %convolution_convert_fusion.2), channel_id=1, source_target_pairs={{0,1},{1,0},{2,3},{3,2},{4,5},{5,4},{6,7},{7,6},{8,9},{9,8},{10,11... | collective-permute-start | bytes 8650760 | tf_op jit(solution)/shard_map/ppermute | solution.py:31
  412.7 31.4 %collective-permute-start.91 = (bf16[1408,1024]{1,0:T(8,128)(2,1)}, bf16[1408,1024]{1,0:T(8,128)(2,1)}, u32[]{:S(2)}, u32[]{:S(2)}) collective-permute-start(bf16[1408,1024]{1,0:T(8,128)(2,1)} %convolution_convert_fusion), channel_id=1, source_target_pairs={{0,1},{1,0},{2,3},{3,2},{4,5},{5,4},{6,7},{7,6},{8,9},{9,8},{10,11... | collective-permute-start | bytes 8650760 | tf_op jit(solution)/shard_map/ppermute | solution.py:31
  428.4 62.9 %collective-permute-start.51 = (bf16[2,64,2048]{2,1,0:T(8,128)(2,1)S(1)}, bf16[2,64,2048]{2,1,0:T(8,128)(2,1)S(1)}, u32[]{:S(2)}, u32[]{:S(2)}) collective-permute-start(bf16[2,64,2048]{2,1,0:T(8,128)(2,1)S(1)} %stack.440), channel_id=1, source_target_pairs={{0,16},{8,24},{16,0},{24,8},{1,17},{9,25},{17,1},{25,9},{2,18},{10... | collective-permute-start | bytes 1572872 | tf_op jit(solution)/shard_map/ppermute | solution.py:27
  436.6 20.0 %collective-permute-start.86 = (bf16[256,1408]{1,0:T(8,128)(2,1)S(1)}, bf16[256,1408]{1,0:T(8,128)(2,1)S(1)}, u32[]{:S(2)}, u32[]{:S(2)}) collective-permute-start(bf16[256,1408]{1,0:T(8,128)(2,1)S(1)} %get-tuple-element.151), channel_id=1, source_target_pairs={{0,24},{8,16},{16,8},{24,0},{1,25},{9,17},{17,9},{25,1},{2,26},{10... | collective-permute-start | bytes 2162696 | tf_op jit(solution)/shard_map/ppermute | solution.py:27
  438.5 49.4 %collective-permute-start.85 = (bf16[256,1408]{1,0:T(8,128)(2,1)S(1)}, bf16[256,1408]{1,0:T(8,128)(2,1)S(1)}, u32[]{:S(2)}, u32[]{:S(2)}) collective-permute-start(bf16[256,1408]{1,0:T(8,128)(2,1)S(1)} %get-tuple-element.152), channel_id=1, source_target_pairs={{0,16},{8,24},{16,0},{24,8},{1,17},{9,25},{17,1},{25,9},{2,18},{10... | collective-permute-start | bytes 2162696 | tf_op jit(solution)/shard_map/ppermute | solution.py:27
  439.8 49.5 %collective-permute-start.84 = (bf16[256,1408]{1,0:T(8,128)(2,1)S(1)}, bf16[256,1408]{1,0:T(8,128)(2,1)S(1)}, u32[]{:S(2)}, u32[]{:S(2)}) collective-permute-start(bf16[256,1408]{1,0:T(8,128)(2,1)S(1)} %get-tuple-element.153), channel_id=1, source_target_pairs={{0,8},{8,0},{16,24},{24,16},{1,9},{9,1},{17,25},{25,17},{2,10},{10... | collective-permute-start | bytes 2162696 | tf_op jit(solution)/shard_map/ppermute | solution.py:27
  444.1 47.7 %collective-permute-start.78 = (bf16[256,1408]{1,0:T(8,128)(2,1)S(1)}, bf16[256,1408]{1,0:T(8,128)(2,1)S(1)}, u32[]{:S(2)}, u32[]{:S(2)}) collective-permute-start(bf16[256,1408]{1,0:T(8,128)(2,1)S(1)} %get-tuple-element.155), channel_id=1, source_target_pairs={{0,24},{8,16},{16,8},{24,0},{1,25},{9,17},{17,9},{25,1},{2,26},{10... | collective-permute-start | bytes 2162696 | tf_op jit(solution)/shard_map/ppermute | solution.py:27
  456.6 77.8 %collective-permute-start.92 = (bf16[1408,1024]{1,0:T(8,128)(2,1)S(1)}, bf16[1408,1024]{1,0:T(8,128)(2,1)S(1)}, u32[]{:S(2)}, u32[]{:S(2)}) collective-permute-start(bf16[1408,1024]{1,0:T(8,128)(2,1)S(1)} %add_convert_fusion), channel_id=1, source_target_pairs={{0,2},{6,4},{1,3},{7,5},{8,10},{14,12},{9,11},{15,13},{16,18},{22,... | collective-permute-start | bytes 8650760 | tf_op jit(solution)/shard_map/ppermute | solution.py:80
  488.0 16.4 %collective-permute-start.77 = (bf16[256,1408]{1,0:T(8,128)(2,1)S(1)}, bf16[256,1408]{1,0:T(8,128)(2,1)S(1)}, u32[]{:S(2)}, u32[]{:S(2)}) collective-permute-start(bf16[256,1408]{1,0:T(8,128)(2,1)S(1)} %get-tuple-element.156), channel_id=1, source_target_pairs={{0,16},{8,24},{16,0},{24,8},{1,17},{9,25},{17,1},{25,9},{2,18},{10... | collective-permute-start | bytes 2162696 | tf_op jit(solution)/shard_map/ppermute | solution.py:27
  489.2 19.1 %collective-permute-start.76 = (bf16[256,1408]{1,0:T(8,128)(2,1)S(1)}, bf16[256,1408]{1,0:T(8,128)(2,1)S(1)}, u32[]{:S(2)}, u32[]{:S(2)}) collective-permute-start(bf16[256,1408]{1,0:T(8,128)(2,1)S(1)} %get-tuple-element.157), channel_id=1, source_target_pairs={{0,8},{8,0},{16,24},{24,16},{1,9},{9,1},{17,25},{25,17},{2,10},{10... | collective-permute-start | bytes 2162696 | tf_op jit(solution)/shard_map/ppermute | solution.py:27
  491.4 28.1 %collective-permute-start.53 = (bf16[2,64,2048]{2,1,0:T(8,128)(2,1)S(1)}, bf16[2,64,2048]{2,1,0:T(8,128)(2,1)S(1)}, u32[]{:S(2)}, u32[]{:S(2)}) collective-permute-start(bf16[2,64,2048]{2,1,0:T(8,128)(2,1)S(1)} %pad_maximum_fusion.22), channel_id=1, source_target_pairs={{0,8},{8,0},{16,24},{24,16},{1,9},{9,1},{17,25},{25,17},{2,10},{10... | collective-permute-start | bytes 1572872 | tf_op jit(solution)/shard_map/ppermute | solution.py:27
  491.8 94.5 %collective-permute-start.87 = (bf16[4,256,1408]{2,1,0:T(8,128)(2,1)S(1)}, bf16[4,256,1408]{2,1,0:T(8,128)(2,1)S(1)}, u32[]{:S(2)}, u32[]{:S(2)}) collective-permute-start(bf16[4,256,1408]{2,1,0:T(8,128)(2,1)S(1)} %pad_maximum_fusion.3), channel_id=1, source_target_pairs={{0,2},{6,4},{1,3},{7,5},{8,10},{14,12},{9,11},{15,13},{16,18},{22,... | collective-permute-start | bytes 8650760 | tf_op jit(solution)/shard_map/ppermute | solution.py:80
  504.4 29.6 %collective-permute-start.62 = (bf16[1024,640]{1,0:T(8,128)(2,1)S(1)}, bf16[1024,640]{1,0:T(8,128)(2,1)S(1)}, u32[]{:S(2)}, u32[]{:S(2)}) collective-permute-start(bf16[1024,640]{1,0:T(8,128)(2,1)S(1)} %convolution_convert_fusion.6), channel_id=1, source_target_pairs={{0,1},{1,0},{2,3},{3,2},{4,5},{5,4},{6,7},{7,6},{8,9},{9,8},{10,11... | collective-permute-start | bytes 3932168 | tf_op jit(solution)/shard_map/ppermute | solution.py:31
  508.3 16.9 %collective-permute-start.52 = (bf16[1,64,2048]{2,1,0:T(8,128)(2,1)S(1)}, bf16[1,64,2048]{2,1,0:T(8,128)(2,1)S(1)}, u32[]{:S(2)}, u32[]{:S(2)}) collective-permute-start(bf16[1,64,2048]{2,1,0:T(8,128)(2,1)S(1)} %add_convert_fusion.8), channel_id=1, source_target_pairs={{0,8},{8,0},{16,24},{24,16},{1,9},{9,1},{17,25},{25,17},{2,10},{10... | collective-permute-start | bytes 786440 | tf_op jit(solution)/shard_map/ppermute | solution.py:27
  519.4 128.7 %collective-permute-start.79 = (bf16[4,256,1408]{2,1,0:T(8,128)(2,1)S(1)}, bf16[4,256,1408]{2,1,0:T(8,128)(2,1)S(1)}, u32[]{:S(2)}, u32[]{:S(2)}) collective-permute-start(bf16[4,256,1408]{2,1,0:T(8,128)(2,1)S(1)} %pad_maximum_fusion.2), channel_id=1, source_target_pairs={{0,2},{6,4},{1,3},{7,5},{8,10},{14,12},{9,11},{15,13},{16,18},{22,... | collective-permute-start | bytes 8650760 | tf_op jit(solution)/shard_map/ppermute | solution.py:80
  534.5 55.6 %collective-permute-start.70 = (bf16[512,1024]{1,0:T(8,128)(2,1)}, bf16[512,1024]{1,0:T(8,128)(2,1)S(1)}, u32[]{:S(2)}, u32[]{:S(2)}) collective-permute-start(bf16[512,1024]{1,0:T(8,128)(2,1)} %convolution_convert_fusion.7), channel_id=1, source_target_pairs={{0,1},{1,0},{2,3},{3,2},{4,5},{5,4},{6,7},{7,6},{8,9},{9,8},{10,11... | collective-permute-start | bytes 3145736 | tf_op jit(solution)/shard_map/ppermute | solution.py:31
  541.9 49.2 %collective-permute-start.55 = (bf16[2,512]{1,0:T(2,128)(2,1)S(1)}, bf16[2,512]{1,0:T(2,128)(2,1)S(1)}, u32[]{:S(2)}, u32[]{:S(2)}) collective-permute-start(bf16[2,512]{1,0:T(2,128)(2,1)S(1)} %get-tuple-element.229), channel_id=1, source_target_pairs={{0,8},{8,0},{16,24},{24,16},{1,9},{9,1},{17,25},{25,17},{2,10},{10... | collective-permute-start | bytes 6152 | tf_op jit(solution)/shard_map/ppermute | solution.py:27
  544.8 48.7 %collective-permute-start.56 = (bf16[2,512]{1,0:T(2,128)(2,1)S(1)}, bf16[2,512]{1,0:T(2,128)(2,1)S(1)}, u32[]{:S(2)}, u32[]{:S(2)}) collective-permute-start(bf16[2,512]{1,0:T(2,128)(2,1)S(1)} %get-tuple-element.230), channel_id=1, source_target_pairs={{0,16},{8,24},{16,0},{24,8},{1,17},{9,25},{17,1},{25,9},{2,18},{10... | collective-permute-start | bytes 6152 | tf_op jit(solution)/shard_map/ppermute | solution.py:27
  586.3 16.0 %collective-permute-start.65 = (bf16[256,640]{1,0:T(8,128)(2,1)S(1)}, bf16[256,640]{1,0:T(8,128)(2,1)S(1)}, u32[]{:S(2)}, u32[]{:S(2)}) collective-permute-start(bf16[256,640]{1,0:T(8,128)(2,1)S(1)} %get-tuple-element.187), channel_id=1, source_target_pairs={{0,24},{8,16},{16,8},{24,0},{1,25},{9,17},{17,9},{25,1},{2,26},{10... | collective-permute-start | bytes 983048 | tf_op jit(solution)/shard_map/ppermute | solution.py:27
  591.2 107.1 %collective-permute-start.93 = (bf16[1408,1024]{1,0:T(8,128)(2,1)}, bf16[1408,1024]{1,0:T(8,128)(2,1)}, u32[]{:S(2)}, u32[]{:S(2)}) collective-permute-start(bf16[1408,1024]{1,0:T(8,128)(2,1)} %add.491), channel_id=1, source_target_pairs={{2,4},{4,2},{3,5},{5,3},{10,12},{12,10},{11,13},{13,11},{18,20},{2... | collective-permute-start | bytes 8650760 | tf_op jit(solution)/shard_map/ppermute | solution.py:82
  593.5 110.5 %collective-permute-start.88 = (bf16[4,256,1408]{2,1,0:T(8,128)(2,1)}, bf16[4,256,1408]{2,1,0:T(8,128)(2,1)}, u32[]{:S(2)}, u32[]{:S(2)}) collective-permute-start(bf16[4,256,1408]{2,1,0:T(8,128)(2,1)} %fusion.99), channel_id=1, source_target_pairs={{2,4},{4,2},{3,5},{5,3},{10,12},{12,10},{11,13},{13,11},{18,20},{2... | collective-permute-start | bytes 8650760 | tf_op jit(solution)/shard_map/ppermute | solution.py:82
  596.5 75.5 %collective-permute-start.71 = (bf16[512,1024]{1,0:T(8,128)(2,1)S(1)}, bf16[512,1024]{1,0:T(8,128)(2,1)S(1)}, u32[]{:S(2)}, u32[]{:S(2)}) collective-permute-start(bf16[512,1024]{1,0:T(8,128)(2,1)S(1)} %add_convert_fusion.4), channel_id=1, source_target_pairs={{0,2},{6,4},{1,3},{7,5},{8,10},{14,12},{9,11},{15,13},{16,18},{22,... | collective-permute-start | bytes 3145736 | tf_op jit(solution)/shard_map/ppermute | solution.py:80
  602.3 49.4 %collective-permute-start.64 = (bf16[256,640]{1,0:T(8,128)(2,1)S(1)}, bf16[256,640]{1,0:T(8,128)(2,1)S(1)}, u32[]{:S(2)}, u32[]{:S(2)}) collective-permute-start(bf16[256,640]{1,0:T(8,128)(2,1)S(1)} %get-tuple-element.188), channel_id=1, source_target_pairs={{0,16},{8,24},{16,0},{24,8},{1,17},{9,25},{17,1},{25,9},{2,18},{10... | collective-permute-start | bytes 983048 | tf_op jit(solution)/shard_map/ppermute | solution.py:27
  651.6 57.1 %collective-permute-start.80 = (bf16[4,256,1408]{2,1,0:T(8,128)(2,1)}, bf16[4,256,1408]{2,1,0:T(8,128)(2,1)}, u32[]{:S(2)}, u32[]{:S(2)}) collective-permute-start(bf16[4,256,1408]{2,1,0:T(8,128)(2,1)} %fusion.100), channel_id=1, source_target_pairs={{2,4},{4,2},{3,5},{5,3},{10,12},{12,10},{11,13},{13,11},{18,20},{2... | collective-permute-start | bytes 8650760 | tf_op jit(solution)/shard_map/ppermute | solution.py:82
  666.5 28.9 %collective-permute-start.66 = (bf16[4,256,640]{2,1,0:T(8,128)(2,1)}, bf16[4,256,640]{2,1,0:T(8,128)(2,1)}, u32[]{:S(2)}, u32[]{:S(2)}) collective-permute-start(bf16[4,256,640]{2,1,0:T(8,128)(2,1)} %pad_maximum_fusion.6), channel_id=1, source_target_pairs={{0,2},{6,4},{1,3},{7,5},{8,10},{14,12},{9,11},{15,13},{16,18},{22,... | collective-permute-start | bytes 3932168 | tf_op jit(solution)/shard_map/ppermute | solution.py:80
  677.2 30.7 %collective-permute-start.34 = (bf16[1,64,2048]{2,1,0:T(8,128)(2,1)S(1)}, bf16[1,64,2048]{2,1,0:T(8,128)(2,1)S(1)}, u32[]{:S(2)}, u32[]{:S(2)}) collective-permute-start(bf16[1,64,2048]{2,1,0:T(8,128)(2,1)S(1)} %get-tuple-element.175), channel_id=1, source_target_pairs={{0,16},{8,24},{16,0},{24,8},{1,17},{9,25},{17,1},{25,9},{2,18},{10... | collective-permute-start | bytes 786440 | tf_op jit(solution)/shard_map/ppermute | solution.py:27
  695.4 108.5 %collective-permute-start.60 = (bf16[4,2,512]{2,0,1:T(4,128)(2,1)S(1)}, bf16[4,2,512]{2,0,1:T(4,128)(2,1)S(1)}, u32[]{:S(2)}, u32[]{:S(2)}) collective-permute-start(bf16[4,2,512]{2,0,1:T(4,128)(2,1)S(1)} %fusion.154), channel_id=1, source_target_pairs={{2,0},{4,6},{3,1},{5,7},{10,8},{12,14},{11,9},{13,15},{18,16},{20,... | collective-permute-start | bytes 24584 | tf_op jit(solution)/shard_map/ppermute | solution.py:84
  698.3 131.1 %collective-permute-start.73 = (bf16[512,1024]{1,0:T(8,128)(2,1)S(1)}, bf16[512,1024]{1,0:T(8,128)(2,1)S(1)}, u32[]{:S(2)}, u32[]{:S(2)}) collective-permute-start(bf16[512,1024]{1,0:T(8,128)(2,1)S(1)} %add.483), channel_id=1, source_target_pairs={{2,0},{4,6},{3,1},{5,7},{10,8},{12,14},{11,9},{13,15},{18,16},{20,... | collective-permute-start | bytes 3145736 | tf_op jit(solution)/shard_map/ppermute | solution.py:84
  704.0 187.2 %collective-permute-start.94 = (bf16[1408,1024]{1,0:T(8,128)(2,1)S(1)}, bf16[1408,1024]{1,0:T(8,128)(2,1)S(1)}, u32[]{:S(2)}, u32[]{:S(2)}) collective-permute-start(bf16[1408,1024]{1,0:T(8,128)(2,1)S(1)} %add.492), channel_id=1, source_target_pairs={{2,0},{4,6},{3,1},{5,7},{10,8},{12,14},{11,9},{13,15},{18,16},{20,... | collective-permute-start | bytes 8650760 | tf_op jit(solution)/shard_map/ppermute | solution.py:84
  707.9 121.7 %collective-permute-start.67 = (bf16[4,256,640]{2,1,0:T(8,128)(2,1)S(1)}, bf16[4,256,640]{2,1,0:T(8,128)(2,1)S(1)}, u32[]{:S(2)}, u32[]{:S(2)}) collective-permute-start(bf16[4,256,640]{2,1,0:T(8,128)(2,1)S(1)} %fusion.98), channel_id=1, source_target_pairs={{2,4},{4,2},{3,5},{5,3},{10,12},{12,10},{11,13},{13,11},{18,20},{2... | collective-permute-start | bytes 3932168 | tf_op jit(solution)/shard_map/ppermute | solution.py:82
  708.7 244.3 %collective-permute-start.89 = (bf16[4,256,1408]{2,1,0:T(8,128)(2,1)S(1)}, bf16[4,256,1408]{2,1,0:T(8,128)(2,1)S(1)}, u32[]{:S(2)}, u32[]{:S(2)}) collective-permute-start(bf16[4,256,1408]{2,1,0:T(8,128)(2,1)S(1)} %fusion.149), channel_id=1, source_target_pairs={{2,0},{4,6},{3,1},{5,7},{10,8},{12,14},{11,9},{13,15},{18,16},{20,... | collective-permute-start | bytes 8650760 | tf_op jit(solution)/shard_map/ppermute | solution.py:84
  803.9 210.9 %collective-permute-start.81 = (bf16[4,256,1408]{2,1,0:T(8,128)(2,1)S(1)}, bf16[4,256,1408]{2,1,0:T(8,128)(2,1)S(1)}, u32[]{:S(2)}, u32[]{:S(2)}) collective-permute-start(bf16[4,256,1408]{2,1,0:T(8,128)(2,1)S(1)} %fusion.150), channel_id=1, source_target_pairs={{2,0},{4,6},{3,1},{5,7},{10,8},{12,14},{11,9},{13,15},{18,16},{20,... | collective-permute-start | bytes 8650760 | tf_op jit(solution)/shard_map/ppermute | solution.py:84
  829.4 203.1 %collective-permute-start.61 = (bf16[4,2,512]{2,0,1:T(4,128)(2,1)S(1)}, bf16[4,2,512]{2,0,1:T(4,128)(2,1)S(1)}, u32[]{:S(2)}, u32[]{:S(2)}) collective-permute-start(bf16[4,2,512]{2,0,1:T(4,128)(2,1)S(1)} %get-tuple-element.140), channel_id=1, source_target_pairs={{0,1},{1,0},{2,3},{3,2},{4,5},{5,4},{6,7},{7,6},{8,9},{9,8},{10,11... | collective-permute-start | bytes 24584 | tf_op jit(solution)/shard_map/ppermute | solution.py:31
  829.6 206.3 %collective-permute-start.74 = (bf16[512,1024]{1,0:T(8,128)(2,1)S(1)}, bf16[512,1024]{1,0:T(8,128)(2,1)}, u32[]{:S(2)}, u32[]{:S(2)}) collective-permute-start(bf16[512,1024]{1,0:T(8,128)(2,1)S(1)} %broadcast_select_fusion.4.own_ref), channel_id=1, source_target_pairs={{0,1},{1,0},{2,3},{3,2},{4,5},{5,4},{6,7},{7,6},{8,9},{9,8},{10,11... | collective-permute-start | bytes 3145736 | tf_op jit(solution)/shard_map/ppermute | solution.py:31
  891.2 141.1 %collective-permute-start.68 = (bf16[4,256,640]{2,1,0:T(8,128)(2,1)S(1)}, bf16[4,256,640]{2,1,0:T(8,128)(2,1)S(1)}, u32[]{:S(2)}, u32[]{:S(2)}) collective-permute-start(bf16[4,256,640]{2,1,0:T(8,128)(2,1)S(1)} %fusion.151), channel_id=1, source_target_pairs={{2,0},{4,6},{3,1},{5,7},{10,8},{12,14},{11,9},{13,15},{18,16},{20,... | collective-permute-start | bytes 3932168 | tf_op jit(solution)/shard_map/ppermute | solution.py:84
  953.0 103.3 %collective-permute-start.95 = (bf16[1408,1024]{1,0:T(8,128)(2,1)}, bf16[1408,1024]{1,0:T(8,128)(2,1)}, u32[]{:S(2)}, u32[]{:S(2)}) collective-permute-start(bf16[1408,1024]{1,0:T(8,128)(2,1)} %broadcast_select_fusion.own_ref), channel_id=1, source_target_pairs={{0,1},{1,0},{2,3},{3,2},{4,5},{5,4},{6,7},{7,6},{8,9},{9,8},{10,11... | collective-permute-start | bytes 8650760 | tf_op jit(solution)/shard_map/ppermute | solution.py:31
  1014.8 60.2 %collective-permute-start.90 = (bf16[4,256,1408]{2,1,0:T(8,128)(2,1)}, bf16[4,256,1408]{2,1,0:T(8,128)(2,1)}, u32[]{:S(2)}, u32[]{:S(2)}) collective-permute-start(bf16[4,256,1408]{2,1,0:T(8,128)(2,1)} %broadcast_select_fusion.1.own_ref), channel_id=1, source_target_pairs={{0,1},{1,0},{2,3},{3,2},{4,5},{5,4},{6,7},{7,6},{8,9},{9,8},{10,11... | collective-permute-start | bytes 8650760 | tf_op jit(solution)/shard_map/ppermute | solution.py:31
  1032.3 33.0 %collective-permute-start.82 = (bf16[4,256,1408]{2,1,0:T(8,128)(2,1)}, bf16[4,256,1408]{2,1,0:T(8,128)(2,1)}, u32[]{:S(2)}, u32[]{:S(2)}) collective-permute-start(bf16[4,256,1408]{2,1,0:T(8,128)(2,1)} %broadcast_select_fusion.2.own_ref), channel_id=1, source_target_pairs={{0,1},{1,0},{2,3},{3,2},{4,5},{5,4},{6,7},{7,6},{8,9},{9,8},{10,11... | collective-permute-start | bytes 8650760 | tf_op jit(solution)/shard_map/ppermute | solution.py:31
  (125 other events, 2677.8 us)

commit v2 on v1

--- a/solution.py
+++ b/solution.py
@@ -1,3 +1,5 @@
+import functools
+
 import jax
 import jax.numpy as jnp
 from jax import lax
@@ -449,6 +451,184 @@
     )(at, q, do, lse, kv, kp, cosine, sine)
 
 
+def add_into(target, other):
+    @pl.loop(0, target.shape[0] // 16)
+    def _(i):
+        at = pl.ds(pl.multiple_of(i * 16, 16), 16)
+        target[at, :] = (target[at, :].astype(F32) + other[at, :].astype(F32)).astype(BF)
+
+
+def sums_kernel(plan, *refs):
+    kinds = len(plan)
+    own, other = refs[:kinds], refs[kinds : 2 * kinds]
+    fin_own, fin_sib = refs[2 * kinds : 3 * kinds], refs[3 * kinds : 4 * kinds]
+    src, swap, first, second, load = (refs[(4 + g) * kinds : (5 + g) * kinds] for g in range(5))
+    (pair_s, pair_r, load_s, swap_s, swap_r, in_s, in_r, mid_s, mid_r, out_s, done_s, back_s, back_r) = refs[
+        9 * kinds :
+    ]
+    f, z, k = lax.axis_index("fsdp"), lax.axis_index("z"), lax.axis_index("core")
+    line = lax.axis_size("z")
+    outer = (z == 0) | (z == line - 1)
+    inner = jnp.logical_not(outer)
+    inward = jnp.where(z < line // 2, z + 1, z - 1)
+    outward = jnp.where(z < line // 2, z - 1, z + 1)
+
+    chunks = []
+    for a, (n, swapped) in enumerate(plan):
+        for i in range(n):
+            chunks.append((a, i, i if swapped else 0))
+    count = len(chunks)
+
+    def remote(source, target, send, recv, where):
+        return pltpu.make_async_remote_copy(
+            src_ref=source,
+            dst_ref=target,
+            send_sem=send,
+            recv_sem=recv,
+            device_id=where,
+            device_id_type=pl.DeviceIdType.MESH,
+        )
+
+    def pair_copy(c):
+        a, i, _ = chunks[c]
+        return remote(other[a].at[i], src[a].at[i], pair_s.at[c], pair_r.at[c], {"core": 1 - k})
+
+    def load_copy(c):
+        a, i, _ = chunks[c]
+        return pltpu.make_async_copy(own[a].at[i], load[a].at[i % 2], load_s.at[c])
+
+    def swap_copy(c):
+        a, i, j = chunks[c]
+        return remote(src[a].at[i], swap[a].at[i], swap_s.at[c], swap_r.at[c], {"fsdp": f ^ j})
+
+    def base(c):
+        a, i, j = chunks[c]
+        return swap[a].at[i] if j else src[a].at[i]
+
+    def in_copy(c):
+        a, i, _ = chunks[c]
+        return remote(base(c), first[a].at[i], in_s.at[c], in_r.at[c], {"z": inward})
+
+    def mid_copy(c):
+        a, i, _ = chunks[c]
+        return remote(first[a].at[i], second[a].at[i], mid_s.at[c], mid_r.at[c], {"z": inward})
+
+    def out_copy(c):
+        a, i, _ = chunks[c]
+        return remote(second[a].at[i], second[a].at[i], out_s.at[c], mid_r.at[c], {"z": outward})
+
+    def keep_copy(c):
+        a, i, _ = chunks[c]
+        return pltpu.make_async_copy(second[a].at[i], fin_own[a].at[i], done_s.at[c])
+
+    def back_copy(c):
+        a, i, _ = chunks[c]
+        return remote(second[a].at[i], fin_sib[a].at[i], back_s.at[c], back_r.at[c], {"core": 1 - k})
+
+    def stage_pair(c):
+        a, i, j = chunks[c]
+        pair_copy(c).wait_recv()
+        load_copy(c).wait()
+        add_into(src[a].at[i], load[a].at[i % 2])
+        nxt = c + 2
+        if nxt < count:
+            load_copy(nxt).start()
+        if j:
+            swap_copy(c).start()
+
+    def stage_in(c):
+        if chunks[c][2]:
+            swap_copy(c).wait_recv()
+
+        @pl.when(outer)
+        def _():
+            in_copy(c).start()
+
+    def stage_mid(c):
+        a, i, _ = chunks[c]
+
+        @pl.when(inner)
+        def _():
+            in_copy(c).wait_recv()
+            add_into(first[a].at[i], base(c))
+            mid_copy(c).start()
+
+    def stage_out(c):
+        a, i, _ = chunks[c]
+
+        @pl.when(inner)
+        def _():
+            mid_copy(c).wait_recv()
+            add_into(second[a].at[i], first[a].at[i])
+            out_copy(c).start()
+
+    def stage_keep(c):
+        @pl.when(outer)
+        def _():
+            out_copy(c).wait_recv()
+
+        keep_copy(c).start()
+        back_copy(c).start()
+
+    for c in range(count):
+        pair_copy(c).start()
+    for c in range(min(2, count)):
+        load_copy(c).start()
+    stages = ((0, stage_pair), (1, stage_in), (2, stage_mid), (4, stage_out), (6, stage_keep))
+    for tick in range(count + stages[-1][0]):
+        for lag, stage in stages:
+            if 0 <= tick - lag < count:
+                stage(tick - lag)
+    for c in range(count):
+        pair_copy(c).wait_send()
+        if chunks[c][2]:
+            swap_copy(c).wait_send()
+        keep_copy(c).wait()
+        back_copy(c).wait_send()
+        back_copy(c).wait_recv()
+
+        @pl.when(outer)
+        def _():
+            in_copy(c).wait_send()
+
+        @pl.when(inner)
+        def _():
+            mid_copy(c).wait_send()
+            out_copy(c).wait_send()
+
+
+def sum_gradients_plain(owns, others, swapped):
+    ends = []
+    for own, other, slabs in zip(owns, others, swapped):
+        value = (own.astype(F32) + to_sibling(other).astype(F32)).astype(BF)
+        if slabs:
+            value = jnp.stack([value[0]] + [along_plane(value[j], j) for j in range(1, value.shape[0])])
+        ends.append(line_sum(value))
+    return ends, [to_sibling(e) for e in ends]
+
+
+def sum_gradients(owns, others, swapped):
+    plan = tuple((x.shape[0], s) for x, s in zip(owns, swapped))
+    count = sum(n for n, _ in plan)
+    shapes = [jax.ShapeDtypeStruct(x.shape, BF) for x in owns]
+    anywhere = pl.BlockSpec(memory_space=pl.ANY)
+    whole = [pltpu.VMEM(x.shape, BF) for x in owns]
+    swaps = [pltpu.VMEM(x.shape if s else (1, 16, 128), BF) for x, s in zip(owns, swapped)]
+    loads = [pltpu.VMEM((2,) + x.shape[1:], BF) for x in owns]
+    size = sum(x.size for x in owns)
+    out = pl.pallas_call(
+        functools.partial(sums_kernel, plan),
+        out_shape=shapes + shapes,
+        in_specs=[anywhere] * (2 * len(owns)),
+        out_specs=[anywhere] * (2 * len(owns)),
+        scratch_shapes=whole + swaps + whole + whole + loads + [pltpu.SemaphoreType.DMA((count,))] * 13,
+        compiler_params=params(has_side_effects=True),
+        cost_estimate=pl.CostEstimate(flops=4 * size, bytes_accessed=400 * size, transcendentals=0),
+        name="sum_gradients",
+    )(*owns, *others)
+    return out[: len(owns)], out[len(owns) :]
+
+
 def rms_backward(row_block, inverse, gain_vec, gradient):
     normed = row_block * inverse
     gain_grad = jnp.sum(gradient * normed, axis=0)
@@ -579,22 +759,19 @@
     def swap_slabs(own):
         return jnp.stack([own[0]] + [along_plane(own[j], j) for j in range(1, count)])
 
-    down_half = line_sum(pair_sum(tn(hidden, branch_mine), tn(hidden, branch_other)))
-    down_grad = join_columns(down_half, to_sibling(down_half), k)
+    terms = {"down": (tn(hidden, branch_mine).astype(BF), tn(hidden, branch_other).astype(BF))}
 
     hidden_grad = nt(branch, w_down)
     gate_back = (hidden_grad * up * sigmoid * (1.0 + gate * (1.0 - sigmoid))).astype(BF)
     up_back = (hidden_grad * gate * sigmoid).astype(BF)
 
-    def slab_grad(left_own, left_other, right):
-        width = right.shape[1]
-        own = pair_sum(tn(left_own, right), tn(left_other, right)).reshape(count, half, width)
-        return line_sum(swap_slabs(own))
-
-    gate_half = slab_grad(n2_own, n2_sib, gate_back)
-    gate_grad = join_rows(gate_half, to_sibling(gate_half), f, k)
-    up_half = slab_grad(n2_own, n2_sib, up_back)
-    up_grad = join_rows(up_half, to_sibling(up_half), f, k)
+    def slab_terms(left_own, left_other, right):
+        return tuple(
+            tn(left, right).astype(BF).reshape(count, half, right.shape[1]) for left in (left_own, left_other)
+        )
+
+    terms["gate"] = slab_terms(n2_own, n2_sib, gate_back)
+    terms["up"] = slab_terms(n2_own, n2_sib, up_back)
 
     back_own = (nt(gate_back, gate_own) + nt(up_back, up_own)).astype(BF)
     back_sib = (nt(gate_back, gate_sib) + nt(up_back, up_sib)).astype(BF)
@@ -611,8 +788,7 @@
 
     back_mine = lax.dynamic_slice_in_dim(attn_back, k * half_depth, half_depth, 1)
     back_other = lax.dynamic_slice_in_dim(attn_back, (1 - k) * half_depth, half_depth, 1)
-    out_half = line_sum(pair_sum(tn(attended, back_mine), tn(attended, back_other)))
-    out_grad = join_columns(out_half, to_sibling(out_half), k)
+    terms["out"] = (tn(attended, back_mine).astype(BF), tn(attended, back_other).astype(BF))
 
     query_back, kv_part = attend_back(at, queries, attended_grad, log_total, kv_all, kp, cosine, sine)
     kv_mine = kv_part[:line].astype(F32) + to_sibling(kv_part[line:]).astype(F32)
@@ -635,17 +811,35 @@
     input_grad = mixed_grad + input_back
 
     n1_own, n1_sib = normed_one[:, :half_depth], normed_one[:, half_depth:]
-    qkv_own = pair_sum(tn(n1_own, qkv_back), tn(n1_sib, qkv_back)).reshape(count, half, q_width + 128)
+    qkv_own, qkv_other = slab_terms(n1_own, n1_sib, qkv_back)
     gains = jnp.stack([gain_one_grad, gain_two_grad]).reshape(2, count, slab)
     gains = jnp.stack(
         [lax.dynamic_index_in_dim(gains, f ^ j, 1, keepdims=False) for j in range(count)]
     ).astype(BF)
-    gains = line_sum(swap_slabs(gains))
-    qkv_half = line_sum(swap_slabs(qkv_own))
-    gains = jnp.sum(gains.astype(F32), axis=0) + jnp.sum(to_sibling(gains).astype(F32), axis=0)
-    qkv_other = to_sibling(qkv_half)
-    query_grad = join_rows(qkv_half[:, :, :q_width], qkv_other[:, :, :q_width], f, k)
-    halves = jnp.stack([qkv_half[:, :, q_width:], qkv_other[:, :, q_width:]])
+    width = q_width + 128
+    gains = jnp.pad(gains, ((0, 0), (0, 14), (0, width - slab)))
+    qkv_own = jnp.concatenate([qkv_own, gains], axis=1)
+    qkv_other = jnp.concatenate([qkv_other, jnp.zeros_like(gains)], axis=1)
+    terms["qkv"] = (qkv_own, qkv_other)
+
+    cut = {"down": (4, -1, half_depth), "out": (2, -1, half_depth)}
+    names = ("down", "gate", "up", "out", "qkv")
+    owns = [terms[n][0].reshape(cut[n]) if n in cut else terms[n][0] for n in names]
+    others = [terms[n][1].reshape(cut[n]) if n in cut else terms[n][1] for n in names]
+    summed = sum_gradients if line == 4 else sum_gradients_plain
+    owns, sibs = summed(owns, others, (False, True, True, False, True))
+    ends = dict(zip(names, zip(owns, sibs)))
+
+    def columns(name):
+        return join_columns(*(x.reshape(-1, half_depth) for x in ends[name]), k)
+
+    down_grad, out_grad = columns("down"), columns("out")
+    gate_grad, up_grad = join_rows(*ends["gate"], f, k), join_rows(*ends["up"], f, k)
+    qkv_half, qkv_sib = ends["qkv"]
+    gains = jnp.sum(qkv_half[:, half : half + 2, :slab].astype(F32), axis=0)
+    gains = gains + jnp.sum(qkv_sib[:, half : half + 2, :slab].astype(F32), axis=0)
+    query_grad = join_rows(qkv_half[:, :half, :q_width], qkv_sib[:, :half, :q_width], f, k)
+    halves = jnp.stack([qkv_half[:, :half, q_width:], qkv_sib[:, :half, q_width:]])
 
     def by_head(lo, hi):
         both = [lax.dynamic_index_in_dim(halves, k ^ h, 0, keepdims=False) for h in range(2)]

time: 1090 us -> 862 us (0.79)
  waiting for transfers between devices: 614 us -> 172 us
  Pallas kernels: 126 us -> 428 us
  starting transfers between devices: 129 us -> 57.8 us
  other arithmetic: 59.6 us -> 30.6 us
    ppermute x18 -> x0, waiting for transfers between devices: 415 us -> none  [the longest x6 308 us: line_sum(): got = lax.ppermute(value, 'z', [(i + 1, i), (count - 2 - i, count - 1 - i)])]
    pallas_call x0 -> x1, Pallas kernels: none -> 302 us  [sum_gradients(): pl.pallas_call(functools.partial(sums_kernel, plan), out_shape=shapes + s...]
    ppermute x18 -> x0, starting transfers between devices: 50.4 us -> none  [the longest x6 31.9 us: line_sum(): got = lax.ppermute(value, 'z', [(i, i + 1), (count - 1 - i, count - 2 - i)])]
    ppermute x56 -> x44, waiting for transfers between devices: 182 us -> 157 us  [along_plane(): return lax.ppermute(value, 'fsdp', [(i, i ^ step) for i in range(count)])]
    add x13 -> x1, other arithmetic: 21.8 us -> 0.01 us  [body(): gains + jnp.sum(qkv_sib[:, half:half + 2, :slab].astype(F32), axis=0)]
    ppermute x56 -> x44, starting transfers between devices: 64 us -> 45.8 us  [along_plane(): return lax.ppermute(value, 'fsdp', [(i, i ^ step) for i in range(count)])]
    unnamed x219 -> x147, local copies, waits for them, and re-layouts: 24.4 us -> 28.3 us
  transfers between devices with their start and end apart: 96 -> 55, of which waited for: 48 -> 31; matrix products, arithmetic and copies ran while one was open for 14% -> 10% of each run, Pallas kernels for 10% -> 8%
where the time goes in v2:
time: 862 us; the launch traced here: 853 us
  Pallas kernels  428 us (50%)
  waiting for transfers between devices  172 us (20%)
  matrix products  90.4 us (10%)
  local copies, waits for them, and re-layouts  65.5 us (8%)
  starting transfers between devices  57.8 us (7%)
  other arithmetic  30.6 us (4%)
    pallas_call x1, Pallas kernels, sum_gradients(): pl.pallas_call(functools.partial(sums_kernel, plan), out_shape=shapes + s...  302 us
    ppermute x44, waiting for transfers between devices, along_plane(): return lax.ppermute(value, 'fsdp', [(i, i ^ step) for i in range(count)])  157 us
    ppermute x44, starting transfers between devices, along_plane(): return lax.ppermute(value, 'fsdp', [(i, i ^ step) for i in range(count)])  45.8 us
    dot_general x6, matrix products, nn(): return jnp.dot(a, b, preferred_element_type=F32)  38.5 us
    unnamed x147, local copies, waits for them, and re-layouts  28.3 us
    pallas_call x3, Pallas kernels, join_rows(): pl.pallas_call(join_kernel, grid_spec=spec, out_shape=jax.ShapeDtypeStruc...  26.7 us
    pallas_call x1, Pallas kernels, attend_back(): pl.pallas_call(attend_back_kernel, grid_spec=spec, out_shape=[jax.ShapeDt...  26.6 us
    dot_general x7, matrix products, nt(): lax.dot_general(a, b, (((1,), (1,)), ((), ())), preferred_element_type=F32)  26.1 us
  transfers between devices with their start and end apart: 55, of which 31 were waited for; matrix products, arithmetic and copies ran while one was open for 10% of the time, Pallas kernels for 8%

profile of v2, /device:TPU:0, one launch (start us, length us, event | category | flops | bytes accessed | tf_op | source)
XLA Modules:
  0.0 853.0 jit_solution(5254530320817522649)
XLA Ops:
  3.1 3.9 collective-permute-start.2
  20.4 4.0 cut_blocks.3
  28.8 4.8 cut_blocks.4
  33.6 3.4 fusion.103
  37.0 4.8 cut_blocks.5
  41.7 3.1 fusion.104
  61.0 8.2 collective-permute-done.35
  74.5 18.8 %collective-permute-done.36 = bf16[1,64,2048]{2,1,0:T(8,128)(2,1)S(1)} collective-permute-done((bf16[1,64,2048]{2,1,0:T(8,128)(2,1)}, bf16[1,64,2048]{2,1,0:T(8,128)(2,1)S(1)}, u32[]{:S(2)}, u32[]{:S(2)}) %collective-permute-start.36) | collective-permute-done | bytes 262176 | tf_op jit(solution)/shard_map/ppermute | solution.py:29
  106.0 20.2 %collective-permute-done.24 = bf16[256,1408]{1,0:T(8,128)(2,1)S(1)} collective-permute-done((bf16[256,1408]{1,0:T(8,128)(2,1)S(1)}, bf16[256,1408]{1,0:T(8,128)(2,1)S(1)}, u32[]{:S(2)}, u32[]{:S(2)}) %collective-permute-start.24) | collective-permute-done | bytes 720928 | tf_op jit(solution)/shard_map/ppermute | solution.py:29
  131.2 12.1 %collective-permute-done.28 = bf16[256,1408]{1,0:T(8,128)(2,1)S(1)} collective-permute-done((bf16[256,1408]{1,0:T(8,128)(2,1)S(1)}, bf16[256,1408]{1,0:T(8,128)(2,1)S(1)}, u32[]{:S(2)}, u32[]{:S(2)}) %collective-permute-start.28) | collective-permute-done | bytes 720928 | tf_op jit(solution)/shard_map/ppermute | solution.py:29
  147.0 4.4 collective-permute-done.5
  152.1 2.3 collective-permute-done.6
  162.6 6.9 qkv_project.1
  175.2 4.6 collective-permute-done.13
  179.8 4.0 collective-permute-done.12
  187.9 17.9 %attend.1 = (bf16[4,128,512]{2,1,0:T(8,128)(2,1)}, f32[4,128,512]{2,1,0:T(8,128)}) custom-call(s32[5]{0:T(128)} %concatenate.188.at_ref, bf16[4,128,512]{2,1,0:T(8,128)(2,1)} %bitcast.446, bf16[8,4,128,128]{3,2,1,0:T(8,128)(2,1)} %copy-done.45, s32[1,1024]{1,0:T(1,128)} %compare_select_fusion.kp_ref), custom_call_target="tpu_custom_call" | custom-call | flops 2147483648 | bytes 4194304 | tf_op jit(solution)/shard_map/attend/pallas_call | solution.py:360
  205.8 2.5 convolution_convert_fusion.6
  209.9 12.5 %collective-permute-done.15 = bf16[2,64,2048]{2,1,0:T(8,128)(2,1)S(1)} collective-permute-done((bf16[2,64,2048]{2,1,0:T(8,128)(2,1)S(1)}, bf16[2,64,2048]{2,1,0:T(8,128)(2,1)S(1)}, u32[]{:S(2)}, u32[]{:S(2)}) %collective-permute-start.15) | collective-permute-done | bytes 524320 | tf_op jit(solution)/shard_map/ppermute | solution.py:29
  223.0 7.1 collective-permute-done.16
  230.9 5.9 collective-permute-done.18
  238.8 5.0 fusion.117
  247.3 8.5 collective-permute-done.21
  257.4 6.3 pick_columns.1
  263.7 4.1 fusion.27
  267.8 3.6 fusion.29
  271.4 3.8 convolution_add_fusion
  275.2 18.1 %multiply_convert_fusion.1 = (bf16[512,1408]{1,0:T(8,128)(2,1)S(1)}, bf16[512,1408]{1,0:T(8,128)(2,1)}, bf16[512,1408]{1,0:T(8,128)(2,1)S(1)}) fusion(f32[512,1408]{1,0:T(8,128)S(1)} %copy-done.54, f32[512,1408]{1,0:T(8,128)S(1)} %convolution_add_fusion, f32[512,1408]{1,0:T(8,128)S(1)} %fusion.29, bf16[1024,1408]{1,0:T(8,128)(2,1)} %bitcast.88, ...), kind=kOutput, calls=%fused_computation.14 | convolution fusion | flops 1488650240 | bytes 16908288 | tf_op jit(solution)/shard_map/dot_general | solution.py:304
  293.3 4.7 fusion.119
  298.0 3.6 fusion.118
  301.7 3.7 add_convert_fusion
  305.3 3.7 add_convert_fusion.1
  310.5 6.3 put_columns.2
  319.1 6.4 convolution_convert_fusion.8
  327.7 3.4 convolution_convert_fusion.1
  331.1 3.4 convolution_convert_fusion.4
  334.6 3.4 convolution_convert_fusion
  342.3 3.3 convolution_convert_fusion.5
  345.6 3.4 convolution_convert_fusion.3
  349.0 4.6 collective-permute-done.39
  355.1 3.3 convolution_convert_fusion.2
  358.4 7.3 collective-permute-done.40
  365.9 2.4 collective-permute-start.42
  368.7 5.5 collective-permute-done.42
  375.2 2.4 collective-permute-start.44
  379.3 5.0 collective-permute-done.44
  387.3 6.3 collective-permute-done.45
  393.6 2.4 collective-permute-done.46
  398.4 26.6 %attend_back.1 = (bf16[4,128,512]{2,1,0:T(8,128)(2,1)}, bf16[8,4,128,128]{3,2,1,0:T(8,128)(2,1)}) custom-call(s32[5]{0:T(128)} %concatenate.188.at_ref, bf16[4,128,512]{2,1,0:T(8,128)(2,1)} %bitcast.447, bf16[4,128,512]{2,1,0:T(8,128)(2,1)} %bitcast.454, f32[4,128,512]{2,1,0:T(8,128)} %get-tuple-element.55.lse_ref, bf16[8,4,128,128]{3,2,1,0:T(8,128)(2,1)} %copy-done.45, ...), custom_call_target="tpu_custom_call" | custom-call | flops 5368709120 | bytes 8388608 | tf_op jit(solution)/shard_map/attend_back/pallas_call | solution.py:439
  430.1 5.1 collective-permute-start.48
  439.6 2.3 collective-permute-done.50
  441.9 2.4 collective-permute-done.49
  444.7 3.2 convolution_convert_fusion.7.x_ref
  447.9 6.5 put_columns.3
  459.3 9.9 %collective-permute-done.51 = bf16[2,64,2048]{2,1,0:T(8,128)(2,1)S(1)} collective-permute-done((bf16[2,64,2048]{2,1,0:T(8,128)(2,1)S(1)}, bf16[2,64,2048]{2,1,0:T(8,128)(2,1)S(1)}, u32[]{:S(2)}, u32[]{:S(2)}) %collective-permute-start.51) | collective-permute-done | bytes 524320 | tf_op jit(solution)/shard_map/ppermute | solution.py:29
  472.4 4.6 collective-permute-done.52
  479.1 5.0 collective-permute-done.54
  486.7 302.4 %sum_gradients.1 = (bf16[4,352,1024]{2,1,0:T(8,128)(2,1)}, bf16[4,256,1408]{2,1,0:T(8,128)(2,1)}, bf16[4,256,1408]{2,1,0:T(8,128)(2,1)}, bf16[2,256,1024]{2,1,0:...) custom-call(bf16[4,352,1024]{2,1,0:T(8,128)(2,1)} %bitcast.381, ...), custom_call_target="tpu_custom_call" | custom-call | flops 22183936 | bytes 2218393600 | tf_op jit(solution)/shard_map/sum_gradients/pallas_call | solution.py:619
  797.6 2.3 copy.34
  804.1 2.3 copy.33
  808.5 6.8 join_rows.3
  815.3 6.2 join_columns.2
  821.5 9.0 %join_columns.3 = f32[1408,2048]{1,0:T(8,128)} custom-call(s32[1]{0:T(128)} %bitcast.33.at_ref, bf16[1408,1024]{1,0:T(8,128)(2,1)} %bitcast.376, bf16[1408,1024]{1,0:T(8,128)(2,1)} %bitcast.377), custom_call_target="tpu_custom_call" | custom-call | tf_op jit(solution)/shard_map/join_columns/pallas_call | solution.py:223
  830.5 9.7 %join_rows.4 = f32[512,5632]{1,0:T(8,128)} custom-call(s32[2]{0:T(128)} %pad_add_fusion.idx_ref.at_ref, bf16[4,256,1408]{2,1,0:T(8,128)(2,1)} %get-tuple-element.63.own_ref, bf16[4,256,1408]{2,1,0:T(8,128)(2,1)} %get-tuple-element.64.sib_ref), custom_call_target="tpu_custom_call" | custom-call | tf_op jit(solution)/shard_map/join_rows/pallas_call | solution.py:201
  840.2 10.2 %join_rows.5 = f32[512,5632]{1,0:T(8,128)} custom-call(s32[2]{0:T(128)} %pad_add_fusion.idx_ref.at_ref, bf16[4,256,1408]{2,1,0:T(8,128)(2,1)} %get-tuple-element.65.own_ref, bf16[4,256,1408]{2,1,0:T(8,128)(2,1)} %get-tuple-element.66.sib_ref), custom_call_target="tpu_custom_call" | custom-call | tf_op jit(solution)/shard_map/join_rows/pallas_call | solution.py:201
  (371 shorter events, 144.5 us)
Async XLA Ops:
  0.6 205.2 %copy-start = (bf16[512,2048]{1,0:T(8,128)(2,1)S(1)}, bf16[512,2048]{1,0:T(8,128)(2,1)}, u32[]{:S(2)}) copy-start(bf16[512,2048]{1,0:T(8,128)(2,1)} %param.23) | copy-start | bytes 6291460
  3.1 45.3 %collective-permute-start.2 = (bf16[4,512]{1,0:T(4,128)(2,1)S(1)}, bf16[4,512]{1,0:T(4,128)(2,1)S(1)}, u32[]{:S(2)}, u32[]{:S(2)}) collective-permute-start(bf16[4,512]{1,0:T(4,128)(2,1)S(1)} %maximum_maximum_fusion.1), channel_id=1, source_target_pairs={{0,24},{8,16},{16,8},{24,0},{1,25},{9,17},{17,9},{25,1},{2,26},{10... | collective-permute-start | bytes 12296 | tf_op jit(solution)/shard_map/ppermute | solution.py:29
  7.0 41.4 %collective-permute-start.1 = (bf16[4,512]{1,0:T(4,128)(2,1)S(1)}, bf16[4,512]{1,0:T(4,128)(2,1)S(1)}, u32[]{:S(2)}, u32[]{:S(2)}) collective-permute-start(bf16[4,512]{1,0:T(4,128)(2,1)S(1)} %maximum_maximum_fusion.1), channel_id=1, source_target_pairs={{0,16},{8,24},{16,0},{24,8},{1,17},{9,25},{17,1},{25,9},{2,18},{10... | collective-permute-start | bytes 12296 | tf_op jit(solution)/shard_map/ppermute | solution.py:29
  7.5 42.9 %collective-permute-start = (bf16[4,512]{1,0:T(4,128)(2,1)S(1)}, bf16[4,512]{1,0:T(4,128)(2,1)S(1)}, u32[]{:S(2)}, u32[]{:S(2)}) collective-permute-start(bf16[4,512]{1,0:T(4,128)(2,1)S(1)} %maximum_maximum_fusion.1), channel_id=1, source_target_pairs={{0,8},{8,0},{16,24},{24,16},{1,9},{9,1},{17,25},{25,17},{2,10},{10... | collective-permute-start | bytes 12296 | tf_op jit(solution)/shard_map/ppermute | solution.py:29
  9.5 63.2 %collective-permute-start.4 = (bf16[1,64,2048]{2,1,0:T(8,128)(2,1)}, bf16[1,64,2048]{2,1,0:T(8,128)(2,1)}, u32[]{:S(2)}, u32[]{:S(2)}) collective-permute-start(bf16[1,64,2048]{2,1,0:T(8,128)(2,1)} %get-tuple-element.156), channel_id=1, source_target_pairs={{0,16},{8,24},{16,0},{24,8},{1,17},{9,25},{17,1},{25,9},{2,18},{10... | collective-permute-start | bytes 786440 | tf_op jit(solution)/shard_map/ppermute | solution.py:29
  11.4 47.4 %collective-permute-start.3 = (bf16[1,64,2048]{2,1,0:T(8,128)(2,1)}, bf16[1,64,2048]{2,1,0:T(8,128)(2,1)}, u32[]{:S(2)}, u32[]{:S(2)}) collective-permute-start(bf16[1,64,2048]{2,1,0:T(8,128)(2,1)} %get-tuple-element.157), channel_id=1, source_target_pairs={{0,8},{8,0},{16,24},{24,16},{1,9},{9,1},{17,25},{25,17},{2,10},{10... | collective-permute-start | bytes 786440 | tf_op jit(solution)/shard_map/ppermute | solution.py:29
  48.3 52.1 %collective-permute-start.9 = (bf16[256,640]{1,0:T(8,128)(2,1)}, bf16[256,640]{1,0:T(8,128)(2,1)}, u32[]{:S(2)}, u32[]{:S(2)}) collective-permute-start(bf16[256,640]{1,0:T(8,128)(2,1)} %get-tuple-element.132), channel_id=1, source_target_pairs={{0,24},{8,16},{16,8},{24,0},{1,25},{9,17},{17,9},{25,1},{2,26},{10... | collective-permute-start | bytes 983048 | tf_op jit(solution)/shard_map/ppermute | solution.py:29
  48.4 49.2 %collective-permute-start.8 = (bf16[256,640]{1,0:T(8,128)(2,1)}, bf16[256,640]{1,0:T(8,128)(2,1)}, u32[]{:S(2)}, u32[]{:S(2)}) collective-permute-start(bf16[256,640]{1,0:T(8,128)(2,1)} %get-tuple-element.133), channel_id=1, source_target_pairs={{0,16},{8,24},{16,0},{24,8},{1,17},{9,25},{17,1},{25,9},{2,18},{10... | collective-permute-start | bytes 983048 | tf_op jit(solution)/shard_map/ppermute | solution.py:29
  50.4 44.8 %collective-permute-start.7 = (bf16[256,640]{1,0:T(8,128)(2,1)}, bf16[256,640]{1,0:T(8,128)(2,1)}, u32[]{:S(2)}, u32[]{:S(2)}) collective-permute-start(bf16[256,640]{1,0:T(8,128)(2,1)} %get-tuple-element.134), channel_id=1, source_target_pairs={{0,8},{8,0},{16,24},{24,16},{1,9},{9,1},{17,25},{25,17},{2,10},{10... | collective-permute-start | bytes 983048 | tf_op jit(solution)/shard_map/ppermute | solution.py:29
  58.8 34.5 %copy-start.32 = (bf16[256,1408]{1,0:T(8,128)(2,1)S(1)}, bf16[256,1408]{1,0:T(8,128)(2,1)}, u32[]{:S(2)}) copy-start(bf16[256,1408]{1,0:T(8,128)(2,1)} %get-tuple-element.104) | copy-start | bytes 2162692
  58.8 36.2 %copy-start.26 = (bf16[1,64,2048]{2,1,0:T(8,128)(2,1)S(1)}, bf16[1,64,2048]{2,1,0:T(8,128)(2,1)}, u32[]{:S(2)}) copy-start(bf16[1,64,2048]{2,1,0:T(8,128)(2,1)} %get-tuple-element.152) | copy-start | bytes 786436
  58.8 10.4 %collective-permute-start.35 = (bf16[1,64,2048]{2,1,0:T(8,128)(2,1)}, bf16[1,64,2048]{2,1,0:T(8,128)(2,1)S(1)}, u32[]{:S(2)}, u32[]{:S(2)}) collective-permute-start(bf16[1,64,2048]{2,1,0:T(8,128)(2,1)} %get-tuple-element.153), channel_id=1, source_target_pairs={{0,8},{8,0},{16,24},{24,16},{1,9},{9,1},{17,25},{25,17},{2,10},{10... | collective-permute-start | bytes 786440 | tf_op jit(solution)/shard_map/ppermute | solution.py:29
  69.2 24.1 %collective-permute-start.36 = (bf16[1,64,2048]{2,1,0:T(8,128)(2,1)}, bf16[1,64,2048]{2,1,0:T(8,128)(2,1)S(1)}, u32[]{:S(2)}, u32[]{:S(2)}) collective-permute-start(bf16[1,64,2048]{2,1,0:T(8,128)(2,1)} %get-tuple-element.152), channel_id=1, source_target_pairs={{0,16},{8,24},{16,0},{24,8},{1,17},{9,25},{17,1},{25,9},{2,18},{10... | collective-permute-start | bytes 786440 | tf_op jit(solution)/shard_map/ppermute | solution.py:29
  72.7 30.2 %copy-start.23 = (bf16[1,256,640]{2,1,0:T(8,128)(2,1)S(1)}, bf16[1,256,640]{2,1,0:T(8,128)(2,1)}, u32[]{:S(2)}) copy-start(bf16[1,256,640]{2,1,0:T(8,128)(2,1)} %get-tuple-element.130) | copy-start | bytes 983044
  72.8 29.5 %collective-permute-start.25 = (bf16[256,1408]{1,0:T(8,128)(2,1)S(1)}, bf16[256,1408]{1,0:T(8,128)(2,1)S(1)}, u32[]{:S(2)}, u32[]{:S(2)}) collective-permute-start(bf16[256,1408]{1,0:T(8,128)(2,1)S(1)} %copy-done.33), channel_id=1, source_target_pairs={{0,24},{8,16},{16,8},{24,0},{1,25},{9,17},{17,9},{25,1},{2,26},{10... | collective-permute-start | bytes 2162696 | tf_op jit(solution)/shard_map/ppermute | solution.py:29
  93.3 32.9 %collective-permute-start.24 = (bf16[256,1408]{1,0:T(8,128)(2,1)S(1)}, bf16[256,1408]{1,0:T(8,128)(2,1)S(1)}, u32[]{:S(2)}, u32[]{:S(2)}) collective-permute-start(bf16[256,1408]{1,0:T(8,128)(2,1)S(1)} %copy-done.32), channel_id=1, source_target_pairs={{0,16},{8,24},{16,0},{24,8},{1,17},{9,25},{17,1},{25,9},{2,18},{10... | collective-permute-start | bytes 2162696 | tf_op jit(solution)/shard_map/ppermute | solution.py:29
  95.2 31.1 %collective-permute-start.23 = (bf16[256,1408]{1,0:T(8,128)(2,1)S(1)}, bf16[256,1408]{1,0:T(8,128)(2,1)S(1)}, u32[]{:S(2)}, u32[]{:S(2)}) collective-permute-start(bf16[256,1408]{1,0:T(8,128)(2,1)S(1)} %copy-done.31), channel_id=1, source_target_pairs={{0,8},{8,0},{16,24},{24,16},{1,9},{9,1},{17,25},{25,17},{2,10},{10... | collective-permute-start | bytes 2162696 | tf_op jit(solution)/shard_map/ppermute | solution.py:29
  97.6 31.8 %collective-permute-start.29 = (bf16[256,1408]{1,0:T(8,128)(2,1)S(1)}, bf16[256,1408]{1,0:T(8,128)(2,1)S(1)}, u32[]{:S(2)}, u32[]{:S(2)}) collective-permute-start(bf16[256,1408]{1,0:T(8,128)(2,1)S(1)} %copy-done.30), channel_id=1, source_target_pairs={{0,24},{8,16},{16,8},{24,0},{1,25},{9,17},{17,9},{25,1},{2,26},{10... | collective-permute-start | bytes 2162696 | tf_op jit(solution)/shard_map/ppermute | solution.py:29
  100.5 42.8 %collective-permute-start.28 = (bf16[256,1408]{1,0:T(8,128)(2,1)S(1)}, bf16[256,1408]{1,0:T(8,128)(2,1)S(1)}, u32[]{:S(2)}, u32[]{:S(2)}) collective-permute-start(bf16[256,1408]{1,0:T(8,128)(2,1)S(1)} %copy-done.29), channel_id=1, source_target_pairs={{0,16},{8,24},{16,0},{24,8},{1,17},{9,25},{17,1},{25,9},{2,18},{10... | collective-permute-start | bytes 2162696 | tf_op jit(solution)/shard_map/ppermute | solution.py:29
  102.2 42.9 %collective-permute-start.27 = (bf16[256,1408]{1,0:T(8,128)(2,1)S(1)}, bf16[256,1408]{1,0:T(8,128)(2,1)S(1)}, u32[]{:S(2)}, u32[]{:S(2)}) collective-permute-start(bf16[256,1408]{1,0:T(8,128)(2,1)S(1)} %copy-done.28), channel_id=1, source_target_pairs={{0,8},{8,0},{16,24},{24,16},{1,9},{9,1},{17,25},{25,17},{2,10},{10... | collective-permute-start | bytes 2162696 | tf_op jit(solution)/shard_map/ppermute | solution.py:29
  126.2 28.2 %collective-permute-start.6 = (bf16[2,64,2048]{2,1,0:T(8,128)(2,1)S(1)}, bf16[2,64,2048]{2,1,0:T(8,128)(2,1)S(1)}, u32[]{:S(2)}, u32[]{:S(2)}) collective-permute-start(bf16[2,64,2048]{2,1,0:T(8,128)(2,1)S(1)} %pad_maximum_fusion.9), channel_id=1, source_target_pairs={{0,16},{8,24},{16,0},{24,8},{1,17},{9,25},{17,1},{25,9},{2,18},{10... | collective-permute-start | bytes 1572872 | tf_op jit(solution)/shard_map/ppermute | solution.py:29
  126.2 25.2 %collective-permute-start.5 = (bf16[2,64,2048]{2,1,0:T(8,128)(2,1)S(1)}, bf16[2,64,2048]{2,1,0:T(8,128)(2,1)S(1)}, u32[]{:S(2)}, u32[]{:S(2)}) collective-permute-start(bf16[2,64,2048]{2,1,0:T(8,128)(2,1)S(1)} %pad_maximum_fusion.8), channel_id=1, source_target_pairs={{0,8},{8,0},{16,24},{24,16},{1,9},{9,1},{17,25},{25,17},{2,10},{10... | collective-permute-start | bytes 1572872 | tf_op jit(solution)/shard_map/ppermute | solution.py:29
  129.4 30.6 %collective-permute-start.38 = (bf16[2,64,2048]{2,1,0:T(8,128)(2,1)S(1)}, bf16[2,64,2048]{2,1,0:T(8,128)(2,1)S(1)}, u32[]{:S(2)}, u32[]{:S(2)}) collective-permute-start(bf16[2,64,2048]{2,1,0:T(8,128)(2,1)S(1)} %pad_maximum_fusion.16), channel_id=1, source_target_pairs={{0,16},{8,24},{16,0},{24,8},{1,17},{9,25},{17,1},{25,9},{2,18},{10... | collective-permute-start | bytes 1572872 | tf_op jit(solution)/shard_map/ppermute | solution.py:29
  143.3 15.0 %collective-permute-start.37 = (bf16[2,64,2048]{2,1,0:T(8,128)(2,1)S(1)}, bf16[2,64,2048]{2,1,0:T(8,128)(2,1)S(1)}, u32[]{:S(2)}, u32[]{:S(2)}) collective-permute-start(bf16[2,64,2048]{2,1,0:T(8,128)(2,1)S(1)} %pad_maximum_fusion.15), channel_id=1, source_target_pairs={{0,8},{8,0},{16,24},{24,16},{1,9},{9,1},{17,25},{25,17},{2,10},{10... | collective-permute-start | bytes 1572872 | tf_op jit(solution)/shard_map/ppermute | solution.py:29
  145.2 15.6 %collective-permute-start.10 = (bf16[4,256,640]{2,1,0:T(8,128)(2,1)S(1)}, bf16[4,256,640]{2,1,0:T(8,128)(2,1)S(1)}, u32[]{:S(2)}, u32[]{:S(2)}) collective-permute-start(bf16[4,256,640]{2,1,0:T(8,128)(2,1)S(1)} %pad_maximum_fusion.4), channel_id=1, source_target_pairs={{0,1},{1,0},{2,3},{3,2},{4,5},{5,4},{6,7},{7,6},{8,9},{9,8},{10,11... | collective-permute-start | bytes 3932168 | tf_op jit(solution)/shard_map/ppermute | solution.py:33
  151.4 112.3 %collective-permute-start.30 = (bf16[4,256,1408]{2,1,0:T(8,128)(2,1)}, bf16[4,256,1408]{2,1,0:T(8,128)(2,1)}, u32[]{:S(2)}, u32[]{:S(2)}) collective-permute-start(bf16[4,256,1408]{2,1,0:T(8,128)(2,1)} %pad_maximum_fusion.1), channel_id=1, source_target_pairs={{0,1},{1,0},{2,3},{3,2},{4,5},{5,4},{6,7},{7,6},{8,9},{9,8},{10,11... | collective-permute-start | bytes 8650760 | tf_op jit(solution)/shard_map/ppermute | solution.py:33
  154.5 113.3 %collective-permute-start.26 = (bf16[4,256,1408]{2,1,0:T(8,128)(2,1)}, bf16[4,256,1408]{2,1,0:T(8,128)(2,1)}, u32[]{:S(2)}, u32[]{:S(2)}) collective-permute-start(bf16[4,256,1408]{2,1,0:T(8,128)(2,1)} %pad_maximum_fusion), channel_id=1, source_target_pairs={{0,1},{1,0},{2,3},{3,2},{4,5},{5,4},{6,7},{7,6},{8,9},{9,8},{10,11... | collective-permute-start | bytes 8650760 | tf_op jit(solution)/shard_map/ppermute | solution.py:33
  169.4 10.4 %collective-permute-start.13 = (bf16[4,128,128]{2,1,0:T(8,128)(2,1)}, bf16[4,128,128]{2,1,0:T(8,128)(2,1)S(1)}, u32[]{:S(2)}, u32[]{:S(2)}) collective-permute-start(bf16[4,128,128]{2,1,0:T(8,128)(2,1)} %bitcast.411), channel_id=1, source_target_pairs={{6,0},{7,1},{14,8},{15,9},{22,16},{23,17},{30,24},{31,25}} | collective-permute-start | bytes 393224 | tf_op jit(solution)/shard_map/ppermute | solution.py:38
  170.7 13.2 %collective-permute-start.12 = (bf16[4,128,128]{2,1,0:T(8,128)(2,1)}, bf16[4,128,128]{2,1,0:T(8,128)(2,1)S(1)}, u32[]{:S(2)}, u32[]{:S(2)}) collective-permute-start(bf16[4,128,128]{2,1,0:T(8,128)(2,1)} %bitcast.412), channel_id=1, source_target_pairs={{4,0},{6,2},{5,1},{7,3},{12,8},{14,10},{13,9},{15,11},{20,16},{22,... | collective-permute-start | bytes 393224 | tf_op jit(solution)/shard_map/ppermute | solution.py:38
  172.0 11.9 %collective-permute-start.11 = (bf16[4,128,128]{2,1,0:T(8,128)(2,1)}, bf16[4,128,128]{2,1,0:T(8,128)(2,1)S(1)}, u32[]{:S(2)}, u32[]{:S(2)}) collective-permute-start(bf16[4,128,128]{2,1,0:T(8,128)(2,1)} %bitcast.413), channel_id=1, source_target_pairs={{2,0},{4,2},{6,4},{3,1},{5,3},{7,5},{10,8},{12,10},{14,12},{11,9},... | collective-permute-start | bytes 393224 | tf_op jit(solution)/shard_map/ppermute | solution.py:38
  184.9 2.0 collective-permute-start.14
  205.8 33.0 %slice-start = ((s8[5767168]{0:T(1024)(128)(4,1)}), s8[4194304]{0:T(1024)(128)(4,1)S(1)}, s32[]{:S(2)}) async-start(s8[5767168]{0:T(1024)(128)(4,1)} %bitcast.444), calls=%async_computation | async-start | bytes 8388608
  208.4 14.0 %collective-permute-start.15 = (bf16[2,64,2048]{2,1,0:T(8,128)(2,1)S(1)}, bf16[2,64,2048]{2,1,0:T(8,128)(2,1)S(1)}, u32[]{:S(2)}, u32[]{:S(2)}) collective-permute-start(bf16[2,64,2048]{2,1,0:T(8,128)(2,1)S(1)} %stack.385), channel_id=1, source_target_pairs={{0,16},{8,24},{16,0},{24,8},{1,17},{9,25},{17,1},{25,9},{2,18},{10... | collective-permute-start | bytes 1572872 | tf_op jit(solution)/shard_map/ppermute | solution.py:29
  209.1 29.7 %slice-start.1 = ((s8[5767168]{0:T(1024)(128)(4,1)}), s8[1572864]{0:T(1024)(128)(4,1)S(1)}, s32[]{:S(2)}) async-start(s8[5767168]{0:T(1024)(128)(4,1)} %bitcast.444), calls=%async_computation.1 | async-start | bytes 3145728
  209.2 13.8 %collective-permute-start.17 = (bf16[2,64,2048]{2,1,0:T(8,128)(2,1)S(1)}, bf16[2,64,2048]{2,1,0:T(8,128)(2,1)S(1)}, u32[]{:S(2)}, u32[]{:S(2)}) collective-permute-start(bf16[2,64,2048]{2,1,0:T(8,128)(2,1)S(1)} %pad_maximum_fusion.11), channel_id=1, source_target_pairs={{0,8},{8,0},{16,24},{24,16},{1,9},{9,1},{17,25},{25,17},{2,10},{10... | collective-permute-start | bytes 1572872 | tf_op jit(solution)/shard_map/ppermute | solution.py:29
  222.5 7.6 collective-permute-start.16
  230.2 6.7 collective-permute-start.18
  237.0 137.8 %copy-start.2 = (f32[1,64,2048]{2,1,0:T(8,128)}, f32[1,64,2048]{2,1,0:T(8,128)S(1)}, u32[]{:S(2)}) copy-start(f32[1,64,2048]{2,1,0:T(8,128)S(1)} %convert_add_fusion.8) | copy-start | bytes 1572868
  237.4 6.4 collective-permute-start.20
  238.2 7.4 collective-permute-start.19
  243.9 11.8 %collective-permute-start.21 = (bf16[2,64,2048]{2,1,0:T(8,128)(2,1)S(1)}, bf16[2,64,2048]{2,1,0:T(8,128)(2,1)S(1)}, u32[]{:S(2)}, u32[]{:S(2)}) collective-permute-start(bf16[2,64,2048]{2,1,0:T(8,128)(2,1)S(1)} %pad_maximum_fusion.12), channel_id=1, source_target_pairs={{0,8},{8,0},{16,24},{24,16},{1,9},{9,1},{17,25},{25,17},{2,10},{10... | collective-permute-start | bytes 1572872 | tf_op jit(solution)/shard_map/ppermute | solution.py:29
  245.6 10.3 %collective-permute-start.22 = (bf16[2,64,2048]{2,1,0:T(8,128)(2,1)S(1)}, bf16[2,64,2048]{2,1,0:T(8,128)(2,1)S(1)}, u32[]{:S(2)}, u32[]{:S(2)}) collective-permute-start(bf16[2,64,2048]{2,1,0:T(8,128)(2,1)S(1)} %pad_maximum_fusion.13), channel_id=1, source_target_pairs={{0,16},{8,24},{16,0},{24,8},{1,17},{9,25},{17,1},{25,9},{2,18},{10... | collective-permute-start | bytes 1572872 | tf_op jit(solution)/shard_map/ppermute | solution.py:29
  325.6 52.5 %copy-start.19 = (bf16[512,2048]{1,0:T(8,128)(2,1)}, bf16[512,2048]{1,0:T(8,128)(2,1)S(1)}, u32[]{:S(2)}) copy-start(bf16[512,2048]{1,0:T(8,128)(2,1)S(1)} %convolution_convert_fusion.8) | copy-start | bytes 6291460
  338.0 20.4 %collective-permute-start.41 = (bf16[2,64,2048]{2,1,0:T(8,128)(2,1)S(1)}, bf16[2,64,2048]{2,1,0:T(8,128)(2,1)S(1)}, u32[]{:S(2)}, u32[]{:S(2)}) collective-permute-start(bf16[2,64,2048]{2,1,0:T(8,128)(2,1)S(1)} %pad_maximum_fusion.17), channel_id=1, source_target_pairs={{0,8},{8,0},{16,24},{24,16},{1,9},{9,1},{17,25},{25,17},{2,10},{10... | collective-permute-start | bytes 1572872 | tf_op jit(solution)/shard_map/ppermute | solution.py:29
  338.7 14.9 %collective-permute-start.39 = (bf16[2,64,2048]{2,1,0:T(8,128)(2,1)S(1)}, bf16[2,64,2048]{2,1,0:T(8,128)(2,1)S(1)}, u32[]{:S(2)}, u32[]{:S(2)}) collective-permute-start(bf16[2,64,2048]{2,1,0:T(8,128)(2,1)S(1)} %stack.387), channel_id=1, source_target_pairs={{0,16},{8,24},{16,0},{24,8},{1,17},{9,25},{17,1},{25,9},{2,18},{10... | collective-permute-start | bytes 1572872 | tf_op jit(solution)/shard_map/ppermute | solution.py:29
  339.9 38.1 %collective-permute-start.33 = (bf16[2,64,2048]{2,1,0:T(8,128)(2,1)S(1)}, bf16[2,64,2048]{2,1,0:T(8,128)(2,1)S(1)}, u32[]{:S(2)}, u32[]{:S(2)}) collective-permute-start(bf16[2,64,2048]{2,1,0:T(8,128)(2,1)S(1)} %pad_maximum_fusion.14), channel_id=1, source_target_pairs={{0,8},{8,0},{16,24},{24,16},{1,9},{9,1},{17,25},{25,17},{2,10},{10... | collective-permute-start | bytes 1572872 | tf_op jit(solution)/shard_map/ppermute | solution.py:29
  341.6 26.6 %collective-permute-start.31 = (bf16[2,64,2048]{2,1,0:T(8,128)(2,1)S(1)}, bf16[2,64,2048]{2,1,0:T(8,128)(2,1)S(1)}, u32[]{:S(2)}, u32[]{:S(2)}) collective-permute-start(bf16[2,64,2048]{2,1,0:T(8,128)(2,1)S(1)} %stack.386), channel_id=1, source_target_pairs={{0,16},{8,24},{16,0},{24,8},{1,17},{9,25},{17,1},{25,9},{2,18},{10... | collective-permute-start | bytes 1572872 | tf_op jit(solution)/shard_map/ppermute | solution.py:29
  353.7 12.0 %collective-permute-start.40 = (bf16[1,64,2048]{2,1,0:T(8,128)(2,1)S(1)}, bf16[1,64,2048]{2,1,0:T(8,128)(2,1)S(1)}, u32[]{:S(2)}, u32[]{:S(2)}) collective-permute-start(bf16[1,64,2048]{2,1,0:T(8,128)(2,1)S(1)} %add_convert_fusion.5), channel_id=1, source_target_pairs={{0,8},{8,0},{16,24},{24,16},{1,9},{9,1},{17,25},{25,17},{2,10},{10... | collective-permute-start | bytes 786440 | tf_op jit(solution)/shard_map/ppermute | solution.py:29
  365.9 8.3 collective-permute-start.42
  368.3 9.7 %collective-permute-start.32 = (bf16[1,64,2048]{2,1,0:T(8,128)(2,1)S(1)}, bf16[1,64,2048]{2,1,0:T(8,128)(2,1)S(1)}, u32[]{:S(2)}, u32[]{:S(2)}) collective-permute-start(bf16[1,64,2048]{2,1,0:T(8,128)(2,1)S(1)} %add_convert_fusion.7), channel_id=1, source_target_pairs={{0,8},{8,0},{16,24},{24,16},{1,9},{9,1},{17,25},{25,17},{2,10},{10... | collective-permute-start | bytes 786440 | tf_op jit(solution)/shard_map/ppermute | solution.py:29
  375.2 9.1 %collective-permute-start.44 = (bf16[1,64,2048]{2,1,0:T(8,128)(2,1)S(1)}, bf16[1,64,2048]{2,1,0:T(8,128)(2,1)S(1)}, u32[]{:S(2)}, u32[]{:S(2)}) collective-permute-start(bf16[1,64,2048]{2,1,0:T(8,128)(2,1)S(1)} %get-tuple-element.150), channel_id=1, source_target_pairs={{0,16},{8,24},{16,0},{24,8},{1,17},{9,25},{17,1},{25,9},{2,18},{10... | collective-permute-start | bytes 786440 | tf_op jit(solution)/shard_map/ppermute | solution.py:29
  377.6 9.0 %collective-permute-start.43 = (bf16[1,64,2048]{2,1,0:T(8,128)(2,1)S(1)}, bf16[1,64,2048]{2,1,0:T(8,128)(2,1)S(1)}, u32[]{:S(2)}, u32[]{:S(2)}) collective-permute-start(bf16[1,64,2048]{2,1,0:T(8,128)(2,1)S(1)} %get-tuple-element.151), channel_id=1, source_target_pairs={{0,8},{8,0},{16,24},{24,16},{1,9},{9,1},{17,25},{25,17},{2,10},{10... | collective-permute-start | bytes 786440 | tf_op jit(solution)/shard_map/ppermute | solution.py:29
  379.2 47.1 %collective-permute-start.34 = (bf16[1,64,2048]{2,1,0:T(8,128)(2,1)S(1)}, bf16[1,64,2048]{2,1,0:T(8,128)(2,1)S(1)}, u32[]{:S(2)}, u32[]{:S(2)}) collective-permute-start(bf16[1,64,2048]{2,1,0:T(8,128)(2,1)S(1)} %get-tuple-element.119), channel_id=1, source_target_pairs={{0,16},{8,24},{16,0},{24,8},{1,17},{9,25},{17,1},{25,9},{2,18},{10... | collective-permute-start | bytes 786440 | tf_op jit(solution)/shard_map/ppermute | solution.py:29
  384.3 9.2 %collective-permute-start.45 = (bf16[2,64,2048]{2,1,0:T(8,128)(2,1)S(1)}, bf16[2,64,2048]{2,1,0:T(8,128)(2,1)S(1)}, u32[]{:S(2)}, u32[]{:S(2)}) collective-permute-start(bf16[2,64,2048]{2,1,0:T(8,128)(2,1)S(1)} %pad_maximum_fusion.18), channel_id=1, source_target_pairs={{0,8},{8,0},{16,24},{24,16},{1,9},{9,1},{17,25},{25,17},{2,10},{10... | collective-permute-start | bytes 1572872 | tf_op jit(solution)/shard_map/ppermute | solution.py:29
  386.7 9.3 %collective-permute-start.46 = (bf16[2,64,2048]{2,1,0:T(8,128)(2,1)S(1)}, bf16[2,64,2048]{2,1,0:T(8,128)(2,1)S(1)}, u32[]{:S(2)}, u32[]{:S(2)}) collective-permute-start(bf16[2,64,2048]{2,1,0:T(8,128)(2,1)S(1)} %pad_maximum_fusion.19), channel_id=1, source_target_pairs={{0,16},{8,24},{16,0},{24,8},{1,17},{9,25},{17,1},{25,9},{2,18},{10... | collective-permute-start | bytes 1572872 | tf_op jit(solution)/shard_map/ppermute | solution.py:29
  398.4 29.8 %copy-start.46 = (bf16[4,128,512]{2,1,0:T(8,128)(2,1)S(1)}, bf16[4,128,512]{2,1,0:T(8,128)(2,1)}, u32[]{:S(2)}) copy-start(bf16[4,128,512]{2,1,0:T(8,128)(2,1)} %get-tuple-element.54) | copy-start | bytes 1572868
  426.2 3.7 collective-permute-start.47
  430.1 9.5 %collective-permute-start.48 = (bf16[4,128,128]{2,1,0:T(8,128)(2,1)S(1)}, bf16[4,128,128]{2,1,0:T(8,128)(2,1)S(1)}, u32[]{:S(2)}, u32[]{:S(2)}) collective-permute-start(bf16[4,128,128]{2,1,0:T(8,128)(2,1)S(1)} %get-tuple-element.147), channel_id=1, source_target_pairs={{0,2},{2,4},{4,6},{1,3},{3,5},{5,7},{8,10},{10,12},{12,14},{9,11},... | collective-permute-start | bytes 393224 | tf_op jit(solution)/shard_map/ppermute | solution.py:38
  435.3 6.6 collective-permute-start.50
  436.6 7.7 collective-permute-start.49
  455.6 13.6 %collective-permute-start.51 = (bf16[2,64,2048]{2,1,0:T(8,128)(2,1)S(1)}, bf16[2,64,2048]{2,1,0:T(8,128)(2,1)S(1)}, u32[]{:S(2)}, u32[]{:S(2)}) collective-permute-start(bf16[2,64,2048]{2,1,0:T(8,128)(2,1)S(1)} %stack.388), channel_id=1, source_target_pairs={{0,16},{8,24},{16,0},{24,8},{1,17},{9,25},{17,1},{25,9},{2,18},{10... | collective-permute-start | bytes 1572872 | tf_op jit(solution)/shard_map/ppermute | solution.py:29
  458.2 14.3 %collective-permute-start.53 = (bf16[2,64,2048]{2,1,0:T(8,128)(2,1)S(1)}, bf16[2,64,2048]{2,1,0:T(8,128)(2,1)S(1)}, u32[]{:S(2)}, u32[]{:S(2)}) collective-permute-start(bf16[2,64,2048]{2,1,0:T(8,128)(2,1)S(1)} %pad_maximum_fusion.20), channel_id=1, source_target_pairs={{0,8},{8,0},{16,24},{24,16},{1,9},{9,1},{17,25},{25,17},{2,10},{10... | collective-permute-start | bytes 1572872 | tf_op jit(solution)/shard_map/ppermute | solution.py:29
  469.3 7.8 collective-permute-start.52
  477.2 6.9 collective-permute-start.54
  (48 other events, 484.0 us)

commit v3 on v2

--- a/solution.py
+++ b/solution.py
@@ -458,26 +458,49 @@
         target[at, :] = (target[at, :].astype(F32) + other[at, :].astype(F32)).astype(BF)
 
 
-def sums_kernel(plan, *refs):
-    kinds = len(plan)
-    own, other = refs[:kinds], refs[kinds : 2 * kinds]
-    fin_own, fin_sib = refs[2 * kinds : 3 * kinds], refs[3 * kinds : 4 * kinds]
-    src, swap, first, second, load = (refs[(4 + g) * kinds : (5 + g) * kinds] for g in range(5))
-    (pair_s, pair_r, load_s, swap_s, swap_r, in_s, in_r, mid_s, mid_r, out_s, done_s, back_s, back_r) = refs[
-        9 * kinds :
-    ]
+def back_kernel(
+    at_ref,
+    own_down, own_gate, own_up, other_down, other_gate, other_up,
+    back_part, out_part, w_out, wqkv_hbm, h1_hbm,
+    mixed, branch_own, x_own, gain_one, gain_two,
+    attended, queries, lse, kv_all, kp, cosine, sine,
+    fin_down, fin_gate, fin_up, fin_out, fin_qkv, fin_gain,
+    sib_down, sib_gate, sib_up, sib_out, sib_qkv, sib_gain,
+    outputs, input_grad,
+    src_down, src_gate, src_up, src_out, src_qkv, src_gain,
+    swap_gate, swap_up, swap_qkv,
+    end_down, end_gate, end_up, end_out, end_qkv, end_gain,
+    load_down, load_gate, give_out, give_qkv, give_gain,
+    landed, landed_out, first_back, first_out, da_all, wide, do_all, dqkv, wqkv, h1,
+    vk, dk_sum, dv_sum, kv_part, kv_land, kv_mine, kv_line, gain_acc, gain_all,
+    pair_s, pair_r, load_s, swap_s, swap_r, in_s, in_r, mid_s, mid_r, out_s, done_s, back_s, back_r, ready,
+    local_s, rs_s, rs_r, ro_s, ro_r, ag_s, ag_r, rq_s, rq_r, kp_s, kp_r, kz_s, kz_r, ga_s, ga_r,
+):
     f, z, k = lax.axis_index("fsdp"), lax.axis_index("z"), lax.axis_index("core")
-    line = lax.axis_size("z")
+    plane, line = lax.axis_size("fsdp"), lax.axis_size("z")
     outer = (z == 0) | (z == line - 1)
     inner = jnp.logical_not(outer)
     inward = jnp.where(z < line // 2, z + 1, z - 1)
     outward = jnp.where(z < line // 2, z - 1, z + 1)
-
-    chunks = []
-    for a, (n, swapped) in enumerate(plan):
-        for i in range(n):
-            chunks.append((a, i, i if swapped else 0))
+    rows, depth = mixed.shape
+    total = plane * rows
+    half_depth = depth // 2
+    half = half_depth // plane
+    q_width = attended.shape[1]
+    pairs = q_width // 128
+    peers = range(1, plane)
+
+    kinds = {
+        "down": (own_down, other_down, src_down, None, end_down, load_down, fin_down, sib_down),
+        "gate": (own_gate, other_gate, src_gate, swap_gate, end_gate, load_gate, fin_gate, sib_gate),
+        "up": (own_up, other_up, src_up, swap_up, end_up, load_gate, fin_up, sib_up),
+        "out": (None, give_out, src_out, None, end_out, None, fin_out, sib_out),
+        "qkv": (None, give_qkv, src_qkv, swap_qkv, end_qkv, None, fin_qkv, sib_qkv),
+        "gain": (None, give_gain, src_gain, None, end_gain, None, fin_gain, sib_gain),
+    }
+    chunks = [(name, i) for name, kind in kinds.items() for i in range(kind[2].shape[0])]
     count = len(chunks)
+    loaded = [c for c in range(count) if kinds[chunks[c][0]][0] is not None]
 
     def remote(source, target, send, recv, where):
         return pltpu.make_async_remote_copy(
@@ -489,55 +512,90 @@
             device_id_type=pl.DeviceIdType.MESH,
         )
 
+    def part(c, which):
+        name, i = chunks[c]
+        return kinds[name][which].at[i]
+
+    def swapped(c):
+        name, i = chunks[c]
+        return i if kinds[name][3] is not None else 0
+
     def pair_copy(c):
-        a, i, _ = chunks[c]
-        return remote(other[a].at[i], src[a].at[i], pair_s.at[c], pair_r.at[c], {"core": 1 - k})
+        name, i = chunks[c]
+        given = kinds[name][1]
+        source = given.at[i] if c in loaded else given.at[i % given.shape[0]]
+        return remote(source, part(c, 2), pair_s.at[c], pair_r.at[c], {"core": 1 - k})
 
     def load_copy(c):
-        a, i, _ = chunks[c]
-        return pltpu.make_async_copy(own[a].at[i], load[a].at[i % 2], load_s.at[c])
+        return pltpu.make_async_copy(part(c, 0), kinds[chunks[c][0]][5].at[c % 2], load_s.at[c])
 
     def swap_copy(c):
-        a, i, j = chunks[c]
-        return remote(src[a].at[i], swap[a].at[i], swap_s.at[c], swap_r.at[c], {"fsdp": f ^ j})
+        return remote(part(c, 2), part(c, 3), swap_s.at[c], swap_r.at[c], {"fsdp": f ^ swapped(c)})
 
     def base(c):
-        a, i, j = chunks[c]
-        return swap[a].at[i] if j else src[a].at[i]
+        return part(c, 3) if swapped(c) else part(c, 2)
 
     def in_copy(c):
-        a, i, _ = chunks[c]
-        return remote(base(c), first[a].at[i], in_s.at[c], in_r.at[c], {"z": inward})
+        return remote(base(c), part(c, 4), in_s.at[c], in_r.at[c], {"z": inward})
 
     def mid_copy(c):
-        a, i, _ = chunks[c]
-        return remote(first[a].at[i], second[a].at[i], mid_s.at[c], mid_r.at[c], {"z": inward})
+        return remote(base(c), part(c, 4), mid_s.at[c], mid_r.at[c], {"z": inward})
 
     def out_copy(c):
-        a, i, _ = chunks[c]
-        return remote(second[a].at[i], second[a].at[i], out_s.at[c], mid_r.at[c], {"z": outward})
+        return remote(part(c, 4), part(c, 4), out_s.at[c], mid_r.at[c], {"z": outward})
 
     def keep_copy(c):
-        a, i, _ = chunks[c]
-        return pltpu.make_async_copy(second[a].at[i], fin_own[a].at[i], done_s.at[c])
+        return pltpu.make_async_copy(part(c, 4), part(c, 6), done_s.at[c])
 
     def back_copy(c):
-        a, i, _ = chunks[c]
-        return remote(second[a].at[i], fin_sib[a].at[i], back_s.at[c], back_r.at[c], {"core": 1 - k})
+        return remote(part(c, 4), part(c, 7), back_s.at[c], back_r.at[c], {"core": 1 - k})
+
+    own_cols = pl.ds(pl.multiple_of(k * half_depth, 128), half_depth)
+    other_cols = pl.ds(pl.multiple_of((1 - k) * half_depth, 128), half_depth)
+
+    def out_term(i, cols):
+        size = src_out.shape[1]
+        right = da_all[:, :, cols].reshape(total, half_depth)
+        return tn(attended[:, i * size : (i + 1) * size], right)
+
+    def qkv_term(i, side):
+        start = side * half_depth + i * half
+        return tn(h1[:, start : start + half], dqkv[...])
+
+    def term(c, side):
+        name, i = chunks[c]
+        if name == "out":
+            return out_term(i, (own_cols, other_cols)[side])
+        if name == "qkv":
+            return qkv_term(i, side)
+        return gain_all[...].astype(F32).sum(axis=0)
+
+    def stage_give(c):
+        name, i = chunks[c]
+        if c in loaded:
+            return
+        given = kinds[name][1]
+        slots = given.shape[0]
+        if i >= slots:
+            pair_copy(c - slots).wait_send()
+        given[i % slots] = term(c, 1).astype(BF)
+        pair_copy(c).start()
 
     def stage_pair(c):
-        a, i, j = chunks[c]
         pair_copy(c).wait_recv()
-        load_copy(c).wait()
-        add_into(src[a].at[i], load[a].at[i % 2])
-        nxt = c + 2
-        if nxt < count:
-            load_copy(nxt).start()
-        if j:
+        if c in loaded:
+            load_copy(c).wait()
+            add_into(part(c, 2), kinds[chunks[c][0]][5].at[c % 2])
+            if c + 2 in loaded:
+                load_copy(c + 2).start()
+        else:
+            target = part(c, 2)
+            target[...] = (target[...].astype(F32) + term(c, 0)).astype(BF)
+        if swapped(c):
             swap_copy(c).start()
 
     def stage_in(c):
-        if chunks[c][2]:
+        if swapped(c):
             swap_copy(c).wait_recv()
 
         @pl.when(outer)
@@ -545,21 +603,21 @@
             in_copy(c).start()
 
     def stage_mid(c):
-        a, i, _ = chunks[c]
-
         @pl.when(inner)
         def _():
             in_copy(c).wait_recv()
-            add_into(first[a].at[i], base(c))
+            add_into(base(c), part(c, 4))
+            pl.semaphore_signal(
+                ready, inc=1, device_id={"z": inward}, device_id_type=pl.DeviceIdType.MESH
+            )
+            pl.semaphore_wait(ready, 1)
             mid_copy(c).start()
 
     def stage_out(c):
-        a, i, _ = chunks[c]
-
         @pl.when(inner)
         def _():
             mid_copy(c).wait_recv()
-            add_into(second[a].at[i], first[a].at[i])
+            add_into(part(c, 4), base(c))
             out_copy(c).start()
 
     def stage_keep(c):
@@ -570,18 +628,224 @@
         keep_copy(c).start()
         back_copy(c).start()
 
-    for c in range(count):
+    def back_send(j):
+        return remote(back_part.at[j], landed.at[j - 1], rs_s.at[j - 1], rs_r.at[j - 1], {"fsdp": f ^ j})
+
+    def out_send(j):
+        return remote(out_part.at[j], landed_out.at[j - 1], ro_s.at[j - 1], ro_r.at[j - 1], {"fsdp": f ^ j})
+
+    def da_send(j):
+        return remote(da_all.at[0], da_all.at[j], ag_s.at[j - 1], ag_r.at[j - 1], {"fsdp": f ^ j})
+
+    def dh_send(j):
+        mine = wide.at[pl.ds(j * rows, rows), :]
+        return remote(mine, landed.at[j - 1], rq_s.at[j - 1], rq_r.at[j - 1], {"fsdp": f ^ j})
+
+    def gain_send(j):
+        return remote(gain_all.at[0], gain_all.at[j], ga_s.at[j - 1], ga_r.at[j - 1], {"fsdp": f ^ j})
+
+    locals_ = [
+        pltpu.make_async_copy(back_part.at[0], first_back, local_s.at[0]),
+        pltpu.make_async_copy(out_part.at[0], first_out, local_s.at[1]),
+        pltpu.make_async_copy(w_out, wide.at[pl.ds(0, w_out.shape[0]), :], local_s.at[2]),
+        pltpu.make_async_copy(wqkv_hbm, wqkv, local_s.at[3]),
+        pltpu.make_async_copy(h1_hbm, h1, local_s.at[4]),
+    ]
+
+    def rms_back(gradient_of, x_ref, gain, acc, write):
+        acc[...] = jnp.zeros_like(acc)
+
+        @pl.loop(0, rows // 16)
+        def _(i):
+            at = pl.ds(pl.multiple_of(i * 16, 16), 16)
+            gradient = gradient_of(at)
+            x = x_ref[at, :].astype(F32)
+            inverse = lax.rsqrt(jnp.mean(x * x, axis=1, keepdims=True) + EPSILON)
+            normed = x * inverse
+            acc[...] += gradient * normed
+            scaled = gradient * gain[...]
+            write(at, inverse * (scaled - normed * jnp.mean(scaled * normed, axis=1, keepdims=True)))
+
+    def piece_mixed():
+        locals_[0].wait()
+        for j in peers:
+            back_send(j).wait_recv()
+
+        def gradient_of(at):
+            value = first_back[at, :].astype(F32)
+            for j in peers:
+                value = value + landed[j - 1, at, :].astype(F32)
+            return value
+
+        def write(at, value):
+            value = value + branch_own[at, :].astype(F32)
+            input_grad[at, :] = value
+            da_all[0, at, :] = value.astype(BF)
+
+        rms_back(gradient_of, mixed, gain_two, gain_acc.at[1], write)
+        for j in peers:
+            da_send(j).start()
+
+    def piece_do():
+        locals_[2].wait()
+        for j in peers:
+            da_send(j).wait_recv()
+            out_send(j).start()
+
+        @pl.loop(0, plane)
+        def _(j):
+            do_all[j] = nt(da_all[j], wide[0 : w_out.shape[0], :]).astype(BF)
+
+    def piece_attend(j):
+        vk[...] = pltpu.roll(kv_all[:, j].reshape(vk.shape).astype(F32), 64, 1).astype(BF)
+        dk_sum[...] = jnp.zeros_like(dk_sum)
+        dv_sum[...] = jnp.zeros_like(dv_sum)
+        place = at_ref[0] - lax.broadcasted_iota(jnp.int32, (rows, 1), 0)
+        limit = jnp.minimum(place, at_ref[1 + j] - 1)
+        lane = lax.broadcasted_iota(jnp.int32, (rows, 128), 1)
+
+        @pl.loop(0, pairs)
+        def _(p):
+            at = pl.ds(pl.multiple_of(p * 128, 128), 128)
+            allowed = kp[...] <= limit
+            q, do = queries[j, :, at], do_all[j, :, at]
+            logs = lse[j, :, at]
+            zero = jnp.zeros_like(q)
+            parts = []
+            for first in (True, False):
+                mine = lane < 64 if first else lane >= 64
+                kv = kv_all[:, j].reshape(vk.shape)
+                keyed, valued = (kv, vk[...]) if first else (vk[...], kv)
+                q_own, do_own = jnp.where(mine, q, zero), jnp.where(mine, do, zero)
+                scores = nt(q_own, keyed) * (HEAD_DIM**-0.5)
+                log_total = logs[:, 0:1] if first else logs[:, 64:65]
+                weights = jnp.where(allowed, jnp.exp(scores - log_total), 0.0)
+                joint = weights * nt(do_own, valued)
+                back = (joint - weights * jnp.sum(joint, axis=1, keepdims=True)).astype(BF)
+                parts.append(nn(back, keyed))
+                dk_sum[...] += tn(back, q_own)
+                dv_sum[...] += tn(weights.astype(BF), do_own)
+            turned = jnp.where(lane < 64, parts[0], parts[1]) * (HEAD_DIM**-0.5)
+            turned = turned * cosine[...] - swap_halves(turned) * sine[...]
+            dqkv[j * rows : (j + 1) * rows, at] = turned.astype(BF)
+
+        dk = dk_sum[...]
+        dv = dv_sum[...]
+        dk = (dk + pltpu.roll(dk, 64, 1)) * (HEAD_DIM**-0.5)
+        dv = dv + pltpu.roll(dv, 64, 1)
+        wide_lane = lax.broadcasted_iota(jnp.int32, dk.shape, 1)
+        packed = jnp.where(wide_lane < 64, dk, dv).astype(BF)
+        kv_part[:, j] = packed.reshape(kv_part.shape[0], rows, 128)
+
+    kv_pair = remote(kv_part.at[pl.ds(line, line)], kv_land, kp_s.at[0], kp_r.at[0], {"core": 1 - k})
+
+    def kv_send(s):
+        return remote(kv_mine.at[s], kv_line.at[s - 1], kz_s.at[s - 1], kz_r.at[s - 1], {"z": z + s})
+
+    def piece_kv_line():
+        kv_pair.wait_recv()
+        for s in range(line):
+            kv_mine[s] = (kv_part[s].astype(F32) + kv_land[s].astype(F32)).astype(BF)
+        for s in range(1, line):
+
+            @pl.when(z + s < line)
+            def _():
+                kv_send(s).start()
+
+    def piece_kv_sum():
+        for s in range(1, line):
+
+            @pl.when(z >= s)
+            def _():
+                kv_send(s).wait_recv()
+                kv_mine[0] = (kv_mine[0].astype(F32) + kv_line[s - 1].astype(F32)).astype(BF)
+
+        lane = lax.broadcasted_iota(jnp.int32, (rows, 128), 1)
+        for j in range(plane):
+            value = kv_mine[0, j].astype(F32)
+            turned = value * cosine[...] - swap_halves(value) * sine[...]
+            value = jnp.where(lane < 64, turned, value).astype(BF)
+            dqkv[j * rows : (j + 1) * rows, q_width : q_width + 128] = value
+
+    def piece_dh():
+        locals_[3].wait()
+        for h in range(2):
+            for j in range(plane):
+                start = pl.multiple_of(((f ^ j) * 2 + (k ^ h)) * half, 128)
+                block = wqkv[(h * plane + j) * half : (h * plane + j + 1) * half, :]
+                wide[0:total, pl.ds(start, half)] = nt(dqkv[...], block).astype(BF)
+        for j in peers:
+            dh_send(j).start()
+
+    def piece_input():
+        for j in peers:
+            dh_send(j).wait_recv()
+
+        def gradient_of(at):
+            value = wide[at, :].astype(F32)
+            for j in peers:
+                value = value + landed[j - 1, at, :].astype(F32)
+            return value
+
+        def write(at, value):
+            input_grad[at, :] = input_grad[at, :] + value
+
+        rms_back(gradient_of, x_own, gain_one, gain_acc.at[0], write)
+        place = lax.broadcasted_iota(jnp.int32, (16, depth), 0)
+        one = jnp.sum(gain_acc[0], axis=0, keepdims=True)
+        two = jnp.sum(gain_acc[1], axis=0, keepdims=True)
+        gain_all[0] = jnp.where(place == 0, one, jnp.where(place == 1, two, 0.0)).astype(BF)
+        for j in peers:
+            gain_send(j).start()
+
+    def piece_outputs():
+        locals_[1].wait()
+        for j in peers:
+            out_send(j).wait_recv()
+
+        @pl.loop(0, rows // 16)
+        def _(i):
+            at = pl.ds(pl.multiple_of(i * 16, 16), 16)
+            value = mixed[at, :] + first_out[at, :].astype(F32)
+            for j in peers:
+                value = value + landed_out[j - 1, at, :].astype(F32)
+            outputs[at, :] = value
+
+    def piece_gain():
+        for j in peers:
+            gain_send(j).wait_recv()
+        locals_[4].wait()
+
+    pieces = {2: [piece_mixed], 4: [piece_do]}
+    for j in range(plane):
+        pieces.setdefault(4 + j, []).append(functools.partial(piece_attend, j))
+    pieces[3 + plane].append(lambda: kv_pair.start())
+    pieces[4 + plane] = [piece_kv_line, piece_outputs]
+    pieces[5 + plane] = [piece_kv_sum, piece_dh]
+    pieces[7 + plane] = [piece_input]
+    pieces[8 + plane] = [piece_gain]
+
+    for j in peers:
+        back_send(j).start()
+    for c in loaded:
         pair_copy(c).start()
-    for c in range(min(2, count)):
+    for c in loaded[:2]:
         load_copy(c).start()
-    stages = ((0, stage_pair), (1, stage_in), (2, stage_mid), (4, stage_out), (6, stage_keep))
+    for copy in locals_:
+        copy.start()
+    stages = ((-1, stage_give), (0, stage_pair), (1, stage_in), (2, stage_mid), (4, stage_out), (6, stage_keep))
     for tick in range(count + stages[-1][0]):
         for lag, stage in stages:
             if 0 <= tick - lag < count:
                 stage(tick - lag)
+        for piece in pieces.get(tick, []):
+            piece()
+
     for c in range(count):
-        pair_copy(c).wait_send()
-        if chunks[c][2]:
+        name, i = chunks[c]
+        if c in loaded or i + kinds[name][1].shape[0] >= kinds[name][2].shape[0]:
+            pair_copy(c).wait_send()
+        if swapped(c):
             swap_copy(c).wait_send()
         keep_copy(c).wait()
         back_copy(c).wait_send()
@@ -596,6 +860,94 @@
             mid_copy(c).wait_send()
             out_copy(c).wait_send()
 
+    for j in peers:
+        back_send(j).wait_send()
+        out_send(j).wait_send()
+        da_send(j).wait_send()
+        dh_send(j).wait_send()
+        gain_send(j).wait_send()
+    kv_pair.wait_send()
+    for s in range(1, line):
+
+        @pl.when(z + s < line)
+        def _():
+            kv_send(s).wait_send()
+
+
+def back_pass(
+    at, own, other, back_part, out_part, w_out, wqkv, h1, mixed, branch_own, x_own, gain_one, gain_two,
+    attended, queries, lse, kv_all, kp, cosine, sine,
+):
+    count, line = lax.axis_size("fsdp"), lax.axis_size("z")
+    rows, depth = mixed.shape
+    total, half_depth = count * rows, depth // 2
+    half = half_depth // count
+    q_width = attended.shape[1]
+    keys = kv_all.shape[0] * rows
+    shapes = [x.shape for x in own] + [
+        (2, q_width // 2, half_depth),
+        (count, half, q_width + 128),
+        (1, 16, depth),
+    ]
+    anywhere = pl.BlockSpec(memory_space=pl.ANY)
+    local = pl.BlockSpec(memory_space=pltpu.VMEM)
+    ends = [jax.ShapeDtypeStruct(s, BF) for s in shapes]
+    act = jax.ShapeDtypeStruct((rows, depth), F32)
+    block = (rows, depth)
+    chunk_count = sum(s[0] for s in shapes)
+    dma = lambda n: pltpu.SemaphoreType.DMA((n,))
+    scratch = (
+        [pltpu.VMEM(s, BF) for s in shapes]
+        + [pltpu.VMEM(shapes[i], BF) for i in (1, 2, 4)]
+        + [pltpu.VMEM(s, BF) for s in shapes]
+        + [pltpu.VMEM((2,) + shapes[i][1:], BF) for i in (0, 1, 3, 4)]
+        + [pltpu.VMEM(shapes[5], BF)]
+        + [
+            pltpu.VMEM((count - 1,) + block, BF),
+            pltpu.VMEM((count - 1,) + block, BF),
+            pltpu.VMEM(block, BF),
+            pltpu.VMEM(block, BF),
+            pltpu.VMEM((count,) + block, BF),
+            pltpu.VMEM((max(total, q_width), depth), BF),
+            pltpu.VMEM((count, rows, q_width), BF),
+            pltpu.VMEM((total, q_width + 128), BF),
+            pltpu.VMEM(wqkv.shape, BF),
+            pltpu.VMEM(h1.shape, BF),
+            pltpu.VMEM((keys, 128), BF),
+            pltpu.VMEM((keys, 128), F32),
+            pltpu.VMEM((keys, 128), F32),
+            pltpu.VMEM(kv_all.shape, BF),
+            pltpu.VMEM((line,) + kv_all.shape[1:], BF),
+            pltpu.VMEM((line,) + kv_all.shape[1:], BF),
+            pltpu.VMEM((line - 1,) + kv_all.shape[1:], BF),
+            pltpu.VMEM((2, 16, depth), F32),
+            pltpu.VMEM((count, 16, depth), BF),
+        ]
+        + [dma(chunk_count)] * 13
+        + [pltpu.SemaphoreType.REGULAR, dma(5)]
+        + [dma(count - 1)] * 8
+        + [dma(1)] * 2
+        + [dma(line - 1)] * 2
+        + [dma(count - 1)] * 2
+    )
+    out = pl.pallas_call(
+        back_kernel,
+        out_shape=ends + ends + [act, act],
+        in_specs=[pl.BlockSpec(memory_space=pltpu.SMEM)] + [anywhere] * 11 + [local] * 12,
+        out_specs=[anywhere] * 12 + [local] * 2,
+        scratch_shapes=scratch,
+        compiler_params=pltpu.CompilerParams(
+            vmem_limit_bytes=62 * 1024 * 1024, has_side_effects=True
+        ),
+        cost_estimate=pl.CostEstimate(
+            flops=10**11, bytes_accessed=10**9, transcendentals=10**7
+        ),
+        name="back_pass",
+    )(
+        at, *own, *other, back_part, out_part, w_out, wqkv, h1, mixed, branch_own, x_own, gain_one, gain_two,
+        attended, queries, lse, kv_all, kp, cosine, sine,
+    )
+    return out[:6], out[6:12], out[12], out[13]
 
 def sum_gradients_plain(owns, others, swapped):
     ends = []
@@ -607,34 +959,64 @@
     return ends, [to_sibling(e) for e in ends]
 
 
-def sum_gradients(owns, others, swapped):
-    plan = tuple((x.shape[0], s) for x, s in zip(owns, swapped))
-    count = sum(n for n, _ in plan)
-    shapes = [jax.ShapeDtypeStruct(x.shape, BF) for x in owns]
-    anywhere = pl.BlockSpec(memory_space=pl.ANY)
-    whole = [pltpu.VMEM(x.shape, BF) for x in owns]
-    swaps = [pltpu.VMEM(x.shape if s else (1, 16, 128), BF) for x, s in zip(owns, swapped)]
-    loads = [pltpu.VMEM((2,) + x.shape[1:], BF) for x in owns]
-    size = sum(x.size for x in owns)
-    out = pl.pallas_call(
-        functools.partial(sums_kernel, plan),
-        out_shape=shapes + shapes,
-        in_specs=[anywhere] * (2 * len(owns)),
-        out_specs=[anywhere] * (2 * len(owns)),
-        scratch_shapes=whole + swaps + whole + whole + loads + [pltpu.SemaphoreType.DMA((count,))] * 13,
-        compiler_params=params(has_side_effects=True),
-        cost_estimate=pl.CostEstimate(flops=4 * size, bytes_accessed=400 * size, transcendentals=0),
-        name="sum_gradients",
-    )(*owns, *others)
-    return out[: len(owns)], out[len(owns) :]
-
-
 def rms_backward(row_block, inverse, gain_vec, gradient):
     normed = row_block * inverse
     gain_grad = jnp.sum(gradient * normed, axis=0)
     scaled = gradient * gain_vec
     back = inverse * (scaled - normed * jnp.mean(scaled * normed, axis=1, keepdims=True))
     return (back, gain_grad)
+
+
+def back_plain(
+    at, own, other, back_part, out_part, w_out, wqkv, h1, mixed, branch_own, x_own, gain_one, gain_two,
+    attended, queries, lse, kv_all, kp, cosine, sine,
+):
+    count, line = lax.axis_size("fsdp"), lax.axis_size("z")
+    k = lax.axis_index("core")
+    rows, depth = mixed.shape
+    total, half_depth = count * rows, depth // 2
+    half = half_depth // count
+    q_width = attended.shape[1]
+    f = lax.axis_index("fsdp")
+    order = jnp.stack([(f ^ j) * 2 + (k ^ h) for h in range(2) for j in range(count)]).astype(jnp.int32)
+    outputs = mixed + plane_reduce(out_part)
+    inv_two = lax.rsqrt(jnp.mean(mixed * mixed, axis=1, keepdims=True) + EPSILON)
+    mixed_back, gain_two_grad = rms_backward(mixed, inv_two, gain_two, plane_reduce(back_part))
+    mixed_grad = branch_own.astype(F32) + mixed_back
+    attn_back = jnp.concatenate(plane_gather(mixed_grad.astype(BF)))
+    attended_grad = nt(attn_back, w_out).astype(BF).reshape(count, rows, q_width)
+    own, other = list(own), list(other)
+    for place, terms in ((k, own), (1 - k, other)):
+        right = lax.dynamic_slice_in_dim(attn_back, place * half_depth, half_depth, 1)
+        terms.append(tn(attended, right).astype(BF).reshape(2, -1, half_depth))
+    query_back, kv_part = attend_back(at, queries, attended_grad, lse, kv_all, kp, cosine, sine)
+    kv_mine = kv_part[:line].astype(F32) + to_sibling(kv_part[line:]).astype(F32)
+    kv_back = kv_mine[0]
+    for s in range(1, line):
+        kv_back = kv_back + along_line(kv_mine[s].astype(BF), s).astype(F32)
+    lead, trail, flat = kv_back[..., :32], kv_back[..., 32:64], kv_back[..., 64:]
+    cos32, sin32 = cosine[:, :32], sine[:, 32:64]
+    kv_back = jnp.concatenate(
+        [lead * cos32 + trail * sin32, trail * cos32 - lead * sin32, flat], axis=-1
+    ).astype(BF)
+    qkv_back = jnp.concatenate(
+        [query_back.reshape(total, q_width), kv_back.reshape(total, 128)], axis=1
+    )
+    normed_back = put_columns(nt(qkv_back, wqkv).astype(BF), order, 2 * count)
+    inputs = x_own.astype(F32)
+    inv_one = lax.rsqrt(jnp.mean(inputs * inputs, axis=1, keepdims=True) + EPSILON)
+    input_back, gain_one_grad = rms_backward(
+        inputs, inv_one, gain_one, plane_reduce(normed_back.reshape(count, rows, depth))
+    )
+    for side, terms in ((0, own), (1, other)):
+        left = h1[:, side * half_depth : (side + 1) * half_depth]
+        terms.append(tn(left, qkv_back).astype(BF).reshape(count, half, q_width + 128))
+    gains = jnp.stack([gain_one_grad, gain_two_grad]).astype(BF)
+    for bit in plane_bits():
+        gains = (gains.astype(F32) + along_plane(gains, bit).astype(F32)).astype(BF)
+    gains = jnp.pad(gains, ((0, 14), (0, 0)))[None]
+    ends, sibs = sum_gradients_plain(own + [gains], other + [gains], (False, True, True, False, True, False))
+    return ends, sibs, outputs, mixed_grad + input_back
 
 
 def body(
@@ -776,70 +1158,26 @@
     back_own = (nt(gate_back, gate_own) + nt(up_back, up_own)).astype(BF)
     back_sib = (nt(gate_back, gate_sib) + nt(up_back, up_sib)).astype(BF)
     normed_back = put_columns(jnp.concatenate([back_own, back_sib], axis=1), order, 2 * count)
-    normed_back = plane_reduce(normed_back.reshape(count, rows, depth))
-
+    normed_back = normed_back.reshape(count, rows, depth)
     out_part = nn(hidden, w_down).astype(BF).reshape(count, rows, depth)
-    outputs = mixed + plane_reduce(out_part)
-
-    mixed_back, gain_two_grad = rms_backward(mixed, inv_two, gain_two, normed_back)
-    mixed_grad = out_back + mixed_back
-    attn_back = jnp.concatenate(plane_gather(mixed_grad.astype(BF)))
-    attended_grad = nt(attn_back, w_out).astype(BF).reshape(count, rows, q_width)
-
-    back_mine = lax.dynamic_slice_in_dim(attn_back, k * half_depth, half_depth, 1)
-    back_other = lax.dynamic_slice_in_dim(attn_back, (1 - k) * half_depth, half_depth, 1)
-    terms["out"] = (tn(attended, back_mine).astype(BF), tn(attended, back_other).astype(BF))
-
-    query_back, kv_part = attend_back(at, queries, attended_grad, log_total, kv_all, kp, cosine, sine)
-    kv_mine = kv_part[:line].astype(F32) + to_sibling(kv_part[line:]).astype(F32)
-    kv_back = kv_mine[0]
-    for s in range(1, line):
-        kv_back = kv_back + along_line(kv_mine[s].astype(BF), s).astype(F32)
-    lead, trail, flat = kv_back[..., :32], kv_back[..., 32:64], kv_back[..., 64:]
-    kv_back = jnp.concatenate(
-        [lead * cos32 + trail * sin32, trail * cos32 - lead * sin32, flat], axis=-1
-    ).astype(BF)
-    qkv_back = jnp.concatenate(
-        [query_back.reshape(total, q_width), kv_back.reshape(total, 128)], axis=1
-    )
-
-    normed_one_back = nt(qkv_back, wqkv_all).astype(BF)
-    normed_one_back = put_columns(normed_one_back, order, 2 * count)
-    normed_one_back = plane_reduce(normed_one_back.reshape(count, rows, depth))
-    inv_one = lax.rsqrt(jnp.mean(inputs * inputs, axis=1, keepdims=True) + EPSILON)
-    input_back, gain_one_grad = rms_backward(inputs, inv_one, gain_one, normed_one_back)
-    input_grad = mixed_grad + input_back
-
-    n1_own, n1_sib = normed_one[:, :half_depth], normed_one[:, half_depth:]
-    qkv_own, qkv_other = slab_terms(n1_own, n1_sib, qkv_back)
-    gains = jnp.stack([gain_one_grad, gain_two_grad]).reshape(2, count, slab)
-    gains = jnp.stack(
-        [lax.dynamic_index_in_dim(gains, f ^ j, 1, keepdims=False) for j in range(count)]
-    ).astype(BF)
-    width = q_width + 128
-    gains = jnp.pad(gains, ((0, 0), (0, 14), (0, width - slab)))
-    qkv_own = jnp.concatenate([qkv_own, gains], axis=1)
-    qkv_other = jnp.concatenate([qkv_other, jnp.zeros_like(gains)], axis=1)
-    terms["qkv"] = (qkv_own, qkv_other)
-
-    cut = {"down": (4, -1, half_depth), "out": (2, -1, half_depth)}
-    names = ("down", "gate", "up", "out", "qkv")
-    owns = [terms[n][0].reshape(cut[n]) if n in cut else terms[n][0] for n in names]
-    others = [terms[n][1].reshape(cut[n]) if n in cut else terms[n][1] for n in names]
-    summed = sum_gradients if line == 4 else sum_gradients_plain
-    owns, sibs = summed(owns, others, (False, True, True, False, True))
-    ends = dict(zip(names, zip(owns, sibs)))
-
-    def columns(name):
-        return join_columns(*(x.reshape(-1, half_depth) for x in ends[name]), k)
-
-    down_grad, out_grad = columns("down"), columns("out")
-    gate_grad, up_grad = join_rows(*ends["gate"], f, k), join_rows(*ends["up"], f, k)
-    qkv_half, qkv_sib = ends["qkv"]
-    gains = jnp.sum(qkv_half[:, half : half + 2, :slab].astype(F32), axis=0)
-    gains = gains + jnp.sum(qkv_sib[:, half : half + 2, :slab].astype(F32), axis=0)
-    query_grad = join_rows(qkv_half[:, :half, :q_width], qkv_sib[:, :half, :q_width], f, k)
-    halves = jnp.stack([qkv_half[:, :half, q_width:], qkv_sib[:, :half, q_width:]])
+    terms["down"] = tuple(t.reshape(4, -1, half_depth) for t in terms["down"])
+    names = ("down", "gate", "up")
+    own, other = [terms[n][0] for n in names], [terms[n][1] for n in names]
+    rest = (mixed, branch_own, x_own, gain_one, gain_two, attended, queries, log_total, kv_all, kp, cosine, sine)
+    run = back_pass if line == 4 and q_width % 256 == 0 else back_plain
+    owns, sibs, outputs, input_grad = run(
+        at, own, other, normed_back, out_part, w_out, wqkv_all, normed_one, *rest
+    )
+
+    def columns(i):
+        return join_columns(*(x[i].reshape(-1, half_depth) for x in (owns, sibs)), k)
+
+    down_grad, out_grad = columns(0), columns(3)
+    gate_grad, up_grad = (join_rows(owns[i], sibs[i], f, k) for i in (1, 2))
+    qkv_half, qkv_sib = owns[4], sibs[4]
+    query_grad = join_rows(qkv_half[:, :, :q_width], qkv_sib[:, :, :q_width], f, k)
+    gains = lax.dynamic_slice_in_dim(owns[5][0, :2], f * slab, slab, 1).astype(F32)
+    halves = jnp.stack([qkv_half[:, :, q_width:], qkv_sib[:, :, q_width:]])
 
     def by_head(lo, hi):
         both = [lax.dynamic_index_in_dim(halves, k ^ h, 0, keepdims=False) for h in range(2)]

time: 862 us -> 743 us (0.86)
  waiting for transfers between devices: 172 us -> 117 us
  matrix products: 90.4 us -> 62.7 us
  starting transfers between devices: 57.8 us -> 38 us
  local copies, waits for them, and re-layouts: 65.5 us -> 48.6 us
  Pallas kernels: 428 us -> 442 us
  other arithmetic: 30.6 us -> 18.7 us
    ppermute x44 -> x28, waiting for transfers between devices: 157 us -> 103 us  [along_plane(): return lax.ppermute(value, 'fsdp', [(i, i ^ step) for i in range(count)])]
    pallas_call x2 -> x1, Pallas kernels: 329 us -> 350 us  [back_pass(): pl.pallas_call(back_kernel, out_shape=ends + ends + [act, act], in_specs=...]
    dot_general x6, matrix products: 38.5 us -> 23.8 us  [nn(): return jnp.dot(a, b, preferred_element_type=F32)]
    ppermute x44 -> x28, starting transfers between devices: 45.8 us -> 33.6 us  [along_plane(): return lax.ppermute(value, 'fsdp', [(i, i ^ step) for i in range(count)])]
    dot_general x7 -> x5, matrix products: 26.1 us -> 18.7 us  [nt(): lax.dot_general(a, b, (((1,), (1,)), ((), ())), preferred_element_type=F32)]
    dot_general x10 -> x6, matrix products: 25.8 us -> 20.2 us  [tn(): lax.dot_general(a, b, (((0,), (0,)), ((), ())), preferred_element_type=F32)]
    unnamed x147 -> x84, local copies, waits for them, and re-layouts: 28.3 us -> 22.8 us
  transfers between devices with their start and end apart: 55 -> 35, of which waited for: 31 -> 19; matrix products, arithmetic and copies ran while one was open for 10% -> 7% of each run, Pallas kernels for 8% -> 6%
where the time goes in v3:
time: 743 us; the launch traced here: 734 us
  Pallas kernels  442 us (59%)
  waiting for transfers between devices  117 us (16%)
  matrix products  62.7 us (8%)
  local copies, waits for them, and re-layouts  48.6 us (7%)
  starting transfers between devices  38 us (5%)
  other arithmetic  18.7 us (3%)
  between operations  7.81 us (1%)
    pallas_call x1, Pallas kernels, back_pass(): pl.pallas_call(back_kernel, out_shape=ends + ends + [act, act], in_specs=...  350 us
    ppermute x28, waiting for transfers between devices, along_plane(): return lax.ppermute(value, 'fsdp', [(i, i ^ step) for i in range(count)])  103 us
    ppermute x28, starting transfers between devices, along_plane(): return lax.ppermute(value, 'fsdp', [(i, i ^ step) for i in range(count)])  33.6 us
    pallas_call x3, Pallas kernels, join_rows(): pl.pallas_call(join_kernel, grid_spec=spec, out_shape=jax.ShapeDtypeStruc...  26.3 us
    dot_general x6, matrix products, nn(): return jnp.dot(a, b, preferred_element_type=F32)  23.8 us
    unnamed x84, local copies, waits for them, and re-layouts  22.8 us
    dot_general x6, matrix products, tn(): lax.dot_general(a, b, (((0,), (0,)), ((), ())), preferred_element_type=F32)  20.2 us
    dot_general x5, matrix products, nt(): lax.dot_general(a, b, (((1,), (1,)), ((), ())), preferred_element_type=F32)  18.7 us
  transfers between devices with their start and end apart: 35, of which 19 were waited for; matrix products, arithmetic and copies ran while one was open for 7% of the time, Pallas kernels for 6%

profile of v3, /device:TPU:0, one launch (start us, length us, event | category | flops | bytes accessed | tf_op | source)
XLA Modules:
  0.0 734.5 jit_solution(18028854812340334465)
XLA Ops:
  3.5 2.9 collective-permute-start
  11.2 4.0 cut_blocks.3
  17.8 2.0 collective-permute-start.7
  25.3 4.8 cut_blocks.5
  30.1 3.1 fusion.48
  33.3 4.8 cut_blocks.4
  38.0 3.2 fusion.47
  46.4 2.0 collective-permute-start.4
  60.7 1.7 bitcast_dynamic-update-slice_fusion.5
  62.4 4.6 collective-permute-done.31
  72.9 2.9 collective-permute-done.32
  78.2 2.0 collective-permute-start.23
  80.9 1.6 collective-permute-start.24
  82.5 7.9 %collective-permute-done.27 = bf16[256,1408]{1,0:T(8,128)(2,1)S(1)} collective-permute-done((bf16[256,1408]{1,0:T(8,128)(2,1)S(1)}, bf16[256,1408]{1,0:T(8,128)(2,1)S(1)}, u32[]{:S(2)}, u32[]{:S(2)}) %collective-permute-start.27) | collective-permute-done | bytes 720928 | tf_op jit(solution)/shard_map/ppermute | solution.py:29
  92.9 17.4 %collective-permute-done.28 = bf16[256,1408]{1,0:T(8,128)(2,1)S(1)} collective-permute-done((bf16[256,1408]{1,0:T(8,128)(2,1)S(1)}, bf16[256,1408]{1,0:T(8,128)(2,1)S(1)}, u32[]{:S(2)}, u32[]{:S(2)}) %collective-permute-start.28) | collective-permute-done | bytes 720928 | tf_op jit(solution)/shard_map/ppermute | solution.py:29
  110.3 2.0 collective-permute-start.6
  112.8 8.6 %collective-permute-done.23 = bf16[256,1408]{1,0:T(8,128)(2,1)S(1)} collective-permute-done((bf16[256,1408]{1,0:T(8,128)(2,1)S(1)}, bf16[256,1408]{1,0:T(8,128)(2,1)S(1)}, u32[]{:S(2)}, u32[]{:S(2)}) %collective-permute-start.23) | collective-permute-done | bytes 720928 | tf_op jit(solution)/shard_map/ppermute | solution.py:29
  121.9 19.3 %collective-permute-done.24 = bf16[256,1408]{1,0:T(8,128)(2,1)S(1)} collective-permute-done((bf16[256,1408]{1,0:T(8,128)(2,1)S(1)}, bf16[256,1408]{1,0:T(8,128)(2,1)S(1)}, u32[]{:S(2)}, u32[]{:S(2)}) %collective-permute-start.24) | collective-permute-done | bytes 720928 | tf_op jit(solution)/shard_map/ppermute | solution.py:29
  142.7 1.8 pad_maximum_fusion
  144.5 3.6 collective-permute-done.5
  148.8 3.4 collective-permute-done.6
  152.9 1.7 bitcast_dynamic-update-slice_fusion.4
  158.5 6.9 qkv_project.1
  168.0 1.8 collective-permute-start.13
  171.4 2.0 collective-permute-done.11
  173.4 9.4 %collective-permute-done.12 = bf16[4,128,128]{2,1,0:T(8,128)(2,1)S(1)} collective-permute-done((bf16[4,128,128]{2,1,0:T(8,128)(2,1)}, bf16[4,128,128]{2,1,0:T(8,128)(2,1)S(1)}, u32[]{:S(2)}, u32[]{:S(2)}) %collective-permute-start.12) | collective-permute-done | bytes 131104 | tf_op jit(solution)/shard_map/ppermute | solution.py:38
  183.9 1.8 collective-permute-done.14
  186.8 17.9 %attend.1 = (bf16[4,128,512]{2,1,0:T(8,128)(2,1)}, f32[4,128,512]{2,1,0:T(8,128)}) custom-call(s32[5]{0:T(128)} %concatenate.135.at_ref, bf16[4,128,512]{2,1,0:T(8,128)(2,1)} %bitcast.320, bf16[8,4,128,128]{3,2,1,0:T(8,128)(2,1)} %copy-done.23, s32[1,1024]{1,0:T(1,128)} %compare_select_fusion.kp_ref.kp), custom_call_target="tpu_custom_call" | custom-call | flops 2147483648 | bytes 4194304 | tf_op jit(solution)/shard_map/attend/pallas_call | solution.py:360
  204.7 3.0 convolution_convert_fusion.6
  207.8 1.6 collective-permute-start.15
  210.1 11.8 %collective-permute-done.15 = bf16[2,64,2048]{2,1,0:T(8,128)(2,1)S(1)} collective-permute-done((bf16[2,64,2048]{2,1,0:T(8,128)(2,1)S(1)}, bf16[2,64,2048]{2,1,0:T(8,128)(2,1)S(1)}, u32[]{:S(2)}, u32[]{:S(2)}) %collective-permute-start.15) | collective-permute-done | bytes 524320 | tf_op jit(solution)/shard_map/ppermute | solution.py:29
  223.3 6.2 collective-permute-done.16
  229.7 1.6 collective-permute-start.18
  232.0 4.3 collective-permute-done.18
  237.4 1.6 collective-permute-start.20
  239.7 4.1 collective-permute-done.20
  243.9 2.4 collective-permute-start.21
  246.3 1.6 collective-permute-start.22
  247.9 6.7 collective-permute-done.21
  257.0 6.3 pick_columns.1
  263.3 4.1 fusion.5
  267.4 3.6 fusion.7
  271.0 1.8 convolution_add_fusion
  272.9 3.8 convolution_add_fusion.1
  276.7 6.0 multiply_convert_fusion
  282.7 1.8 fusion.58
  284.5 3.6 fusion.59
  288.2 3.4 convolution_convert_fusion
  291.5 3.4 convolution_convert_fusion.3
  295.0 3.4 convolution_convert_fusion.1
  298.4 3.4 convolution_convert_fusion.4
  301.8 3.7 add_convert_fusion.1
  305.5 3.7 add_convert_fusion
  310.6 6.4 put_columns.1
  317.0 7.5 %convolution_convert_fusion.7 = bf16[512,2048]{1,0:T(8,128)(2,1)} fusion(bf16[512,1408]{1,0:T(8,128)(2,1)S(1)} %get-tuple-element.105, bf16[1408,2048]{1,0:T(8,128)(2,1)} %param.27), kind=kOutput, calls=%fused_computation.9 | convolution fusion | flops 2953838592 | bytes 9306112 | tf_op jit(solution)/shard_map/dot_general | solution.py:304
  324.5 3.3 convolution_convert_fusion.2
  327.8 3.3 convolution_convert_fusion.5
  331.0 349.6 %back_pass.1 = (bf16[4,352,1024]{2,1,0:T(8,128)(2,1)}, bf16[4,256,1408]{2,1,0:T(8,128)(2,1)}, bf16[4,256,1408]{2,1,0:T(8,128)(2,1)}, bf16[2,256,1024]{2,1,0:T(8,...) custom-call(s32[5]{0:T(128)} %concatenate.135.at_ref, ...), custom_call_target="tpu_custom_call" | custom-call | flops 99999997952 | bytes 1000000000 | tf_op jit(solution)/shard_map/back_pass/pallas_call | solution.py:933
  681.7 2.3 slice.303.own_ref
  690.0 9.0 %join_columns.3 = f32[1408,2048]{1,0:T(8,128)} custom-call(s32[1]{0:T(128)} %bitcast.34.at_ref, bf16[1408,1024]{1,0:T(8,128)(2,1)} %bitcast.263, bf16[1408,1024]{1,0:T(8,128)(2,1)} %bitcast.264), custom_call_target="tpu_custom_call" | custom-call | tf_op jit(solution)/shard_map/join_columns/pallas_call | solution.py:223
  699.0 9.7 %join_rows.5 = f32[512,5632]{1,0:T(8,128)} custom-call(s32[2]{0:T(128)} %pad_add_fusion.idx_ref.at_ref, bf16[4,256,1408]{2,1,0:T(8,128)(2,1)} %get-tuple-element.67.own_ref, bf16[4,256,1408]{2,1,0:T(8,128)(2,1)} %get-tuple-element.68.sib_ref), custom_call_target="tpu_custom_call" | custom-call | tf_op jit(solution)/shard_map/join_rows/pallas_call | solution.py:201
  708.7 9.7 %join_rows.4 = f32[512,5632]{1,0:T(8,128)} custom-call(s32[2]{0:T(128)} %pad_add_fusion.idx_ref.at_ref, bf16[4,256,1408]{2,1,0:T(8,128)(2,1)} %get-tuple-element.65.own_ref, bf16[4,256,1408]{2,1,0:T(8,128)(2,1)} %get-tuple-element.66.sib_ref), custom_call_target="tpu_custom_call" | custom-call | tf_op jit(solution)/shard_map/join_rows/pallas_call | solution.py:201
  718.3 6.2 join_columns.2
  724.5 7.0 join_rows.3
  (221 shorter events, 71.3 us)
Async XLA Ops:
  0.6 7.4 %copy-start = (bf16[512,256]{1,0:T(8,128)(2,1)S(1)}, bf16[512,256]{1,0:T(8,128)(2,1)}, u32[]{:S(2)}) copy-start(bf16[512,256]{1,0:T(8,128)(2,1)} %param.21) | copy-start | bytes 786436
  3.5 42.9 %collective-permute-start = (bf16[4,512]{1,0:T(4,128)(2,1)}, bf16[4,512]{1,0:T(4,128)(2,1)S(1)}, u32[]{:S(2)}, u32[]{:S(2)}) collective-permute-start(bf16[4,512]{1,0:T(4,128)(2,1)} %maximum_maximum_fusion.1), channel_id=1, source_target_pairs={{0,8},{8,0},{16,24},{24,16},{1,9},{9,1},{17,25},{25,17},{2,10},{10... | collective-permute-start | bytes 12296 | tf_op jit(solution)/shard_map/ppermute | solution.py:29
  6.5 39.9 %collective-permute-start.1 = (bf16[4,512]{1,0:T(4,128)(2,1)}, bf16[4,512]{1,0:T(4,128)(2,1)S(1)}, u32[]{:S(2)}, u32[]{:S(2)}) collective-permute-start(bf16[4,512]{1,0:T(4,128)(2,1)} %maximum_maximum_fusion.1), channel_id=1, source_target_pairs={{0,16},{8,24},{16,0},{24,8},{1,17},{9,25},{17,1},{25,9},{2,18},{10... | collective-permute-start | bytes 12296 | tf_op jit(solution)/shard_map/ppermute | solution.py:29
  8.0 40.4 %collective-permute-start.2 = (bf16[4,512]{1,0:T(4,128)(2,1)}, bf16[4,512]{1,0:T(4,128)(2,1)}, u32[]{:S(2)}, u32[]{:S(2)}) collective-permute-start(bf16[4,512]{1,0:T(4,128)(2,1)} %maximum_maximum_fusion.1), channel_id=1, source_target_pairs={{0,24},{8,16},{16,8},{24,0},{1,25},{9,17},{17,9},{25,1},{2,26},{10... | collective-permute-start | bytes 12296 | tf_op jit(solution)/shard_map/ppermute | solution.py:29
  16.6 4.8 copy-start.2
  17.8 59.5 %collective-permute-start.7 = (bf16[256,640]{1,0:T(8,128)(2,1)}, bf16[256,640]{1,0:T(8,128)(2,1)S(1)}, u32[]{:S(2)}, u32[]{:S(2)}) collective-permute-start(bf16[256,640]{1,0:T(8,128)(2,1)} %get-tuple-element.122), channel_id=1, source_target_pairs={{0,8},{8,0},{16,24},{24,16},{1,9},{9,1},{17,25},{25,17},{2,10},{10... | collective-permute-start | bytes 983048 | tf_op jit(solution)/shard_map/ppermute | solution.py:29
  19.8 58.4 %collective-permute-start.8 = (bf16[256,640]{1,0:T(8,128)(2,1)}, bf16[256,640]{1,0:T(8,128)(2,1)S(1)}, u32[]{:S(2)}, u32[]{:S(2)}) collective-permute-start(bf16[256,640]{1,0:T(8,128)(2,1)} %get-tuple-element.121), channel_id=1, source_target_pairs={{0,16},{8,24},{16,0},{24,8},{1,17},{9,25},{17,1},{25,9},{2,18},{10... | collective-permute-start | bytes 983048 | tf_op jit(solution)/shard_map/ppermute | solution.py:29
  38.0 3.2 copy-start.19
  42.2 29.1 %copy-start.6 = (bf16[128,2048]{1,0:T(8,128)(2,1)}, bf16[128,2048]{1,0:T(8,128)(2,1)S(1)}, u32[]{:S(2)}) copy-start(bf16[128,2048]{1,0:T(8,128)(2,1)S(1)} %get-tuple-element.98.branch_own) | copy-start | bytes 1572868
  46.4 34.5 %collective-permute-start.9 = (bf16[256,640]{1,0:T(8,128)(2,1)}, bf16[256,640]{1,0:T(8,128)(2,1)}, u32[]{:S(2)}, u32[]{:S(2)}) collective-permute-start(bf16[256,640]{1,0:T(8,128)(2,1)} %get-tuple-element.120), channel_id=1, source_target_pairs={{0,24},{8,16},{16,8},{24,0},{1,25},{9,17},{17,9},{25,1},{2,26},{10... | collective-permute-start | bytes 983048 | tf_op jit(solution)/shard_map/ppermute | solution.py:29
  46.4 24.8 %collective-permute-start.4 = (bf16[1,64,2048]{2,1,0:T(8,128)(2,1)S(1)}, bf16[1,64,2048]{2,1,0:T(8,128)(2,1)}, u32[]{:S(2)}, u32[]{:S(2)}) collective-permute-start(bf16[1,64,2048]{2,1,0:T(8,128)(2,1)S(1)} %get-tuple-element.139), channel_id=1, source_target_pairs={{0,16},{8,24},{16,0},{24,8},{1,17},{9,25},{17,1},{25,9},{2,18},{10... | collective-permute-start | bytes 786440 | tf_op jit(solution)/shard_map/ppermute | solution.py:29
  48.4 12.0 %collective-permute-start.3 = (bf16[1,64,2048]{2,1,0:T(8,128)(2,1)}, bf16[1,64,2048]{2,1,0:T(8,128)(2,1)}, u32[]{:S(2)}, u32[]{:S(2)}) collective-permute-start(bf16[1,64,2048]{2,1,0:T(8,128)(2,1)} %get-tuple-element.140), channel_id=1, source_target_pairs={{0,8},{8,0},{16,24},{24,16},{1,9},{9,1},{17,25},{25,17},{2,10},{10... | collective-permute-start | bytes 786440 | tf_op jit(solution)/shard_map/ppermute | solution.py:29
  58.4 12.0 %copy-start.12 = (bf16[1,64,2048]{2,1,0:T(8,128)(2,1)S(1)}, bf16[1,64,2048]{2,1,0:T(8,128)(2,1)}, u32[]{:S(2)}) copy-start(bf16[1,64,2048]{2,1,0:T(8,128)(2,1)} %get-tuple-element.136) | copy-start | bytes 786436
  58.4 12.9 %copy-start.18 = (bf16[256,1408]{1,0:T(8,128)(2,1)S(1)}, bf16[256,1408]{1,0:T(8,128)(2,1)}, u32[]{:S(2)}) copy-start(bf16[256,1408]{1,0:T(8,128)(2,1)} %get-tuple-element.113) | copy-start | bytes 2162692
  60.4 15.4 %copy-start.17 = (bf16[256,1408]{1,0:T(8,128)(2,1)S(1)}, bf16[256,1408]{1,0:T(8,128)(2,1)}, u32[]{:S(2)}) copy-start(bf16[256,1408]{1,0:T(8,128)(2,1)} %get-tuple-element.112) | copy-start | bytes 2162692
  60.4 16.9 %copy-start.11 = (bf16[1,64,2048]{2,1,0:T(8,128)(2,1)S(1)}, bf16[1,64,2048]{2,1,0:T(8,128)(2,1)}, u32[]{:S(2)}) copy-start(bf16[1,64,2048]{2,1,0:T(8,128)(2,1)} %get-tuple-element.135) | copy-start | bytes 786436
  60.4 6.6 collective-permute-start.31
  67.0 8.8 %collective-permute-start.32 = (bf16[1,64,2048]{2,1,0:T(8,128)(2,1)}, bf16[1,64,2048]{2,1,0:T(8,128)(2,1)S(1)}, u32[]{:S(2)}, u32[]{:S(2)}) collective-permute-start(bf16[1,64,2048]{2,1,0:T(8,128)(2,1)} %get-tuple-element.135), channel_id=1, source_target_pairs={{0,16},{8,24},{16,0},{24,8},{1,17},{9,25},{17,1},{25,9},{2,18},{10... | collective-permute-start | bytes 786440 | tf_op jit(solution)/shard_map/ppermute | solution.py:29
  69.2 8.1 %copy-start.16 = (bf16[256,1408]{1,0:T(8,128)(2,1)S(1)}, bf16[256,1408]{1,0:T(8,128)(2,1)}, u32[]{:S(2)}) copy-start(bf16[256,1408]{1,0:T(8,128)(2,1)} %get-tuple-element.111) | copy-start | bytes 2162692
  70.4 7.8 %copy-start.15 = (bf16[256,1408]{1,0:T(8,128)(2,1)S(1)}, bf16[256,1408]{1,0:T(8,128)(2,1)}, u32[]{:S(2)}) copy-start(bf16[256,1408]{1,0:T(8,128)(2,1)} %get-tuple-element.109) | copy-start | bytes 2162692
  70.4 10.5 %copy-start.14 = (bf16[256,1408]{1,0:T(8,128)(2,1)S(1)}, bf16[256,1408]{1,0:T(8,128)(2,1)}, u32[]{:S(2)}) copy-start(bf16[256,1408]{1,0:T(8,128)(2,1)} %get-tuple-element.108) | copy-start | bytes 2162692
  70.4 20.0 %copy-start.13 = (bf16[256,1408]{1,0:T(8,128)(2,1)S(1)}, bf16[256,1408]{1,0:T(8,128)(2,1)}, u32[]{:S(2)}) copy-start(bf16[256,1408]{1,0:T(8,128)(2,1)} %get-tuple-element.107) | copy-start | bytes 2162692
  70.4 20.3 %copy-start.8 = (bf16[1,256,640]{2,1,0:T(8,128)(2,1)S(1)}, bf16[1,256,640]{2,1,0:T(8,128)(2,1)}, u32[]{:S(2)}) copy-start(bf16[1,256,640]{2,1,0:T(8,128)(2,1)} %get-tuple-element.118) | copy-start | bytes 983044
  71.3 19.1 %collective-permute-start.27 = (bf16[256,1408]{1,0:T(8,128)(2,1)S(1)}, bf16[256,1408]{1,0:T(8,128)(2,1)S(1)}, u32[]{:S(2)}, u32[]{:S(2)}) collective-permute-start(bf16[256,1408]{1,0:T(8,128)(2,1)S(1)} %copy-done.18), channel_id=1, source_target_pairs={{0,8},{8,0},{16,24},{24,16},{1,9},{9,1},{17,25},{25,17},{2,10},{10... | collective-permute-start | bytes 2162696 | tf_op jit(solution)/shard_map/ppermute | solution.py:29
  75.7 34.5 %collective-permute-start.28 = (bf16[256,1408]{1,0:T(8,128)(2,1)S(1)}, bf16[256,1408]{1,0:T(8,128)(2,1)S(1)}, u32[]{:S(2)}, u32[]{:S(2)}) collective-permute-start(bf16[256,1408]{1,0:T(8,128)(2,1)S(1)} %copy-done.17), channel_id=1, source_target_pairs={{0,16},{8,24},{16,0},{24,8},{1,17},{9,25},{17,1},{25,9},{2,18},{10... | collective-permute-start | bytes 2162696 | tf_op jit(solution)/shard_map/ppermute | solution.py:29
  77.3 33.0 %collective-permute-start.29 = (bf16[256,1408]{1,0:T(8,128)(2,1)S(1)}, bf16[256,1408]{1,0:T(8,128)(2,1)S(1)}, u32[]{:S(2)}, u32[]{:S(2)}) collective-permute-start(bf16[256,1408]{1,0:T(8,128)(2,1)S(1)} %copy-done.16), channel_id=1, source_target_pairs={{0,24},{8,16},{16,8},{24,0},{1,25},{9,17},{17,9},{25,1},{2,26},{10... | collective-permute-start | bytes 2162696 | tf_op jit(solution)/shard_map/ppermute | solution.py:29
  78.2 43.2 %collective-permute-start.23 = (bf16[256,1408]{1,0:T(8,128)(2,1)S(1)}, bf16[256,1408]{1,0:T(8,128)(2,1)S(1)}, u32[]{:S(2)}, u32[]{:S(2)}) collective-permute-start(bf16[256,1408]{1,0:T(8,128)(2,1)S(1)} %copy-done.15), channel_id=1, source_target_pairs={{0,8},{8,0},{16,24},{24,16},{1,9},{9,1},{17,25},{25,17},{2,10},{10... | collective-permute-start | bytes 2162696 | tf_op jit(solution)/shard_map/ppermute | solution.py:29
  80.9 11.0 %copy-start.21 = (bf16[8,256,640]{2,1,0:T(8,128)(2,1)S(1)}, bf16[8,256,640]{2,1,0:T(8,128)(2,1)}, u32[]{:S(2)}) copy-start(bf16[8,256,640]{2,1,0:T(8,128)(2,1)} %constant_dynamic-update-slice_fusion.2) | copy-start | bytes 7864324
  80.9 60.3 %collective-permute-start.24 = (bf16[256,1408]{1,0:T(8,128)(2,1)S(1)}, bf16[256,1408]{1,0:T(8,128)(2,1)S(1)}, u32[]{:S(2)}, u32[]{:S(2)}) collective-permute-start(bf16[256,1408]{1,0:T(8,128)(2,1)S(1)} %copy-done.14), channel_id=1, source_target_pairs={{0,16},{8,24},{16,0},{24,8},{1,17},{9,25},{17,1},{25,9},{2,18},{10... | collective-permute-start | bytes 2162696 | tf_op jit(solution)/shard_map/ppermute | solution.py:29
  90.4 52.3 %collective-permute-start.25 = (bf16[256,1408]{1,0:T(8,128)(2,1)S(1)}, bf16[256,1408]{1,0:T(8,128)(2,1)S(1)}, u32[]{:S(2)}, u32[]{:S(2)}) collective-permute-start(bf16[256,1408]{1,0:T(8,128)(2,1)S(1)} %copy-done.13), channel_id=1, source_target_pairs={{0,24},{8,16},{16,8},{24,0},{1,25},{9,17},{17,9},{25,1},{2,26},{10... | collective-permute-start | bytes 2162696 | tf_op jit(solution)/shard_map/ppermute | solution.py:29
  110.3 37.8 %collective-permute-start.5 = (bf16[2,64,2048]{2,1,0:T(8,128)(2,1)S(1)}, bf16[2,64,2048]{2,1,0:T(8,128)(2,1)S(1)}, u32[]{:S(2)}, u32[]{:S(2)}) collective-permute-start(bf16[2,64,2048]{2,1,0:T(8,128)(2,1)S(1)} %pad_maximum_fusion.4), channel_id=1, source_target_pairs={{0,8},{8,0},{16,24},{24,16},{1,9},{9,1},{17,25},{25,17},{2,10},{10... | collective-permute-start | bytes 1572872 | tf_op jit(solution)/shard_map/ppermute | solution.py:29
  110.3 41.9 %collective-permute-start.6 = (bf16[2,64,2048]{2,1,0:T(8,128)(2,1)S(1)}, bf16[2,64,2048]{2,1,0:T(8,128)(2,1)S(1)}, u32[]{:S(2)}, u32[]{:S(2)}) collective-permute-start(bf16[2,64,2048]{2,1,0:T(8,128)(2,1)S(1)} %pad_maximum_fusion.5), channel_id=1, source_target_pairs={{0,16},{8,24},{16,0},{24,8},{1,17},{9,25},{17,1},{25,9},{2,18},{10... | collective-permute-start | bytes 1572872 | tf_op jit(solution)/shard_map/ppermute | solution.py:29
  121.4 34.7 %collective-permute-start.33 = (bf16[2,64,2048]{2,1,0:T(8,128)(2,1)S(1)}, bf16[2,64,2048]{2,1,0:T(8,128)(2,1)S(1)}, u32[]{:S(2)}, u32[]{:S(2)}) collective-permute-start(bf16[2,64,2048]{2,1,0:T(8,128)(2,1)S(1)} %pad_maximum_fusion.10), channel_id=1, source_target_pairs={{0,8},{8,0},{16,24},{24,16},{1,9},{9,1},{17,25},{25,17},{2,10},{10... | collective-permute-start | bytes 1572872 | tf_op jit(solution)/shard_map/ppermute | solution.py:29
  141.2 26.8 %collective-permute-start.34 = (bf16[2,64,2048]{2,1,0:T(8,128)(2,1)}, bf16[2,64,2048]{2,1,0:T(8,128)(2,1)S(1)}, u32[]{:S(2)}, u32[]{:S(2)}) collective-permute-start(bf16[2,64,2048]{2,1,0:T(8,128)(2,1)} %pad_maximum_fusion.11), channel_id=1, source_target_pairs={{0,16},{8,24},{16,0},{24,8},{1,17},{9,25},{17,1},{25,9},{2,18},{10... | collective-permute-start | bytes 1572872 | tf_op jit(solution)/shard_map/ppermute | solution.py:29
  142.7 14.1 %collective-permute-start.10 = (bf16[4,256,640]{2,1,0:T(8,128)(2,1)S(1)}, bf16[4,256,640]{2,1,0:T(8,128)(2,1)S(1)}, u32[]{:S(2)}, u32[]{:S(2)}) collective-permute-start(bf16[4,256,640]{2,1,0:T(8,128)(2,1)S(1)} %pad_maximum_fusion.3), channel_id=1, source_target_pairs={{0,1},{1,0},{2,3},{3,2},{4,5},{5,4},{6,7},{7,6},{8,9},{9,8},{10,11... | collective-permute-start | bytes 3932168 | tf_op jit(solution)/shard_map/ppermute | solution.py:33
  148.1 115.2 %collective-permute-start.30 = (bf16[4,256,1408]{2,1,0:T(8,128)(2,1)S(1)}, bf16[4,256,1408]{2,1,0:T(8,128)(2,1)}, u32[]{:S(2)}, u32[]{:S(2)}) collective-permute-start(bf16[4,256,1408]{2,1,0:T(8,128)(2,1)S(1)} %pad_maximum_fusion.1), channel_id=1, source_target_pairs={{0,1},{1,0},{2,3},{3,2},{4,5},{5,4},{6,7},{7,6},{8,9},{9,8},{10,11... | collective-permute-start | bytes 8650760 | tf_op jit(solution)/shard_map/ppermute | solution.py:33
  152.2 115.2 %collective-permute-start.26 = (bf16[4,256,1408]{2,1,0:T(8,128)(2,1)}, bf16[4,256,1408]{2,1,0:T(8,128)(2,1)}, u32[]{:S(2)}, u32[]{:S(2)}) collective-permute-start(bf16[4,256,1408]{2,1,0:T(8,128)(2,1)} %pad_maximum_fusion), channel_id=1, source_target_pairs={{0,1},{1,0},{2,3},{3,2},{4,5},{5,4},{6,7},{7,6},{8,9},{9,8},{10,11... | collective-permute-start | bytes 8650760 | tf_op jit(solution)/shard_map/ppermute | solution.py:33
  157.0 1.5 copy-start.22
  165.4 8.0 %collective-permute-start.11 = (bf16[4,128,128]{2,1,0:T(8,128)(2,1)}, bf16[4,128,128]{2,1,0:T(8,128)(2,1)S(1)}, u32[]{:S(2)}, u32[]{:S(2)}) collective-permute-start(bf16[4,128,128]{2,1,0:T(8,128)(2,1)} %bitcast.289), channel_id=1, source_target_pairs={{2,0},{4,2},{6,4},{3,1},{5,3},{7,5},{10,8},{12,10},{14,12},{11,9},... | collective-permute-start | bytes 393224 | tf_op jit(solution)/shard_map/ppermute | solution.py:38
  166.6 16.2 %collective-permute-start.12 = (bf16[4,128,128]{2,1,0:T(8,128)(2,1)}, bf16[4,128,128]{2,1,0:T(8,128)(2,1)S(1)}, u32[]{:S(2)}, u32[]{:S(2)}) collective-permute-start(bf16[4,128,128]{2,1,0:T(8,128)(2,1)} %bitcast.290), channel_id=1, source_target_pairs={{4,0},{6,2},{5,1},{7,3},{12,8},{14,10},{13,9},{15,11},{20,16},{22,... | collective-permute-start | bytes 393224 | tf_op jit(solution)/shard_map/ppermute | solution.py:38
  168.0 14.8 %collective-permute-start.13 = (bf16[4,128,128]{2,1,0:T(8,128)(2,1)}, bf16[4,128,128]{2,1,0:T(8,128)(2,1)S(1)}, u32[]{:S(2)}, u32[]{:S(2)}) collective-permute-start(bf16[4,128,128]{2,1,0:T(8,128)(2,1)} %bitcast.291), channel_id=1, source_target_pairs={{6,0},{7,1},{14,8},{15,9},{22,16},{23,17},{30,24},{31,25}} | collective-permute-start | bytes 393224 | tf_op jit(solution)/shard_map/ppermute | solution.py:38
  183.8 2.0 collective-permute-start.14
  185.8 1.0 copy-start.23
  207.8 14.0 %collective-permute-start.15 = (bf16[2,64,2048]{2,1,0:T(8,128)(2,1)S(1)}, bf16[2,64,2048]{2,1,0:T(8,128)(2,1)S(1)}, u32[]{:S(2)}, u32[]{:S(2)}) collective-permute-start(bf16[2,64,2048]{2,1,0:T(8,128)(2,1)S(1)} %stack.300), channel_id=1, source_target_pairs={{0,16},{8,24},{16,0},{24,8},{1,17},{9,25},{17,1},{25,9},{2,18},{10... | collective-permute-start | bytes 1572872 | tf_op jit(solution)/shard_map/ppermute | solution.py:29
  209.5 13.8 %collective-permute-start.17 = (bf16[2,64,2048]{2,1,0:T(8,128)(2,1)S(1)}, bf16[2,64,2048]{2,1,0:T(8,128)(2,1)S(1)}, u32[]{:S(2)}, u32[]{:S(2)}) collective-permute-start(bf16[2,64,2048]{2,1,0:T(8,128)(2,1)S(1)} %pad_maximum_fusion.7), channel_id=1, source_target_pairs={{0,8},{8,0},{16,24},{24,16},{1,9},{9,1},{17,25},{25,17},{2,10},{10... | collective-permute-start | bytes 1572872 | tf_op jit(solution)/shard_map/ppermute | solution.py:29
  221.9 7.6 %collective-permute-start.16 = (bf16[1,64,2048]{2,1,0:T(8,128)(2,1)S(1)}, bf16[1,64,2048]{2,1,0:T(8,128)(2,1)S(1)}, u32[]{:S(2)}, u32[]{:S(2)}) collective-permute-start(bf16[1,64,2048]{2,1,0:T(8,128)(2,1)S(1)} %add_convert_fusion.3), channel_id=1, source_target_pairs={{0,8},{8,0},{16,24},{24,16},{1,9},{9,1},{17,25},{25,17},{2,10},{10... | collective-permute-start | bytes 786440 | tf_op jit(solution)/shard_map/ppermute | solution.py:29
  229.7 6.7 collective-permute-start.18
  236.7 7.2 copy-start.3
  236.9 9.3 %collective-permute-start.19 = (bf16[1,64,2048]{2,1,0:T(8,128)(2,1)S(1)}, bf16[1,64,2048]{2,1,0:T(8,128)(2,1)S(1)}, u32[]{:S(2)}, u32[]{:S(2)}) collective-permute-start(bf16[1,64,2048]{2,1,0:T(8,128)(2,1)S(1)} %get-tuple-element.138), channel_id=1, source_target_pairs={{0,8},{8,0},{16,24},{24,16},{1,9},{9,1},{17,25},{25,17},{2,10},{10... | collective-permute-start | bytes 786440 | tf_op jit(solution)/shard_map/ppermute | solution.py:29
  237.4 6.4 collective-permute-start.20
  243.9 10.7 %collective-permute-start.21 = (bf16[2,64,2048]{2,1,0:T(8,128)(2,1)S(1)}, bf16[2,64,2048]{2,1,0:T(8,128)(2,1)S(1)}, u32[]{:S(2)}, u32[]{:S(2)}) collective-permute-start(bf16[2,64,2048]{2,1,0:T(8,128)(2,1)S(1)} %pad_maximum_fusion.8), channel_id=1, source_target_pairs={{0,8},{8,0},{16,24},{24,16},{1,9},{9,1},{17,25},{25,17},{2,10},{10... | collective-permute-start | bytes 1572872 | tf_op jit(solution)/shard_map/ppermute | solution.py:29
  246.3 9.2 %collective-permute-start.22 = (bf16[2,64,2048]{2,1,0:T(8,128)(2,1)S(1)}, bf16[2,64,2048]{2,1,0:T(8,128)(2,1)S(1)}, u32[]{:S(2)}, u32[]{:S(2)}) collective-permute-start(bf16[2,64,2048]{2,1,0:T(8,128)(2,1)S(1)} %pad_maximum_fusion.9), channel_id=1, source_target_pairs={{0,16},{8,24},{16,0},{24,8},{1,17},{9,25},{17,1},{25,9},{2,18},{10... | collective-permute-start | bytes 1572872 | tf_op jit(solution)/shard_map/ppermute | solution.py:29
  255.6 1.3 copy-start.4
  263.3 4.1 copy-start.5
  271.0 5.7 slice-start
  272.8 3.8 slice-start.1
  272.8 3.8 copy-start.20
  291.5 3.4 copy-start.24
  680.6 3.4 copy-start.7
  724.5 7.0 copy-start.10
  731.5 1.6 copy-start.9
  731.5 2.6 copy-start.1

commit v4 on v3

--- a/solution.py
+++ b/solution.py
@@ -2,6 +2,7 @@
 
 import jax
 import jax.numpy as jnp
+import numpy as np
 from jax import lax
 from jax.experimental import pallas as pl
 from jax.experimental.pallas import tpu as pltpu
@@ -451,6 +452,812 @@
     )(at, q, do, lse, kv, kp, cosine, sine)
 
 
+def rms_backward(row_block, inverse, gain_vec, gradient):
+    normed = row_block * inverse
+    gain_grad = jnp.sum(gradient * normed, axis=0)
+    scaled = gradient * gain_vec
+    back = inverse * (scaled - normed * jnp.mean(scaled * normed, axis=1, keepdims=True))
+    return (back, gain_grad)
+
+
+def body_plain(
+    tokens, cotangent, lengths, attn_gain, w_query, w_key, w_value, w_out, mlp_gain, w_gate, w_up, w_down
+):
+    seqs, rows, depth = tokens.shape
+    count, line = lax.axis_size("fsdp"), lax.axis_size("z")
+    f, z, k = lax.axis_index("fsdp"), lax.axis_index("z"), lax.axis_index("core")
+    slot = rows * line * 2
+    total = count * rows
+    slab = depth // count
+    half = slab // 2
+    q_width = HEADS * HEAD_DIM // count
+    shared = max(1, count // KV_HEADS)
+
+    x_own = tokens.reshape(rows, depth)
+    chunk = 2 * z + k
+    first_pos = slot - 1 - chunk * rows
+
+    length = lengths[0]
+    words = jnp.zeros((slab,), F32).at[0].set((length // 64).astype(F32)).at[1].set((length % 64).astype(F32))
+    note = jnp.stack([attn_gain, mlp_gain, words.astype(BF), jnp.zeros((slab,), BF)])
+    notes = [note] + [along_plane(note, j) for j in range(1, count)]
+    notes_abs = [lax.dynamic_index_in_dim(jnp.stack(notes), f ^ i, 0, keepdims=False) for i in range(count)]
+    gain_one = jnp.concatenate([n[0] for n in notes_abs]).astype(F32).reshape(1, depth)
+    gain_two = jnp.concatenate([n[1] for n in notes_abs]).astype(F32).reshape(1, depth)
+    all_lengths = jnp.stack(
+        [n[2, 0].astype(jnp.int32) * 64 + n[2, 1].astype(jnp.int32) for n in notes]
+    )
+
+    x_all = jnp.concatenate(plane_gather(x_own))
+
+    wq = cut_blocks(w_query, f, k, count)
+    key_cols = lax.dynamic_slice_in_dim(w_key, k * half, half, 0).reshape(half, KV_HEADS, HEAD_DIM)
+    value_cols = lax.dynamic_slice_in_dim(w_value, k * half, half, 0).reshape(half, KV_HEADS, HEAD_DIM)
+
+    def head_of(j):
+        return (f ^ j) // shared
+
+    wkv = jnp.stack(
+        [
+            jnp.concatenate(
+                [
+                    lax.dynamic_index_in_dim(key_cols, head_of(j), 1, keepdims=False),
+                    lax.dynamic_index_in_dim(value_cols, head_of(j), 1, keepdims=False),
+                ],
+                axis=1,
+            )
+            for j in range(count)
+        ]
+    )
+    wqkv = jnp.concatenate([wq, wkv], axis=2)
+    wqkv_own = jnp.stack([wqkv[0]] + [along_plane(wqkv[j], j) for j in range(1, count)])
+    wqkv_sib = to_sibling(wqkv_own)
+    wqkv_all = jnp.concatenate([wqkv_own, wqkv_sib]).reshape(depth, q_width + 128)
+
+    def fetch(weight):
+        cut = cut_blocks(weight, f, k, count)
+        width = cut.shape[2]
+        own = jnp.stack([cut[0]] + [along_plane(cut[j], j) for j in range(1, count)])
+        sib = to_sibling(own)
+        return own.reshape(depth // 2, width), sib.reshape(depth // 2, width)
+
+    gate_own, gate_sib = fetch(w_gate)
+    up_own, up_sib = fetch(w_up)
+
+    order = jnp.stack([(f ^ j) * 2 + (k ^ h) for h in range(2) for j in range(count)]).astype(jnp.int32)
+
+    half_dim = HEAD_DIM // 2
+    frequency = jnp.power(ROPE_BASE, jnp.arange(half_dim, dtype=F32) * (-2.0 / HEAD_DIM))
+    positions = first_pos - jnp.arange(rows, dtype=jnp.int32)
+    angles = positions.astype(F32)[:, None] * frequency[None, :]
+    cos32, sin32 = jnp.cos(angles), jnp.sin(angles)
+    cosine = jnp.concatenate([cos32] * 4, axis=1)
+    sine = jnp.concatenate([-sin32, sin32, -sin32, sin32], axis=1)
+
+    normed_one, queries, kv = qkv_project(order, x_all, gain_one, wqkv_all, cosine, sine, rows)
+    queries = queries.reshape(count, rows, q_width)
+    kv = kv.reshape(count, rows, 128)
+
+    mine = [kv] + [along_line(kv, -s) for s in range(1, line)]
+    mine = jnp.stack(mine)
+    kv_all = jnp.concatenate([mine, to_sibling(mine)])
+    places = []
+    for h in range(2):
+        for s in range(line):
+            start = slot - 1 - (2 * (z + s) + (k ^ h)) * rows
+            places.append(start - jnp.arange(rows, dtype=jnp.int32))
+    kp = jnp.concatenate(places)
+    kp = jnp.where(kp < 0, FAR, kp).reshape(1, -1)
+    at = jnp.concatenate([first_pos.reshape(1), all_lengths]).astype(jnp.int32)
+
+    attended, log_total = attend(at, queries, kv_all, kp)
+    attended = attended.reshape(total, q_width)
+
+    mixed_part = nn(attended, w_out).astype(BF).reshape(count, rows, depth)
+    inputs = x_own.astype(F32)
+    mixed = inputs + plane_reduce(mixed_part)
+    inv_two = lax.rsqrt(jnp.mean(mixed * mixed, axis=1, keepdims=True) + EPSILON)
+    normed_two_own = (mixed * inv_two * gain_two).astype(BF)
+    normed_two = jnp.concatenate(plane_gather(normed_two_own))
+    normed_two = pick_columns(normed_two, order, 2 * count)
+    n2_own, n2_sib = normed_two[:, : depth // 2], normed_two[:, depth // 2 :]
+
+    valid = (positions < length).astype(F32)[:, None]
+    out_back = cotangent.reshape(rows, depth).astype(F32) * valid
+    branch_own = out_back.astype(BF)
+    branch = jnp.concatenate(plane_gather(branch_own))
+
+    gate = nn(n2_own, gate_own) + nn(n2_sib, gate_sib)
+    up = nn(n2_own, up_own) + nn(n2_sib, up_sib)
+    sigmoid = jax.nn.sigmoid(gate)
+    hidden = (gate * sigmoid * up).astype(BF)
+
+    half_depth = depth // 2
+    branch_mine = lax.dynamic_slice_in_dim(branch, k * half_depth, half_depth, 1)
+    branch_other = lax.dynamic_slice_in_dim(branch, (1 - k) * half_depth, half_depth, 1)
+
+    def pair_sum(own, other):
+        return (own + to_sibling(other.astype(BF)).astype(F32)).astype(BF)
+
+    def swap_slabs(own):
+        return jnp.stack([own[0]] + [along_plane(own[j], j) for j in range(1, count)])
+
+    down_half = line_sum(pair_sum(tn(hidden, branch_mine), tn(hidden, branch_other)))
+    down_grad = join_columns(down_half, to_sibling(down_half), k)
+
+    hidden_grad = nt(branch, w_down)
+    gate_back = (hidden_grad * up * sigmoid * (1.0 + gate * (1.0 - sigmoid))).astype(BF)
+    up_back = (hidden_grad * gate * sigmoid).astype(BF)
+
+    def slab_grad(left_own, left_other, right):
+        width = right.shape[1]
+        own = pair_sum(tn(left_own, right), tn(left_other, right)).reshape(count, half, width)
+        return line_sum(swap_slabs(own))
+
+    gate_half = slab_grad(n2_own, n2_sib, gate_back)
+    gate_grad = join_rows(gate_half, to_sibling(gate_half), f, k)
+    up_half = slab_grad(n2_own, n2_sib, up_back)
+    up_grad = join_rows(up_half, to_sibling(up_half), f, k)
+
+    back_own = (nt(gate_back, gate_own) + nt(up_back, up_own)).astype(BF)
+    back_sib = (nt(gate_back, gate_sib) + nt(up_back, up_sib)).astype(BF)
+    normed_back = put_columns(jnp.concatenate([back_own, back_sib], axis=1), order, 2 * count)
+    normed_back = plane_reduce(normed_back.reshape(count, rows, depth))
+
+    out_part = nn(hidden, w_down).astype(BF).reshape(count, rows, depth)
+    outputs = mixed + plane_reduce(out_part)
+
+    mixed_back, gain_two_grad = rms_backward(mixed, inv_two, gain_two, normed_back)
+    mixed_grad = out_back + mixed_back
+    attn_back = jnp.concatenate(plane_gather(mixed_grad.astype(BF)))
+    attended_grad = nt(attn_back, w_out).astype(BF).reshape(count, rows, q_width)
+
+    back_mine = lax.dynamic_slice_in_dim(attn_back, k * half_depth, half_depth, 1)
+    back_other = lax.dynamic_slice_in_dim(attn_back, (1 - k) * half_depth, half_depth, 1)
+    out_half = line_sum(pair_sum(tn(attended, back_mine), tn(attended, back_other)))
+    out_grad = join_columns(out_half, to_sibling(out_half), k)
+
+    query_back, kv_part = attend_back(at, queries, attended_grad, log_total, kv_all, kp, cosine, sine)
+    kv_mine = kv_part[:line].astype(F32) + to_sibling(kv_part[line:]).astype(F32)
+    kv_back = kv_mine[0]
+    for s in range(1, line):
+        kv_back = kv_back + along_line(kv_mine[s].astype(BF), s).astype(F32)
+    lead, trail, flat = kv_back[..., :32], kv_back[..., 32:64], kv_back[..., 64:]
+    kv_back = jnp.concatenate(
+        [lead * cos32 + trail * sin32, trail * cos32 - lead * sin32, flat], axis=-1
+    ).astype(BF)
+    qkv_back = jnp.concatenate(
+        [query_back.reshape(total, q_width), kv_back.reshape(total, 128)], axis=1
+    )
+
+    normed_one_back = nt(qkv_back, wqkv_all).astype(BF)
+    normed_one_back = put_columns(normed_one_back, order, 2 * count)
+    normed_one_back = plane_reduce(normed_one_back.reshape(count, rows, depth))
+    inv_one = lax.rsqrt(jnp.mean(inputs * inputs, axis=1, keepdims=True) + EPSILON)
+    input_back, gain_one_grad = rms_backward(inputs, inv_one, gain_one, normed_one_back)
+    input_grad = mixed_grad + input_back
+
+    n1_own, n1_sib = normed_one[:, :half_depth], normed_one[:, half_depth:]
+    qkv_own = pair_sum(tn(n1_own, qkv_back), tn(n1_sib, qkv_back)).reshape(count, half, q_width + 128)
+    gains = jnp.stack([gain_one_grad, gain_two_grad]).reshape(2, count, slab)
+    gains = jnp.stack(
+        [lax.dynamic_index_in_dim(gains, f ^ j, 1, keepdims=False) for j in range(count)]
+    ).astype(BF)
+    gains = line_sum(swap_slabs(gains))
+    qkv_half = line_sum(swap_slabs(qkv_own))
+    gains = jnp.sum(gains.astype(F32), axis=0) + jnp.sum(to_sibling(gains).astype(F32), axis=0)
+    qkv_other = to_sibling(qkv_half)
+    query_grad = join_rows(qkv_half[:, :, :q_width], qkv_other[:, :, :q_width], f, k)
+    halves = jnp.stack([qkv_half[:, :, q_width:], qkv_other[:, :, q_width:]])
+
+    def by_head(lo, hi):
+        both = [lax.dynamic_index_in_dim(halves, k ^ h, 0, keepdims=False) for h in range(2)]
+        both = jnp.concatenate(both, axis=1).astype(F32)[:, :, lo:hi]
+        cols = jnp.stack([lax.dynamic_index_in_dim(both, f ^ i, 0, keepdims=False) for i in range(count)])
+        cols = cols.reshape(KV_HEADS, shared, slab, HEAD_DIM).sum(1)
+        return jnp.transpose(cols, (1, 0, 2)).reshape(slab, KV_HEADS * HEAD_DIM)
+
+    key_grad = by_head(0, 64)
+    value_grad = by_head(64, 128)
+
+    return (
+        outputs.reshape(seqs, rows, depth),
+        input_grad.reshape(seqs, rows, depth),
+        gains[0],
+        query_grad,
+        key_grad,
+        value_grad,
+        out_grad,
+        gains[1],
+        gate_grad,
+        up_grad,
+        down_grad,
+    )
+
+
+def rotary_parts(slot, rows):
+    lane = np.arange(128) % (HEAD_DIM // 2)
+    frequency = ROPE_BASE ** (lane * (-2.0 / HEAD_DIM))
+    starts = (slot - 1 - rows * np.arange(slot // rows))[:, None] * frequency[None, :]
+    steps = np.arange(rows)[:, None] * frequency[None, :]
+    return [jnp.asarray(t(a), F32) for a in (starts, steps) for t in (np.cos, np.sin)]
+
+
+def front_kernel(
+    length_ref, attn_gain, mlp_gain, start_cos, start_sin, step_cos, step_sin,
+    tokens, cotangent, w_query, w_key, w_value, w_out, w_gate, w_up, w_down,
+    h1, queries, lse, attended, mixed, n2, hidden, gate_back, up_back, back_part, out_part,
+    gain_one, gain_two, limits, cosine, sine, kp,
+    kv_out, branch_out, wqkv_out,
+    notes, x_all, wqkv, keys_in, values_in, kv_give, gate_own, gate_sib, up_own, up_sib, down,
+    kv_all, vk, w_o, part, landed, relay, relayed, n2_all, branch_all, cot_in,
+    local_s, note_s, note_r, tok_s, tok_r, tof_s, tof_r, wq_s, wq_r, wk_s, wk_r, wp_s, wp_r, wkp_s, wkp_r,
+    kz_s, kz_r, kp_s, kp_r, gt_s, gt_r, up_s, up_r, gz_s, gz_r, gs_s, gs_r, us_s, us_r,
+    bt_s, bt_r, btf_s, btf_r, mx_s, mx_r, nt_s, nt_r, ntf_s, ntf_r,
+):
+    f, z, k = lax.axis_index("fsdp"), lax.axis_index("z"), lax.axis_index("core")
+    plane, line = 4, 4
+    rows, depth = tokens.shape
+    total = plane * rows
+    slab = depth // plane
+    half = slab // 2
+    hr = rows // 2
+    q_width = w_out.shape[0]
+    pairs = q_width // 128
+    ff = w_down.shape[0]
+    keys = vk.shape[0]
+    slot = rows * line * 2
+    even = z % 2 == 0
+    across = z + 1 - 2 * (z % 2)
+    peers = (1, 2, 3)
+    first_pos = slot - 1 - (2 * z + k) * rows
+
+    def remote(source, target, send, recv, where):
+        return pltpu.make_async_remote_copy(
+            src_ref=source,
+            dst_ref=target,
+            send_sem=send,
+            recv_sem=recv,
+            device_id=where,
+            device_id_type=pl.DeviceIdType.MESH,
+        )
+
+    sib = {"core": 1 - k}
+
+    def chip(j):
+        return {"fsdp": f ^ j}
+
+    def cols(weight, j, side, width):
+        start = pl.multiple_of((f ^ j) * width, 128)
+        return weight.at[pl.ds(pl.multiple_of((k ^ side) * half, 16), half), pl.ds(start, width)]
+
+    class Gather:
+        def __init__(self, source, target, send, recv, fsend, frecv):
+            self.near = {
+                j: remote(source, target.at[j], send.at[j - 1], recv.at[j - 1], chip(j)) for j in (1, 2)
+            }
+            self.far = {
+                j: remote(
+                    target.at[j, pl.ds((j - 1) * hr, hr), :],
+                    target.at[3, pl.ds((j - 1) * hr, hr), :],
+                    fsend.at[j - 1],
+                    frecv.at[j - 1],
+                    chip(3 - j),
+                )
+                for j in (1, 2)
+            }
+
+        def start(self):
+            for j in (1, 2):
+                self.near[j].start()
+
+        def forward(self):
+            for j in (1, 2):
+                self.near[j].wait_recv()
+                self.far[j].start()
+
+        def arrive(self):
+            for j in (1, 2):
+                self.far[j].wait_recv()
+
+        def close(self):
+            for j in (1, 2):
+                self.near[j].wait_send()
+                self.far[j].wait_send()
+
+    def note_send(j):
+        return remote(notes.at[0], notes.at[j], note_s.at[j - 1], note_r.at[j - 1], chip(j))
+
+    token_gather = Gather(tokens, x_all, tok_s, tok_r, tof_s, tof_r)
+    branch_gather = Gather(branch_all.at[0], branch_all, bt_s, bt_r, btf_s, btf_r)
+    n2_gather = Gather(n2_all.at[0], n2_all, nt_s, nt_r, ntf_s, ntf_r)
+
+    def wq_send(j):
+        target = wqkv.at[pl.ds(j * half, half), pl.ds(0, q_width)]
+        return remote(cols(w_query, j, 0, q_width), target, wq_s.at[j - 1], wq_r.at[j - 1], chip(j))
+
+    def wk_send(j):
+        target = wqkv.at[pl.ds(j * half, half), pl.ds(q_width, 128)]
+        return remote(kv_give.at[j], target, wk_s.at[j - 1], wk_r.at[j - 1], chip(j))
+
+    def wp_send(j):
+        source = wqkv.at[pl.ds(j * half, half), :]
+        target = wqkv.at[pl.ds((plane + j) * half, half), :]
+        return remote(source, target, wp_s.at[j - 1], wp_r.at[j - 1], sib)
+
+    def kv_send(s):
+        return remote(kv_all.at[0], kv_all.at[s], kz_s.at[s - 1], kz_r.at[s - 1], {"z": z - s})
+
+    def kv_pair(s):
+        return remote(kv_all.at[s], kv_all.at[line + s], kp_s.at[s], kp_r.at[s], sib)
+
+    def gate_send(j):
+        return remote(cols(w_gate, j, 0, ff), gate_own.at[j], gt_s.at[j - 1], gt_r.at[j - 1], chip(j))
+
+    def up_send(j):
+        return remote(cols(w_up, j, 0, ff), up_own.at[j], up_s.at[j - 1], up_r.at[j - 1], chip(j))
+
+    gate_across = remote(gate_own.at[3], gate_own.at[3], gz_s.at[0], gz_r.at[0], {"z": across})
+    up_across = remote(up_own.at[3], up_own.at[3], gz_s.at[0], gz_r.at[0], {"z": across})
+
+    def gate_pair(j):
+        return remote(gate_own.at[j], gate_sib.at[j], gs_s.at[j - 1], gs_r.at[j - 1], sib)
+
+    def up_pair(j):
+        return remote(up_own.at[j], up_sib.at[j], us_s.at[j - 1], us_r.at[j - 1], sib)
+
+    def span(which):
+        return pl.ds(which * hr, hr)
+
+    mix_first = {
+        "one": remote(part.at[1, span(0), :], landed.at[0, span(0), :], mx_s.at[0], mx_r.at[0], chip(1)),
+        "two": remote(part.at[2, span(1), :], landed.at[1, span(1), :], mx_s.at[1], mx_r.at[1], chip(2)),
+        "far_one": remote(part.at[3, span(0), :], relay.at[0], mx_s.at[2], mx_r.at[2], chip(1)),
+        "far_two": remote(part.at[3, span(1), :], relay.at[1], mx_s.at[3], mx_r.at[3], chip(2)),
+        "late_two": remote(relayed.at[0], landed.at[1, span(0), :], mx_s.at[4], mx_r.at[4], chip(2)),
+        "late_one": remote(relayed.at[1], landed.at[0, span(1), :], mx_s.at[5], mx_r.at[5], chip(1)),
+    }
+
+    local = [
+        pltpu.make_async_copy(source, target, local_s.at[n])
+        for n, (source, target) in enumerate(
+            [
+                (tokens, x_all.at[0]),
+                (w_key, keys_in),
+                (w_value, values_in),
+                (cols(w_query, 0, 0, q_width), wqkv.at[pl.ds(0, half), pl.ds(0, q_width)]),
+                (cols(w_query, 0, 1, q_width), wqkv.at[pl.ds(plane * half, half), pl.ds(0, q_width)]),
+                (cotangent, cot_in),
+                (w_out, w_o),
+                (cols(w_gate, 0, 0, ff), gate_own.at[0]),
+                (cols(w_gate, 0, 1, ff), gate_sib.at[0]),
+                (cols(w_up, 0, 0, ff), up_own.at[0]),
+                (cols(w_up, 0, 1, ff), up_sib.at[0]),
+                (w_down, down),
+            ]
+        )
+    ]
+
+    length = length_ref[0]
+    place = lax.broadcasted_iota(jnp.int32, (16, slab), 0)
+    high, low = (length // 64).astype(F32), (length % 64).astype(F32)
+    note = jnp.where(place == 0, attn_gain[...].astype(F32), mlp_gain[...].astype(F32))
+    note = jnp.where(place == 2, high, jnp.where(place == 3, low, note))
+    notes[0] = note.astype(BF)
+    for j in peers:
+        note_send(j).start()
+    token_gather.start()
+    for j in (3, 1, 2):
+        wq_send(j).start()
+    for copy in local:
+        copy.start()
+
+    local[1].wait()
+    local[2].wait()
+
+    def head_columns(j, side):
+        at = pl.ds(pl.multiple_of((k ^ side) * half, 16), half)
+        head = f ^ j
+        width = KV_HEADS * HEAD_DIM
+        key = pltpu.roll(keys_in[at, :].astype(F32), (width - head * 64) % width, 1)[:, :128]
+        value = pltpu.roll(values_in[at, :].astype(F32), (width - head * 64 + 64) % width, 1)[:, :128]
+        lane = lax.broadcasted_iota(jnp.int32, key.shape, 1)
+        return jnp.where(lane < 64, key, value).astype(BF)
+
+    for j in (3, 1, 2):
+        kv_give[j] = head_columns(j, 0)
+        wk_send(j).start()
+    wqkv[0:half, q_width : q_width + 128] = head_columns(0, 0)
+    wqkv[plane * half : (plane + 1) * half, q_width : q_width + 128] = head_columns(0, 1)
+
+    chunk = pl.ds(2 * z + k, 1)
+    cos_at, sin_at = start_cos[chunk, :], start_sin[chunk, :]
+    lane = lax.broadcasted_iota(jnp.int32, (rows, 128), 1)
+    cosine[...] = cos_at * step_cos[...] + sin_at * step_sin[...]
+    turn = sin_at * step_cos[...] - cos_at * step_sin[...]
+    sine[...] = jnp.where(lane % 64 < 32, -turn, turn)
+    for h in range(2):
+        for s in range(line):
+            start = slot - 1 - (2 * (z + s) + (k ^ h)) * rows
+            spot = start - lax.broadcasted_iota(jnp.int32, (8, rows), 1)
+            spot = jnp.where(spot < 0, FAR, spot).astype(F32)
+            kp[:, (h * line + s) * rows : (h * line + s + 1) * rows] = spot
+
+    for s in range(1, line):
+
+        @pl.when(z + s >= line)
+        def _():
+            kv_all[s] = jnp.zeros(kv_all.shape[1:], BF)
+            kv_all[line + s] = jnp.zeros(kv_all.shape[1:], BF)
+
+    local[5].wait()
+    row_pos = (first_pos - lax.broadcasted_iota(jnp.int32, (rows, 1), 0)).astype(F32)
+    valid = row_pos < jnp.full((rows, 1), length.astype(F32))
+    branch_all[0] = jnp.where(valid, cot_in[...].astype(F32), 0.0).astype(BF)
+
+    token_gather.forward()
+    for j in (1, 2, 3):
+        wq_send(j).wait_recv()
+        wk_send(j).wait_recv()
+        wp_send(j).start()
+
+    @pl.when(even)
+    def _():
+        gate_send(3).start()
+
+    @pl.when(jnp.logical_not(even))
+    def _():
+        up_send(3).start()
+
+    for j in (1, 2):
+        gate_send(j).start()
+    for j in (1, 2):
+        up_send(j).start()
+
+    for j in peers:
+        note_send(j).wait_recv()
+    for j in range(plane):
+        at = pl.ds(pl.multiple_of((f ^ j) * slab, 128), slab)
+        gain_one[:, at] = jnp.broadcast_to(notes[j, 0:1, :].astype(F32), (8, slab))
+        gain_two[:, at] = jnp.broadcast_to(notes[j, 1:2, :].astype(F32), (8, slab))
+        theirs = notes[j, 2:3, 0:1].astype(F32) * 64.0 + notes[j, 3:4, 0:1].astype(F32)
+        limits[j] = jnp.broadcast_to(jnp.minimum(row_pos, theirs - 1.0), (rows, 128))
+
+    def normalize(j, x_ref):
+        @pl.loop(0, rows // 16)
+        def _(i):
+            at = pl.ds(pl.multiple_of(i * 16, 16), 16)
+            x = x_ref[at, :].astype(F32)
+            inverse = lax.rsqrt(jnp.mean(x * x, axis=1, keepdims=True) + EPSILON)
+            to = pl.ds(pl.multiple_of(j * rows + i * 16, 16), 16)
+            for h in range(2):
+                for b in range(plane):
+                    from_ = pl.ds(pl.multiple_of(((f ^ b) * 2 + (k ^ h)) * half, 128), half)
+                    value = x_ref[at, from_].astype(F32) * inverse * gain_one[0:1, from_]
+                    c = (h * plane + b) * half
+                    h1[to, c : c + half] = value.astype(BF)
+
+    local[0].wait()
+    normalize(0, x_all.at[0])
+    normalize(1, x_all.at[1])
+    normalize(2, x_all.at[2])
+    token_gather.arrive()
+    normalize(3, x_all.at[3])
+    local[3].wait()
+    local[4].wait()
+    for j in (1, 2, 3):
+        wp_send(j).wait_recv()
+
+    kv_cols = nn(h1[...], wqkv[:, q_width : q_width + 128])
+    for j in range(plane):
+        value = kv_cols[j * rows : (j + 1) * rows]
+        turned = value * cosine[...] + swap_halves(value) * sine[...]
+        kv_all[0, j] = jnp.where(lane < 64, turned, value).astype(BF)
+    for s in range(1, line):
+
+        @pl.when(z >= s)
+        def _():
+            kv_send(s).start()
+
+    kv_pair(0).start()
+    branch_gather.start()
+
+    @pl.loop(0, pairs // 2)
+    def _(p):
+        at = pl.ds(pl.multiple_of(p * 256, 256), 256)
+        out = nn(h1[...], wqkv[:, at])
+        for j in range(plane):
+            for c in range(2):
+                value = out[j * rows : (j + 1) * rows, c * 128 : (c + 1) * 128]
+                turned = value * cosine[...] + swap_halves(value) * sine[...]
+                queries[j, :, pl.ds(pl.multiple_of(p * 256 + c * 128, 128), 128)] = turned.astype(BF)
+
+    for s in range(1, line):
+
+        @pl.when(z + s < line)
+        def _():
+            kv_send(s).wait_recv()
+            kv_pair(s).start()
+
+    @pl.when(even)
+    def _():
+        gate_send(3).wait_recv()
+        gate_across.start()
+
+    @pl.when(jnp.logical_not(even))
+    def _():
+        up_send(3).wait_recv()
+        up_across.start()
+
+    kv_pair(0).wait_recv()
+    for s in range(1, line):
+
+        @pl.when(z + s < line)
+        def _():
+            kv_pair(s).wait_recv()
+
+    local[6].wait()
+
+    def attend_block(j):
+        vk[...] = pltpu.roll(kv_all[:, j].reshape(keys, 128).astype(F32), 64, 1).astype(BF)
+        limit = limits[j, :, 0:1]
+
+        @pl.loop(0, pairs)
+        def _(p):
+            at = pl.ds(pl.multiple_of(p * 128, 128), 128)
+            allowed = kp[0:1, :] <= limit
+            q = queries[j, :, at]
+            zero = jnp.zeros_like(q)
+            outs, logs = [], []
+            for first in (True, False):
+                mine = lane < 64 if first else lane >= 64
+                kv = kv_all[:, j].reshape(keys, 128)
+                keyed, valued = (kv, vk[...]) if first else (vk[...], kv)
+                scores = nt(jnp.where(mine, q, zero), keyed) * (HEAD_DIM**-0.5)
+                scores = jnp.where(allowed, scores, MASKED)
+                top = jnp.max(scores, axis=1, keepdims=True)
+                weights = jnp.exp(scores - top)
+                sums = jnp.sum(weights, axis=1, keepdims=True)
+                outs.append(nn(weights.astype(BF), valued) / sums)
+                logs.append(jnp.broadcast_to(top + jnp.log(sums), (rows, 128)))
+            attended[j * rows : (j + 1) * rows, at] = jnp.where(lane < 64, outs[0], outs[1]).astype(BF)
+            lse[j, :, at] = jnp.where(lane < 64, logs[0], logs[1])
+
+        part[j] = nn(attended[j * rows : (j + 1) * rows, :], w_o[...]).astype(BF)
+
+    attend_block(3)
+    mix_first["far_one"].start()
+    mix_first["far_two"].start()
+    branch_gather.forward()
+    attend_block(1)
+    mix_first["one"].start()
+    attend_block(2)
+    mix_first["two"].start()
+
+    def relay_on(far, late, which, j):
+        mix_first[far].wait_recv()
+        value = relay[which].astype(F32) + part[j, which * hr : (which + 1) * hr, :].astype(F32)
+        relayed[which] = value.astype(BF)
+        mix_first[late].start()
+
+    relay_on("far_one", "late_two", 0, 2)
+    relay_on("far_two", "late_one", 1, 1)
+    attend_block(0)
+    for name in ("one", "late_one", "two", "late_two"):
+        mix_first[name].wait_recv()
+
+    @pl.loop(0, rows // 16)
+    def _(i):
+        at = pl.ds(pl.multiple_of(i * 16, 16), 16)
+        value = x_all[0, at, :].astype(F32) + part[0, at, :].astype(F32)
+        value = value + landed[0, at, :].astype(F32) + landed[1, at, :].astype(F32)
+        mixed[at, :] = value
+        inverse = lax.rsqrt(jnp.mean(value * value, axis=1, keepdims=True) + EPSILON)
+        n2_all[0, at, :] = (value * inverse * gain_two[0:1, :]).astype(BF)
+
+    n2_gather.start()
+
+    for j in (1, 2):
+        gate_send(j).wait_recv()
+        gate_pair(j).start()
+    n2_gather.forward()
+    for j in (1, 2):
+        up_send(j).wait_recv()
+        up_pair(j).start()
+
+    @pl.when(even)
+    def _():
+        up_across.wait_recv()
+
+    @pl.when(jnp.logical_not(even))
+    def _():
+        gate_across.wait_recv()
+
+    gate_pair(3).start()
+    up_pair(3).start()
+    branch_gather.arrive()
+    n2_gather.arrive()
+
+    @pl.loop(0, total // 16)
+    def _(i):
+        at = pl.ds(pl.multiple_of(i * 16, 16), 16)
+        j = i // (rows // 16)
+        from_row = pl.ds(pl.multiple_of((i % (rows // 16)) * 16, 16), 16)
+        for h in range(2):
+            for b in range(plane):
+                from_ = pl.ds(pl.multiple_of(((f ^ b) * 2 + (k ^ h)) * half, 128), half)
+                c = (h * plane + b) * half
+                n2[at, c : c + half] = n2_all[j, from_row, from_]
+
+    for n in range(7, 12):
+        local[n].wait()
+    for j in peers:
+        gate_pair(j).wait_recv()
+        up_pair(j).wait_recv()
+
+    def feed(at):
+        width = at.size
+        n2_own, n2_sib = n2[:, 0 : depth // 2], n2[:, depth // 2 : depth]
+
+        def through(own, other):
+            first = nn(n2_own, own[:, :, at].reshape(depth // 2, width))
+            return first + nn(n2_sib, other[:, :, at].reshape(depth // 2, width))
+
+        gate = through(gate_own, gate_sib)
+        up = through(up_own, up_sib)
+        sigmoid = 1.0 / (1.0 + jnp.exp(-gate))
+        hidden[:, at] = (gate * sigmoid * up).astype(BF)
+        grad = nt(branch_all[...].reshape(total, depth), down[at, :])
+        gate_back[:, at] = (grad * up * sigmoid * (1.0 + gate * (1.0 - sigmoid))).astype(BF)
+        up_back[:, at] = (grad * gate * sigmoid).astype(BF)
+
+    @pl.loop(0, ff // 256)
+    def _(n):
+        feed(pl.ds(pl.multiple_of(n * 256, 256), 256))
+
+    if ff % 256:
+        feed(pl.ds(ff // 256 * 256, ff % 256))
+
+    for h, gate_side, up_side in ((0, gate_own, up_own), (1, gate_sib, up_sib)):
+
+        @pl.loop(0, plane)
+        def _(b):
+            to = pl.ds(pl.multiple_of(((f ^ b) * 2 + (k ^ h)) * half, 128), half)
+            value = nt(gate_back[...], gate_side[b]) + nt(up_back[...], up_side[b])
+            back_part[:, to] = value.astype(BF)
+
+    @pl.loop(0, depth // 256)
+    def _(n):
+        at = pl.ds(pl.multiple_of(n * 256, 256), 256)
+        out_part[:, at] = nn(hidden[...], down[:, at]).astype(BF)
+
+    stores = [
+        pltpu.make_async_copy(kv_all, kv_out, local_s.at[12]),
+        pltpu.make_async_copy(branch_all, branch_out, local_s.at[13]),
+        pltpu.make_async_copy(wqkv, wqkv_out, local_s.at[14]),
+    ]
+    for copy in stores:
+        copy.start()
+    for gather in (token_gather, branch_gather, n2_gather):
+        gather.close()
+    for copy in mix_first.values():
+        copy.wait_send()
+    for j in peers:
+        note_send(j).wait_send()
+        wq_send(j).wait_send()
+        wk_send(j).wait_send()
+        wp_send(j).wait_send()
+        gate_pair(j).wait_send()
+        up_pair(j).wait_send()
+    for j in (1, 2):
+        gate_send(j).wait_send()
+        up_send(j).wait_send()
+
+    @pl.when(even)
+    def _():
+        gate_send(3).wait_send()
+        gate_across.wait_send()
+
+    @pl.when(jnp.logical_not(even))
+    def _():
+        up_send(3).wait_send()
+        up_across.wait_send()
+
+    kv_pair(0).wait_send()
+    for s in range(1, line):
+
+        @pl.when(z >= s)
+        def _():
+            kv_send(s).wait_send()
+
+        @pl.when(z + s < line)
+        def _():
+            kv_pair(s).wait_send()
+
+    for copy in stores:
+        copy.wait()
+
+
+def front_pass(tokens, cotangent, lengths, attn_gain, mlp_gain, w_query, w_key, w_value, w_out, w_gate, w_up, w_down):
+    rows, depth = tokens.shape
+    plane, line = 4, 4
+    total, slab = plane * rows, depth // plane
+    half = slab // 2
+    q_width = HEADS * HEAD_DIM // plane
+    width = q_width + 128
+    ff = w_down.shape[0]
+    slot = rows * line * 2
+    keys = slot
+    act = (rows, depth)
+    local = pl.BlockSpec(memory_space=pltpu.VMEM)
+    anywhere = pl.BlockSpec(memory_space=pl.ANY)
+    dma = lambda n: pltpu.SemaphoreType.DMA((n,))
+    kv_shape = (2 * line, plane, rows, 128)
+    sds = jax.ShapeDtypeStruct
+    outs = [
+        sds((total, depth), BF),
+        sds((plane, rows, q_width), BF),
+        sds((plane, rows, q_width), F32),
+        sds((total, q_width), BF),
+        sds(act, F32),
+        sds((total, depth), BF),
+        sds((total, ff), BF),
+        sds((total, ff), BF),
+        sds((total, ff), BF),
+        sds((total, depth), BF),
+        sds((total, depth), BF),
+        sds((8, depth), F32),
+        sds((8, depth), F32),
+        sds((plane, rows, 128), F32),
+        sds((rows, 128), F32),
+        sds((rows, 128), F32),
+        sds((8, keys), F32),
+        sds(kv_shape, BF),
+        sds((plane,) + act, BF),
+        sds((depth, width), BF),
+    ]
+    slabs = pltpu.VMEM((plane, half, ff), BF)
+    scratch = [
+        pltpu.VMEM((plane, 16, slab), BF),
+        pltpu.VMEM((plane,) + act, BF),
+        pltpu.VMEM((depth, width), BF),
+        pltpu.VMEM(w_key.shape, BF),
+        pltpu.VMEM(w_value.shape, BF),
+        pltpu.VMEM((plane, half, 128), BF),
+        slabs,
+        slabs,
+        slabs,
+        slabs,
+        pltpu.VMEM(w_down.shape, BF),
+        pltpu.VMEM(kv_shape, BF),
+        pltpu.VMEM((keys, 128), BF),
+        pltpu.VMEM(w_out.shape, BF),
+        pltpu.VMEM((plane,) + act, BF),
+        pltpu.VMEM((2,) + act, BF),
+        pltpu.VMEM((2, rows // 2, depth), BF),
+        pltpu.VMEM((2, rows // 2, depth), BF),
+        pltpu.VMEM((plane,) + act, BF),
+        pltpu.VMEM((plane,) + act, BF),
+        pltpu.VMEM(act, BF),
+    ]
+    sems = [15, 3, 3, 2, 2, 2, 2, 3, 3, 3, 3, 3, 3, 1, 1, 3, 3, 4, 4, 3, 3, 3, 3, 1, 1, 3, 3, 3, 3]
+    sems += [2, 2, 2, 2, 6, 6, 2, 2, 2, 2]
+    return pl.pallas_call(
+        front_kernel,
+        out_shape=outs,
+        in_specs=[pl.BlockSpec(memory_space=pltpu.SMEM)] + [local] * 6 + [anywhere] * 9,
+        out_specs=[local] * 17 + [anywhere] * 3,
+        scratch_shapes=scratch + [dma(n) for n in sems],
+        compiler_params=pltpu.CompilerParams(
+            vmem_limit_bytes=62 * 1024 * 1024, has_side_effects=True
+        ),
+        name="front_pass",
+    )(
+        lengths, attn_gain.reshape(1, slab), mlp_gain.reshape(1, slab), *rotary_parts(slot, rows),
+        tokens, cotangent, w_query, w_key, w_value, w_out, w_gate, w_up, w_down,
+    )
+
+
 def add_into(target, other):
     @pl.loop(0, target.shape[0] // 16)
     def _(i):
@@ -459,7 +1266,7 @@
 
 
 def back_kernel(
-    at_ref,
+    limits,
     own_down, own_gate, own_up, other_down, other_gate, other_up,
     back_part, out_part, w_out, wqkv_hbm, h1_hbm,
     mixed, branch_own, x_own, gain_one, gain_two,
@@ -663,7 +1470,7 @@
             inverse = lax.rsqrt(jnp.mean(x * x, axis=1, keepdims=True) + EPSILON)
             normed = x * inverse
             acc[...] += gradient * normed
-            scaled = gradient * gain[...]
+            scaled = gradient * gain[0:1, :]
             write(at, inverse * (scaled - normed * jnp.mean(scaled * normed, axis=1, keepdims=True)))
 
     def piece_mixed():
@@ -700,14 +1507,13 @@
         vk[...] = pltpu.roll(kv_all[:, j].reshape(vk.shape).astype(F32), 64, 1).astype(BF)
         dk_sum[...] = jnp.zeros_like(dk_sum)
         dv_sum[...] = jnp.zeros_like(dv_sum)
-        place = at_ref[0] - lax.broadcasted_iota(jnp.int32, (rows, 1), 0)
-        limit = jnp.minimum(place, at_ref[1 + j] - 1)
+        limit = limits[j, :, 0:1]
         lane = lax.broadcasted_iota(jnp.int32, (rows, 128), 1)
 
         @pl.loop(0, pairs)
         def _(p):
             at = pl.ds(pl.multiple_of(p * 128, 128), 128)
-            allowed = kp[...] <= limit
+            allowed = kp[0:1, :] <= limit
             q, do = queries[j, :, at], do_all[j, :, at]
             logs = lse[j, :, at]
             zero = jnp.zeros_like(q)
@@ -875,7 +1681,7 @@
 
 
 def back_pass(
-    at, own, other, back_part, out_part, w_out, wqkv, h1, mixed, branch_own, x_own, gain_one, gain_two,
+    limits, own, other, back_part, out_part, w_out, wqkv, h1, mixed, branch_own, x_own, gain_one, gain_two,
     attended, queries, lse, kv_all, kp, cosine, sine,
 ):
     count, line = lax.axis_size("fsdp"), lax.axis_size("z")
@@ -933,7 +1739,7 @@
     out = pl.pallas_call(
         back_kernel,
         out_shape=ends + ends + [act, act],
-        in_specs=[pl.BlockSpec(memory_space=pltpu.SMEM)] + [anywhere] * 11 + [local] * 12,
+        in_specs=[local] + [anywhere] * 11 + [local] * 12,
         out_specs=[anywhere] * 12 + [local] * 2,
         scratch_shapes=scratch,
         compiler_params=pltpu.CompilerParams(
@@ -944,229 +1750,40 @@
         ),
         name="back_pass",
     )(
-        at, *own, *other, back_part, out_part, w_out, wqkv, h1, mixed, branch_own, x_own, gain_one, gain_two,
+        limits, *own, *other, back_part, out_part, w_out, wqkv, h1, mixed, branch_own, x_own, gain_one, gain_two,
         attended, queries, lse, kv_all, kp, cosine, sine,
     )
     return out[:6], out[6:12], out[12], out[13]
-
-def sum_gradients_plain(owns, others, swapped):
-    ends = []
-    for own, other, slabs in zip(owns, others, swapped):
-        value = (own.astype(F32) + to_sibling(other).astype(F32)).astype(BF)
-        if slabs:
-            value = jnp.stack([value[0]] + [along_plane(value[j], j) for j in range(1, value.shape[0])])
-        ends.append(line_sum(value))
-    return ends, [to_sibling(e) for e in ends]
-
-
-def rms_backward(row_block, inverse, gain_vec, gradient):
-    normed = row_block * inverse
-    gain_grad = jnp.sum(gradient * normed, axis=0)
-    scaled = gradient * gain_vec
-    back = inverse * (scaled - normed * jnp.mean(scaled * normed, axis=1, keepdims=True))
-    return (back, gain_grad)
-
-
-def back_plain(
-    at, own, other, back_part, out_part, w_out, wqkv, h1, mixed, branch_own, x_own, gain_one, gain_two,
-    attended, queries, lse, kv_all, kp, cosine, sine,
-):
-    count, line = lax.axis_size("fsdp"), lax.axis_size("z")
-    k = lax.axis_index("core")
-    rows, depth = mixed.shape
-    total, half_depth = count * rows, depth // 2
-    half = half_depth // count
-    q_width = attended.shape[1]
-    f = lax.axis_index("fsdp")
-    order = jnp.stack([(f ^ j) * 2 + (k ^ h) for h in range(2) for j in range(count)]).astype(jnp.int32)
-    outputs = mixed + plane_reduce(out_part)
-    inv_two = lax.rsqrt(jnp.mean(mixed * mixed, axis=1, keepdims=True) + EPSILON)
-    mixed_back, gain_two_grad = rms_backward(mixed, inv_two, gain_two, plane_reduce(back_part))
-    mixed_grad = branch_own.astype(F32) + mixed_back
-    attn_back = jnp.concatenate(plane_gather(mixed_grad.astype(BF)))
-    attended_grad = nt(attn_back, w_out).astype(BF).reshape(count, rows, q_width)
-    own, other = list(own), list(other)
-    for place, terms in ((k, own), (1 - k, other)):
-        right = lax.dynamic_slice_in_dim(attn_back, place * half_depth, half_depth, 1)
-        terms.append(tn(attended, right).astype(BF).reshape(2, -1, half_depth))
-    query_back, kv_part = attend_back(at, queries, attended_grad, lse, kv_all, kp, cosine, sine)
-    kv_mine = kv_part[:line].astype(F32) + to_sibling(kv_part[line:]).astype(F32)
-    kv_back = kv_mine[0]
-    for s in range(1, line):
-        kv_back = kv_back + along_line(kv_mine[s].astype(BF), s).astype(F32)
-    lead, trail, flat = kv_back[..., :32], kv_back[..., 32:64], kv_back[..., 64:]
-    cos32, sin32 = cosine[:, :32], sine[:, 32:64]
-    kv_back = jnp.concatenate(
-        [lead * cos32 + trail * sin32, trail * cos32 - lead * sin32, flat], axis=-1
-    ).astype(BF)
-    qkv_back = jnp.concatenate(
-        [query_back.reshape(total, q_width), kv_back.reshape(total, 128)], axis=1
-    )
-    normed_back = put_columns(nt(qkv_back, wqkv).astype(BF), order, 2 * count)
-    inputs = x_own.astype(F32)
-    inv_one = lax.rsqrt(jnp.mean(inputs * inputs, axis=1, keepdims=True) + EPSILON)
-    input_back, gain_one_grad = rms_backward(
-        inputs, inv_one, gain_one, plane_reduce(normed_back.reshape(count, rows, depth))
-    )
-    for side, terms in ((0, own), (1, other)):
-        left = h1[:, side * half_depth : (side + 1) * half_depth]
-        terms.append(tn(left, qkv_back).astype(BF).reshape(count, half, q_width + 128))
-    gains = jnp.stack([gain_one_grad, gain_two_grad]).astype(BF)
-    for bit in plane_bits():
-        gains = (gains.astype(F32) + along_plane(gains, bit).astype(F32)).astype(BF)
-    gains = jnp.pad(gains, ((0, 14), (0, 0)))[None]
-    ends, sibs = sum_gradients_plain(own + [gains], other + [gains], (False, True, True, False, True, False))
-    return ends, sibs, outputs, mixed_grad + input_back
 
 
 def body(
     tokens, cotangent, lengths, attn_gain, w_query, w_key, w_value, w_out, mlp_gain, w_gate, w_up, w_down
 ):
     seqs, rows, depth = tokens.shape
-    count, line = lax.axis_size("fsdp"), lax.axis_size("z")
-    f, z, k = lax.axis_index("fsdp"), lax.axis_index("z"), lax.axis_index("core")
-    slot = rows * line * 2
-    total = count * rows
+    count = lax.axis_size("fsdp")
+    f, k = lax.axis_index("fsdp"), lax.axis_index("core")
     slab = depth // count
-    half = slab // 2
+    half, half_depth = slab // 2, depth // 2
     q_width = HEADS * HEAD_DIM // count
-    shared = max(1, count // KV_HEADS)
-
     x_own = tokens.reshape(rows, depth)
-    chunk = 2 * z + k
-    first_pos = slot - 1 - chunk * rows
-
-    length = lengths[0]
-    words = jnp.zeros((slab,), F32).at[0].set((length // 64).astype(F32)).at[1].set((length % 64).astype(F32))
-    note = jnp.stack([attn_gain, mlp_gain, words.astype(BF), jnp.zeros((slab,), BF)])
-    notes = [note] + [along_plane(note, j) for j in range(1, count)]
-    notes_abs = [lax.dynamic_index_in_dim(jnp.stack(notes), f ^ i, 0, keepdims=False) for i in range(count)]
-    gain_one = jnp.concatenate([n[0] for n in notes_abs]).astype(F32).reshape(1, depth)
-    gain_two = jnp.concatenate([n[1] for n in notes_abs]).astype(F32).reshape(1, depth)
-    all_lengths = jnp.stack(
-        [n[2, 0].astype(jnp.int32) * 64 + n[2, 1].astype(jnp.int32) for n in notes]
-    )
-
-    x_all = jnp.concatenate(plane_gather(x_own))
-
-    wq = cut_blocks(w_query, f, k, count)
-    key_cols = lax.dynamic_slice_in_dim(w_key, k * half, half, 0).reshape(half, KV_HEADS, HEAD_DIM)
-    value_cols = lax.dynamic_slice_in_dim(w_value, k * half, half, 0).reshape(half, KV_HEADS, HEAD_DIM)
-
-    def head_of(j):
-        return (f ^ j) // shared
-
-    wkv = jnp.stack(
-        [
-            jnp.concatenate(
-                [
-                    lax.dynamic_index_in_dim(key_cols, head_of(j), 1, keepdims=False),
-                    lax.dynamic_index_in_dim(value_cols, head_of(j), 1, keepdims=False),
-                ],
-                axis=1,
-            )
-            for j in range(count)
-        ]
-    )
-    wqkv = jnp.concatenate([wq, wkv], axis=2)
-    wqkv_own = jnp.stack([wqkv[0]] + [along_plane(wqkv[j], j) for j in range(1, count)])
-    wqkv_sib = to_sibling(wqkv_own)
-    wqkv_all = jnp.concatenate([wqkv_own, wqkv_sib]).reshape(depth, q_width + 128)
-
-    def fetch(weight):
-        cut = cut_blocks(weight, f, k, count)
-        width = cut.shape[2]
-        own = jnp.stack([cut[0]] + [along_plane(cut[j], j) for j in range(1, count)])
-        sib = to_sibling(own)
-        return own.reshape(depth // 2, width), sib.reshape(depth // 2, width)
-
-    gate_own, gate_sib = fetch(w_gate)
-    up_own, up_sib = fetch(w_up)
-
-    order = jnp.stack([(f ^ j) * 2 + (k ^ h) for h in range(2) for j in range(count)]).astype(jnp.int32)
-
-    half_dim = HEAD_DIM // 2
-    frequency = jnp.power(ROPE_BASE, jnp.arange(half_dim, dtype=F32) * (-2.0 / HEAD_DIM))
-    positions = first_pos - jnp.arange(rows, dtype=jnp.int32)
-    angles = positions.astype(F32)[:, None] * frequency[None, :]
-    cos32, sin32 = jnp.cos(angles), jnp.sin(angles)
-    cosine = jnp.concatenate([cos32] * 4, axis=1)
-    sine = jnp.concatenate([-sin32, sin32, -sin32, sin32], axis=1)
-
-    normed_one, queries, kv = qkv_project(order, x_all, gain_one, wqkv_all, cosine, sine, rows)
-    queries = queries.reshape(count, rows, q_width)
-    kv = kv.reshape(count, rows, 128)
-
-    mine = [kv] + [along_line(kv, -s) for s in range(1, line)]
-    mine = jnp.stack(mine)
-    kv_all = jnp.concatenate([mine, to_sibling(mine)])
-    places = []
-    for h in range(2):
-        for s in range(line):
-            start = slot - 1 - (2 * (z + s) + (k ^ h)) * rows
-            places.append(start - jnp.arange(rows, dtype=jnp.int32))
-    kp = jnp.concatenate(places)
-    kp = jnp.where(kp < 0, FAR, kp).reshape(1, -1)
-    at = jnp.concatenate([first_pos.reshape(1), all_lengths]).astype(jnp.int32)
-
-    attended, log_total = attend(at, queries, kv_all, kp)
-    attended = attended.reshape(total, q_width)
-
-    mixed_part = nn(attended, w_out).astype(BF).reshape(count, rows, depth)
-    inputs = x_own.astype(F32)
-    mixed = inputs + plane_reduce(mixed_part)
-    inv_two = lax.rsqrt(jnp.mean(mixed * mixed, axis=1, keepdims=True) + EPSILON)
-    normed_two_own = (mixed * inv_two * gain_two).astype(BF)
-    normed_two = jnp.concatenate(plane_gather(normed_two_own))
-    normed_two = pick_columns(normed_two, order, 2 * count)
-    n2_own, n2_sib = normed_two[:, : depth // 2], normed_two[:, depth // 2 :]
-
-    valid = (positions < length).astype(F32)[:, None]
-    out_back = cotangent.reshape(rows, depth).astype(F32) * valid
-    branch_own = out_back.astype(BF)
-    branch = jnp.concatenate(plane_gather(branch_own))
-
-    gate = nn(n2_own, gate_own) + nn(n2_sib, gate_sib)
-    up = nn(n2_own, up_own) + nn(n2_sib, up_sib)
-    sigmoid = jax.nn.sigmoid(gate)
-    hidden = (gate * sigmoid * up).astype(BF)
-
-    half_depth = depth // 2
-    branch_mine = lax.dynamic_slice_in_dim(branch, k * half_depth, half_depth, 1)
-    branch_other = lax.dynamic_slice_in_dim(branch, (1 - k) * half_depth, half_depth, 1)
-
-    def pair_sum(own, other):
-        return (own + to_sibling(other.astype(BF)).astype(F32)).astype(BF)
-
-    def swap_slabs(own):
-        return jnp.stack([own[0]] + [along_plane(own[j], j) for j in range(1, count)])
-
-    terms = {"down": (tn(hidden, branch_mine).astype(BF), tn(hidden, branch_other).astype(BF))}
-
-    hidden_grad = nt(branch, w_down)
-    gate_back = (hidden_grad * up * sigmoid * (1.0 + gate * (1.0 - sigmoid))).astype(BF)
-    up_back = (hidden_grad * gate * sigmoid).astype(BF)
-
-    def slab_terms(left_own, left_other, right):
-        return tuple(
-            tn(left, right).astype(BF).reshape(count, half, right.shape[1]) for left in (left_own, left_other)
-        )
-
-    terms["gate"] = slab_terms(n2_own, n2_sib, gate_back)
-    terms["up"] = slab_terms(n2_own, n2_sib, up_back)
-
-    back_own = (nt(gate_back, gate_own) + nt(up_back, up_own)).astype(BF)
-    back_sib = (nt(gate_back, gate_sib) + nt(up_back, up_sib)).astype(BF)
-    normed_back = put_columns(jnp.concatenate([back_own, back_sib], axis=1), order, 2 * count)
-    normed_back = normed_back.reshape(count, rows, depth)
-    out_part = nn(hidden, w_down).astype(BF).reshape(count, rows, depth)
-    terms["down"] = tuple(t.reshape(4, -1, half_depth) for t in terms["down"])
-    names = ("down", "gate", "up")
-    own, other = [terms[n][0] for n in names], [terms[n][1] for n in names]
-    rest = (mixed, branch_own, x_own, gain_one, gain_two, attended, queries, log_total, kv_all, kp, cosine, sine)
-    run = back_pass if line == 4 and q_width % 256 == 0 else back_plain
-    owns, sibs, outputs, input_grad = run(
-        at, own, other, normed_back, out_part, w_out, wqkv_all, normed_one, *rest
+    (
+        h1, queries, lse, attended, mixed, n2, hidden, gate_back, up_back, back_part, out_part,
+        gain_one, gain_two, limits, cosine, sine, kp, kv_all, branch, wqkv,
+    ) = front_pass(
+        x_own, cotangent.reshape(rows, depth), lengths, attn_gain, mlp_gain,
+        w_query, w_key, w_value, w_out, w_gate, w_up, w_down,
+    )
+    flat = branch.reshape(count * rows, depth)
+    own, other = [], []
+    for terms, side in ((own, 0), (other, 1)):
+        right = lax.dynamic_slice_in_dim(flat, (k ^ side) * half_depth, half_depth, 1)
+        left = n2[:, side * half_depth : (side + 1) * half_depth]
+        terms.append(tn(hidden, right).astype(BF).reshape(4, -1, half_depth))
+        terms.append(tn(left, gate_back).astype(BF).reshape(count, half, -1))
+        terms.append(tn(left, up_back).astype(BF).reshape(count, half, -1))
+    owns, sibs, outputs, input_grad = back_pass(
+        limits, own, other, back_part.reshape(count, rows, depth), out_part.reshape(count, rows, depth), w_out,
+        wqkv, h1, mixed, branch[0], x_own, gain_one, gain_two, attended, queries, lse, kv_all, kp, cosine, sine,
     )
 
     def columns(i):
@@ -1183,19 +1800,15 @@
         both = [lax.dynamic_index_in_dim(halves, k ^ h, 0, keepdims=False) for h in range(2)]
         both = jnp.concatenate(both, axis=1).astype(F32)[:, :, lo:hi]
         cols = jnp.stack([lax.dynamic_index_in_dim(both, f ^ i, 0, keepdims=False) for i in range(count)])
-        cols = cols.reshape(KV_HEADS, shared, slab, HEAD_DIM).sum(1)
         return jnp.transpose(cols, (1, 0, 2)).reshape(slab, KV_HEADS * HEAD_DIM)
-
-    key_grad = by_head(0, 64)
-    value_grad = by_head(64, 128)
 
     return (
         outputs.reshape(seqs, rows, depth),
         input_grad.reshape(seqs, rows, depth),
         gains[0],
         query_grad,
-        key_grad,
-        value_grad,
+        by_head(0, 64),
+        by_head(64, 128),
         out_grad,
         gains[1],
         gate_grad,
@@ -1209,8 +1822,9 @@
     split = Mesh(mesh.devices.reshape(count, ctx // 2, 2), ("fsdp", "z", "core"))
     act = P("fsdp", ("z", "core"), None)
     row, mat = P("fsdp"), P("fsdp", None)
+    fast = count == 4 and count == KV_HEADS and ctx == 8
     return jax.shard_map(
-        body,
+        body if fast else body_plain,
         mesh=split,
         in_specs=(act, act, row, row, mat, mat, mat, mat, row, mat, mat, mat),
         out_specs=(act, act, row, mat, mat, mat, mat, row, mat, mat, mat),

time: 743 us -> 618 us (0.83)
  Pallas kernels: 442 us -> 569 us
  waiting for transfers between devices: 117 us -> 0 us
  matrix products: 62.7 us -> 22.1 us
  starting transfers between devices: 38 us -> 0 us
  local copies, waits for them, and re-layouts: 48.6 us -> 14.3 us
  other arithmetic: 18.7 us -> 1.01 us
    pallas_call x7 -> x1, Pallas kernels: 51 us -> 176 us  [front_pass(): pl.pallas_call(front_kernel, out_shape=outs, in_specs=[pl.BlockSpec(memor...]
    ppermute x35 -> x0, waiting for transfers between devices: 117 us -> none  [the longest x28 103 us: along_plane(): return lax.ppermute(value, 'fsdp', [(i, i ^ step) for i in range(count)])]
    dot_general x11 -> x0, matrix products: 42.5 us -> none  [the longest x6 23.8 us: nn(): return jnp.dot(a, b, preferred_element_type=F32)]
    ppermute x35 -> x0, starting transfers between devices: 38 us -> none  [the longest x28 33.6 us: along_plane(): return lax.ppermute(value, 'fsdp', [(i, i ^ step) for i in range(count)])]
    unnamed x84 -> x20, local copies, waits for them, and re-layouts: 22.8 us -> 3.96 us
    slice x9 -> x0, local copies, waits for them, and re-layouts: 11.5 us -> none  [the longest x2 6.35 us: fetch(): cut[0]]
    another operation x19 -> x1, other arithmetic: 10 us -> 0.58 us  [join_rows(): jnp.stack([f, k])]
  transfers between devices with their start and end apart: 35 -> 0, of which waited for: 19 -> 0; matrix products, arithmetic and copies ran while one was open for 7% -> 0% of each run, Pallas kernels for 6% -> 0%
where the time goes in v4:
time: 618 us; the launch traced here: 608 us
  Pallas kernels  569 us (92%)
  matrix products  22.1 us (4%)
  local copies, waits for them, and re-layouts  14.3 us (2%)
    pallas_call x1, Pallas kernels, back_pass(): pl.pallas_call(back_kernel, out_shape=ends + ends + [act, act], in_specs=...  352 us
    pallas_call x1, Pallas kernels, front_pass(): pl.pallas_call(front_kernel, out_shape=outs, in_specs=[pl.BlockSpec(memor...  176 us
    pallas_call x3, Pallas kernels, join_rows(): pl.pallas_call(join_kernel, grid_spec=spec, out_shape=jax.ShapeDtypeStruc...  26.3 us
    dot_general x6, matrix products, tn(): lax.dot_general(a, b, (((0,), (0,)), ((), ())), preferred_element_type=F32)  22.1 us
    pallas_call x2, Pallas kernels, join_columns(): pl.pallas_call(join_kernel, grid_spec=spec, out_shape=jax.ShapeDtypeStruc...  15.2 us

profile of v4, /device:TPU:0, one launch (start us, length us, event | category | flops | bytes accessed | tf_op | source)
XLA Modules:
  0.0 608.4 jit_solution(15740316641352140007)
XLA Ops:
  0.7 1.3 reshape.93.attn_gain
  1.9 1.3 reshape.94.mlp_gain
  3.8 176.1 %front_pass.1 = (bf16[512,2048]{1,0:T(8,128)(2,1)}, bf16[4,128,512]{2,1,0:T(8,128)(2,1)}, f32[4,128,512]{2,1,0:T(8,128)}, bf16[512,512]{1,0:T(8,128)(2,1)}, f32[...) custom-call(s32[1]{0:T(128)S(6)} %copy.33.length_ref, ...), custom_call_target="tpu_custom_call" | custom-call | tf_op jit(solution)/shard_map/front_pass/pallas_call | solution.py:1245
  180.0 0.0 copy-start.3
  180.0 0.0 copy-start.7
  180.0 5.1 convolution_convert_fusion.2
  185.1 0.0 copy-done.3
  185.1 0.0 copy-done.7
  185.1 0.0 copy-start.4
  185.1 0.0 copy-start.6
  185.1 3.3 convolution_convert_fusion.5
  188.4 0.0 copy-done.4
  188.4 0.0 copy-done.6
  188.4 0.0 copy-start.5
  188.4 3.4 convolution_convert_fusion
  191.8 0.0 copy-done.5
  191.8 3.4 convolution_convert_fusion.1
  195.2 3.4 convolution_convert_fusion.3
  198.6 3.4 convolution_convert_fusion.4
  202.1 0.8 slice_bitcast_fusion.branch_own
  202.9 351.5 %back_pass.1 = (bf16[4,352,1024]{2,1,0:T(8,128)(2,1)}, bf16[4,256,1408]{2,1,0:T(8,128)(2,1)}, bf16[4,256,1408]{2,1,0:T(8,128)(2,1)}, bf16[2,256,1024]{2,1,0:T(8,...) custom-call(f32[4,128,128]{2,1,0:T(8,128)} %get-tuple-element.44.lim, ...), custom_call_target="tpu_custom_call" | custom-call | flops 99999997952 | bytes 1000000000 | tf_op jit(solution)/shard_map/back_pass/pallas_call | solution.py:1739
  554.4 9.0 %join_columns.3 = f32[1408,2048]{1,0:T(8,128)} custom-call(s32[1]{0:T(128)} %bitcast.16.at_ref, bf16[1408,1024]{1,0:T(8,128)(2,1)} %bitcast.43, bf16[1408,1024]{1,0:T(8,128)(2,1)} %bitcast.44), custom_call_target="tpu_custom_call" | custom-call | tf_op jit(solution)/shard_map/join_columns/pallas_call | solution.py:224
  563.4 0.6 pad_add_fusion.at_ref
  564.0 9.7 %join_rows.5 = f32[512,5632]{1,0:T(8,128)} custom-call(s32[2]{0:T(128)} %pad_add_fusion.at_ref, bf16[4,256,1408]{2,1,0:T(8,128)(2,1)} %get-tuple-element.73.own_ref, bf16[4,256,1408]{2,1,0:T(8,128)(2,1)} %get-tuple-element.74.sib_ref), custom_call_target="tpu_custom_call" | custom-call | tf_op jit(solution)/shard_map/join_rows/pallas_call | solution.py:202
  573.7 9.7 %join_rows.4 = f32[512,5632]{1,0:T(8,128)} custom-call(s32[2]{0:T(128)} %pad_add_fusion.at_ref, bf16[4,256,1408]{2,1,0:T(8,128)(2,1)} %get-tuple-element.71.own_ref, bf16[4,256,1408]{2,1,0:T(8,128)(2,1)} %get-tuple-element.72.sib_ref), custom_call_target="tpu_custom_call" | custom-call | tf_op jit(solution)/shard_map/join_rows/pallas_call | solution.py:202
  583.4 6.2 %join_columns.2 = f32[512,2048]{1,0:T(8,128)} custom-call(s32[1]{0:T(128)} %bitcast.16.at_ref, bf16[512,1024]{1,0:T(8,128)(2,1)} %bitcast.47, bf16[512,1024]{1,0:T(8,128)(2,1)} %bitcast.48), custom_call_target="tpu_custom_call" | custom-call | tf_op jit(solution)/shard_map/join_columns/pallas_call | solution.py:224
  589.5 1.1 slice_bitcast_fusion.1
  590.6 0.2 fusion.9
  590.8 0.1 maximum_convert_fusion
  590.9 0.3 fusion.13
  591.3 0.1 constant_dynamic-slice_fusion.3
  591.4 0.1 maximum_bitcast_fusion.1
  591.4 0.3 copy.28
  591.8 1.0 copy.30
  592.8 0.1 constant_dynamic-slice_fusion.7
  592.8 0.1 maximum_bitcast_fusion
  592.9 0.0 copy-start
  592.9 0.3 copy.27
  593.2 1.0 copy.29
  594.2 2.3 slice.43.own_ref
  596.5 0.0 copy-done
  596.5 1.1 slice.44.sib_ref
  597.6 0.0 copy-start.2
  597.6 7.0 %join_rows.3 = f32[512,2048]{1,0:T(8,128)} custom-call(s32[2]{0:T(128)} %pad_add_fusion.at_ref, bf16[4,256,512]{2,1,0:T(8,128)(2,1)} %slice.43.own_ref, bf16[4,256,512]{2,1,0:T(8,128)(2,1)} %slice.44.sib_ref), custom_call_target="tpu_custom_call" | custom-call | tf_op jit(solution)/shard_map/join_rows/pallas_call | solution.py:202
  604.5 0.0 copy-start.1
  604.5 0.9 slice.41
  605.4 0.6 fusion.14
  606.0 0.0 copy-done.2
  606.0 1.0 copy.34
  607.0 0.0 copy-done.1
  607.0 1.0 copy.35
  (1 shorter events, 0.0 us)
Async XLA Ops:
  180.0 5.1 copy-start.3
  180.0 5.1 copy-start.7
  185.1 3.3 copy-start.4
  185.1 3.3 copy-start.6
  188.4 3.4 copy-start.5
  592.9 3.6 copy-start
  597.6 8.4 %copy-start.2 = (f32[128,2048]{1,0:T(8,128)S(1)}, f32[128,2048]{1,0:T(8,128)}, u32[]{:S(2)}) copy-start(f32[128,2048]{1,0:T(8,128)} %get-tuple-element.64) | copy-start | bytes 3145732
  604.5 2.4 copy-start.1

commit v5 on v4

--- a/solution.py
+++ b/solution.py
@@ -1575,6 +1575,7 @@
 
     def piece_dh():
         locals_[3].wait()
+        locals_[4].wait()
         for h in range(2):
             for j in range(plane):
                 start = pl.multiple_of(((f ^ j) * 2 + (k ^ h)) * half, 128)
@@ -1620,16 +1621,31 @@
     def piece_gain():
         for j in peers:
             gain_send(j).wait_recv()
-        locals_[4].wait()
-
-    pieces = {2: [piece_mixed], 4: [piece_do]}
+
+    def when(lags):
+        give, pair, ahead, enter, middle, leave, keep = lags
+        events = []
+        for c in range(count):
+            if c not in loaded:
+                events.append((c + give, 0, stage_give, c))
+            events.append((max(c - ahead, 0) if c in loaded else c + pair, 1, stage_pair, c))
+            events.append((c + enter, 2, stage_in, c))
+            events.append((c + middle, 3, stage_mid, c))
+            events.append((c + leave, 4, stage_out, c))
+            events.append((c + keep, 5, stage_keep, c))
+        return events
+
+    events = when((-2, -1, 3, 1, 2, 3, 4))
+    order = {
+        piece_mixed: 2, piece_do: 4, piece_kv_line: 8, piece_outputs: 8, piece_kv_sum: 9, piece_dh: 9,
+        piece_input: 11, piece_gain: 12,
+    }
+    events += [(tick, 6 + n, piece, None) for n, (piece, tick) in enumerate(order.items())]
+    attend_at = (4, 5, 6, 7)
     for j in range(plane):
-        pieces.setdefault(4 + j, []).append(functools.partial(piece_attend, j))
-    pieces[3 + plane].append(lambda: kv_pair.start())
-    pieces[4 + plane] = [piece_kv_line, piece_outputs]
-    pieces[5 + plane] = [piece_kv_sum, piece_dh]
-    pieces[7 + plane] = [piece_input]
-    pieces[8 + plane] = [piece_gain]
+        events.append((attend_at[j], 14 + j, piece_attend, j))
+    events.append((attend_at[-1], 18, kv_pair.start, None))
+    events.sort(key=lambda e: e[:2])
 
     for j in peers:
         back_send(j).start()
@@ -1639,13 +1655,8 @@
         load_copy(c).start()
     for copy in locals_:
         copy.start()
-    stages = ((-1, stage_give), (0, stage_pair), (1, stage_in), (2, stage_mid), (4, stage_out), (6, stage_keep))
-    for tick in range(count + stages[-1][0]):
-        for lag, stage in stages:
-            if 0 <= tick - lag < count:
-                stage(tick - lag)
-        for piece in pieces.get(tick, []):
-            piece()
+    for _, _, act, which in events:
+        act() if which is None else act(which)
 
     for c in range(count):
         name, i = chunks[c]
@@ -1756,15 +1767,140 @@
     return out[:6], out[6:12], out[12], out[13]
 
 
+def finish_kernel(
+    own_down, own_gate, own_up, own_out, own_qkv, own_gain, sib_down, sib_gate, sib_up, sib_out, sib_qkv,
+    down, gate, up, out, query, key, value, attn_gain, mlp_gain,
+    low_rows, low_cols, high_rows, high_cols, kv, kv_high, gain_in, gain_high, load_s, store_s, side_s,
+):
+    f, k = lax.axis_index("fsdp"), lax.axis_index("core")
+    plane = lax.axis_size("fsdp")
+    half, ff = own_gate.shape[1], own_gate.shape[2]
+    half_depth = own_down.shape[2]
+    slab = 2 * half
+    q_width = own_qkv.shape[2] - 128
+    tasks = []
+    for side, (d, o, g, u, q) in enumerate(
+        ((own_down, own_out, own_gate, own_up, own_qkv), (sib_down, sib_out, sib_gate, sib_up, sib_qkv))
+    ):
+        rows_at = pl.ds(pl.multiple_of((k ^ side) * half, 8), half)
+        cols_at = pl.ds(pl.multiple_of((k ^ side) * half_depth, 128), half_depth)
+        for source, target in ((d, down), (o, out)):
+            for i in range(source.shape[0]):
+                size = source.shape[1]
+                tasks.append((source.at[i], target.at[pl.ds(i * size, size), cols_at], 0))
+        for source, target in ((g, gate), (u, up)):
+            for j in range(plane):
+                to = pl.ds(pl.multiple_of((f ^ j) * ff, 128), ff)
+                tasks.append((source.at[j], target.at[rows_at, to], 1))
+        for j in range(plane):
+            to = pl.ds(pl.multiple_of((f ^ j) * q_width, 128), q_width)
+            tasks.append((q.at[j, :, pl.ds(0, q_width)], query.at[rows_at, to], 1))
+    slots = low_rows.shape[0]
+
+    def window(buffer, n, shape):
+        return buffer.at[n % slots, pl.ds(0, shape[0]), pl.ds(0, shape[1])]
+
+    def load(n):
+        source, _, kind = tasks[n]
+        low = (low_rows, low_cols)[kind]
+        return pltpu.make_async_copy(source, window(low, n, source.shape), load_s.at[n])
+
+    def store(n):
+        source, target, kind = tasks[n]
+        high = (high_rows, high_cols)[kind]
+        return pltpu.make_async_copy(window(high, n, source.shape), target, store_s.at[n])
+
+    sides = [
+        pltpu.make_async_copy(own_gain.at[0], gain_in, side_s.at[0]),
+        pltpu.make_async_copy(own_qkv.at[:, :, pl.ds(q_width, 128)], kv.at[0], side_s.at[1]),
+        pltpu.make_async_copy(sib_qkv.at[:, :, pl.ds(q_width, 128)], kv.at[1], side_s.at[2]),
+    ]
+    for n in range(slots):
+        load(n).start()
+    for copy in sides:
+        copy.start()
+    for n in range(len(tasks)):
+        source, _, kind = tasks[n]
+        shape = source.shape
+        low, high = ((low_rows, high_rows), (low_cols, high_cols))[kind]
+        load(n).wait()
+        if n >= slots:
+            store(n - slots).wait()
+
+        @pl.loop(0, shape[0] // 16)
+        def _(i):
+            at = pl.ds(pl.multiple_of(i * 16, 16), 16)
+            high[n % slots, at, 0 : shape[1]] = low[n % slots, at, 0 : shape[1]].astype(F32)
+
+        store(n).start()
+        if n + slots < len(tasks):
+            load(n + slots).start()
+    for copy in sides:
+        copy.wait()
+    mine = pl.ds(pl.multiple_of(f * slab, 128), slab)
+    gain_high[...] = gain_in[...].astype(F32)
+    attn_gain[...] = gain_high[0:1, mine]
+    mlp_gain[...] = gain_high[1:2, mine]
+    lane = lax.broadcasted_iota(jnp.int32, (half, 128), 1)
+    for side in range(2):
+        rows_at = pl.ds(pl.multiple_of((k ^ side) * half, 8), half)
+        for pair in range(plane // 2):
+            first = kv[side, f ^ (2 * pair)].astype(F32)
+            second = kv[side, f ^ (2 * pair + 1)].astype(F32)
+            at = slice(pair * 128, (pair + 1) * 128)
+            key[rows_at, at] = jnp.where(lane < 64, first, pltpu.roll(second, 64, 1))
+            value[rows_at, at] = jnp.where(lane < 64, pltpu.roll(first, 64, 1), second)
+    for n in range(max(0, len(tasks) - slots), len(tasks)):
+        store(n).wait()
+
+
+def finish(owns, sibs):
+    plane = lax.axis_size("fsdp")
+    down, gate, _, out, qkv, gain = (x.shape for x in owns)
+    depth = 2 * down[2]
+    slab = 2 * gate[1]
+    q_width = qkv[2] - 128
+    sds = jax.ShapeDtypeStruct
+    shapes = [
+        (down[0] * down[1], depth), (slab, plane * gate[2]), (slab, plane * gate[2]), (out[0] * out[1], depth),
+        (slab, plane * q_width), (slab, KV_HEADS * HEAD_DIM), (slab, KV_HEADS * HEAD_DIM), (1, slab), (1, slab),
+    ]
+    slots = 4
+    tall = (slots, max(down[1], out[1]), down[2])
+    wide = (slots, gate[1], max(gate[2], q_width))
+    count = 2 * (down[0] + out[0] + 3 * plane)
+    anywhere, local = pl.BlockSpec(memory_space=pl.ANY), pl.BlockSpec(memory_space=pltpu.VMEM)
+    return pl.pallas_call(
+        finish_kernel,
+        out_shape=[sds(s, F32) for s in shapes],
+        in_specs=[anywhere] * 11,
+        out_specs=[anywhere] * 5 + [local] * 4,
+        scratch_shapes=[
+            pltpu.VMEM(tall, BF),
+            pltpu.VMEM(wide, BF),
+            pltpu.VMEM(tall, F32),
+            pltpu.VMEM(wide, F32),
+            pltpu.VMEM((2, plane, gate[1], 128), BF),
+            pltpu.VMEM((16, 128), F32),
+            pltpu.VMEM(gain[1:], BF),
+            pltpu.VMEM(gain[1:], F32),
+            pltpu.SemaphoreType.DMA((count,)),
+            pltpu.SemaphoreType.DMA((count,)),
+            pltpu.SemaphoreType.DMA((3,)),
+        ],
+        compiler_params=params(),
+        name="finish",
+    )(*owns, *sibs[:5])
+
+
 def body(
     tokens, cotangent, lengths, attn_gain, w_query, w_key, w_value, w_out, mlp_gain, w_gate, w_up, w_down
 ):
     seqs, rows, depth = tokens.shape
     count = lax.axis_size("fsdp")
-    f, k = lax.axis_index("fsdp"), lax.axis_index("core")
+    k = lax.axis_index("core")
     slab = depth // count
     half, half_depth = slab // 2, depth // 2
-    q_width = HEADS * HEAD_DIM // count
     x_own = tokens.reshape(rows, depth)
     (
         h1, queries, lse, attended, mixed, n2, hidden, gate_back, up_back, back_part, out_part,
@@ -1786,31 +1922,16 @@
         wqkv, h1, mixed, branch[0], x_own, gain_one, gain_two, attended, queries, lse, kv_all, kp, cosine, sine,
     )
 
-    def columns(i):
-        return join_columns(*(x[i].reshape(-1, half_depth) for x in (owns, sibs)), k)
-
-    down_grad, out_grad = columns(0), columns(3)
-    gate_grad, up_grad = (join_rows(owns[i], sibs[i], f, k) for i in (1, 2))
-    qkv_half, qkv_sib = owns[4], sibs[4]
-    query_grad = join_rows(qkv_half[:, :, :q_width], qkv_sib[:, :, :q_width], f, k)
-    gains = lax.dynamic_slice_in_dim(owns[5][0, :2], f * slab, slab, 1).astype(F32)
-    halves = jnp.stack([qkv_half[:, :, q_width:], qkv_sib[:, :, q_width:]])
-
-    def by_head(lo, hi):
-        both = [lax.dynamic_index_in_dim(halves, k ^ h, 0, keepdims=False) for h in range(2)]
-        both = jnp.concatenate(both, axis=1).astype(F32)[:, :, lo:hi]
-        cols = jnp.stack([lax.dynamic_index_in_dim(both, f ^ i, 0, keepdims=False) for i in range(count)])
-        return jnp.transpose(cols, (1, 0, 2)).reshape(slab, KV_HEADS * HEAD_DIM)
-
+    down_grad, gate_grad, up_grad, out_grad, query_grad, key_grad, value_grad, gain_a, gain_m = finish(owns, sibs)
     return (
         outputs.reshape(seqs, rows, depth),
         input_grad.reshape(seqs, rows, depth),
-        gains[0],
+        gain_a.reshape(slab),
         query_grad,
-        by_head(0, 64),
-        by_head(64, 128),
+        key_grad,
+        value_grad,
         out_grad,
-        gains[1],
+        gain_m.reshape(slab),
         gate_grad,
         up_grad,
         down_grad,

time: 618 us -> 544 us (0.88)
  Pallas kernels: 569 us -> 503 us
  local copies, waits for them, and re-layouts: 14.3 us -> 6.98 us
    pallas_call x1, Pallas kernels: 352 us -> 303 us  [back_pass(): pl.pallas_call(back_kernel, out_shape=ends + ends + [act, act], in_specs=...]
    pallas_call x5 -> x1, Pallas kernels: 41.5 us -> 23.9 us  [finish(): pl.pallas_call(finish_kernel, out_shape=[sds(s, F32) for s in shapes], in...]
where the time goes in v5:
time: 544 us; the launch traced here: 534 us
  Pallas kernels  503 us (92%)
  matrix products  22.1 us (4%)
  local copies, waits for them, and re-layouts  6.98 us (1%)
    pallas_call x1, Pallas kernels, back_pass(): pl.pallas_call(back_kernel, out_shape=ends + ends + [act, act], in_specs=...  303 us
    pallas_call x1, Pallas kernels, front_pass(): pl.pallas_call(front_kernel, out_shape=outs, in_specs=[pl.BlockSpec(memor...  176 us
    pallas_call x1, Pallas kernels, finish(): pl.pallas_call(finish_kernel, out_shape=[sds(s, F32) for s in shapes], in...  23.9 us
    dot_general x6, matrix products, tn(): lax.dot_general(a, b, (((0,), (0,)), ((), ())), preferred_element_type=F32)  22.1 us

profile of v5, /device:TPU:0, one launch (start us, length us, event | category | flops | bytes accessed | tf_op | source)
XLA Modules:
  0.0 533.9 jit_solution(11355558665681056515)
XLA Ops:
  1.3 1.3 reshape.73.attn_gain
  2.6 1.3 reshape.74.mlp_gain
  3.8 176.0 %front_pass.1 = (bf16[512,2048]{1,0:T(8,128)(2,1)}, bf16[4,128,512]{2,1,0:T(8,128)(2,1)}, f32[4,128,512]{2,1,0:T(8,128)}, bf16[512,512]{1,0:T(8,128)(2,1)}, f32[...) custom-call(s32[1]{0:T(128)S(6)} %copy.29.length_ref, ...), custom_call_target="tpu_custom_call" | custom-call | tf_op jit(solution)/shard_map/front_pass/pallas_call | solution.py:1245
  179.8 1.9 slice_bitcast_fusion.branch_own
  181.7 0.0 copy-start.2
  181.7 0.0 copy-start.6
  181.7 5.1 convolution_convert_fusion.2
  186.8 0.0 copy-done.2
  186.8 0.0 copy-done.6
  186.8 0.0 copy-start.3
  186.8 0.0 copy-start.5
  186.8 3.3 convolution_convert_fusion.5
  190.1 0.0 copy-done.3
  190.1 0.0 copy-done.5
  190.1 3.4 convolution_convert_fusion.1
  193.5 0.0 copy-start.4
  193.5 3.4 convolution_convert_fusion.4
  196.9 0.0 copy-done.4
  196.9 3.4 convolution_convert_fusion
  200.3 3.4 convolution_convert_fusion.3
  203.8 303.2 %back_pass.1 = (bf16[4,352,1024]{2,1,0:T(8,128)(2,1)}, bf16[4,256,1408]{2,1,0:T(8,128)(2,1)}, bf16[4,256,1408]{2,1,0:T(8,128)(2,1)}, bf16[2,256,1024]{2,1,0:T(8,...) custom-call(f32[4,128,128]{2,1,0:T(8,128)} %get-tuple-element.53.lim, ...), custom_call_target="tpu_custom_call" | custom-call | flops 99999997952 | bytes 1000000000 | tf_op jit(solution)/shard_map/back_pass/pallas_call | solution.py:1750
  507.0 0.0 copy-start.1
  507.0 23.9 %finish.1 = (f32[1408,2048]{1,0:T(8,128)}, f32[512,5632]{1,0:T(8,128)}, f32[512,5632]{1,0:T(8,128)}, f32[512,2048]{1,0:T(8,128)}, f32[512,2048]{1,0:T(8,128)}, /...) custom-call(bf16[4,352,1024]{2,1,0:T(8,128)(2,1)} %get-tuple-element.75.own_down, ...), custom_call_target="tpu_custom_call" | custom-call | tf_op jit(solution)/shard_map/finish/pallas_call | solution.py:1873
  530.9 0.0 copy-start
  530.9 0.0 copy-done.1
  530.9 1.0 copy.30
  531.9 0.6 copy-done
  532.5 1.0 copy.31
Async XLA Ops:
  181.7 5.1 copy-start.2
  181.7 5.1 copy-start.6
  186.8 3.3 copy-start.3
  186.8 3.3 copy-start.5
  193.5 3.4 copy-start.4
  507.0 23.9 %copy-start.1 = (f32[128,2048]{1,0:T(8,128)S(1)}, f32[128,2048]{1,0:T(8,128)}, u32[]{:S(2)}) copy-start(f32[128,2048]{1,0:T(8,128)} %get-tuple-element.73) | copy-start | bytes 3145732
  530.9 1.6 copy-start

commit v6 on v5

--- a/solution.py
+++ b/solution.py
@@ -19,6 +19,9 @@
 BF = jnp.bfloat16
 F32 = jnp.float32
 VMEM_BYTES = 56 * 1024 * 1024
+LAGS = (-4, -3, -4, 0, 2, 4, 6)
+STEPS = (5, 9, 16, 16, 19, 19, 24, 26)
+ATTEND = (10, 13)
 
 
 def params(**kw):
@@ -686,12 +689,14 @@
 def front_kernel(
     length_ref, attn_gain, mlp_gain, start_cos, start_sin, step_cos, step_sin,
     tokens, cotangent, w_query, w_key, w_value, w_out, w_gate, w_up, w_down,
-    h1, queries, lse, attended, mixed, n2, hidden, gate_back, up_back, back_part, out_part,
-    gain_one, gain_two, limits, cosine, sine, kp,
-    kv_out, branch_out, wqkv_out,
+    h1_out, queries_out, lse_out, attended_out, mixed_out, n2_out, limits_out, cosine_out, sine_out, kp_out,
+    gain_one_out, gain_two_out, kv_out, branch_out, wqkv_out, gate_back_out, up_back_out, back_out, out_out,
+    own_down, other_down,
+    h1, queries, lse, attended, mixed, n2, limits, cosine, sine, kp, gain_one, gain_two,
+    hidden, gate_back, up_back, back_part, out_part, down_own, down_other,
     notes, x_all, wqkv, keys_in, values_in, kv_give, gate_own, gate_sib, up_own, up_sib, down,
     kv_all, vk, w_o, part, landed, relay, relayed, n2_all, branch_all, cot_in,
-    local_s, note_s, note_r, tok_s, tok_r, tof_s, tof_r, wq_s, wq_r, wk_s, wk_r, wp_s, wp_r, wkp_s, wkp_r,
+    local_s, store_s, note_s, note_r, tok_s, tok_r, tof_s, tof_r, wq_s, wq_r, wk_s, wk_r, wp_s, wp_r, wkp_s, wkp_r,
     kz_s, kz_r, kp_s, kp_r, gt_s, gt_r, up_s, up_r, gz_s, gz_r, gs_s, gs_r, us_s, us_r,
     bt_s, bt_r, btf_s, btf_r, mx_s, mx_r, nt_s, nt_r, ntf_s, ntf_r,
 ):
@@ -797,8 +802,49 @@
     def up_send(j):
         return remote(cols(w_up, j, 0, ff), up_own.at[j], up_s.at[j - 1], up_r.at[j - 1], chip(j))
 
-    gate_across = remote(gate_own.at[3], gate_own.at[3], gz_s.at[0], gz_r.at[0], {"z": across})
-    up_across = remote(up_own.at[3], up_own.at[3], gz_s.at[0], gz_r.at[0], {"z": across})
+    def gate_across(j):
+        return remote(gate_own.at[j], gate_own.at[j], gz_s.at[j - 1], gz_r.at[j - 1], {"z": across})
+
+    def up_across(j):
+        return remote(up_own.at[j], up_own.at[j], gz_s.at[j - 1], gz_r.at[j - 1], {"z": across})
+
+    def by_parity(act_even, act_odd):
+        @pl.when(even)
+        def _():
+            act_even()
+
+        @pl.when(jnp.logical_not(even))
+        def _():
+            act_odd()
+
+    def fetch_start():
+        by_parity(
+            lambda: [gate_send(j).start() for j in (3, 1, 2)], lambda: [up_send(j).start() for j in (3, 1, 2)]
+        )
+
+    def fetch_on(j):
+        def gate_on():
+            gate_send(j).wait_recv()
+            gate_across(j).start()
+            gate_pair(j).start()
+
+        def up_on():
+            up_send(j).wait_recv()
+            up_across(j).start()
+            up_pair(j).start()
+
+        by_parity(gate_on, up_on)
+
+    def cross_on(j):
+        def up_on():
+            up_across(j).wait_recv()
+            up_pair(j).start()
+
+        def gate_on():
+            gate_across(j).wait_recv()
+            gate_pair(j).start()
+
+        by_parity(up_on, gate_on)
 
     def gate_pair(j):
         return remote(gate_own.at[j], gate_sib.at[j], gs_s.at[j - 1], gs_r.at[j - 1], sib)
@@ -838,6 +884,17 @@
         )
     ]
 
+    stored = [
+        (h1, h1_out), (queries, queries_out), (lse, lse_out), (attended, attended_out), (mixed, mixed_out),
+        (n2, n2_out), (limits, limits_out), (cosine, cosine_out), (sine, sine_out), (kp, kp_out),
+        (gain_one, gain_one_out), (gain_two, gain_two_out), (kv_all, kv_out), (branch_all, branch_out),
+        (wqkv, wqkv_out), (gate_back, gate_back_out), (up_back, up_back_out), (back_part, back_out),
+        (out_part, out_out), (down_own, own_down), (down_other, other_down),
+    ]
+
+    def store(n):
+        return pltpu.make_async_copy(*stored[n], store_s.at[n])
+
     length = length_ref[0]
     place = lax.broadcasted_iota(jnp.int32, (16, slab), 0)
     high, low = (length // 64).astype(F32), (length % 64).astype(F32)
@@ -901,18 +958,7 @@
         wk_send(j).wait_recv()
         wp_send(j).start()
 
-    @pl.when(even)
-    def _():
-        gate_send(3).start()
-
-    @pl.when(jnp.logical_not(even))
-    def _():
-        up_send(3).start()
-
-    for j in (1, 2):
-        gate_send(j).start()
-    for j in (1, 2):
-        up_send(j).start()
+    fetch_start()
 
     for j in peers:
         note_send(j).wait_recv()
@@ -979,16 +1025,8 @@
             kv_send(s).wait_recv()
             kv_pair(s).start()
 
-    @pl.when(even)
-    def _():
-        gate_send(3).wait_recv()
-        gate_across.start()
-
-    @pl.when(jnp.logical_not(even))
-    def _():
-        up_send(3).wait_recv()
-        up_across.start()
-
+    fetch_on(1)
+    fetch_on(2)
     kv_pair(0).wait_recv()
     for s in range(1, line):
 
@@ -998,7 +1036,16 @@
 
     local[6].wait()
 
-    def attend_block(j):
+    def relay_on(far, late, which, j):
+        mix_first[far].wait_recv()
+        value = relay[which].astype(F32) + part[j, which * hr : (which + 1) * hr, :].astype(F32)
+        relayed[which] = value.astype(BF)
+        mix_first[late].start()
+
+    @pl.loop(0, plane)
+    def _(t):
+        j = plane - 1 - t
+        here = pl.ds(pl.multiple_of(j * rows, 16), rows)
         vk[...] = pltpu.roll(kv_all[:, j].reshape(keys, 128).astype(F32), 64, 1).astype(BF)
         limit = limits[j, :, 0:1]
 
@@ -1020,29 +1067,33 @@
                 sums = jnp.sum(weights, axis=1, keepdims=True)
                 outs.append(nn(weights.astype(BF), valued) / sums)
                 logs.append(jnp.broadcast_to(top + jnp.log(sums), (rows, 128)))
-            attended[j * rows : (j + 1) * rows, at] = jnp.where(lane < 64, outs[0], outs[1]).astype(BF)
+            attended[here, at] = jnp.where(lane < 64, outs[0], outs[1]).astype(BF)
             lse[j, :, at] = jnp.where(lane < 64, logs[0], logs[1])
 
-        part[j] = nn(attended[j * rows : (j + 1) * rows, :], w_o[...]).astype(BF)
-
-    attend_block(3)
-    mix_first["far_one"].start()
-    mix_first["far_two"].start()
-    branch_gather.forward()
-    attend_block(1)
-    mix_first["one"].start()
-    attend_block(2)
-    mix_first["two"].start()
-
-    def relay_on(far, late, which, j):
-        mix_first[far].wait_recv()
-        value = relay[which].astype(F32) + part[j, which * hr : (which + 1) * hr, :].astype(F32)
-        relayed[which] = value.astype(BF)
-        mix_first[late].start()
-
-    relay_on("far_one", "late_two", 0, 2)
-    relay_on("far_two", "late_one", 1, 1)
-    attend_block(0)
+        part[j] = nn(attended[here, :], w_o[...]).astype(BF)
+
+        @pl.when(t == 0)
+        def _():
+            mix_first["far_one"].start()
+            mix_first["far_two"].start()
+            branch_gather.forward()
+
+        @pl.when(t == 1)
+        def _():
+            mix_first["two"].start()
+            fetch_on(3)
+
+        @pl.when(t == 2)
+        def _():
+            mix_first["one"].start()
+            relay_on("far_one", "late_two", 0, 2)
+            relay_on("far_two", "late_one", 1, 1)
+
+    early_stores = [store(n) for n in range(12)]
+    for n in (0, 1, 2, 3, 6, 7, 8, 9, 10, 11):
+        early_stores[n].start()
+    cross_on(1)
+    cross_on(2)
     for name in ("one", "late_one", "two", "late_two"):
         mix_first[name].wait_recv()
 
@@ -1056,26 +1107,10 @@
         n2_all[0, at, :] = (value * inverse * gain_two[0:1, :]).astype(BF)
 
     n2_gather.start()
-
-    for j in (1, 2):
-        gate_send(j).wait_recv()
-        gate_pair(j).start()
+    early_stores[4].start()
+    branch_gather.arrive()
     n2_gather.forward()
-    for j in (1, 2):
-        up_send(j).wait_recv()
-        up_pair(j).start()
-
-    @pl.when(even)
-    def _():
-        up_across.wait_recv()
-
-    @pl.when(jnp.logical_not(even))
-    def _():
-        gate_across.wait_recv()
-
-    gate_pair(3).start()
-    up_pair(3).start()
-    branch_gather.arrive()
+    cross_on(3)
     n2_gather.arrive()
 
     @pl.loop(0, total // 16)
@@ -1089,6 +1124,10 @@
                 c = (h * plane + b) * half
                 n2[at, c : c + half] = n2_all[j, from_row, from_]
 
+    early_stores[5].start()
+    later = [store(n) for n in range(12, 19)]
+    for n in range(3):
+        later[n].start()
     for n in range(7, 12):
         local[n].wait()
     for j in peers:
@@ -1126,18 +1165,34 @@
             value = nt(gate_back[...], gate_side[b]) + nt(up_back[...], up_side[b])
             back_part[:, to] = value.astype(BF)
 
+    later[3].start()
+    later[4].start()
+    later[5].start()
+
+    def down_term(at, side, target):
+        spot = pl.ds(pl.multiple_of((k ^ side) * (depth // 2), 128), depth // 2)
+        right = branch_all[:, :, spot].reshape(total, depth // 2)
+        target[at, :] = tn(hidden[:, at], right).astype(BF)
+
+    for side, target in ((0, down_own), (1, down_other)):
+
+        @pl.loop(0, ff // 256)
+        def _(n):
+            down_term(pl.ds(pl.multiple_of(n * 256, 256), 256), side, target)
+
+        if ff % 256:
+            down_term(pl.ds(ff // 256 * 256, ff % 256), side, target)
+
+    ends = [store(19), store(20)]
+    for copy in ends:
+        copy.start()
+
     @pl.loop(0, depth // 256)
     def _(n):
         at = pl.ds(pl.multiple_of(n * 256, 256), 256)
         out_part[:, at] = nn(hidden[...], down[:, at]).astype(BF)
 
-    stores = [
-        pltpu.make_async_copy(kv_all, kv_out, local_s.at[12]),
-        pltpu.make_async_copy(branch_all, branch_out, local_s.at[13]),
-        pltpu.make_async_copy(wqkv, wqkv_out, local_s.at[14]),
-    ]
-    for copy in stores:
-        copy.start()
+    later[6].start()
     for gather in (token_gather, branch_gather, n2_gather):
         gather.close()
     for copy in mix_first.values():
@@ -1149,19 +1204,10 @@
         wp_send(j).wait_send()
         gate_pair(j).wait_send()
         up_pair(j).wait_send()
-    for j in (1, 2):
-        gate_send(j).wait_send()
-        up_send(j).wait_send()
-
-    @pl.when(even)
-    def _():
-        gate_send(3).wait_send()
-        gate_across.wait_send()
-
-    @pl.when(jnp.logical_not(even))
-    def _():
-        up_send(3).wait_send()
-        up_across.wait_send()
+    by_parity(
+        lambda: [c(j).wait_send() for j in peers for c in (gate_send, gate_across)],
+        lambda: [c(j).wait_send() for j in peers for c in (up_send, up_across)],
+    )
 
     kv_pair(0).wait_send()
     for s in range(1, line):
@@ -1174,7 +1220,7 @@
         def _():
             kv_pair(s).wait_send()
 
-    for copy in stores:
+    for copy in early_stores + later + ends:
         copy.wait()
 
 
@@ -1201,23 +1247,26 @@
         sds((total, q_width), BF),
         sds(act, F32),
         sds((total, depth), BF),
-        sds((total, ff), BF),
+        sds((plane, rows, 128), F32),
+        sds((rows, 128), F32),
+        sds((rows, 128), F32),
+        sds((8, keys), F32),
+        sds((8, depth), F32),
+        sds((8, depth), F32),
+        sds(kv_shape, BF),
+        sds((plane,) + act, BF),
+        sds((depth, width), BF),
         sds((total, ff), BF),
         sds((total, ff), BF),
         sds((total, depth), BF),
         sds((total, depth), BF),
-        sds((8, depth), F32),
-        sds((8, depth), F32),
-        sds((plane, rows, 128), F32),
-        sds((rows, 128), F32),
-        sds((rows, 128), F32),
-        sds((8, keys), F32),
-        sds(kv_shape, BF),
-        sds((plane,) + act, BF),
-        sds((depth, width), BF),
+        sds((ff, depth // 2), BF),
+        sds((ff, depth // 2), BF),
     ]
+    held = [pltpu.VMEM(o.shape, o.dtype) for o in outs]
+    held = held[:12] + [pltpu.VMEM((total, ff), BF)] + held[15:]
     slabs = pltpu.VMEM((plane, half, ff), BF)
-    scratch = [
+    scratch = held + [
         pltpu.VMEM((plane, 16, slab), BF),
         pltpu.VMEM((plane,) + act, BF),
         pltpu.VMEM((depth, width), BF),
@@ -1240,13 +1289,13 @@
         pltpu.VMEM((plane,) + act, BF),
         pltpu.VMEM(act, BF),
     ]
-    sems = [15, 3, 3, 2, 2, 2, 2, 3, 3, 3, 3, 3, 3, 1, 1, 3, 3, 4, 4, 3, 3, 3, 3, 1, 1, 3, 3, 3, 3]
+    sems = [12, 21, 3, 3, 2, 2, 2, 2, 3, 3, 3, 3, 3, 3, 1, 1, 3, 3, 4, 4, 3, 3, 3, 3, 3, 3, 3, 3, 3, 3]
     sems += [2, 2, 2, 2, 6, 6, 2, 2, 2, 2]
     return pl.pallas_call(
         front_kernel,
         out_shape=outs,
         in_specs=[pl.BlockSpec(memory_space=pltpu.SMEM)] + [local] * 6 + [anywhere] * 9,
-        out_specs=[local] * 17 + [anywhere] * 3,
+        out_specs=[anywhere] * 21,
         scratch_shapes=scratch + [dma(n) for n in sems],
         compiler_params=pltpu.CompilerParams(
             vmem_limit_bytes=62 * 1024 * 1024, has_side_effects=True
@@ -1267,9 +1316,8 @@
 
 def back_kernel(
     limits,
-    own_down, own_gate, own_up, other_down, other_gate, other_up,
-    back_part, out_part, w_out, wqkv_hbm, h1_hbm,
-    mixed, branch_own, x_own, gain_one, gain_two,
+    own_down, other_down, back_part, out_part, w_out, wqkv_hbm, h1_hbm, n2_hbm,
+    gate_back, up_back, mixed, branch_own, x_own, gain_one, gain_two,
     attended, queries, lse, kv_all, kp, cosine, sine,
     fin_down, fin_gate, fin_up, fin_out, fin_qkv, fin_gain,
     sib_down, sib_gate, sib_up, sib_out, sib_qkv, sib_gain,
@@ -1277,8 +1325,8 @@
     src_down, src_gate, src_up, src_out, src_qkv, src_gain,
     swap_gate, swap_up, swap_qkv,
     end_down, end_gate, end_up, end_out, end_qkv, end_gain,
-    load_down, load_gate, give_out, give_qkv, give_gain,
-    landed, landed_out, first_back, first_out, da_all, wide, do_all, dqkv, wqkv, h1,
+    load_down, give_gate, give_out, give_qkv, give_gain,
+    landed, landed_out, first_back, first_out, da_all, wide, do_all, dqkv, wqkv, left,
     vk, dk_sum, dv_sum, kv_part, kv_land, kv_mine, kv_line, gain_acc, gain_all,
     pair_s, pair_r, load_s, swap_s, swap_r, in_s, in_r, mid_s, mid_r, out_s, done_s, back_s, back_r, ready,
     local_s, rs_s, rs_r, ro_s, ro_r, ag_s, ag_r, rq_s, rq_r, kp_s, kp_r, kz_s, kz_r, ga_s, ga_r,
@@ -1299,8 +1347,8 @@
 
     kinds = {
         "down": (own_down, other_down, src_down, None, end_down, load_down, fin_down, sib_down),
-        "gate": (own_gate, other_gate, src_gate, swap_gate, end_gate, load_gate, fin_gate, sib_gate),
-        "up": (own_up, other_up, src_up, swap_up, end_up, load_gate, fin_up, sib_up),
+        "gate": (None, give_gate, src_gate, swap_gate, end_gate, None, fin_gate, sib_gate),
+        "up": (None, give_gate, src_up, swap_up, end_up, None, fin_up, sib_up),
         "out": (None, give_out, src_out, None, end_out, None, fin_out, sib_out),
         "qkv": (None, give_qkv, src_qkv, swap_qkv, end_qkv, None, fin_qkv, sib_qkv),
         "gain": (None, give_gain, src_gain, None, end_gain, None, fin_gain, sib_gain),
@@ -1308,6 +1356,11 @@
     chunks = [(name, i) for name, kind in kinds.items() for i in range(kind[2].shape[0])]
     count = len(chunks)
     loaded = [c for c in range(count) if kinds[chunks[c][0]][0] is not None]
+
+    def group(c):
+        return kinds[chunks[c][0]][1].shape[0]
+
+    heads = [c for c in range(count) if c not in loaded and chunks[c][1] % group(c) == 0]
 
     def remote(source, target, send, recv, where):
         return pltpu.make_async_remote_copy(
@@ -1325,22 +1378,26 @@
 
     def swapped(c):
         name, i = chunks[c]
-        return i if kinds[name][3] is not None else 0
+        return i // group(c) if kinds[name][3] is not None else 0
 
     def pair_copy(c):
         name, i = chunks[c]
         given = kinds[name][1]
-        source = given.at[i] if c in loaded else given.at[i % given.shape[0]]
+        source = given.at[i % given.shape[0]]
         return remote(source, part(c, 2), pair_s.at[c], pair_r.at[c], {"core": 1 - k})
 
     def load_copy(c):
         return pltpu.make_async_copy(part(c, 0), kinds[chunks[c][0]][5].at[c % 2], load_s.at[c])
 
+    def landing(c):
+        name, i = chunks[c]
+        return kinds[name][3].at[i - group(c)]
+
     def swap_copy(c):
-        return remote(part(c, 2), part(c, 3), swap_s.at[c], swap_r.at[c], {"fsdp": f ^ swapped(c)})
+        return remote(part(c, 2), landing(c), swap_s.at[c], swap_r.at[c], {"fsdp": f ^ swapped(c)})
 
     def base(c):
-        return part(c, 3) if swapped(c) else part(c, 2)
+        return landing(c) if swapped(c) else part(c, 2)
 
     def in_copy(c):
         return remote(base(c), part(c, 4), in_s.at[c], in_r.at[c], {"z": inward})
@@ -1360,46 +1417,49 @@
     own_cols = pl.ds(pl.multiple_of(k * half_depth, 128), half_depth)
     other_cols = pl.ds(pl.multiple_of((1 - k) * half_depth, 128), half_depth)
 
-    def out_term(i, cols):
-        size = src_out.shape[1]
-        right = da_all[:, :, cols].reshape(total, half_depth)
-        return tn(attended[:, i * size : (i + 1) * size], right)
-
-    def qkv_term(i, side):
-        start = side * half_depth + i * half
-        return tn(h1[:, start : start + half], dqkv[...])
+    def slab_term(i, side, right):
+        start = side * half_depth + i * (half // 2)
+        return tn(left[:, start : start + half], right)
 
     def term(c, side):
         name, i = chunks[c]
+        if name == "gate":
+            return slab_term(i, side, gate_back[...])
+        if name == "up":
+            return slab_term(i, side, up_back[...])
+        if name == "qkv":
+            return slab_term(i, side, dqkv[...])
         if name == "out":
-            return out_term(i, (own_cols, other_cols)[side])
-        if name == "qkv":
-            return qkv_term(i, side)
+            size = src_out.shape[1]
+            right = da_all[:, :, (own_cols, other_cols)[side]].reshape(total, half_depth)
+            return tn(attended[:, i * size : (i + 2) * size], right)
         return gain_all[...].astype(F32).sum(axis=0)
 
     def stage_give(c):
-        name, i = chunks[c]
-        if c in loaded:
-            return
-        given = kinds[name][1]
-        slots = given.shape[0]
-        if i >= slots:
-            pair_copy(c - slots).wait_send()
-        given[i % slots] = term(c, 1).astype(BF)
-        pair_copy(c).start()
+        given = kinds[chunks[c][0]][1]
+        if c - 1 not in loaded and kinds[chunks[c - 1][0]][1] is given:
+            for n in range(group(c)):
+                pair_copy(c - 1 - n).wait_send()
+        given[...] = term(c, 1).astype(BF).reshape(given.shape)
+        for n in range(group(c)):
+            pair_copy(c + n).start()
+
+    def stage_load(c):
+        pair_copy(c).wait_recv()
+        load_copy(c).wait()
+        add_into(part(c, 2), load_down.at[c % 2])
+        if c + 2 in loaded:
+            load_copy(c + 2).start()
 
     def stage_pair(c):
-        pair_copy(c).wait_recv()
-        if c in loaded:
-            load_copy(c).wait()
-            add_into(part(c, 2), kinds[chunks[c][0]][5].at[c % 2])
-            if c + 2 in loaded:
-                load_copy(c + 2).start()
-        else:
-            target = part(c, 2)
-            target[...] = (target[...].astype(F32) + term(c, 0)).astype(BF)
-        if swapped(c):
-            swap_copy(c).start()
+        value = term(c, 0)
+        size = value.shape[0] // group(c)
+        for n in range(group(c)):
+            pair_copy(c + n).wait_recv()
+            target = part(c + n, 2)
+            target[...] = (target[...].astype(F32) + value[n * size : (n + 1) * size]).astype(BF)
+            if swapped(c + n):
+                swap_copy(c + n).start()
 
     def stage_in(c):
         if swapped(c):
@@ -1456,7 +1516,8 @@
         pltpu.make_async_copy(out_part.at[0], first_out, local_s.at[1]),
         pltpu.make_async_copy(w_out, wide.at[pl.ds(0, w_out.shape[0]), :], local_s.at[2]),
         pltpu.make_async_copy(wqkv_hbm, wqkv, local_s.at[3]),
-        pltpu.make_async_copy(h1_hbm, h1, local_s.at[4]),
+        pltpu.make_async_copy(n2_hbm, left, local_s.at[4]),
+        pltpu.make_async_copy(h1_hbm, left, local_s.at[5]),
     ]
 
     def rms_back(gradient_of, x_ref, gain, acc, write):
@@ -1503,7 +1564,13 @@
         def _(j):
             do_all[j] = nt(da_all[j], wide[0 : w_out.shape[0], :]).astype(BF)
 
-    def piece_attend(j):
+    def piece_attend(j0):
+        @pl.loop(j0, j0 + 2)
+        def _(j):
+            attend_one(j)
+
+    def attend_one(j):
+        here = pl.ds(pl.multiple_of(j * rows, 16), rows)
         vk[...] = pltpu.roll(kv_all[:, j].reshape(vk.shape).astype(F32), 64, 1).astype(BF)
         dk_sum[...] = jnp.zeros_like(dk_sum)
         dv_sum[...] = jnp.zeros_like(dv_sum)
@@ -1533,7 +1600,7 @@
                 dv_sum[...] += tn(weights.astype(BF), do_own)
             turned = jnp.where(lane < 64, parts[0], parts[1]) * (HEAD_DIM**-0.5)
             turned = turned * cosine[...] - swap_halves(turned) * sine[...]
-            dqkv[j * rows : (j + 1) * rows, at] = turned.astype(BF)
+            dqkv[here, at] = turned.astype(BF)
 
         dk = dk_sum[...]
         dv = dv_sum[...]
@@ -1575,7 +1642,6 @@
 
     def piece_dh():
         locals_[3].wait()
-        locals_[4].wait()
         for h in range(2):
             for j in range(plane):
                 start = pl.multiple_of(((f ^ j) * 2 + (k ^ h)) * half, 128)
@@ -1622,29 +1688,27 @@
         for j in peers:
             gain_send(j).wait_recv()
 
-    def when(lags):
-        give, pair, ahead, enter, middle, leave, keep = lags
-        events = []
-        for c in range(count):
-            if c not in loaded:
-                events.append((c + give, 0, stage_give, c))
-            events.append((max(c - ahead, 0) if c in loaded else c + pair, 1, stage_pair, c))
-            events.append((c + enter, 2, stage_in, c))
-            events.append((c + middle, 3, stage_mid, c))
-            events.append((c + leave, 4, stage_out, c))
-            events.append((c + keep, 5, stage_keep, c))
-        return events
-
-    events = when((-2, -1, 3, 1, 2, 3, 4))
-    order = {
-        piece_mixed: 2, piece_do: 4, piece_kv_line: 8, piece_outputs: 8, piece_kv_sum: 9, piece_dh: 9,
-        piece_input: 11, piece_gain: 12,
-    }
-    events += [(tick, 6 + n, piece, None) for n, (piece, tick) in enumerate(order.items())]
-    attend_at = (4, 5, 6, 7)
-    for j in range(plane):
-        events.append((attend_at[j], 14 + j, piece_attend, j))
-    events.append((attend_at[-1], 18, kv_pair.start, None))
+    give_lag, pair_lag, load_lag, in_lag, mid_lag, out_lag, keep_lag = LAGS
+    events = []
+    for c in loaded:
+        events.append((max(c + load_lag, 0), 1, stage_load, c))
+    for c in heads:
+        events.append((c + give_lag, 0, stage_give, c))
+        events.append((c + pair_lag, 1, stage_pair, c))
+    for c in range(count):
+        events.append((c + in_lag, 2, stage_in, c))
+        events.append((c + mid_lag, 3, stage_mid, c))
+        events.append((c + out_lag, 4, stage_out, c))
+        events.append((c + keep_lag, 5, stage_keep, c))
+    steps = (piece_mixed, piece_do, piece_kv_line, piece_outputs, piece_kv_sum, piece_dh, piece_input, piece_gain)
+    events += [(tick, 6 + n, piece, None) for n, (piece, tick) in enumerate(zip(steps, STEPS))]
+    for j in range(0, plane, 2):
+        events.append((ATTEND[j // 2], 20 + j, piece_attend, j))
+    events.append((ATTEND[-1], 30, kv_pair.start, None))
+    first_qkv = [c for c in heads if chunks[c][0] == "qkv"][0]
+    last_up = [c for c in heads if chunks[c][0] == "up"][-1]
+    events.append((last_up + pair_lag, 31, locals_[5].start, None))
+    events.append((first_qkv + give_lag, -1, locals_[5].wait, None))
     events.sort(key=lambda e: e[:2])
 
     for j in peers:
@@ -1653,14 +1717,16 @@
         pair_copy(c).start()
     for c in loaded[:2]:
         load_copy(c).start()
-    for copy in locals_:
+    for copy in locals_[:5]:
         copy.start()
+    locals_[4].wait()
     for _, _, act, which in events:
         act() if which is None else act(which)
 
     for c in range(count):
-        name, i = chunks[c]
-        if c in loaded or i + kinds[name][1].shape[0] >= kinds[name][2].shape[0]:
+        given = kinds[chunks[c][0]][1]
+        later = [n for n in heads if n > c and kinds[chunks[n][0]][1] is given]
+        if c in loaded or not later:
             pair_copy(c).wait_send()
         if swapped(c):
             swap_copy(c).wait_send()
@@ -1692,8 +1758,8 @@
 
 
 def back_pass(
-    limits, own, other, back_part, out_part, w_out, wqkv, h1, mixed, branch_own, x_own, gain_one, gain_two,
-    attended, queries, lse, kv_all, kp, cosine, sine,
+    limits, own_down, other_down, back_part, out_part, w_out, wqkv, h1, n2, gate_back, up_back,
+    mixed, branch_own, x_own, gain_one, gain_two, attended, queries, lse, kv_all, kp, cosine, sine,
 ):
     count, line = lax.axis_size("fsdp"), lax.axis_size("z")
     rows, depth = mixed.shape
@@ -1701,9 +1767,14 @@
     half = half_depth // count
     q_width = attended.shape[1]
     keys = kv_all.shape[0] * rows
-    shapes = [x.shape for x in own] + [
-        (2, q_width // 2, half_depth),
-        (count, half, q_width + 128),
+    ff = gate_back.shape[1]
+    slabs = (2 * count, half // 2, ff)
+    shapes = [
+        own_down.shape,
+        slabs,
+        slabs,
+        (4, q_width // 4, half_depth),
+        (2 * count, half // 2, q_width + 128),
         (1, 16, depth),
     ]
     anywhere = pl.BlockSpec(memory_space=pl.ANY)
@@ -1715,7 +1786,7 @@
     dma = lambda n: pltpu.SemaphoreType.DMA((n,))
     scratch = (
         [pltpu.VMEM(s, BF) for s in shapes]
-        + [pltpu.VMEM(shapes[i], BF) for i in (1, 2, 4)]
+        + [pltpu.VMEM((shapes[i][0] - 2,) + shapes[i][1:], BF) for i in (1, 2, 4)]
         + [pltpu.VMEM(s, BF) for s in shapes]
         + [pltpu.VMEM((2,) + shapes[i][1:], BF) for i in (0, 1, 3, 4)]
         + [pltpu.VMEM(shapes[5], BF)]
@@ -1741,7 +1812,7 @@
             pltpu.VMEM((count, 16, depth), BF),
         ]
         + [dma(chunk_count)] * 13
-        + [pltpu.SemaphoreType.REGULAR, dma(5)]
+        + [pltpu.SemaphoreType.REGULAR, dma(6)]
         + [dma(count - 1)] * 8
         + [dma(1)] * 2
         + [dma(line - 1)] * 2
@@ -1750,7 +1821,7 @@
     out = pl.pallas_call(
         back_kernel,
         out_shape=ends + ends + [act, act],
-        in_specs=[local] + [anywhere] * 11 + [local] * 12,
+        in_specs=[local] + [anywhere] * 8 + [local] * 14,
         out_specs=[anywhere] * 12 + [local] * 2,
         scratch_shapes=scratch,
         compiler_params=pltpu.CompilerParams(
@@ -1761,8 +1832,8 @@
         ),
         name="back_pass",
     )(
-        limits, *own, *other, back_part, out_part, w_out, wqkv, h1, mixed, branch_own, x_own, gain_one, gain_two,
-        attended, queries, lse, kv_all, kp, cosine, sine,
+        limits, own_down, other_down, back_part, out_part, w_out, wqkv, h1, n2, gate_back, up_back,
+        mixed, branch_own, x_own, gain_one, gain_two, attended, queries, lse, kv_all, kp, cosine, sine,
     )
     return out[:6], out[6:12], out[12], out[13]
 
@@ -1898,30 +1969,26 @@
 ):
     seqs, rows, depth = tokens.shape
     count = lax.axis_size("fsdp")
-    k = lax.axis_index("core")
     slab = depth // count
-    half, half_depth = slab // 2, depth // 2
     x_own = tokens.reshape(rows, depth)
     (
-        h1, queries, lse, attended, mixed, n2, hidden, gate_back, up_back, back_part, out_part,
-        gain_one, gain_two, limits, cosine, sine, kp, kv_all, branch, wqkv,
+        h1, queries, lse, attended, mixed, n2, limits, cosine, sine, kp, gain_one, gain_two, kv_all, branch, wqkv,
+        gate_back, up_back, back_part, out_part, own_down, other_down,
     ) = front_pass(
         x_own, cotangent.reshape(rows, depth), lengths, attn_gain, mlp_gain,
         w_query, w_key, w_value, w_out, w_gate, w_up, w_down,
     )
-    flat = branch.reshape(count * rows, depth)
-    own, other = [], []
-    for terms, side in ((own, 0), (other, 1)):
-        right = lax.dynamic_slice_in_dim(flat, (k ^ side) * half_depth, half_depth, 1)
-        left = n2[:, side * half_depth : (side + 1) * half_depth]
-        terms.append(tn(hidden, right).astype(BF).reshape(4, -1, half_depth))
-        terms.append(tn(left, gate_back).astype(BF).reshape(count, half, -1))
-        terms.append(tn(left, up_back).astype(BF).reshape(count, half, -1))
+    own_down, other_down = (x.reshape(8, -1, depth // 2) for x in (own_down, other_down))
     owns, sibs, outputs, input_grad = back_pass(
-        limits, own, other, back_part.reshape(count, rows, depth), out_part.reshape(count, rows, depth), w_out,
-        wqkv, h1, mixed, branch[0], x_own, gain_one, gain_two, attended, queries, lse, kv_all, kp, cosine, sine,
+        limits, own_down, other_down, back_part.reshape(count, rows, depth), out_part.reshape(count, rows, depth),
+        w_out, wqkv, h1, n2, gate_back, up_back,
+        mixed, branch[0], x_own, gain_one, gain_two, attended, queries, lse, kv_all, kp, cosine, sine,
     )
 
+    def whole(x):
+        return x.reshape(4, -1, x.shape[2]) if x.shape[0] > 1 else x
+
+    owns, sibs = [whole(x) for x in owns], [whole(x) for x in sibs]
     down_grad, gate_grad, up_grad, out_grad, query_grad, key_grad, value_grad, gain_a, gain_m = finish(owns, sibs)
     return (
         outputs.reshape(seqs, rows, depth),

time: 544 us -> 491 us (0.903)
  Pallas kernels: 503 us -> 479 us
  matrix products: 22.1 us -> 0 us
    dot_general x6 -> x0, matrix products: 22.1 us -> none  [tn(): lax.dot_general(a, b, (((0,), (0,)), ((), ())), preferred_element_type=F32)]
    pallas_call x1, Pallas kernels: 176 us -> 159 us  [front_pass(): pl.pallas_call(front_kernel, out_shape=outs, in_specs=[pl.BlockSpec(memor...]
    pallas_call x1, Pallas kernels: 303 us -> 295 us  [back_pass(): pl.pallas_call(back_kernel, out_shape=ends + ends + [act, act], in_specs=...]
where the time goes in v6:
time: 491 us; the launch traced here: 486 us
  Pallas kernels  479 us (98%)
  local copies, waits for them, and re-layouts  6.35 us (1%)
    pallas_call x1, Pallas kernels, back_pass(): pl.pallas_call(back_kernel, out_shape=ends + ends + [act, act], in_specs=...  295 us
    pallas_call x1, Pallas kernels, front_pass(): pl.pallas_call(front_kernel, out_shape=outs, in_specs=[pl.BlockSpec(memor...  159 us
    pallas_call x1, Pallas kernels, finish(): pl.pallas_call(finish_kernel, out_shape=[sds(s, F32) for s in shapes], in...  24.3 us

profile of v6, /device:TPU:0, one launch (start us, length us, event | category | flops | bytes accessed | tf_op | source)
XLA Modules:
  0.0 486.4 jit_solution(17832039534138380404)
XLA Ops:
  1.3 1.3 reshape.82.attn_gain
  2.5 1.3 reshape.83.mlp_gain
  3.8 159.2 %front_pass.1 = (bf16[512,2048]{1,0:T(8,128)(2,1)}, bf16[4,128,512]{2,1,0:T(8,128)(2,1)}, f32[4,128,512]{2,1,0:T(8,128)}, bf16[512,512]{1,0:T(8,128)(2,1)}, f32[...) custom-call(s32[1]{0:T(128)S(6)} %copy.29.length_ref, ...), custom_call_target="tpu_custom_call" | custom-call | tf_op jit(solution)/shard_map/front_pass/pallas_call | solution.py:1294
  163.0 1.9 slice_bitcast_fusion.branch_own
  164.9 295.1 %back_pass.1 = (bf16[8,176,1024]{2,1,0:T(8,128)(2,1)}, bf16[8,128,1408]{2,1,0:T(8,128)(2,1)}, bf16[8,128,1408]{2,1,0:T(8,128)(2,1)}, bf16[4,128,1024]{2,1,0:T(8,...) custom-call(f32[4,128,128]{2,1,0:T(8,128)} %get-tuple-element.54.lim, ...), custom_call_target="tpu_custom_call" | custom-call | flops 99999997952 | bytes 1000000000 | tf_op jit(solution)/shard_map/back_pass/pallas_call | solution.py:1821
  460.0 0.0 copy-start.1
  460.1 0.0 copy-start
  460.1 24.3 %finish.1 = (f32[1408,2048]{1,0:T(8,128)}, f32[512,5632]{1,0:T(8,128)}, f32[512,5632]{1,0:T(8,128)}, f32[512,2048]{1,0:T(8,128)}, f32[512,2048]{1,0:T(8,128)}, /...) custom-call(bf16[4,352,1024]{2,1,0:T(8,128)(2,1)} %bitcast.20, ...), custom_call_target="tpu_custom_call" | custom-call | tf_op jit(solution)/shard_map/finish/pallas_call | solution.py:1944
  484.4 0.0 copy-done.1
  484.4 1.0 copy.30
  485.4 0.0 copy-done
  485.4 1.0 copy.31
Async XLA Ops:
  460.0 24.4 %copy-start.1 = (f32[128,2048]{1,0:T(8,128)S(1)}, f32[128,2048]{1,0:T(8,128)}, u32[]{:S(2)}) copy-start(f32[128,2048]{1,0:T(8,128)} %get-tuple-element.75) | copy-start | bytes 3145732
  460.1 25.3 %copy-start = (f32[128,2048]{1,0:T(8,128)S(1)}, f32[128,2048]{1,0:T(8,128)}, u32[]{:S(2)}) copy-start(f32[128,2048]{1,0:T(8,128)} %get-tuple-element.76) | copy-start | bytes 3145732

commit v7 on v6

--- a/solution.py
+++ b/solution.py
@@ -19,9 +19,9 @@
 BF = jnp.bfloat16
 F32 = jnp.float32
 VMEM_BYTES = 56 * 1024 * 1024
-LAGS = (-4, -3, -4, 0, 2, 4, 6)
-STEPS = (5, 9, 16, 16, 19, 19, 24, 26)
-ATTEND = (10, 13)
+LAGS = (0, 2, 4, 6)
+AHEAD = (1, 4)
+STEPS = (0, 1, 6, 11, 12, 13, 14, 16, 17, 19, 23, 23, 22, 27, 29)
 
 
 def params(**kw):
@@ -687,13 +687,13 @@
 
 
 def front_kernel(
-    length_ref, attn_gain, mlp_gain, start_cos, start_sin, step_cos, step_sin,
+    length_ref, both_gains, start_cos, start_sin, step_cos, step_sin,
     tokens, cotangent, w_query, w_key, w_value, w_out, w_gate, w_up, w_down,
     h1_out, queries_out, lse_out, attended_out, mixed_out, n2_out, limits_out, cosine_out, sine_out, kp_out,
-    gain_one_out, gain_two_out, kv_out, branch_out, wqkv_out, gate_back_out, up_back_out, back_out, out_out,
-    own_down, other_down,
+    gain_one_out, gain_two_out, kv_out, branch_out, wqkv_out, gate_back_out, up_back_out, hidden_out,
+    gate_own_out, gate_sib_out, up_own_out, up_sib_out,
     h1, queries, lse, attended, mixed, n2, limits, cosine, sine, kp, gain_one, gain_two,
-    hidden, gate_back, up_back, back_part, out_part, down_own, down_other,
+    gate_back, up_back, hidden, grad,
     notes, x_all, wqkv, keys_in, values_in, kv_give, gate_own, gate_sib, up_own, up_sib, down,
     kv_all, vk, w_o, part, landed, relay, relayed, n2_all, branch_all, cot_in,
     local_s, store_s, note_s, note_r, tok_s, tok_r, tof_s, tof_r, wq_s, wq_r, wk_s, wk_r, wp_s, wp_r, wkp_s, wkp_r,
@@ -888,8 +888,8 @@
         (h1, h1_out), (queries, queries_out), (lse, lse_out), (attended, attended_out), (mixed, mixed_out),
         (n2, n2_out), (limits, limits_out), (cosine, cosine_out), (sine, sine_out), (kp, kp_out),
         (gain_one, gain_one_out), (gain_two, gain_two_out), (kv_all, kv_out), (branch_all, branch_out),
-        (wqkv, wqkv_out), (gate_back, gate_back_out), (up_back, up_back_out), (back_part, back_out),
-        (out_part, out_out), (down_own, own_down), (down_other, other_down),
+        (wqkv, wqkv_out), (gate_back, gate_back_out), (up_back, up_back_out), (hidden, hidden_out),
+        (gate_own, gate_own_out), (gate_sib, gate_sib_out), (up_own, up_own_out), (up_sib, up_sib_out),
     ]
 
     def store(n):
@@ -898,7 +898,7 @@
     length = length_ref[0]
     place = lax.broadcasted_iota(jnp.int32, (16, slab), 0)
     high, low = (length // 64).astype(F32), (length % 64).astype(F32)
-    note = jnp.where(place == 0, attn_gain[...].astype(F32), mlp_gain[...].astype(F32))
+    note = jnp.where(place == 0, both_gains[0:1, :].astype(F32), both_gains[1:2, :].astype(F32))
     note = jnp.where(place == 2, high, jnp.where(place == 3, low, note))
     notes[0] = note.astype(BF)
     for j in peers:
@@ -1035,6 +1035,14 @@
             kv_pair(s).wait_recv()
 
     local[6].wait()
+
+    def by_columns(act):
+        @pl.loop(0, ff // 256)
+        def _(n):
+            act(pl.ds(pl.multiple_of(n * 256, 256), 256))
+
+        if ff % 256:
+            act(pl.ds(ff // 256 * 256, ff % 256))
 
     def relay_on(far, late, which, j):
         mix_first[far].wait_recv()
@@ -1109,8 +1117,22 @@
     n2_gather.start()
     early_stores[4].start()
     branch_gather.arrive()
+    local[11].wait()
+
+    def down_grad(at):
+        grad[:, at] = nt(branch_all[...].reshape(total, depth), down[at, :])
+
+    by_columns(down_grad)
     n2_gather.forward()
     cross_on(3)
+    for n in range(7, 11):
+        local[n].wait()
+    for j in peers:
+        gate_pair(j).wait_recv()
+        up_pair(j).wait_recv()
+    weight_stores = [store(n) for n in range(18, 22)]
+    for copy in weight_stores:
+        copy.start()
     n2_gather.arrive()
 
     @pl.loop(0, total // 16)
@@ -1125,14 +1147,9 @@
                 n2[at, c : c + half] = n2_all[j, from_row, from_]
 
     early_stores[5].start()
-    later = [store(n) for n in range(12, 19)]
+    later = [store(n) for n in range(12, 18)]
     for n in range(3):
         later[n].start()
-    for n in range(7, 12):
-        local[n].wait()
-    for j in peers:
-        gate_pair(j).wait_recv()
-        up_pair(j).wait_recv()
 
     def feed(at):
         width = at.size
@@ -1146,53 +1163,13 @@
         up = through(up_own, up_sib)
         sigmoid = 1.0 / (1.0 + jnp.exp(-gate))
         hidden[:, at] = (gate * sigmoid * up).astype(BF)
-        grad = nt(branch_all[...].reshape(total, depth), down[at, :])
-        gate_back[:, at] = (grad * up * sigmoid * (1.0 + gate * (1.0 - sigmoid))).astype(BF)
-        up_back[:, at] = (grad * gate * sigmoid).astype(BF)
-
-    @pl.loop(0, ff // 256)
-    def _(n):
-        feed(pl.ds(pl.multiple_of(n * 256, 256), 256))
-
-    if ff % 256:
-        feed(pl.ds(ff // 256 * 256, ff % 256))
-
-    for h, gate_side, up_side in ((0, gate_own, up_own), (1, gate_sib, up_sib)):
-
-        @pl.loop(0, plane)
-        def _(b):
-            to = pl.ds(pl.multiple_of(((f ^ b) * 2 + (k ^ h)) * half, 128), half)
-            value = nt(gate_back[...], gate_side[b]) + nt(up_back[...], up_side[b])
-            back_part[:, to] = value.astype(BF)
-
-    later[3].start()
-    later[4].start()
-    later[5].start()
-
-    def down_term(at, side, target):
-        spot = pl.ds(pl.multiple_of((k ^ side) * (depth // 2), 128), depth // 2)
-        right = branch_all[:, :, spot].reshape(total, depth // 2)
-        target[at, :] = tn(hidden[:, at], right).astype(BF)
-
-    for side, target in ((0, down_own), (1, down_other)):
-
-        @pl.loop(0, ff // 256)
-        def _(n):
-            down_term(pl.ds(pl.multiple_of(n * 256, 256), 256), side, target)
-
-        if ff % 256:
-            down_term(pl.ds(ff // 256 * 256, ff % 256), side, target)
-
-    ends = [store(19), store(20)]
-    for copy in ends:
-        copy.start()
-
-    @pl.loop(0, depth // 256)
-    def _(n):
-        at = pl.ds(pl.multiple_of(n * 256, 256), 256)
-        out_part[:, at] = nn(hidden[...], down[:, at]).astype(BF)
-
-    later[6].start()
+        back = grad[:, at]
+        gate_back[:, at] = (back * up * sigmoid * (1.0 + gate * (1.0 - sigmoid))).astype(BF)
+        up_back[:, at] = (back * gate * sigmoid).astype(BF)
+
+    by_columns(feed)
+    for n in range(3, 6):
+        later[n].start()
     for gather in (token_gather, branch_gather, n2_gather):
         gather.close()
     for copy in mix_first.values():
@@ -1220,7 +1197,7 @@
         def _():
             kv_pair(s).wait_send()
 
-    for copy in early_stores + later + ends:
+    for copy in early_stores + later + weight_stores:
         copy.wait()
 
 
@@ -1258,13 +1235,10 @@
         sds((depth, width), BF),
         sds((total, ff), BF),
         sds((total, ff), BF),
-        sds((total, depth), BF),
-        sds((total, depth), BF),
-        sds((ff, depth // 2), BF),
-        sds((ff, depth // 2), BF),
-    ]
+        sds((total, ff), BF),
+    ] + [sds((plane, half, ff), BF)] * 4
     held = [pltpu.VMEM(o.shape, o.dtype) for o in outs]
-    held = held[:12] + [pltpu.VMEM((total, ff), BF)] + held[15:]
+    held = held[:12] + held[15:18] + [pltpu.VMEM((total, ff), F32)]
     slabs = pltpu.VMEM((plane, half, ff), BF)
     scratch = held + [
         pltpu.VMEM((plane, 16, slab), BF),
@@ -1289,20 +1263,20 @@
         pltpu.VMEM((plane,) + act, BF),
         pltpu.VMEM(act, BF),
     ]
-    sems = [12, 21, 3, 3, 2, 2, 2, 2, 3, 3, 3, 3, 3, 3, 1, 1, 3, 3, 4, 4, 3, 3, 3, 3, 3, 3, 3, 3, 3, 3]
+    sems = [12, 22, 3, 3, 2, 2, 2, 2, 3, 3, 3, 3, 3, 3, 1, 1, 3, 3, 4, 4, 3, 3, 3, 3, 3, 3, 3, 3, 3, 3]
     sems += [2, 2, 2, 2, 6, 6, 2, 2, 2, 2]
     return pl.pallas_call(
         front_kernel,
         out_shape=outs,
-        in_specs=[pl.BlockSpec(memory_space=pltpu.SMEM)] + [local] * 6 + [anywhere] * 9,
-        out_specs=[anywhere] * 21,
+        in_specs=[pl.BlockSpec(memory_space=pltpu.SMEM)] + [local] * 5 + [anywhere] * 9,
+        out_specs=[anywhere] * 22,
         scratch_shapes=scratch + [dma(n) for n in sems],
         compiler_params=pltpu.CompilerParams(
             vmem_limit_bytes=62 * 1024 * 1024, has_side_effects=True
         ),
         name="front_pass",
     )(
-        lengths, attn_gain.reshape(1, slab), mlp_gain.reshape(1, slab), *rotary_parts(slot, rows),
+        lengths, jnp.stack([attn_gain, mlp_gain]), *rotary_parts(slot, rows),
         tokens, cotangent, w_query, w_key, w_value, w_out, w_gate, w_up, w_down,
     )
 
@@ -1315,24 +1289,26 @@
 
 
 def back_kernel(
-    limits,
-    own_down, other_down, back_part, out_part, w_out, wqkv_hbm, h1_hbm, n2_hbm,
-    gate_back, up_back, mixed, branch_own, x_own, gain_one, gain_two,
-    attended, queries, lse, kv_all, kp, cosine, sine,
+    limits_in, gate_back_in, up_back_in, hidden_in, mixed_in, x_own_in, gain_one_in, gain_two_in,
+    attended_in, queries_in, lse_in, kv_all_in, kp_in, cosine_in, sine_in,
+    branch, w_out, w_down, wqkv, h1_hbm, n2_hbm, gate_own, gate_sib, up_own, up_sib,
     fin_down, fin_gate, fin_up, fin_out, fin_qkv, fin_gain,
     sib_down, sib_gate, sib_up, sib_out, sib_qkv, sib_gain,
-    outputs, input_grad,
+    outputs, input_grad_out,
+    limits, gate_back, up_back, hidden, mixed, x_own, gain_one, gain_two,
+    attended, queries, lse, kv_all, kp, cosine, sine, branch_own, input_grad,
     src_down, src_gate, src_up, src_out, src_qkv, src_gain,
     swap_gate, swap_up, swap_qkv,
     end_down, end_gate, end_up, end_out, end_qkv, end_gain,
-    load_down, give_gate, give_out, give_qkv, give_gain,
-    landed, landed_out, first_back, first_out, da_all, wide, do_all, dqkv, wqkv, left,
+    give_down, give_gate, give_out, give_qkv, give_gain,
+    landed, landed_out, weights, down_blocks, qkv_blocks, part, da_all, wide, do_all, dqkv, left,
     vk, dk_sum, dv_sum, kv_part, kv_land, kv_mine, kv_line, gain_acc, gain_all,
-    pair_s, pair_r, load_s, swap_s, swap_r, in_s, in_r, mid_s, mid_r, out_s, done_s, back_s, back_r, ready,
-    local_s, rs_s, rs_r, ro_s, ro_r, ag_s, ag_r, rq_s, rq_r, kp_s, kp_r, kz_s, kz_r, ga_s, ga_r,
+    pair_s, pair_r, swap_s, swap_r, in_s, in_r, mid_s, mid_r, out_s, done_s, back_s, back_r, ready,
+    local_s, weight_s, rs_s, rs_r, ro_s, ro_r, ag_s, ag_r, rq_s, rq_r, kp_s, kp_r, kz_s, kz_r, ga_s, ga_r,
 ):
     f, z, k = lax.axis_index("fsdp"), lax.axis_index("z"), lax.axis_index("core")
     plane, line = lax.axis_size("fsdp"), lax.axis_size("z")
+    branch_flat = branch
     outer = (z == 0) | (z == line - 1)
     inner = jnp.logical_not(outer)
     inward = jnp.where(z < line // 2, z + 1, z - 1)
@@ -1346,21 +1322,20 @@
     peers = range(1, plane)
 
     kinds = {
-        "down": (own_down, other_down, src_down, None, end_down, load_down, fin_down, sib_down),
-        "gate": (None, give_gate, src_gate, swap_gate, end_gate, None, fin_gate, sib_gate),
-        "up": (None, give_gate, src_up, swap_up, end_up, None, fin_up, sib_up),
-        "out": (None, give_out, src_out, None, end_out, None, fin_out, sib_out),
-        "qkv": (None, give_qkv, src_qkv, swap_qkv, end_qkv, None, fin_qkv, sib_qkv),
-        "gain": (None, give_gain, src_gain, None, end_gain, None, fin_gain, sib_gain),
+        "down": (src_down, None, end_down, give_down, fin_down, sib_down),
+        "gate": (src_gate, swap_gate, end_gate, give_gate, fin_gate, sib_gate),
+        "up": (src_up, swap_up, end_up, give_gate, fin_up, sib_up),
+        "out": (src_out, None, end_out, give_out, fin_out, sib_out),
+        "qkv": (src_qkv, swap_qkv, end_qkv, give_qkv, fin_qkv, sib_qkv),
+        "gain": (src_gain, None, end_gain, give_gain, fin_gain, sib_gain),
     }
-    chunks = [(name, i) for name, kind in kinds.items() for i in range(kind[2].shape[0])]
+    chunks = [(name, i) for name, kind in kinds.items() for i in range(kind[0].shape[0])]
     count = len(chunks)
-    loaded = [c for c in range(count) if kinds[chunks[c][0]][0] is not None]
 
     def group(c):
-        return kinds[chunks[c][0]][1].shape[0]
-
-    heads = [c for c in range(count) if c not in loaded and chunks[c][1] % group(c) == 0]
+        return kinds[chunks[c][0]][3].shape[0]
+
+    heads = [c for c in range(count) if chunks[c][1] % group(c) == 0]
 
     def remote(source, target, send, recv, where):
         return pltpu.make_async_remote_copy(
@@ -1372,47 +1347,51 @@
             device_id_type=pl.DeviceIdType.MESH,
         )
 
-    def part(c, which):
+    def swapped(c):
+        name, i = chunks[c]
+        return i // group(c) if kinds[name][1] is not None else 0
+
+    def source(c):
+        return part_of(c, 0)
+
+    def part_of(c, which):
         name, i = chunks[c]
         return kinds[name][which].at[i]
 
-    def swapped(c):
-        name, i = chunks[c]
-        return i // group(c) if kinds[name][3] is not None else 0
+    def given(c):
+        return kinds[chunks[c][0]][3]
+
+    def end(c):
+        return part_of(c, 2)
 
     def pair_copy(c):
-        name, i = chunks[c]
-        given = kinds[name][1]
-        source = given.at[i % given.shape[0]]
-        return remote(source, part(c, 2), pair_s.at[c], pair_r.at[c], {"core": 1 - k})
-
-    def load_copy(c):
-        return pltpu.make_async_copy(part(c, 0), kinds[chunks[c][0]][5].at[c % 2], load_s.at[c])
+        start = given(c).at[chunks[c][1] % group(c)]
+        return remote(start, source(c), pair_s.at[c], pair_r.at[c], {"core": 1 - k})
 
     def landing(c):
         name, i = chunks[c]
-        return kinds[name][3].at[i - group(c)]
+        return kinds[name][1].at[i - group(c)]
 
     def swap_copy(c):
-        return remote(part(c, 2), landing(c), swap_s.at[c], swap_r.at[c], {"fsdp": f ^ swapped(c)})
+        return remote(source(c), landing(c), swap_s.at[c], swap_r.at[c], {"fsdp": f ^ swapped(c)})
 
     def base(c):
-        return landing(c) if swapped(c) else part(c, 2)
+        return landing(c) if swapped(c) else source(c)
 
     def in_copy(c):
-        return remote(base(c), part(c, 4), in_s.at[c], in_r.at[c], {"z": inward})
+        return remote(base(c), end(c), in_s.at[c], in_r.at[c], {"z": inward})
 
     def mid_copy(c):
-        return remote(base(c), part(c, 4), mid_s.at[c], mid_r.at[c], {"z": inward})
+        return remote(base(c), end(c), mid_s.at[c], mid_r.at[c], {"z": inward})
 
     def out_copy(c):
-        return remote(part(c, 4), part(c, 4), out_s.at[c], mid_r.at[c], {"z": outward})
+        return remote(end(c), end(c), out_s.at[c], mid_r.at[c], {"z": outward})
 
     def keep_copy(c):
-        return pltpu.make_async_copy(part(c, 4), part(c, 6), done_s.at[c])
+        return pltpu.make_async_copy(end(c), part_of(c, 4), done_s.at[c])
 
     def back_copy(c):
-        return remote(part(c, 4), part(c, 7), back_s.at[c], back_r.at[c], {"core": 1 - k})
+        return remote(end(c), part_of(c, 5), back_s.at[c], back_r.at[c], {"core": 1 - k})
 
     own_cols = pl.ds(pl.multiple_of(k * half_depth, 128), half_depth)
     other_cols = pl.ds(pl.multiple_of((1 - k) * half_depth, 128), half_depth)
@@ -1423,6 +1402,9 @@
 
     def term(c, side):
         name, i = chunks[c]
+        if name == "down":
+            right = wide[0:total, (own_cols, other_cols)[side]]
+            return tn(hidden[:, i * 128 : (i + 1) * 128], right)
         if name == "gate":
             return slab_term(i, side, gate_back[...])
         if name == "up":
@@ -1436,27 +1418,20 @@
         return gain_all[...].astype(F32).sum(axis=0)
 
     def stage_give(c):
-        given = kinds[chunks[c][0]][1]
-        if c - 1 not in loaded and kinds[chunks[c - 1][0]][1] is given:
+        slots = given(c)
+        if c and given(c - 1) is slots:
             for n in range(group(c)):
                 pair_copy(c - 1 - n).wait_send()
-        given[...] = term(c, 1).astype(BF).reshape(given.shape)
+        slots[...] = term(c, 1).astype(BF).reshape(slots.shape)
         for n in range(group(c)):
             pair_copy(c + n).start()
-
-    def stage_load(c):
-        pair_copy(c).wait_recv()
-        load_copy(c).wait()
-        add_into(part(c, 2), load_down.at[c % 2])
-        if c + 2 in loaded:
-            load_copy(c + 2).start()
 
     def stage_pair(c):
         value = term(c, 0)
         size = value.shape[0] // group(c)
         for n in range(group(c)):
             pair_copy(c + n).wait_recv()
-            target = part(c + n, 2)
+            target = source(c + n)
             target[...] = (target[...].astype(F32) + value[n * size : (n + 1) * size]).astype(BF)
             if swapped(c + n):
                 swap_copy(c + n).start()
@@ -1473,7 +1448,7 @@
         @pl.when(inner)
         def _():
             in_copy(c).wait_recv()
-            add_into(base(c), part(c, 4))
+            add_into(base(c), end(c))
             pl.semaphore_signal(
                 ready, inc=1, device_id={"z": inward}, device_id_type=pl.DeviceIdType.MESH
             )
@@ -1484,7 +1459,7 @@
         @pl.when(inner)
         def _():
             mid_copy(c).wait_recv()
-            add_into(part(c, 4), base(c))
+            add_into(end(c), base(c))
             out_copy(c).start()
 
     def stage_keep(c):
@@ -1496,10 +1471,12 @@
         back_copy(c).start()
 
     def back_send(j):
-        return remote(back_part.at[j], landed.at[j - 1], rs_s.at[j - 1], rs_r.at[j - 1], {"fsdp": f ^ j})
+        mine = part.at[pl.ds(j * rows, rows), :]
+        return remote(mine, landed.at[j - 1], rs_s.at[j - 1], rs_r.at[j - 1], {"fsdp": f ^ j})
 
     def out_send(j):
-        return remote(out_part.at[j], landed_out.at[j - 1], ro_s.at[j - 1], ro_r.at[j - 1], {"fsdp": f ^ j})
+        mine = part.at[pl.ds(j * rows, rows), :]
+        return remote(mine, landed_out.at[j - 1], ro_s.at[j - 1], ro_r.at[j - 1], {"fsdp": f ^ j})
 
     def da_send(j):
         return remote(da_all.at[0], da_all.at[j], ag_s.at[j - 1], ag_r.at[j - 1], {"fsdp": f ^ j})
@@ -1511,14 +1488,79 @@
     def gain_send(j):
         return remote(gain_all.at[0], gain_all.at[j], ga_s.at[j - 1], ga_r.at[j - 1], {"fsdp": f ^ j})
 
-    locals_ = [
-        pltpu.make_async_copy(back_part.at[0], first_back, local_s.at[0]),
-        pltpu.make_async_copy(out_part.at[0], first_out, local_s.at[1]),
-        pltpu.make_async_copy(w_out, wide.at[pl.ds(0, w_out.shape[0]), :], local_s.at[2]),
-        pltpu.make_async_copy(wqkv_hbm, wqkv, local_s.at[3]),
-        pltpu.make_async_copy(n2_hbm, left, local_s.at[4]),
-        pltpu.make_async_copy(h1_hbm, left, local_s.at[5]),
-    ]
+    moves = {
+        "branch": (branch_flat, wide.at[pl.ds(0, total), :]), "hidden": (hidden_in, hidden), "n2": (n2_hbm, left),
+        "gate_back": (gate_back_in, gate_back), "up_back": (up_back_in, up_back), "mixed": (mixed_in, mixed),
+        "branch_own": (branch_flat.at[pl.ds(0, rows), :], branch_own), "gain_two": (gain_two_in, gain_two),
+        "queries": (queries_in, queries), "lse": (lse_in, lse), "kv_all": (kv_all_in, kv_all),
+        "limits": (limits_in, limits), "kp": (kp_in, kp), "cosine": (cosine_in, cosine), "sine": (sine_in, sine),
+        "attended": (attended_in, attended), "x_own": (x_own_in, x_own), "gain_one": (gain_one_in, gain_one),
+        "w_out": (w_out, wide.at[pl.ds(0, w_out.shape[0]), :]), "h1": (h1_hbm, left),
+        "outputs": (mixed, outputs), "input_grad": (input_grad, input_grad_out),
+    }
+    moves = {
+        name: pltpu.make_async_copy(*ends, local_s.at[n]) for n, (name, ends) in enumerate(moves.items())
+    }
+
+    def weight_loads(h, j):
+        pairs_of = ((gate_own, up_own), (gate_sib, up_sib))[h]
+        return [
+            pltpu.make_async_copy(w.at[j], weights.at[j % 2, n], weight_s.at[j % 2, n])
+            for n, w in enumerate(pairs_of)
+        ]
+
+    def columns_of(h, j):
+        return pl.ds(pl.multiple_of(((f ^ j) * 2 + (k ^ h)) * half, 128), half)
+
+    def piece_back(h):
+        @pl.loop(0, plane)
+        def _(j):
+            @pl.when(j + 1 < plane)
+            def _():
+                for copy in weight_loads(h, j + 1):
+                    copy.start()
+
+            for copy in weight_loads(h, j):
+                copy.wait()
+            value = nt(gate_back[...], weights[j % 2, 0]) + nt(up_back[...], weights[j % 2, 1])
+            part[:, columns_of(h, j)] = value.astype(BF)
+
+        if h == 0:
+            for copy in weight_loads(1, 0):
+                copy.start()
+        if h == 1:
+            for j in peers:
+                back_send(j).start()
+
+    def down_at(b):
+        size = depth // 8
+        return pl.ds(pl.multiple_of(b * size, size), size)
+
+    def down_load(b):
+        return pltpu.make_async_copy(w_down.at[:, down_at(b)], down_blocks.at[b % 2], weight_s.at[b % 2, 0])
+
+    def piece_out(h):
+        if h == 0:
+            for j in peers:
+                back_send(j).wait_send()
+            down_load(0).start()
+
+        @pl.loop(4 * h, 4 * h + 4)
+        def _(b):
+            @pl.when(b + 1 < 8)
+            def _():
+                down_load(b + 1).start()
+
+            down_load(b).wait()
+            part[:, down_at(b)] = nn(hidden[...], down_blocks[b % 2]).astype(BF)
+
+        if h == 1:
+            for j in peers:
+                out_send(j).start()
+
+    def dh_load(b):
+        block = wqkv.at[pl.ds(pl.multiple_of(b * half, half), half), :]
+        return pltpu.make_async_copy(block, qkv_blocks.at[b % 2], weight_s.at[b % 2, 0])
 
     def rms_back(gradient_of, x_ref, gain, acc, write):
         acc[...] = jnp.zeros_like(acc)
@@ -1535,12 +1577,13 @@
             write(at, inverse * (scaled - normed * jnp.mean(scaled * normed, axis=1, keepdims=True)))
 
     def piece_mixed():
-        locals_[0].wait()
+        for name in ("mixed", "branch_own", "gain_two"):
+            moves[name].wait()
         for j in peers:
             back_send(j).wait_recv()
 
         def gradient_of(at):
-            value = first_back[at, :].astype(F32)
+            value = part[at, :].astype(F32)
             for j in peers:
                 value = value + landed[j - 1, at, :].astype(F32)
             return value
@@ -1555,10 +1598,9 @@
             da_send(j).start()
 
     def piece_do():
-        locals_[2].wait()
+        moves["w_out"].wait()
         for j in peers:
             da_send(j).wait_recv()
-            out_send(j).start()
 
         @pl.loop(0, plane)
         def _(j):
@@ -1641,16 +1683,23 @@
             dqkv[j * rows : (j + 1) * rows, q_width : q_width + 128] = value
 
     def piece_dh():
-        locals_[3].wait()
-        for h in range(2):
-            for j in range(plane):
-                start = pl.multiple_of(((f ^ j) * 2 + (k ^ h)) * half, 128)
-                block = wqkv[(h * plane + j) * half : (h * plane + j + 1) * half, :]
-                wide[0:total, pl.ds(start, half)] = nt(dqkv[...], block).astype(BF)
+        dh_load(0).start()
+
+        @pl.loop(0, 2 * plane)
+        def _(b):
+            @pl.when(b + 1 < 2 * plane)
+            def _():
+                dh_load(b + 1).start()
+
+            dh_load(b).wait()
+            wide[0:total, columns_of(b // plane, b % plane)] = nt(dqkv[...], qkv_blocks[b % 2]).astype(BF)
+
         for j in peers:
             dh_send(j).start()
 
     def piece_input():
+        for name in ("x_own", "gain_one"):
+            moves[name].wait()
         for j in peers:
             dh_send(j).wait_recv()
 
@@ -1664,6 +1713,7 @@
             input_grad[at, :] = input_grad[at, :] + value
 
         rms_back(gradient_of, x_own, gain_one, gain_acc.at[0], write)
+        moves["input_grad"].start()
         place = lax.broadcasted_iota(jnp.int32, (16, depth), 0)
         one = jnp.sum(gain_acc[0], axis=0, keepdims=True)
         two = jnp.sum(gain_acc[1], axis=0, keepdims=True)
@@ -1672,61 +1722,76 @@
             gain_send(j).start()
 
     def piece_outputs():
-        locals_[1].wait()
         for j in peers:
             out_send(j).wait_recv()
 
         @pl.loop(0, rows // 16)
         def _(i):
             at = pl.ds(pl.multiple_of(i * 16, 16), 16)
-            value = mixed[at, :] + first_out[at, :].astype(F32)
+            value = mixed[at, :] + part[at, :].astype(F32)
             for j in peers:
                 value = value + landed_out[j - 1, at, :].astype(F32)
-            outputs[at, :] = value
+            mixed[at, :] = value
+
+        moves["outputs"].start()
 
     def piece_gain():
         for j in peers:
             gain_send(j).wait_recv()
 
-    give_lag, pair_lag, load_lag, in_lag, mid_lag, out_lag, keep_lag = LAGS
+    in_lag, mid_lag, out_lag, keep_lag = LAGS
     events = []
-    for c in loaded:
-        events.append((max(c + load_lag, 0), 1, stage_load, c))
+
+    def give_tick(c):
+        return c - (AHEAD[1] if kinds[chunks[c][0]][1] is not None else AHEAD[0])
+
     for c in heads:
-        events.append((c + give_lag, 0, stage_give, c))
-        events.append((c + pair_lag, 1, stage_pair, c))
+        events.append((give_tick(c), 0, stage_give, c))
+        events.append((give_tick(c) + 1, 1, stage_pair, c))
     for c in range(count):
         events.append((c + in_lag, 2, stage_in, c))
         events.append((c + mid_lag, 3, stage_mid, c))
         events.append((c + out_lag, 4, stage_out, c))
         events.append((c + keep_lag, 5, stage_keep, c))
-    steps = (piece_mixed, piece_do, piece_kv_line, piece_outputs, piece_kv_sum, piece_dh, piece_input, piece_gain)
-    events += [(tick, 6 + n, piece, None) for n, (piece, tick) in enumerate(zip(steps, STEPS))]
-    for j in range(0, plane, 2):
-        events.append((ATTEND[j // 2], 20 + j, piece_attend, j))
-    events.append((ATTEND[-1], 30, kv_pair.start, None))
-    first_qkv = [c for c in heads if chunks[c][0] == "qkv"][0]
-    last_up = [c for c in heads if chunks[c][0] == "up"][-1]
-    events.append((last_up + pair_lag, 31, locals_[5].start, None))
-    events.append((first_qkv + give_lag, -1, locals_[5].wait, None))
+    steps = (
+        (piece_back, 0), (piece_back, 1), piece_mixed, piece_do, (piece_out, 0), (piece_out, 1), (piece_attend, 0),
+        (piece_attend, 2), kv_pair.start, piece_kv_line, piece_kv_sum, piece_dh, piece_outputs, piece_input, piece_gain,
+    )
+    for n, (step, tick) in enumerate(zip(steps, STEPS)):
+        act, which = step if isinstance(step, tuple) else (step, None)
+        events.append((tick, 6 + n, act, which))
+
+    def head_of(name, which):
+        return [c for c in heads if chunks[c][0] == name][which]
+
+    def wait_for(*names):
+        def act():
+            for name in names:
+                moves[name].wait()
+
+        return act
+
+    events.append((give_tick(head_of("down", 0)), -1, wait_for("branch", "hidden"), None))
+    first = min(STEPS[0], give_tick(head_of("gate", 0)))
+    events.append((first, 5.2, wait_for("n2", "gate_back", "up_back"), None))
+    events.append((give_tick(head_of("down", -1)) + 1, 31, moves["w_out"].start, None))
+    events.append((give_tick(head_of("up", -1)) + 1, 31, moves["h1"].start, None))
+    events.append((give_tick(head_of("qkv", 0)), -1, moves["h1"].wait, None))
+    events.append((give_tick(head_of("out", 0)), -1, moves["attended"].wait, None))
+    attending = ("queries", "lse", "kv_all", "limits", "kp", "cosine", "sine")
+    events.append((STEPS[6], 5.5, wait_for(*attending), None))
     events.sort(key=lambda e: e[:2])
 
-    for j in peers:
-        back_send(j).start()
-    for c in loaded:
-        pair_copy(c).start()
-    for c in loaded[:2]:
-        load_copy(c).start()
-    for copy in locals_[:5]:
+    for name, move in moves.items():
+        if name not in ("w_out", "h1", "outputs", "input_grad"):
+            move.start()
+    for copy in weight_loads(0, 0):
         copy.start()
-    locals_[4].wait()
     for _, _, act, which in events:
         act() if which is None else act(which)
 
     for c in range(count):
-        given = kinds[chunks[c][0]][1]
-        later = [n for n in heads if n > c and kinds[chunks[n][0]][1] is given]
-        if c in loaded or not later:
+        if not [n for n in heads if n > c and given(n) is given(c)]:
             pair_copy(c).wait_send()
         if swapped(c):
             swap_copy(c).wait_send()
@@ -1743,8 +1808,9 @@
             mid_copy(c).wait_send()
             out_copy(c).wait_send()
 
+    moves["outputs"].wait()
+    moves["input_grad"].wait()
     for j in peers:
-        back_send(j).wait_send()
         out_send(j).wait_send()
         da_send(j).wait_send()
         dh_send(j).wait_send()
@@ -1757,20 +1823,18 @@
             kv_send(s).wait_send()
 
 
-def back_pass(
-    limits, own_down, other_down, back_part, out_part, w_out, wqkv, h1, n2, gate_back, up_back,
-    mixed, branch_own, x_own, gain_one, gain_two, attended, queries, lse, kv_all, kp, cosine, sine,
-):
+def back_pass(held, far):
     count, line = lax.axis_size("fsdp"), lax.axis_size("z")
+    mixed, attended, kv_all, hidden = held[4], held[8], held[11], held[3]
     rows, depth = mixed.shape
     total, half_depth = count * rows, depth // 2
     half = half_depth // count
     q_width = attended.shape[1]
+    ff = hidden.shape[1]
     keys = kv_all.shape[0] * rows
-    ff = gate_back.shape[1]
     slabs = (2 * count, half // 2, ff)
     shapes = [
-        own_down.shape,
+        (ff // 128, 128, half_depth),
         slabs,
         slabs,
         (4, q_width // 4, half_depth),
@@ -1778,29 +1842,31 @@
         (1, 16, depth),
     ]
     anywhere = pl.BlockSpec(memory_space=pl.ANY)
-    local = pl.BlockSpec(memory_space=pltpu.VMEM)
     ends = [jax.ShapeDtypeStruct(s, BF) for s in shapes]
     act = jax.ShapeDtypeStruct((rows, depth), F32)
     block = (rows, depth)
     chunk_count = sum(s[0] for s in shapes)
-    dma = lambda n: pltpu.SemaphoreType.DMA((n,))
+    dma = lambda *n: pltpu.SemaphoreType.DMA(n)
+    groups = (1, 2, 2, 2, 1)
     scratch = (
-        [pltpu.VMEM(s, BF) for s in shapes]
+        [pltpu.VMEM(x.shape, x.dtype) for x in held]
+        + [pltpu.VMEM(block, BF), pltpu.VMEM(block, F32)]
+        + [pltpu.VMEM(s, BF) for s in shapes]
         + [pltpu.VMEM((shapes[i][0] - 2,) + shapes[i][1:], BF) for i in (1, 2, 4)]
         + [pltpu.VMEM(s, BF) for s in shapes]
-        + [pltpu.VMEM((2,) + shapes[i][1:], BF) for i in (0, 1, 3, 4)]
-        + [pltpu.VMEM(shapes[5], BF)]
+        + [pltpu.VMEM((g,) + shapes[i][1:], BF) for g, i in zip(groups, (0, 1, 3, 4, 5))]
         + [
             pltpu.VMEM((count - 1,) + block, BF),
             pltpu.VMEM((count - 1,) + block, BF),
-            pltpu.VMEM(block, BF),
-            pltpu.VMEM(block, BF),
+            pltpu.VMEM((2, 2, half, ff), BF),
+            pltpu.VMEM((2, ff, depth // 8), BF),
+            pltpu.VMEM((2, half, q_width + 128), BF),
+            pltpu.VMEM((total, depth), BF),
             pltpu.VMEM((count,) + block, BF),
             pltpu.VMEM((max(total, q_width), depth), BF),
             pltpu.VMEM((count, rows, q_width), BF),
             pltpu.VMEM((total, q_width + 128), BF),
-            pltpu.VMEM(wqkv.shape, BF),
-            pltpu.VMEM(h1.shape, BF),
+            pltpu.VMEM((total, depth), BF),
             pltpu.VMEM((keys, 128), BF),
             pltpu.VMEM((keys, 128), F32),
             pltpu.VMEM((keys, 128), F32),
@@ -1811,8 +1877,8 @@
             pltpu.VMEM((2, 16, depth), F32),
             pltpu.VMEM((count, 16, depth), BF),
         ]
-        + [dma(chunk_count)] * 13
-        + [pltpu.SemaphoreType.REGULAR, dma(6)]
+        + [dma(chunk_count)] * 12
+        + [pltpu.SemaphoreType.REGULAR, dma(22), dma(2, 2)]
         + [dma(count - 1)] * 8
         + [dma(1)] * 2
         + [dma(line - 1)] * 2
@@ -1821,27 +1887,21 @@
     out = pl.pallas_call(
         back_kernel,
         out_shape=ends + ends + [act, act],
-        in_specs=[local] + [anywhere] * 8 + [local] * 14,
-        out_specs=[anywhere] * 12 + [local] * 2,
+        in_specs=[anywhere] * (len(held) + len(far)),
+        out_specs=[anywhere] * 14,
         scratch_shapes=scratch,
         compiler_params=pltpu.CompilerParams(
-            vmem_limit_bytes=62 * 1024 * 1024, has_side_effects=True
-        ),
-        cost_estimate=pl.CostEstimate(
-            flops=10**11, bytes_accessed=10**9, transcendentals=10**7
+            vmem_limit_bytes=63 * 1024 * 1024, has_side_effects=True
         ),
         name="back_pass",
-    )(
-        limits, own_down, other_down, back_part, out_part, w_out, wqkv, h1, n2, gate_back, up_back,
-        mixed, branch_own, x_own, gain_one, gain_two, attended, queries, lse, kv_all, kp, cosine, sine,
-    )
+    )(*held, *far)
     return out[:6], out[6:12], out[12], out[13]
 
 
 def finish_kernel(
     own_down, own_gate, own_up, own_out, own_qkv, own_gain, sib_down, sib_gate, sib_up, sib_out, sib_qkv,
-    down, gate, up, out, query, key, value, attn_gain, mlp_gain,
-    low_rows, low_cols, high_rows, high_cols, kv, kv_high, gain_in, gain_high, load_s, store_s, side_s,
+    outputs_in, input_grad_in, outputs, input_grad, down, gate, up, out, query, key, value, attn_gain, mlp_gain,
+    low_rows, low_cols, high_rows, high_cols, kv, acts, gain_in, gain_high, load_s, store_s, side_s,
 ):
     f, k = lax.axis_index("fsdp"), lax.axis_index("core")
     plane = lax.axis_size("fsdp")
@@ -1885,6 +1945,8 @@
         pltpu.make_async_copy(own_gain.at[0], gain_in, side_s.at[0]),
         pltpu.make_async_copy(own_qkv.at[:, :, pl.ds(q_width, 128)], kv.at[0], side_s.at[1]),
         pltpu.make_async_copy(sib_qkv.at[:, :, pl.ds(q_width, 128)], kv.at[1], side_s.at[2]),
+        pltpu.make_async_copy(outputs_in, acts.at[0], side_s.at[3]),
+        pltpu.make_async_copy(input_grad_in, acts.at[1], side_s.at[4]),
     ]
     for n in range(slots):
         load(n).start()
@@ -1908,6 +1970,12 @@
             load(n + slots).start()
     for copy in sides:
         copy.wait()
+    lasts = [
+        pltpu.make_async_copy(acts.at[0], outputs, side_s.at[5]),
+        pltpu.make_async_copy(acts.at[1], input_grad, side_s.at[6]),
+    ]
+    for copy in lasts:
+        copy.start()
     mine = pl.ds(pl.multiple_of(f * slab, 128), slab)
     gain_high[...] = gain_in[...].astype(F32)
     attn_gain[...] = gain_high[0:1, mine]
@@ -1923,9 +1991,11 @@
             value[rows_at, at] = jnp.where(lane < 64, pltpu.roll(first, 64, 1), second)
     for n in range(max(0, len(tasks) - slots), len(tasks)):
         store(n).wait()
-
-
-def finish(owns, sibs):
+    for copy in lasts:
+        copy.wait()
+
+
+def finish(owns, sibs, outputs, input_grad):
     plane = lax.axis_size("fsdp")
     down, gate, _, out, qkv, gain = (x.shape for x in owns)
     depth = 2 * down[2]
@@ -1933,6 +2003,7 @@
     q_width = qkv[2] - 128
     sds = jax.ShapeDtypeStruct
     shapes = [
+        outputs.shape, input_grad.shape,
         (down[0] * down[1], depth), (slab, plane * gate[2]), (slab, plane * gate[2]), (out[0] * out[1], depth),
         (slab, plane * q_width), (slab, KV_HEADS * HEAD_DIM), (slab, KV_HEADS * HEAD_DIM), (1, slab), (1, slab),
     ]
@@ -1944,24 +2015,24 @@
     return pl.pallas_call(
         finish_kernel,
         out_shape=[sds(s, F32) for s in shapes],
-        in_specs=[anywhere] * 11,
-        out_specs=[anywhere] * 5 + [local] * 4,
+        in_specs=[anywhere] * 13,
+        out_specs=[anywhere] * 7 + [local] * 4,
         scratch_shapes=[
             pltpu.VMEM(tall, BF),
             pltpu.VMEM(wide, BF),
             pltpu.VMEM(tall, F32),
             pltpu.VMEM(wide, F32),
             pltpu.VMEM((2, plane, gate[1], 128), BF),
-            pltpu.VMEM((16, 128), F32),
+            pltpu.VMEM((2,) + outputs.shape, F32),
             pltpu.VMEM(gain[1:], BF),
             pltpu.VMEM(gain[1:], F32),
             pltpu.SemaphoreType.DMA((count,)),
             pltpu.SemaphoreType.DMA((count,)),
-            pltpu.SemaphoreType.DMA((3,)),
+            pltpu.SemaphoreType.DMA((7,)),
         ],
         compiler_params=params(),
         name="finish",
-    )(*owns, *sibs[:5])
+    )(*owns, *sibs[:5], outputs, input_grad)
 
 
 def body(
@@ -1973,23 +2044,26 @@
     x_own = tokens.reshape(rows, depth)
     (
         h1, queries, lse, attended, mixed, n2, limits, cosine, sine, kp, gain_one, gain_two, kv_all, branch, wqkv,
-        gate_back, up_back, back_part, out_part, own_down, other_down,
+        gate_back, up_back, hidden, gate_own, gate_sib, up_own, up_sib,
     ) = front_pass(
         x_own, cotangent.reshape(rows, depth), lengths, attn_gain, mlp_gain,
         w_query, w_key, w_value, w_out, w_gate, w_up, w_down,
     )
-    own_down, other_down = (x.reshape(8, -1, depth // 2) for x in (own_down, other_down))
-    owns, sibs, outputs, input_grad = back_pass(
-        limits, own_down, other_down, back_part.reshape(count, rows, depth), out_part.reshape(count, rows, depth),
-        w_out, wqkv, h1, n2, gate_back, up_back,
-        mixed, branch[0], x_own, gain_one, gain_two, attended, queries, lse, kv_all, kp, cosine, sine,
+    held = (
+        limits, gate_back, up_back, hidden, mixed, x_own, gain_one, gain_two,
+        attended, queries, lse, kv_all, kp, cosine, sine,
     )
+    branch = branch.reshape(count * rows, depth)
+    far = (branch, w_out, w_down, wqkv, h1, n2, gate_own, gate_sib, up_own, up_sib)
+    owns, sibs, outputs, input_grad = back_pass(held, far)
 
     def whole(x):
         return x.reshape(4, -1, x.shape[2]) if x.shape[0] > 1 else x
 
     owns, sibs = [whole(x) for x in owns], [whole(x) for x in sibs]
-    down_grad, gate_grad, up_grad, out_grad, query_grad, key_grad, value_grad, gain_a, gain_m = finish(owns, sibs)
+    (
+        outputs, input_grad, down_grad, gate_grad, up_grad, out_grad, query_grad, key_grad, value_grad, gain_a, gain_m
+    ) = finish(owns, sibs, outputs, input_grad)
     return (
         outputs.reshape(seqs, rows, depth),
         input_grad.reshape(seqs, rows, depth),

time: 491 us -> 464 us (0.945)
  Pallas kernels: 479 us -> 457 us
  local copies, waits for them, and re-layouts: 6.35 us -> 1.36 us
    pallas_call x1, Pallas kernels: 159 us -> 140 us  [front_pass(): pl.pallas_call(front_kernel, out_shape=outs, in_specs=[pl.BlockSpec(memor...]
where the time goes in v7:
time: 464 us; the launch traced here: 461 us
  Pallas kernels  457 us (98%)
    pallas_call x1, Pallas kernels, back_pass(): pl.pallas_call(back_kernel, out_shape=ends + ends + [act, act], in_specs=...  293 us
    pallas_call x1, Pallas kernels, front_pass(): pl.pallas_call(front_kernel, out_shape=outs, in_specs=[pl.BlockSpec(memor...  140 us
    pallas_call x1, Pallas kernels, finish(): pl.pallas_call(finish_kernel, out_shape=[sds(s, F32) for s in shapes], in...  25.1 us

profile of v7, /device:TPU:0, one launch (start us, length us, event | category | flops | bytes accessed | tf_op | source)
XLA Modules:
  0.0 460.8 jit_solution(14518152393261385572)
XLA Ops:
  1.3 0.7 stack.9
  2.0 0.7 stack.10
  2.7 0.6 pad_maximum_fusion.both_gains
  3.2 139.5 %front_pass.1 = (bf16[512,2048]{1,0:T(8,128)(2,1)}, bf16[4,128,512]{2,1,0:T(8,128)(2,1)}, f32[4,128,512]{2,1,0:T(8,128)}, bf16[512,512]{1,0:T(8,128)(2,1)}, f32[...) custom-call(s32[1]{0:T(128)S(6)} %copy.27.length_ref, ...), custom_call_target="tpu_custom_call" | custom-call | tf_op jit(solution)/shard_map/front_pass/pallas_call | solution.py:1268
  142.8 292.7 %back_pass.1 = (bf16[11,128,1024]{2,1,0:T(8,128)(2,1)}, bf16[8,128,1408]{2,1,0:T(8,128)(2,1)}, bf16[8,128,1408]{2,1,0:T(8,128)(2,1)}, bf16[4,128,1024]{2,1,0:T(8...) custom-call(f32[4,128,128]{2,1,0:T(8,128)} %get-tuple-element.57.lim, ...), custom_call_target="tpu_custom_call" | custom-call | tf_op jit(solution)/shard_map/back_pass/pallas_call | solution.py:1887
  435.5 25.1 %finish.1 = (f32[128,2048]{1,0:T(8,128)}, f32[128,2048]{1,0:T(8,128)}, f32[1408,2048]{1,0:T(8,128)}, f32[512,5632]{1,0:T(8,128)}, f32[512,5632]{1,0:T(8,128)}, /...) custom-call(bf16[4,352,1024]{2,1,0:T(8,128)(2,1)} %bitcast.15, ...), custom_call_target="tpu_custom_call" | custom-call | tf_op jit(solution)/shard_map/finish/pallas_call | solution.py:2015

commit v8 on v7

--- a/solution.py
+++ b/solution.py
@@ -21,7 +21,7 @@
 VMEM_BYTES = 56 * 1024 * 1024
 LAGS = (0, 2, 4, 6)
 AHEAD = (1, 4)
-STEPS = (0, 1, 6, 11, 12, 13, 14, 16, 17, 19, 23, 23, 22, 27, 29)
+STEPS = (0, 1, 7, 12, 13, 14, 15, 16, 17, 18, 18, 20, 24, 24, 23, 28, 30)
 
 
 def params(**kw):
@@ -696,7 +696,7 @@
     gate_back, up_back, hidden, grad,
     notes, x_all, wqkv, keys_in, values_in, kv_give, gate_own, gate_sib, up_own, up_sib, down,
     kv_all, vk, w_o, part, landed, relay, relayed, n2_all, branch_all, cot_in,
-    local_s, store_s, note_s, note_r, tok_s, tok_r, tof_s, tof_r, wq_s, wq_r, wk_s, wk_r, wp_s, wp_r, wkp_s, wkp_r,
+    local_s, store_s, wx_s, wx_r, note_s, note_r, tok_s, tok_r, tof_s, tof_r, wq_s, wq_r, wk_s, wk_r, wp_s, wp_r, wkp_s, wkp_r,
     kz_s, kz_r, kp_s, kp_r, gt_s, gt_r, up_s, up_r, gz_s, gz_r, gs_s, gs_r, us_s, us_r,
     bt_s, bt_r, btf_s, btf_r, mx_s, mx_r, nt_s, nt_r, ntf_s, ntf_r,
 ):
@@ -790,6 +790,10 @@
         target = wqkv.at[pl.ds((plane + j) * half, half), :]
         return remote(source, target, wp_s.at[j - 1], wp_r.at[j - 1], sib)
 
+    def w_across(j):
+        block = wqkv.at[pl.ds(j * half, half), :]
+        return remote(block, block, wx_s.at[j - 1], wx_r.at[j - 1], {"z": across})
+
     def kv_send(s):
         return remote(kv_all.at[0], kv_all.at[s], kz_s.at[s - 1], kz_r.at[s - 1], {"z": z - s})
 
@@ -903,9 +907,8 @@
     notes[0] = note.astype(BF)
     for j in peers:
         note_send(j).start()
+    by_parity(lambda: wq_send(3).start(), lambda: [wq_send(j).start() for j in (1, 2)])
     token_gather.start()
-    for j in (3, 1, 2):
-        wq_send(j).start()
     for copy in local:
         copy.start()
 
@@ -923,7 +926,7 @@
 
     for j in (3, 1, 2):
         kv_give[j] = head_columns(j, 0)
-        wk_send(j).start()
+    by_parity(lambda: wk_send(3).start(), lambda: [wk_send(j).start() for j in (1, 2)])
     wqkv[0:half, q_width : q_width + 128] = head_columns(0, 0)
     wqkv[plane * half : (plane + 1) * half, q_width : q_width + 128] = head_columns(0, 1)
 
@@ -952,12 +955,14 @@
     valid = row_pos < jnp.full((rows, 1), length.astype(F32))
     branch_all[0] = jnp.where(valid, cot_in[...].astype(F32), 0.0).astype(BF)
 
-    token_gather.forward()
-    for j in (1, 2, 3):
+    def projections_on(j):
         wq_send(j).wait_recv()
         wk_send(j).wait_recv()
+        w_across(j).start()
         wp_send(j).start()
 
+    by_parity(lambda: projections_on(3), lambda: [projections_on(j) for j in (1, 2)])
+    token_gather.forward()
     fetch_start()
 
     for j in peers:
@@ -985,8 +990,18 @@
 
     local[0].wait()
     normalize(0, x_all.at[0])
-    normalize(1, x_all.at[1])
-    normalize(2, x_all.at[2])
+
+    def projections_in(js):
+        for j in js:
+            w_across(j).wait_recv()
+            wp_send(j).start()
+
+    by_parity(lambda: projections_in((1, 2)), lambda: projections_in((3,)))
+
+    @pl.loop(1, 3)
+    def _(j):
+        normalize(j, x_all.at[j])
+
     token_gather.arrive()
     normalize(3, x_all.at[3])
     local[3].wait()
@@ -1116,6 +1131,19 @@
 
     n2_gather.start()
     early_stores[4].start()
+
+    def pack(j):
+        @pl.loop(0, rows // 16)
+        def _(i):
+            at = pl.ds(pl.multiple_of(i * 16, 16), 16)
+            to = pl.ds(pl.multiple_of(j * rows + i * 16, 16), 16)
+            for h in range(2):
+                for b in range(plane):
+                    from_ = pl.ds(pl.multiple_of(((f ^ b) * 2 + (k ^ h)) * half, 128), half)
+                    c = (h * plane + b) * half
+                    n2[to, c : c + half] = n2_all[j, at, from_]
+
+    pack(0)
     branch_gather.arrive()
     local[11].wait()
 
@@ -1124,6 +1152,11 @@
 
     by_columns(down_grad)
     n2_gather.forward()
+
+    @pl.loop(1, 3)
+    def _(j):
+        pack(j)
+
     cross_on(3)
     for n in range(7, 11):
         local[n].wait()
@@ -1135,17 +1168,7 @@
         copy.start()
     n2_gather.arrive()
 
-    @pl.loop(0, total // 16)
-    def _(i):
-        at = pl.ds(pl.multiple_of(i * 16, 16), 16)
-        j = i // (rows // 16)
-        from_row = pl.ds(pl.multiple_of((i % (rows // 16)) * 16, 16), 16)
-        for h in range(2):
-            for b in range(plane):
-                from_ = pl.ds(pl.multiple_of(((f ^ b) * 2 + (k ^ h)) * half, 128), half)
-                c = (h * plane + b) * half
-                n2[at, c : c + half] = n2_all[j, from_row, from_]
-
+    pack(3)
     early_stores[5].start()
     later = [store(n) for n in range(12, 18)]
     for n in range(3):
@@ -1176,11 +1199,14 @@
         copy.wait_send()
     for j in peers:
         note_send(j).wait_send()
-        wq_send(j).wait_send()
-        wk_send(j).wait_send()
         wp_send(j).wait_send()
         gate_pair(j).wait_send()
         up_pair(j).wait_send()
+    projections = (wq_send, wk_send, w_across)
+    by_parity(
+        lambda: [c(3).wait_send() for c in projections],
+        lambda: [c(j).wait_send() for j in (1, 2) for c in projections],
+    )
     by_parity(
         lambda: [c(j).wait_send() for j in peers for c in (gate_send, gate_across)],
         lambda: [c(j).wait_send() for j in peers for c in (up_send, up_across)],
@@ -1263,7 +1289,7 @@
         pltpu.VMEM((plane,) + act, BF),
         pltpu.VMEM(act, BF),
     ]
-    sems = [12, 22, 3, 3, 2, 2, 2, 2, 3, 3, 3, 3, 3, 3, 1, 1, 3, 3, 4, 4, 3, 3, 3, 3, 3, 3, 3, 3, 3, 3]
+    sems = [12, 22, 3, 3, 3, 3, 2, 2, 2, 2, 3, 3, 3, 3, 3, 3, 1, 1, 3, 3, 4, 4, 3, 3, 3, 3, 3, 3, 3, 3, 3, 3]
     sems += [2, 2, 2, 2, 6, 6, 2, 2, 2, 2]
     return pl.pallas_call(
         front_kernel,
@@ -1301,7 +1327,7 @@
     swap_gate, swap_up, swap_qkv,
     end_down, end_gate, end_up, end_out, end_qkv, end_gain,
     give_down, give_gate, give_out, give_qkv, give_gain,
-    landed, landed_out, weights, down_blocks, qkv_blocks, part, da_all, wide, do_all, dqkv, left,
+    turned, landed, landed_out, weights, down_blocks, qkv_blocks, part, da_all, wide, do_all, dqkv, left,
     vk, dk_sum, dv_sum, kv_part, kv_land, kv_mine, kv_line, gain_acc, gain_all,
     pair_s, pair_r, swap_s, swap_r, in_s, in_r, mid_s, mid_r, out_s, done_s, back_s, back_r, ready,
     local_s, weight_s, rs_s, rs_r, ro_s, ro_r, ag_s, ag_r, rq_s, rq_r, kp_s, kp_r, kz_s, kz_r, ga_s, ga_r,
@@ -1393,46 +1419,67 @@
     def back_copy(c):
         return remote(end(c), part_of(c, 5), back_s.at[c], back_r.at[c], {"core": 1 - k})
 
-    own_cols = pl.ds(pl.multiple_of(k * half_depth, 128), half_depth)
-    other_cols = pl.ds(pl.multiple_of((1 - k) * half_depth, 128), half_depth)
-
-    def slab_term(i, side, right):
-        start = side * half_depth + i * (half // 2)
-        return tn(left[:, start : start + half], right)
-
-    def term(c, side):
+    def term(c, side, act):
         name, i = chunks[c]
+        if name == "gain":
+            act(slice(None), gain_all[...].astype(F32).sum(axis=0))
+            return
+        start = pl.multiple_of((k ^ side) * half_depth, 128)
         if name == "down":
-            right = wide[0:total, (own_cols, other_cols)[side]]
-            return tn(hidden[:, i * 128 : (i + 1) * 128], right)
-        if name == "gate":
-            return slab_term(i, side, gate_back[...])
-        if name == "up":
-            return slab_term(i, side, up_back[...])
-        if name == "qkv":
-            return slab_term(i, side, dqkv[...])
-        if name == "out":
-            size = src_out.shape[1]
-            right = da_all[:, :, (own_cols, other_cols)[side]].reshape(total, half_depth)
-            return tn(attended[:, i * size : (i + 2) * size], right)
-        return gain_all[...].astype(F32).sum(axis=0)
+            size, width = 128, half_depth
+            turned[0:size, :] = hidden[:, i * size : (i + 1) * size].T
+        elif name == "out":
+            size, width = 2 * src_out.shape[1], half_depth
+            turned[0:size, :] = attended[:, i * size // 2 : i * size // 2 + size].T
+        else:
+            size, width = half, source(c).shape[1]
+            at = side * half_depth + i * (half // 2)
+            turned[0:size, :] = left[:, at : at + half].T
+
+        def block(first, span):
+            if name == "down":
+                right = wide[0:total, pl.ds(start + first, span)]
+            elif name == "out":
+                right = da_all[:, :, pl.ds(start + first, span)].reshape(total, span)
+            else:
+                right = {"gate": gate_back, "up": up_back, "qkv": dqkv}[name][:, pl.ds(first, span)]
+            act(pl.ds(first, span), nn(turned[0:size, :], right))
+
+        @pl.loop(0, width // 256)
+        def _(n):
+            block(pl.multiple_of(n * 256, 256), 256)
+
+        if width % 256:
+            block(width // 256 * 256, width % 256)
 
     def stage_give(c):
         slots = given(c)
         if c and given(c - 1) is slots:
             for n in range(group(c)):
                 pair_copy(c - 1 - n).wait_send()
-        slots[...] = term(c, 1).astype(BF).reshape(slots.shape)
+        size = slots.shape[1]
+
+        def act(lanes, value):
+            for n in range(group(c)):
+                slots[n, :, lanes] = value[n * size : (n + 1) * size].astype(BF)
+
+        term(c, 1, act)
         for n in range(group(c)):
             pair_copy(c + n).start()
 
     def stage_pair(c):
-        value = term(c, 0)
-        size = value.shape[0] // group(c)
         for n in range(group(c)):
             pair_copy(c + n).wait_recv()
-            target = source(c + n)
-            target[...] = (target[...].astype(F32) + value[n * size : (n + 1) * size]).astype(BF)
+        size = source(c).shape[0]
+
+        def act(lanes, value):
+            for n in range(group(c)):
+                target = source(c + n)
+                added = target[:, lanes].astype(F32) + value[n * size : (n + 1) * size]
+                target[:, lanes] = added.astype(BF)
+
+        term(c, 0, act)
+        for n in range(group(c)):
             if swapped(c + n):
                 swap_copy(c + n).start()
 
@@ -1606,12 +1653,7 @@
         def _(j):
             do_all[j] = nt(da_all[j], wide[0 : w_out.shape[0], :]).astype(BF)
 
-    def piece_attend(j0):
-        @pl.loop(j0, j0 + 2)
-        def _(j):
-            attend_one(j)
-
-    def attend_one(j):
+    def piece_attend(j):
         here = pl.ds(pl.multiple_of(j * rows, 16), rows)
         vk[...] = pltpu.roll(kv_all[:, j].reshape(vk.shape).astype(F32), 64, 1).astype(BF)
         dk_sum[...] = jnp.zeros_like(dk_sum)
@@ -1640,9 +1682,9 @@
                 parts.append(nn(back, keyed))
                 dk_sum[...] += tn(back, q_own)
                 dv_sum[...] += tn(weights.astype(BF), do_own)
-            turned = jnp.where(lane < 64, parts[0], parts[1]) * (HEAD_DIM**-0.5)
-            turned = turned * cosine[...] - swap_halves(turned) * sine[...]
-            dqkv[here, at] = turned.astype(BF)
+            rotated = jnp.where(lane < 64, parts[0], parts[1]) * (HEAD_DIM**-0.5)
+            rotated = rotated * cosine[...] - swap_halves(rotated) * sine[...]
+            dqkv[here, at] = rotated.astype(BF)
 
         dk = dk_sum[...]
         dv = dv_sum[...]
@@ -1678,8 +1720,8 @@
         lane = lax.broadcasted_iota(jnp.int32, (rows, 128), 1)
         for j in range(plane):
             value = kv_mine[0, j].astype(F32)
-            turned = value * cosine[...] - swap_halves(value) * sine[...]
-            value = jnp.where(lane < 64, turned, value).astype(BF)
+            rotated = value * cosine[...] - swap_halves(value) * sine[...]
+            value = jnp.where(lane < 64, rotated, value).astype(BF)
             dqkv[j * rows : (j + 1) * rows, q_width : q_width + 128] = value
 
     def piece_dh():
@@ -1755,7 +1797,7 @@
         events.append((c + keep_lag, 5, stage_keep, c))
     steps = (
         (piece_back, 0), (piece_back, 1), piece_mixed, piece_do, (piece_out, 0), (piece_out, 1), (piece_attend, 0),
-        (piece_attend, 2), kv_pair.start, piece_kv_line, piece_kv_sum, piece_dh, piece_outputs, piece_input, piece_gain,
+        (piece_attend, 1), (piece_attend, 2), (piece_attend, 3), kv_pair.start, piece_kv_line, piece_kv_sum, piece_dh, piece_outputs, piece_input, piece_gain,
     )
     for n, (step, tick) in enumerate(zip(steps, STEPS)):
         act, which = step if isinstance(step, tuple) else (step, None)
@@ -1856,6 +1898,7 @@
         + [pltpu.VMEM(s, BF) for s in shapes]
         + [pltpu.VMEM((g,) + shapes[i][1:], BF) for g, i in zip(groups, (0, 1, 3, 4, 5))]
         + [
+            pltpu.VMEM((max(half, q_width // 2, 128), total), BF),
             pltpu.VMEM((count - 1,) + block, BF),
             pltpu.VMEM((count - 1,) + block, BF),
             pltpu.VMEM((2, 2, half, ff), BF),
@@ -2007,7 +2050,7 @@
         (down[0] * down[1], depth), (slab, plane * gate[2]), (slab, plane * gate[2]), (out[0] * out[1], depth),
         (slab, plane * q_width), (slab, KV_HEADS * HEAD_DIM), (slab, KV_HEADS * HEAD_DIM), (1, slab), (1, slab),
     ]
-    slots = 4
+    slots = 6
     tall = (slots, max(down[1], out[1]), down[2])
     wide = (slots, gate[1], max(gate[2], q_width))
     count = 2 * (down[0] + out[0] + 3 * plane)

time: 464 us -> 455 us (0.981)
  Pallas kernels: 457 us -> 450 us
    pallas_call x1, Pallas kernels: 140 us -> 133 us  [front_pass(): pl.pallas_call(front_kernel, out_shape=outs, in_specs=[pl.BlockSpec(memor...]
where the time goes in v8:
time: 455 us; the launch traced here: 453 us
  Pallas kernels  450 us (99%)
    pallas_call x1, Pallas kernels, back_pass(): pl.pallas_call(back_kernel, out_shape=ends + ends + [act, act], in_specs=...  292 us
    pallas_call x1, Pallas kernels, front_pass(): pl.pallas_call(front_kernel, out_shape=outs, in_specs=[pl.BlockSpec(memor...  133 us
    pallas_call x1, Pallas kernels, finish(): pl.pallas_call(finish_kernel, out_shape=[sds(s, F32) for s in shapes], in...  24.5 us

profile of v8, /device:TPU:0, one launch (start us, length us, event | category | flops | bytes accessed | tf_op | source)
XLA Modules:
  0.0 453.3 jit_solution(12686001441409218967)
XLA Ops:
  1.3 0.7 stack.9
  2.0 0.7 stack.10
  2.7 0.6 pad_maximum_fusion.both_gains
  3.2 133.3 %front_pass.1 = (bf16[512,2048]{1,0:T(8,128)(2,1)}, bf16[4,128,512]{2,1,0:T(8,128)(2,1)}, f32[4,128,512]{2,1,0:T(8,128)}, bf16[512,512]{1,0:T(8,128)(2,1)}, f32[...) custom-call(s32[1]{0:T(128)S(6)} %copy.27.length_ref, ...), custom_call_target="tpu_custom_call" | custom-call | tf_op jit(solution)/shard_map/front_pass/pallas_call | solution.py:1294
  136.5 292.1 %back_pass.1 = (bf16[11,128,1024]{2,1,0:T(8,128)(2,1)}, bf16[8,128,1408]{2,1,0:T(8,128)(2,1)}, bf16[8,128,1408]{2,1,0:T(8,128)(2,1)}, bf16[4,128,1024]{2,1,0:T(8...) custom-call(f32[4,128,128]{2,1,0:T(8,128)} %get-tuple-element.57.lim, ...), custom_call_target="tpu_custom_call" | custom-call | tf_op jit(solution)/shard_map/back_pass/pallas_call | solution.py:1930
  428.6 24.5 %finish.1 = (f32[128,2048]{1,0:T(8,128)}, f32[128,2048]{1,0:T(8,128)}, f32[1408,2048]{1,0:T(8,128)}, f32[512,5632]{1,0:T(8,128)}, f32[512,5632]{1,0:T(8,128)}, /...) custom-call(bf16[4,352,1024]{2,1,0:T(8,128)(2,1)} %bitcast.15, ...), custom_call_target="tpu_custom_call" | custom-call | tf_op jit(solution)/shard_map/finish/pallas_call | solution.py:2058

commit v9 on v8

--- a/solution.py
+++ b/solution.py
@@ -687,7 +687,7 @@
 
 
 def front_kernel(
-    length_ref, both_gains, start_cos, start_sin, step_cos, step_sin,
+    length_ref, attn_gain, mlp_gain, start_cos, start_sin, step_cos, step_sin,
     tokens, cotangent, w_query, w_key, w_value, w_out, w_gate, w_up, w_down,
     h1_out, queries_out, lse_out, attended_out, mixed_out, n2_out, limits_out, cosine_out, sine_out, kp_out,
     gain_one_out, gain_two_out, kv_out, branch_out, wqkv_out, gate_back_out, up_back_out, hidden_out,
@@ -902,7 +902,7 @@
     length = length_ref[0]
     place = lax.broadcasted_iota(jnp.int32, (16, slab), 0)
     high, low = (length // 64).astype(F32), (length % 64).astype(F32)
-    note = jnp.where(place == 0, both_gains[0:1, :].astype(F32), both_gains[1:2, :].astype(F32))
+    note = jnp.where(place == 0, attn_gain[...].astype(F32)[None, :], mlp_gain[...].astype(F32)[None, :])
     note = jnp.where(place == 2, high, jnp.where(place == 3, low, note))
     notes[0] = note.astype(BF)
     for j in peers:
@@ -1294,7 +1294,7 @@
     return pl.pallas_call(
         front_kernel,
         out_shape=outs,
-        in_specs=[pl.BlockSpec(memory_space=pltpu.SMEM)] + [local] * 5 + [anywhere] * 9,
+        in_specs=[pl.BlockSpec(memory_space=pltpu.SMEM)] + [local] * 6 + [anywhere] * 9,
         out_specs=[anywhere] * 22,
         scratch_shapes=scratch + [dma(n) for n in sems],
         compiler_params=pltpu.CompilerParams(
@@ -1302,7 +1302,7 @@
         ),
         name="front_pass",
     )(
-        lengths, jnp.stack([attn_gain, mlp_gain]), *rotary_parts(slot, rows),
+        lengths, attn_gain, mlp_gain, *rotary_parts(slot, rows),
         tokens, cotangent, w_query, w_key, w_value, w_out, w_gate, w_up, w_down,
     )
 
@@ -1356,6 +1356,7 @@
         "gain": (src_gain, None, end_gain, give_gain, fin_gain, sib_gain),
     }
     chunks = [(name, i) for name, kind in kinds.items() for i in range(kind[0].shape[0])]
+    chunks.insert(len(chunks) - 5, chunks.pop())
     count = len(chunks)
 
     def group(c):
@@ -1454,9 +1455,8 @@
 
     def stage_give(c):
         slots = given(c)
-        if c and given(c - 1) is slots:
-            for n in range(group(c)):
-                pair_copy(c - 1 - n).wait_send()
+        for n in [n for n in range(c) if given(n) is slots][-group(c) :]:
+            pair_copy(n).wait_send()
         size = slots.shape[1]
 
         def act(lanes, value):
@@ -2050,7 +2050,7 @@
         (down[0] * down[1], depth), (slab, plane * gate[2]), (slab, plane * gate[2]), (out[0] * out[1], depth),
         (slab, plane * q_width), (slab, KV_HEADS * HEAD_DIM), (slab, KV_HEADS * HEAD_DIM), (1, slab), (1, slab),
     ]
-    slots = 6
+    slots = 8
     tall = (slots, max(down[1], out[1]), down[2])
     wide = (slots, gate[1], max(gate[2], q_width))
     count = 2 * (down[0] + out[0] + 3 * plane)

time: 455 us -> 452 us (level)
  no operation moved by 1% of the time
where the time goes in v9:
time: 452 us; the launch traced here: 451 us
  Pallas kernels  450 us (100%)
    pallas_call x1, Pallas kernels, back_pass(): pl.pallas_call(back_kernel, out_shape=ends + ends + [act, act], in_specs=...  292 us
    pallas_call x1, Pallas kernels, front_pass(): pl.pallas_call(front_kernel, out_shape=outs, in_specs=[pl.BlockSpec(memor...  133 us
    pallas_call x1, Pallas kernels, finish(): pl.pallas_call(finish_kernel, out_shape=[sds(s, F32) for s in shapes], in...  24.1 us

profile of v9, /device:TPU:0, one launch (start us, length us, event | category | flops | bytes accessed | tf_op | source)
XLA Modules:
  0.0 451.1 jit_solution(4212995862761953168)
XLA Ops:
  1.3 133.4 %front_pass.1 = (bf16[512,2048]{1,0:T(8,128)(2,1)}, bf16[4,128,512]{2,1,0:T(8,128)(2,1)}, f32[4,128,512]{2,1,0:T(8,128)}, bf16[512,512]{1,0:T(8,128)(2,1)}, f32[...) custom-call(s32[1]{0:T(128)S(6)} %copy.27.length_ref, ...), custom_call_target="tpu_custom_call" | custom-call | tf_op jit(solution)/shard_map/front_pass/pallas_call | solution.py:1294
  134.7 292.2 %back_pass.1 = (bf16[11,128,1024]{2,1,0:T(8,128)(2,1)}, bf16[8,128,1408]{2,1,0:T(8,128)(2,1)}, bf16[8,128,1408]{2,1,0:T(8,128)(2,1)}, bf16[4,128,1024]{2,1,0:T(8...) custom-call(f32[4,128,128]{2,1,0:T(8,128)} %get-tuple-element.57.lim, ...), custom_call_target="tpu_custom_call" | custom-call | tf_op jit(solution)/shard_map/back_pass/pallas_call | solution.py:1930
  426.9 24.1 %finish.1 = (f32[128,2048]{1,0:T(8,128)}, f32[128,2048]{1,0:T(8,128)}, f32[1408,2048]{1,0:T(8,128)}, f32[512,5632]{1,0:T(8,128)}, f32[512,5632]{1,0:T(8,128)}, /...) custom-call(bf16[4,352,1024]{2,1,0:T(8,128)(2,1)} %bitcast.15, ...), custom_call_target="tpu_custom_call" | custom-call | tf_op jit(solution)/shard_map/finish/pallas_call | solution.py:2058

commit v10 on v9

--- a/solution.py
+++ b/solution.py
@@ -1788,7 +1788,7 @@
         return c - (AHEAD[1] if kinds[chunks[c][0]][1] is not None else AHEAD[0])
 
     for c in heads:
-        events.append((give_tick(c), 0, stage_give, c))
+        events.append((give_tick(c), 4.5, stage_give, c))
         events.append((give_tick(c) + 1, 1, stage_pair, c))
     for c in range(count):
         events.append((c + in_lag, 2, stage_in, c))

time: 452 us -> 453 us (level)
  no operation moved by 1% of the time
where the time goes in v10:
time: 453 us; the launch traced here: 452 us
  Pallas kernels  451 us (100%)
    pallas_call x1, Pallas kernels, back_pass(): pl.pallas_call(back_kernel, out_shape=ends + ends + [act, act], in_specs=...  293 us
    pallas_call x1, Pallas kernels, front_pass(): pl.pallas_call(front_kernel, out_shape=outs, in_specs=[pl.BlockSpec(memor...  133 us
    pallas_call x1, Pallas kernels, finish(): pl.pallas_call(finish_kernel, out_shape=[sds(s, F32) for s in shapes], in...  24.1 us

profile of v10, /device:TPU:0, one launch (start us, length us, event | category | flops | bytes accessed | tf_op | source)
XLA Modules:
  0.0 452.1 jit_solution(16902687335047284179)
XLA Ops:
  1.3 133.4 %front_pass.1 = (bf16[512,2048]{1,0:T(8,128)(2,1)}, bf16[4,128,512]{2,1,0:T(8,128)(2,1)}, f32[4,128,512]{2,1,0:T(8,128)}, bf16[512,512]{1,0:T(8,128)(2,1)}, f32[...) custom-call(s32[1]{0:T(128)S(6)} %copy.27.length_ref, ...), custom_call_target="tpu_custom_call" | custom-call | tf_op jit(solution)/shard_map/front_pass/pallas_call | solution.py:1294
  134.7 293.1 %back_pass.1 = (bf16[11,128,1024]{2,1,0:T(8,128)(2,1)}, bf16[8,128,1408]{2,1,0:T(8,128)(2,1)}, bf16[8,128,1408]{2,1,0:T(8,128)(2,1)}, bf16[4,128,1024]{2,1,0:T(8...) custom-call(f32[4,128,128]{2,1,0:T(8,128)} %get-tuple-element.57.lim, ...), custom_call_target="tpu_custom_call" | custom-call | tf_op jit(solution)/shard_map/back_pass/pallas_call | solution.py:1930
  427.8 24.1 %finish.1 = (f32[128,2048]{1,0:T(8,128)}, f32[128,2048]{1,0:T(8,128)}, f32[1408,2048]{1,0:T(8,128)}, f32[512,5632]{1,0:T(8,128)}, f32[512,5632]{1,0:T(8,128)}, /...) custom-call(bf16[4,352,1024]{2,1,0:T(8,128)(2,1)} %bitcast.15, ...), custom_call_target="tpu_custom_call" | custom-call | tf_op jit(solution)/shard_map/finish/pallas_call | solution.py:2058
